TPU v7x, 32 devices: a whole 2x2x4 slice. The times are simulated.
32 devices in a mesh: seq: 4 (over y, x), batch: 8 (over z, core).
Axes of the slice: x: 2, y: 2, z: 4, core: 2. Of those that a mesh axis runs over, the one named last changes fastest.
Arguments:
- layer_input: bfloat16 [16, 1024, 1536], P('batch', 'seq'), may hold values from -6 to 6
- cotangent: bfloat16 [16, 1024, 1536], P('batch', 'seq'), may hold values from -6 to 6
- token_mask: int32 [16, 1024], P('batch', 'seq'), may hold values 0 or 1
- document_ids: int32 [16, 1024], P('batch'), may hold values from 0 to 3, never falling along the last dimension, each value on 1 to 512 neighbouring positions
- attn_gain: bfloat16 [1536], P(('seq', 'batch')), may hold values from 0.099609375 to 1.8984375
- w_query: bfloat16 [1536, 1536], P(('seq', 'batch')), may hold values from -0.15625 to 0.15625
- w_key: bfloat16 [1536, 768], P(('seq', 'batch')), may hold values from -0.15625 to 0.15625
- w_value: bfloat16 [1536, 768], P(('seq', 'batch')), may hold values from -0.15625 to 0.15625
- w_output: bfloat16 [1536, 1536], P(('seq', 'batch')), may hold values from -1.75 to 1.75
- mlp_gain: bfloat16 [1536], P(('seq', 'batch')), may hold values from 0.099609375 to 1.8984375
- w_gate: bfloat16 [1536, 4096], P(('seq', 'batch')), may hold values from -0.15625 to 0.15625
- w_up: bfloat16 [1536, 4096], P(('seq', 'batch')), may hold values from -0.15625 to 0.15625
- w_down: bfloat16 [4096, 1536], P(('seq', 'batch')), may hold values from -0.09375 to 0.09375
Outputs:
- layer_output: bfloat16 [16, 1024, 1536], P('batch', 'seq')
- input_grad: bfloat16 [16, 1024, 1536], P('batch', 'seq')
- grad_attn_gain: float32 [1536], P(('seq', 'batch'))
- grad_query: float32 [1536, 1536], P(('seq', 'batch'))
- grad_key: float32 [1536, 768], P(('seq', 'batch'))
- grad_value: float32 [1536, 768], P(('seq', 'batch'))
- grad_output: float32 [1536, 1536], P(('seq', 'batch'))
- grad_mlp_gain: float32 [1536], P(('seq', 'batch'))
- grad_gate: float32 [1536, 4096], P(('seq', 'batch'))
- grad_up: float32 [1536, 4096], P(('seq', 'batch'))
- grad_down: float32 [4096, 1536], P(('seq', 'batch'))
Inputs may be any that keep to these rules, and one draw needn't show every extreme that they name: `document_ids`: along each sequence the document numbers never fall; each document holds at most 512 positions, and one holds exactly that many.
All inputs are finite; a program needn't handle non-finite values. No bound on the sum of `token_mask` on one device may be relied on, other than what follows from the above.
Results may differ from a plain program's by a relative error of at most 0.014.
The roundings to bfloat16 on the way count: a program that leaves them out, or rounds other values in their place, can miss the bound.
Values may be sent and summed in bfloat16 or wider, within the bound.
A program may use at most 320 MiB of HBM per device.

v0:
```python
import math

import jax
import jax.numpy as jnp
from jax import lax
from jax.sharding import PartitionSpec as P

HEADS = 16
KV = 8
HD = 96


EPSILON = 1e-05
ROPE_BASE = 10000.0


def inverse_rms(field):
    return lax.rsqrt(jnp.mean(field * field, axis=-1, keepdims=True) + EPSILON)


def half_turn(field):
    middle = field.shape[-1] // 2
    return jnp.concatenate([-field[..., middle:], field[..., :middle]], axis=-1)


def rope_tables(length, width):
    middle = width // 2
    freqs = ROPE_BASE ** (-2.0 * jnp.arange(middle, dtype=jnp.float32) / width)
    angles = jnp.arange(length, dtype=jnp.float32)[:, None] * freqs[None, :]
    cosine = jnp.concatenate([jnp.cos(angles), jnp.cos(angles)], axis=-1)
    sine = jnp.concatenate([jnp.sin(angles), jnp.sin(angles)], axis=-1)
    return (cosine, sine)


def rotate_ahead(field, cosine, sine):
    return field * cosine[:, None, :] + half_turn(field) * sine[:, None, :]


def rotate_behind(field, cosine, sine):
    return field * cosine[:, None, :] - half_turn(field) * sine[:, None, :]


def outer_sum(left, right):
    return lax.dot_general(
        left, right, (((0,), (0,)), ((), ())), preferred_element_type=jnp.float32
    )


def back_product(left, right):
    return lax.dot_general(
        left, right, (((1,), (1,)), ((), ())), preferred_element_type=jnp.float32
    )


def fetch_attention(attn_gain, w_query, w_key, w_value, w_output):
    return (
        lax.all_gather(attn_gain, ("seq", "batch"), axis=0, tiled=True),
        lax.all_gather(w_query, ("seq", "batch"), axis=0, tiled=True),
        lax.all_gather(w_key, ("seq", "batch"), axis=0, tiled=True),
        lax.all_gather(w_value, ("seq", "batch"), axis=0, tiled=True),
        lax.all_gather(w_output, ("seq", "batch"), axis=0, tiled=True),
    )


def fetch_feedforward(mlp_gain, w_gate, w_up, w_down):
    return (
        lax.all_gather(mlp_gain, ("seq", "batch"), axis=0, tiled=True),
        lax.all_gather(w_gate, ("seq", "batch"), axis=0, tiled=True),
        lax.all_gather(w_up, ("seq", "batch"), axis=0, tiled=True),
        lax.all_gather(w_down, ("seq", "batch"), axis=0, tiled=True),
    )


def block_scores(query_block, keys, documents, start, block, scale):
    length = keys.shape[0]
    scores = (
        jnp.einsum("qjhd,kjd->jhqk", query_block, keys, preferred_element_type=jnp.float32) * scale
    )
    key_pos = jnp.arange(length, dtype=jnp.int32)
    query_pos = start + jnp.arange(block, dtype=jnp.int32)
    query_docs = lax.dynamic_slice_in_dim(documents, start, block, 0)
    allowed = (key_pos[None, :] <= query_pos[:, None]) & (query_docs[:, None] == documents[None, :])
    return jnp.where(allowed[None, None], scores, -1e30)


def attention_forward(queries, keys, values, documents, block, scale):
    length = queries.shape[0]
    count = length // block

    def one_block(index):
        start = index * block
        query_block = lax.dynamic_slice_in_dim(queries, start, block, 0)
        scores = block_scores(query_block, keys, documents, start, block, scale)
        peak_score = jnp.max(scores, axis=-1, keepdims=True)
        weights = jnp.exp(scores - peak_score)
        totals = jnp.sum(weights, axis=-1, keepdims=True)
        probs = (weights / totals).astype(jnp.bfloat16)
        result = jnp.einsum("jhqk,kjd->qjhd", probs, values, preferred_element_type=jnp.float32)
        return (
            result.astype(jnp.bfloat16).reshape(block, -1),
            (peak_score + jnp.log(totals))[..., 0],
        )

    results, sums = lax.map(one_block, jnp.arange(count, dtype=jnp.int32))
    return (results.reshape(length, -1), sums)


def attention_backward(queries, keys, values, documents, sums, grad_out, block, scale):
    length = queries.shape[0]
    count = length // block

    def one_block(carry, member):
        grad_keys, grad_values = carry
        index, sums_block = member
        start = index * block
        query_block = lax.dynamic_slice_in_dim(queries, start, block, 0)
        grad_block = lax.dynamic_slice_in_dim(grad_out, start, block, 0)
        scores = block_scores(query_block, keys, documents, start, block, scale)
        probs = jnp.exp(scores - sums_block[..., None])
        grad_probs = jnp.einsum(
            "qjhd,kjd->jhqk", grad_block, values, preferred_element_type=jnp.float32
        )
        centre = jnp.sum(probs * grad_probs, axis=-1, keepdims=True)
        grad_scores = (probs * (grad_probs - centre)).astype(jnp.bfloat16)
        grad_query = (
            jnp.einsum("jhqk,kjd->qjhd", grad_scores, keys, preferred_element_type=jnp.float32)
            * scale
        )
        grad_keys = (
            grad_keys
            + jnp.einsum(
                "jhqk,qjhd->kjd", grad_scores, query_block, preferred_element_type=jnp.float32
            )
            * scale
        )
        grad_values = grad_values + jnp.einsum(
            "jhqk,qjhd->kjd",
            probs.astype(jnp.bfloat16),
            grad_block,
            preferred_element_type=jnp.float32,
        )
        return ((grad_keys, grad_values), grad_query)

    empty = jnp.zeros(keys.shape, jnp.float32)
    (grad_keys, grad_values), grad_query = lax.scan(
        one_block, (empty, empty), (jnp.arange(count, dtype=jnp.int32), sums)
    )
    return (
        grad_query.reshape(length, queries.shape[1] * queries.shape[2], queries.shape[3]),
        grad_keys,
        grad_values,
    )


def body(
    layer_input,
    cotangent,
    token_mask,
    document_ids,
    attn_gain,
    w_query,
    w_key,
    w_value,
    w_output,
    mlp_gain,
    w_gate,
    w_up,
    w_down,
):
    parts = lax.axis_size("seq")
    micro_count = layer_input.shape[0]
    shard = layer_input.shape[1]
    length = shard * parts
    heads_here = HEADS // parts
    kv_here = max(1, KV // parts)
    copies = parts * kv_here // KV
    per_kv = heads_here // kv_here
    block = min(512, length)
    scale = 1.0 / math.sqrt(HD)
    cosine, sine = rope_tables(length, HD)
    attn_set = None
    mlp_set = None
    attn_total = None
    mlp_total = None
    outputs = []
    input_grads = []
    kept = {
        "normed": [],
        "normed_two": [],
        "activated": [],
        "seed_low": [],
        "gate_low": [],
        "up_low": [],
        "grad_low": [],
        "mixed": [],
        "query_back": [],
        "key_back": [],
        "value_back": [],
    }
    gain_one_total = None
    gain_two_total = None
    for micro in range(micro_count):
        attn_set = fetch_attention(attn_gain, w_query, w_key, w_value, w_output)
        mlp_set = fetch_feedforward(mlp_gain, w_gate, w_up, w_down)
        gain_one = attn_set[0].astype(jnp.float32)
        gain_two = mlp_set[0].astype(jnp.float32)
        documents = document_ids[micro]
        inputs = layer_input[micro].astype(jnp.float32)
        inv_one = inverse_rms(inputs)
        unit_one = inputs * inv_one
        normed = (unit_one * gain_one).astype(jnp.bfloat16)
        queries = jnp.dot(normed, attn_set[1], preferred_element_type=jnp.float32).astype(
            jnp.bfloat16
        )
        keys_lin = jnp.dot(normed, attn_set[2], preferred_element_type=jnp.float32).astype(
            jnp.bfloat16
        )
        values_lin = jnp.dot(normed, attn_set[3], preferred_element_type=jnp.float32).astype(
            jnp.bfloat16
        )
        queries = queries.reshape(shard, parts, heads_here * HD)
        key_slots = jnp.repeat(keys_lin.reshape(shard, KV, HD), copies, axis=1).reshape(
            shard, parts, kv_here * HD
        )
        value_slots = jnp.repeat(values_lin.reshape(shard, KV, HD), copies, axis=1).reshape(
            shard, parts, kv_here * HD
        )
        pairs = jnp.concatenate([key_slots, value_slots], axis=-1)
        query_heads, pair_heads = (
            lax.all_to_all(queries, "seq", split_axis=1, concat_axis=0, tiled=True),
            lax.all_to_all(pairs, "seq", split_axis=1, concat_axis=0, tiled=True),
        )
        query_rot = rotate_ahead(
            query_heads.reshape(length, heads_here, HD).astype(jnp.float32), cosine, sine
        )
        query_rot = query_rot.astype(jnp.bfloat16).reshape(length, kv_here, per_kv, HD)
        key_heads = pair_heads[:, 0, : kv_here * HD].reshape(length, kv_here, HD)
        key_rot = rotate_ahead(key_heads.astype(jnp.float32), cosine, sine).astype(jnp.bfloat16)
        value_heads = pair_heads[:, 0, kv_here * HD :].reshape(length, kv_here, HD)
        attended, sums = attention_forward(query_rot, key_rot, value_heads, documents, block, scale)
        mixed = lax.all_to_all(
            attended.reshape(length, 1, heads_here * HD),
            "seq",
            split_axis=0,
            concat_axis=1,
            tiled=True,
        )
        mixed = mixed.reshape(shard, HEADS * HD)
        hidden_state = inputs + jnp.dot(mixed, attn_set[4], preferred_element_type=jnp.float32)
        inv_two = inverse_rms(hidden_state)
        unit_two = hidden_state * inv_two
        normed_two = (unit_two * gain_two).astype(jnp.bfloat16)
        gate = jnp.dot(normed_two, mlp_set[1], preferred_element_type=jnp.float32)
        upward = jnp.dot(normed_two, mlp_set[2], preferred_element_type=jnp.float32)
        sigma = jax.nn.sigmoid(gate)
        activated = (gate * sigma * upward).astype(jnp.bfloat16)
        output = hidden_state + jnp.dot(activated, mlp_set[3], preferred_element_type=jnp.float32)
        outputs.append(output.astype(jnp.bfloat16))
        seed = cotangent[micro].astype(jnp.float32) * token_mask[micro].astype(jnp.float32)[:, None]
        seed_low = seed.astype(jnp.bfloat16)
        grad_act = back_product(seed_low, mlp_set[3])
        grad_up_low = (grad_act * gate * sigma).astype(jnp.bfloat16)
        grad_gate_low = (grad_act * upward * sigma * (1.0 + gate * (1.0 - sigma))).astype(
            jnp.bfloat16
        )
        grad_normed_two = back_product(grad_gate_low, mlp_set[1]) + back_product(
            grad_up_low, mlp_set[2]
        )
        grad_gain_two = jnp.sum(grad_normed_two * unit_two, axis=0)
        scaled_two = grad_normed_two * gain_two
        grad_hidden = seed + inv_two * (
            scaled_two - unit_two * jnp.mean(scaled_two * unit_two, axis=-1, keepdims=True)
        )
        gain_two_total = grad_gain_two if gain_two_total is None else gain_two_total + grad_gain_two
        kept["normed_two"].append(normed_two)
        kept["activated"].append(activated)
        kept["seed_low"].append(seed_low)
        kept["gate_low"].append(grad_gate_low)
        kept["up_low"].append(grad_up_low)
        grad_low = grad_hidden.astype(jnp.bfloat16)
        grad_mixed = (
            back_product(grad_low, attn_set[4])
            .astype(jnp.bfloat16)
            .reshape(shard, parts, heads_here * HD)
        )
        grad_heads = lax.all_to_all(
            grad_mixed, "seq", split_axis=1, concat_axis=0, tiled=True
        ).reshape(length, kv_here, per_kv, HD)
        grad_query_rot, grad_key_rot, grad_values = attention_backward(
            query_rot, key_rot, value_heads, documents, sums, grad_heads, block, scale
        )
        grad_query_heads = (
            rotate_behind(grad_query_rot, cosine, sine)
            .astype(jnp.bfloat16)
            .reshape(length, 1, heads_here * HD)
        )
        grad_key_heads = rotate_behind(grad_key_rot, cosine, sine)
        grad_pairs = jnp.concatenate(
            [
                grad_key_heads.reshape(length, kv_here * HD),
                grad_values.reshape(length, kv_here * HD),
            ],
            axis=-1,
        )
        query_back = lax.all_to_all(
            grad_query_heads, "seq", split_axis=0, concat_axis=1, tiled=True
        ).reshape(shard, HEADS * HD)
        pair_back = lax.all_to_all(
            grad_pairs.reshape(length, 1, 2 * kv_here * HD).astype(jnp.bfloat16),
            "seq",
            split_axis=0,
            concat_axis=1,
            tiled=True,
        ).astype(jnp.float32)
        key_back = pair_back[:, :, : kv_here * HD].reshape(shard, KV, copies, HD).sum(axis=2)
        value_back = pair_back[:, :, kv_here * HD :].reshape(shard, KV, copies, HD).sum(axis=2)
        key_back = key_back.reshape(shard, KV * HD).astype(jnp.bfloat16)
        value_back = value_back.reshape(shard, KV * HD).astype(jnp.bfloat16)
        grad_normed = (
            back_product(query_back, attn_set[1])
            + back_product(key_back, attn_set[2])
            + back_product(value_back, attn_set[3])
        )
        grad_gain_one = jnp.sum(grad_normed * unit_one, axis=0)
        scaled_one = grad_normed * gain_one
        grad_input = grad_hidden + inv_one * (
            scaled_one - unit_one * jnp.mean(scaled_one * unit_one, axis=-1, keepdims=True)
        )
        input_grads.append(grad_input.astype(jnp.bfloat16))
        gain_one_total = grad_gain_one if gain_one_total is None else gain_one_total + grad_gain_one
        kept["normed"].append(normed)
        kept["mixed"].append(mixed)
        kept["grad_low"].append(grad_low)
        kept["query_back"].append(query_back)
        kept["key_back"].append(key_back)
        kept["value_back"].append(value_back)
    rows = {name: jnp.concatenate(values, axis=0) for name, values in kept.items()}
    attn_total = (
        lax.psum_scatter(gain_one_total, ("seq", "batch"), scatter_dimension=0, tiled=True),
        lax.psum_scatter(
            outer_sum(rows["normed"], rows["query_back"]),
            ("seq", "batch"),
            scatter_dimension=0,
            tiled=True,
        ),
        lax.psum_scatter(
            outer_sum(rows["normed"], rows["key_back"]),
            ("seq", "batch"),
            scatter_dimension=0,
            tiled=True,
        ),
        lax.psum_scatter(
            outer_sum(rows["normed"], rows["value_back"]),
            ("seq", "batch"),
            scatter_dimension=0,
            tiled=True,
        ),
        lax.psum_scatter(
            outer_sum(rows["mixed"], rows["grad_low"]),
            ("seq", "batch"),
            scatter_dimension=0,
            tiled=True,
        ),
    )
    mlp_total = (
        lax.psum_scatter(gain_two_total, ("seq", "batch"), scatter_dimension=0, tiled=True),
        lax.psum_scatter(
            outer_sum(rows["normed_two"], rows["gate_low"]),
            ("seq", "batch"),
            scatter_dimension=0,
            tiled=True,
        ),
        lax.psum_scatter(
            outer_sum(rows["normed_two"], rows["up_low"]),
            ("seq", "batch"),
            scatter_dimension=0,
            tiled=True,
        ),
        lax.psum_scatter(
            outer_sum(rows["activated"], rows["seed_low"]),
            ("seq", "batch"),
            scatter_dimension=0,
            tiled=True,
        ),
    )
    return (
        jnp.stack(outputs, axis=0),
        jnp.stack(input_grads, axis=0),
        attn_total[0],
        attn_total[1],
        attn_total[2],
        attn_total[3],
        attn_total[4],
        mlp_total[0],
        mlp_total[1],
        mlp_total[2],
        mlp_total[3],
    )


def solution(mesh):
    placed = (
        P("batch", "seq", None),
        P("batch", "seq", None),
        P("batch", "seq"),
        P("batch", None),
        P(("seq", "batch")),
        P(("seq", "batch"), None),
        P(("seq", "batch"), None),
        P(("seq", "batch"), None),
        P(("seq", "batch"), None),
        P(("seq", "batch")),
        P(("seq", "batch"), None),
        P(("seq", "batch"), None),
        P(("seq", "batch"), None),
    )
    return jax.shard_map(
        body,
        mesh=mesh,
        in_specs=placed,
        out_specs=(
            P("batch", "seq", None),
            P("batch", "seq", None),
            P(("seq", "batch")),
            P(("seq", "batch"), None),
            P(("seq", "batch"), None),
            P(("seq", "batch"), None),
            P(("seq", "batch"), None),
            P(("seq", "batch")),
            P(("seq", "batch"), None),
            P(("seq", "batch"), None),
            P(("seq", "batch"), None),
        ),
        check_vma=False,
    )
```

profile of v0, /device:TPU:0, one launch (start us, length us, event | category | flops | bytes accessed | tf_op | source)
XLA Modules:
  0.0 2154.9 jit_solution(5780896583125261295)
XLA Ops:
  12.8 42.2 %all-reduce.5 = (bf16[1536]{0:T(1024)(128)(2,1)S(1)}, bf16[1536]{0:T(1024)(128)(2,1)}) all-reduce(bf16[1536]{0:T(1024)(128)(2,1)S(1)} %dynamic-update-slice, bf16[1536]{0:T(1024)(128)(2,1)S(1)} %dynamic-update-slice.1), channel_id=1, replica_groups=mesh['seq'=4,'batch'=8] {'seq','batch'}, use_global_device_ids=true, to_apply=%add | all-reduce | flops 3072 | bytes 12288
  57.8 13.4 all-gather.12.cloned.1.call-done
  73.8 56.8 %all-gather.10.cloned.1.call-done = bf16[1536,768]{1,0:T(8,128)(2,1)} async-done(((bf16[48,768]{1,0:T(8,128)(2,1)}), bf16[1536,768]{1,0:T(8,128)(2,1)}) %all-gather.10.cloned.1.call-update) | async-done | bytes 2359312 | tf_op jit(solution)/shard_map/all_gather | solution.py:59
  157.1 10.7 all-to-all-done.4
  171.5 28.2 %all-gather.8.cloned.1.call-done = bf16[1536,1536]{1,0:T(8,128)(2,1)} async-done(((bf16[48,1536]{1,0:T(8,128)(2,1)}), bf16[1536,1536]{1,0:T(8,128)(2,1)}) %all-gather.8.cloned.1.call-update) | async-done | bytes 4718608 | tf_op jit(solution)/shard_map/all_gather | solution.py:58
  252.2 21.7 %while.55 = (s32[]{:T(128)}, bf16[2,512,384]{2,1,0:T(8,128)(2,1)}, f32[2,2,2,512]{3,2,1,0:T(2,128)S(1)}, s32[2]{0:T(128)S(1)}, s32[1024]{0:T(1024)S(1)}, /*index...) while((s32[]{:T(128)}, bf16[2,512,384]{2,1,0:T(8,128)(2,1)}, ...), condition=%wide.region_10.11_spmd, body=%wide.region_7.10_spmd.sunk | while | flops 832240128 | bytes 30488788 | solution.py:104
  283.4 21.3 while.54
  320.5 5.9 all-to-all-done.2
  343.3 33.0 %all-gather.16.cloned.1.call-done = bf16[1536,4096]{1,0:T(8,128)(2,1)} async-done(((bf16[48,4096]{1,0:T(8,128)(2,1)}), bf16[1536,4096]{1,0:T(8,128)(2,1)}) %all-gather.16.cloned.1.call-update) | async-done | bytes 12582928 | tf_op jit(solution)/shard_map/all_gather | solution.py:68
  376.3 9.6 fusion.194
  385.9 87.6 %all-gather.18.cloned.1.call-done = bf16[1536,4096]{1,0:T(8,128)(2,1)} async-done(((bf16[48,4096]{1,0:T(8,128)(2,1)}), bf16[1536,4096]{1,0:T(8,128)(2,1)}) %all-gather.18.cloned.1.call-update) | async-done | bytes 12582928 | tf_op jit(solution)/shard_map/all_gather | solution.py:69
  473.5 9.5 fusion.195
  483.0 87.9 %all-gather.20.cloned.1.call-done = bf16[4096,1536]{1,0:T(8,128)(2,1)} async-done(((bf16[128,1536]{1,0:T(8,128)(2,1)}), bf16[4096,1536]{1,0:T(8,128)(2,1)}) %all-gather.20.cloned.1.call-update) | async-done | bytes 12582928 | tf_op jit(solution)/shard_map/all_gather | solution.py:70
  570.9 10.8 multiply_convert_fusion.2
  581.7 8.7 fusion.198
  590.5 10.4 multiply_reduce_fusion.1
  600.9 6.7 fusion.196
  607.6 9.7 fusion.197
  617.3 15.7 multiply_convert_fusion
  633.1 10.0 fusion.200
  643.0 11.2 multiply_reduce_fusion
  670.0 6.5 all-to-all-done.6
  686.3 75.6 %while.56 = (s32[]{:T(128)}, f32[1024,2,96]{0,2,1:T(8,128)S(1)}, f32[1024,2,96]{0,2,1:T(8,128)}, f32[2,512,2,2,96]{1,0,4,3,2:T(2,128)}, s32[2]{0:T(128)S(1)}, /*...) while((s32[]{:T(128)}, f32[1024,2,96]{0,2,1:T(8,128)S(1)}, ...), condition=%wide.region_15.16_spmd.clone, body=%wide.region_13.15_spmd.clone.sunk | while | flops 2047474176 | bytes 137828784 | solution.py:145
  709.2 14.9 dynamic_update_slice.37
  739.7 5.0 fusion.321
  747.0 14.9 dynamic_update_slice.37
  767.2 74.2 %while.57 = (s32[]{:T(128)}, f32[1024,2,96]{0,2,1:T(8,128)S(1)}, f32[1024,2,96]{0,2,1:T(8,128)}, f32[2,512,2,2,96]{1,0,4,3,2:T(2,128)}, s32[2]{0:T(128)S(1)}, /*...) while((s32[]{:T(128)}, f32[1024,2,96]{0,2,1:T(8,128)S(1)}, ...), condition=%wide.region_20.21_spmd.clone, body=%wide.region_18.20_spmd.clone.sunk | while | flops 2047474176 | bytes 137894352 | solution.py:145
  789.2 14.9 dynamic_update_slice.38
  819.0 5.0 fusion.336
  826.3 14.9 dynamic_update_slice.38
  853.7 7.4 all-to-all-done.11
  867.5 7.3 all-to-all-done.8
  889.9 5.4 fusion.144
  919.9 7.7 all-to-all-done.10
  933.4 14.5 all-to-all-done.7
  949.8 6.6 fusion.140
  957.8 14.1 fusion.92
  972.0 14.2 fusion.96
  987.6 14.6 fusion.100
  1003.6 8.9 fusion.106
  1012.6 7.1 fusion.107
  1031.1 39.9 %all-reduce.4 = (f32[1536]{0:T(1024)S(1)}, f32[1536]{0:T(1024)S(1)}) all-reduce(f32[1536]{0:T(1024)S(1)} %add.262, f32[1536]{0:T(1024)S(1)} %add.263), channel_id=2, replica_groups=mesh['seq'=4,'batch'=8] {'seq','batch'}, use_global_device_ids=true, to_apply=%region_24.25.clone | all-reduce | flops 3072 | bytes 24576
  1076.6 32.0 %reduce-scatter.12.cloned.1.call-done = f32[48,768]{1,0:T(8,128)} async-done(((f32[1536,768]{1,0:T(8,128)}), f32[48,768]{1,0:T(8,128)}) %reduce-scatter.12.cloned.1.call-update) | async-done | bytes 147472 | tf_op jit(solution)/shard_map/reduce_scatter | solution.py:352
  1108.7 141.0 %reduce-scatter.14.cloned.1.call-done = f32[48,1536]{1,0:T(8,128)} async-done(((f32[1536,1536]{1,0:T(8,128)}), f32[48,1536]{1,0:T(8,128)}) %reduce-scatter.14.cloned.1.call-update) | async-done | bytes 294928 | tf_op jit(solution)/shard_map/reduce_scatter | solution.py:358
  1249.7 142.1 %reduce-scatter.8.cloned.1.call-done = f32[48,1536]{1,0:T(8,128)} async-done(((f32[1536,1536]{1,0:T(8,128)}), f32[48,1536]{1,0:T(8,128)}) %reduce-scatter.8.cloned.1.call-update) | async-done | bytes 294928 | tf_op jit(solution)/shard_map/reduce_scatter | solution.py:340
  1391.8 251.3 %reduce-scatter.16.cloned.1.call-done = f32[48,4096]{1,0:T(8,128)} async-done(((f32[1536,4096]{1,0:T(8,128)}), f32[48,4096]{1,0:T(8,128)}) %reduce-scatter.16.cloned.1.call-update) | async-done | bytes 786448 | tf_op jit(solution)/shard_map/reduce_scatter | solution.py:367
  1643.1 253.2 %reduce-scatter.18.cloned.1.call-done = f32[48,4096]{1,0:T(8,128)} async-done(((f32[1536,4096]{1,0:T(8,128)}), f32[48,4096]{1,0:T(8,128)}) %reduce-scatter.18.cloned.1.call-update) | async-done | bytes 786448 | tf_op jit(solution)/shard_map/reduce_scatter | solution.py:373
  1896.3 251.9 %reduce-scatter.20.cloned.1.call-done = f32[128,1536]{1,0:T(8,128)} async-done(((f32[4096,1536]{1,0:T(8,128)}), f32[128,1536]{1,0:T(8,128)}) %reduce-scatter.20.cloned.1.call-update) | async-done | bytes 786448 | tf_op jit(solution)/shard_map/reduce_scatter | solution.py:379
  (526 shorter events, 369.6 us)
Async XLA Ops:
  7.2 64.0 %all-gather.12.cloned.1.call-start = ((), (), s32[]{:S(2)}) async-start(), calls=%async_computation.21 | async-start | bytes 2433024 | tf_op jit(solution)/shard_map/all_gather | solution.py:60
  7.9 122.7 %all-gather.10.cloned.1.call-start = ((), (), s32[]{:S(2)}) async-start(), calls=%async_computation.20 | async-start | bytes 2433024 | tf_op jit(solution)/shard_map/all_gather | solution.py:59
  8.7 191.0 %all-gather.8.cloned.1.call-start = ((), (), s32[]{:S(2)}) async-start(), calls=%async_computation.19 | async-start | bytes 4866048 | tf_op jit(solution)/shard_map/all_gather | solution.py:58
  9.4 325.5 %all-gather.14.cloned.1.call-start = ((), (), s32[]{:S(2)}) async-start(), calls=%async_computation.22 | async-start | bytes 4866048 | tf_op jit(solution)/shard_map/all_gather | solution.py:61
  10.0 366.3 %all-gather.16.cloned.1.call-start = ((), (), s32[]{:S(2)}) async-start(), calls=%async_computation.23 | async-start | bytes 12976128 | tf_op jit(solution)/shard_map/all_gather | solution.py:68
  10.6 462.9 %all-gather.18.cloned.1.call-start = ((), (), s32[]{:S(2)}) async-start(), calls=%async_computation.24 | async-start | bytes 12976128 | tf_op jit(solution)/shard_map/all_gather | solution.py:69
  11.2 559.7 %all-gather.20.cloned.1.call-start = ((), (), s32[]{:S(2)}) async-start(), calls=%async_computation.25 | async-start | bytes 12976128 | tf_op jit(solution)/shard_map/all_gather | solution.py:70
  57.8 72.8 %copy-start.66 = (bf16[256,1536]{1,0:T(8,128)(2,1)}, bf16[256,1536]{1,0:T(8,128)(2,1)S(1)}, u32[]{:S(2)}) copy-start(bf16[256,1536]{1,0:T(8,128)(2,1)S(1)} %get-tuple-element.511) | copy-start | bytes 2359300
  134.2 16.0 all-to-all-start.1
  145.1 9.3 copy-start.56
  145.1 9.3 copy-start.57
  150.2 17.6 all-to-all-start.4
  154.5 78.4 %copy-start.19 = (f32[1024,96]{0,1:T(8,128)}, f32[1024,96]{0,1:T(8,128)S(1)}, u32[]{:S(2)}) copy-start(f32[1024,96]{0,1:T(8,128)S(1)} %get-tuple-element.561) | copy-start | bytes 1179652
  154.5 94.3 %copy-start.17 = (f32[1024,96]{0,1:T(8,128)}, f32[1024,96]{0,1:T(8,128)S(1)}, u32[]{:S(2)}) copy-start(f32[1024,96]{0,1:T(8,128)S(1)} %get-tuple-element.562) | copy-start | bytes 1179652
  204.8 16.1 all-to-all-start
  220.9 19.8 all-to-all-start.3
  278.4 30.6 %all-to-all-start.5 = ((bf16[4,2,49152]{2,1,0:T(2,128)(2,1)}), bf16[4,2,49152]{2,1,0:T(2,128)(2,1)}, u32[]{:S(2)}, u32[]{:S(2)}) async-start(bf16[4,2,49152]{2,1,0:T(2,128)(2,1)} %reshape.691), calls=%async_computation.5 | async-start | bytes 1572864 | tf_op jit(solution)/shard_map/all_to_all | solution.py:241
  309.0 17.4 all-to-all-start.2
  320.5 19.5 copy-start.29
  343.3 130.2 %copy-start.72 = (bf16[256,1536]{1,0:T(8,128)(2,1)}, bf16[256,1536]{1,0:T(8,128)(2,1)S(1)}, u32[]{:S(2)}) copy-start(bf16[256,1536]{1,0:T(8,128)(2,1)S(1)} %multiply_convert_fusion.7) | copy-start | bytes 2359300
  385.9 185.0 %copy-start.68 = (bf16[256,1536]{1,0:T(8,128)(2,1)S(1)}, bf16[256,1536]{1,0:T(8,128)(2,1)}, u32[]{:S(2)}) copy-start(bf16[256,1536]{1,0:T(8,128)(2,1)} %get-tuple-element.517) | copy-start | bytes 2359300
  581.7 8.8 copy-start.98
  581.7 8.8 copy-start.15
  581.7 8.8 copy-start.35
  581.7 8.8 copy-start.91
  581.7 8.8 copy-start.95
  607.6 9.7 copy-start.70
  633.1 26.0 %slice-start = ((s8[4718592]{0:T(1024)(128)(4,1)}), s8[4194304]{0:T(1024)(128)(4,1)S(1)}, s32[]{:S(2)}) async-start(s8[4718592]{0:T(1024)(128)(4,1)} %bitcast.517), calls=%async_computation.33 | async-start | bytes 8388608
  643.0 11.3 copy-start.40
  643.0 11.3 copy-start.85
  643.0 11.3 copy-start.87
  643.0 16.0 slice-start.1
  661.5 15.0 all-to-all-start.6
  676.5 85.5 %all-to-all-start.9 = ((bf16[256,4,384]{2,0,1:T(8,128)(2,1)}), bf16[256,4,384]{2,0,1:T(8,128)(2,1)}, u32[]{:S(2)}, u32[]{:S(2)}) async-start(bf16[256,4,384]{2,0,1:T(8,128)(2,1)} %bitcast.409), calls=%async_computation.9 | async-start | bytes 1572864 | tf_op jit(solution)/shard_map/all_to_all | solution.py:286
  846.7 14.3 all-to-all-start.11
  861.0 13.7 all-to-all-start.8
  864.5 212.1 %reduce-scatter.10.cloned.1.call-start = ((), (), s32[]{:S(2)}) async-start(), calls=%async_computation.27 | async-start | bytes 4866048 | tf_op jit(solution)/shard_map/reduce_scatter | solution.py:346
  881.6 227.0 %reduce-scatter.12.cloned.1.call-start = ((), (), s32[]{:S(2)}) async-start(), calls=%async_computation.28 | async-start | bytes 4866048 | tf_op jit(solution)/shard_map/reduce_scatter | solution.py:352
  888.0 361.7 %reduce-scatter.14.cloned.1.call-start = ((), (), s32[]{:S(2)}) async-start(), calls=%async_computation.29 | async-start | bytes 9732096 | tf_op jit(solution)/shard_map/reduce_scatter | solution.py:358
  913.8 13.7 all-to-all-start.10
  927.6 20.3 all-to-all-start.7
  931.1 460.7 %reduce-scatter.8.cloned.1.call-start = ((), (), s32[]{:S(2)}) async-start(), calls=%async_computation.26 | async-start | bytes 9732096 | tf_op jit(solution)/shard_map/reduce_scatter | solution.py:340
  956.4 686.6 %reduce-scatter.16.cloned.1.call-start = ((), (), s32[]{:S(2)}) async-start(), calls=%async_computation.30 | async-start | bytes 25952256 | tf_op jit(solution)/shard_map/reduce_scatter | solution.py:367
  972.0 924.3 %reduce-scatter.18.cloned.1.call-start = ((), (), s32[]{:S(2)}) async-start(), calls=%async_computation.31 | async-start | bytes 25952256 | tf_op jit(solution)/shard_map/reduce_scatter | solution.py:373
  986.2 1162.0 %reduce-scatter.20.cloned.1.call-start = ((), (), s32[]{:S(2)}) async-start(), calls=%async_computation.32 | async-start | bytes 25952256 | tf_op jit(solution)/shard_map/reduce_scatter | solution.py:379
  1003.6 8.9 copy-start.16
  1003.6 8.9 copy-start.99
  1003.6 17.4 slice-start.2
  (95 other events, 288.1 us)
Sparse Core Ops, SparseCore 0:
  11.1 60.1 all-gather.11
  74.2 56.3 all-gather.9
  133.6 66.0 all-gather.7
  202.6 67.2 all-gather.13
  272.7 103.5 all-gather.15
  379.2 94.3 all-gather.17
  476.5 94.3 all-gather.19
  881.8 113.6 reduce-scatter.9
  1002.4 106.1 reduce-scatter.11
  1115.0 134.6 reduce-scatter.13
  1257.2 134.5 reduce-scatter.7
  1398.6 244.4 reduce-scatter.15
  1651.2 245.0 reduce-scatter.17
  1903.1 245.0 reduce-scatter.19
where the time goes:
time: 2170 us; the launch traced here: 2150 us
  waiting for transfers between devices  1450 us (67%)
  matrix products  308 us (14%)
  local copies, waits for them, and re-layouts  170 us (8%)
  blocking collectives  82 us (4%)
  other arithmetic  74.4 us (3%)
  starting transfers between devices  47.6 us (2%)
    reduce_scatter x1, waiting for transfers between devices, body(): lax.psum_scatter(outer_sum(rows['normed_two'], rows['up_low']), ('seq', '...  253 us
    reduce_scatter x1, waiting for transfers between devices, body(): lax.psum_scatter(outer_sum(rows['activated'], rows['seed_low']), ('seq',...  252 us
    reduce_scatter x1, waiting for transfers between devices, body(): lax.psum_scatter(outer_sum(rows['normed_two'], rows['gate_low']), ('seq',...  251 us
    reduce_scatter x1, waiting for transfers between devices, body(): lax.psum_scatter(outer_sum(rows['normed'], rows['query_back']), ('seq', '...  142 us
    reduce_scatter x1, waiting for transfers between devices, body(): lax.psum_scatter(outer_sum(rows['mixed'], rows['grad_low']), ('seq', 'bat...  141 us
    all_gather x1, waiting for transfers between devices, fetch_feedforward(): lax.all_gather(w_down, ('seq', 'batch'), axis=0, tiled=True)  87.9 us
    all_gather x1, waiting for transfers between devices, fetch_feedforward(): lax.all_gather(w_up, ('seq', 'batch'), axis=0, tiled=True)  87.6 us
    unnamed x2, blocking collectives  82 us
  transfers between devices with their start and end apart: 26, of which 22 were waited for; matrix products, arithmetic and copies ran while one was open for 16% of the time, Pallas kernels for 0%

commit v1 on v0

--- a/solution.py
+++ b/solution.py
@@ -3,6 +3,7 @@
 import jax
 import jax.numpy as jnp
 from jax import lax
+from jax.sharding import Mesh
 from jax.sharding import PartitionSpec as P
 
 HEADS = 16
@@ -398,38 +399,298 @@
     )
 
 
+AXES = ("y", "x", "z", "core")
+SIZES = (2, 2, 4, 2)
+
+
+def route(move):
+    pairs = []
+    for y in range(2):
+        for x in range(2):
+            for z in range(4):
+                for c in range(2):
+                    ty, tx, tz, tc = move(y, x, z, c)
+                    pairs.append(
+                        (((y * 2 + x) * 4 + z) * 2 + c, ((ty * 2 + tx) * 4 + tz) * 2 + tc)
+                    )
+    return pairs
+
+
+def send(value, move):
+    return lax.ppermute(value, AXES, route(move))
+
+
+def to_core(value):
+    return send(value, lambda y, x, z, c: (y, x, z, 1 - c))
+
+
+def to_x(value):
+    return send(value, lambda y, x, z, c: (y, 1 - x, z, c))
+
+
+def to_y(value):
+    return send(value, lambda y, x, z, c: (1 - y, x, z, c))
+
+
+def to_z(value, k):
+    return send(value, lambda y, x, z, c: (y, x, z ^ k, c))
+
+
+def in_order(mine, other, place, axis=0):
+    first = jnp.where(place == 0, mine, other)
+    second = jnp.where(place == 0, other, mine)
+    return jnp.concatenate([first, second], axis=axis)
+
+
+def pick(value, place, axis=0):
+    return lax.dynamic_index_in_dim(value, place, axis, keepdims=False)
+
+
+def plane_turn(tokens, x):
+    got = [
+        send(pick(tokens, x ^ a), lambda y, x_, z, c, a=a: (c, x_ ^ a, z, y)) for a in range(2)
+    ]
+    return in_order(got[0][None], got[1][None], x)
+
+
+def gather_line(block, z):
+    got = [block[None]] + [to_z(block, k)[None] for k in (1, 2, 3)]
+    low = in_order(got[0], got[1], z & 1)
+    high = in_order(got[2], got[3], z & 1)
+    return in_order(low, high, z >> 1)
+
+
+def gather_all(block, y, x, z, x_first):
+    line = gather_line(block, z)
+    if x_first:
+        pair = in_order(line[None], to_x(line)[None], x)
+        return in_order(pair[None], to_y(pair)[None], y).reshape((16,) + block.shape)
+    pair = in_order(line[None], to_y(line)[None], y)
+    return in_order(pair[:, None], to_x(pair)[:, None], x, axis=1).reshape((16,) + block.shape)
+
+
+def scatter_all(total, y, x, z, y_first):
+    rest = total.shape[1:]
+    total = total.reshape((2, 2, 4) + rest)
+    low = jnp.bfloat16
+    if y_first:
+        got = to_y(pick(total, 1 - y).astype(low))
+        half = pick(total, y).astype(jnp.float32) + got.astype(jnp.float32)
+        got = to_x(pick(half, 1 - x).astype(low))
+        line = pick(half, x) + got.astype(jnp.float32)
+    else:
+        got = to_x(pick(total, 1 - x, 1).astype(low))
+        half = pick(total, x, 1).astype(jnp.float32) + got.astype(jnp.float32)
+        got = to_y(pick(half, 1 - y).astype(low))
+        line = pick(half, y) + got.astype(jnp.float32)
+    result = pick(line, z)
+    for k in (1, 2, 3):
+        result = result + to_z(pick(line, z ^ k).astype(low), k).astype(jnp.float32)
+    return result
+
+
+def add_all(value):
+    value = value + to_core(value)
+    value = value + to_x(value)
+    value = value + to_y(value)
+    value = value + to_z(value, 1)
+    return value + to_z(value, 2)
+
+
+def fast_body(
+    layer_input,
+    cotangent,
+    token_mask,
+    document_ids,
+    attn_gain,
+    w_query,
+    w_key,
+    w_value,
+    w_output,
+    mlp_gain,
+    w_gate,
+    w_up,
+    w_down,
+):
+    f32, low = jnp.float32, jnp.bfloat16
+    y, x, z, core = (lax.axis_index(name) for name in AXES)
+    device = ((y * 2 + x) * 4 + z) * 2 + core
+    quarter = layer_input.shape[1]
+    half_len = 2 * quarter
+    length = 2 * half_len
+    width = layer_input.shape[2]
+    rows = w_query.shape[0]
+    units = w_gate.shape[1]
+    heads, kvs = HEADS // 2, KV // 2
+    scale = 1.0 / math.sqrt(HD)
+    cosine, sine = rope_tables(length, HD)
+
+    own = plane_turn(layer_input, x).reshape(half_len, width)
+    masked = cotangent * token_mask.astype(low)[:, :, None]
+    seed_low = plane_turn(masked, x).reshape(half_len, width)
+    other_docs = to_core(document_ids)
+    documents = pick(jnp.where(core == y, document_ids, other_docs), x)
+
+    gains = jnp.stack([attn_gain, mlp_gain])[:, None]
+    gains = in_order(gains, to_core(gains), core, axis=1).reshape(1, -1)
+    gains = gather_all(gains, y, x, z, True).reshape(16, 2, 2 * rows)
+    gains = jnp.moveaxis(gains, 1, 0).reshape(2, width).astype(f32)
+
+    def halves(weight):
+        return weight.reshape(rows, 2, -1)
+
+    qkv = jnp.concatenate([halves(w_query), halves(w_key), halves(w_value)], axis=2)
+    gate_up = [weight.reshape(rows, -1, 2, 128) for weight in (w_gate, w_up)]
+
+    def swap_in(mine, sent):
+        return in_order(mine[None], to_core(sent)[None], core).reshape(2 * rows, -1)
+
+    qkv = swap_in(pick(qkv, core, 1), pick(qkv, 1 - core, 1))
+    qkv = gather_all(qkv, y, x, z, True).reshape(width, -1)
+    out_w = gather_all(w_output, y, x, z, False).reshape(2, 8, rows, width)
+    out_got = to_core(pick(out_w, 1 - core))
+    out_w = in_order(pick(out_w, core)[:, None], out_got[:, None], core, axis=1).reshape(-1, width)
+    gate_up = [
+        swap_in(
+            pick(weight, core, 2).reshape(rows, -1), pick(weight, 1 - core, 2).reshape(rows, -1)
+        )
+        for weight in gate_up
+    ]
+    gate_w = gather_all(gate_up[0], y, x, z, True).reshape(width, -1)
+    up_w = gather_all(gate_up[1], y, x, z, False).reshape(width, -1)
+    down_l = gather_all(w_down[:, : width // 2], y, x, z, True).reshape(units // 2, -1)
+    down_r = gather_all(w_down[:, width // 2 :], y, x, z, False).reshape(units // 2, -1)
+    down_w = jnp.concatenate([down_l, down_r], axis=1)
+
+    def both(mine):
+        return in_order(mine, to_core(mine), core)
+
+    def join(part):
+        part = part.reshape(2, half_len, width)
+        return pick(part, core) + to_core(pick(part, 1 - core))
+
+    inputs = own.astype(f32)
+    inv_one = inverse_rms(inputs)
+    unit_one = inputs * inv_one
+    normed = both((unit_one * gains[0]).astype(low))
+    seed_full = both(seed_low)
+    qkv_lin = jnp.dot(normed, qkv, preferred_element_type=f32).astype(low)
+    q_cols, k_cols = heads * HD, kvs * HD
+    query_rot = rotate_ahead(
+        qkv_lin[:, :q_cols].reshape(length, heads, HD).astype(f32), cosine, sine
+    ).astype(low)
+    query_rot = query_rot.reshape(length, kvs, 2, HD)
+    key_rot = rotate_ahead(
+        qkv_lin[:, q_cols : q_cols + k_cols].reshape(length, kvs, HD).astype(f32), cosine, sine
+    ).astype(low)
+    value_heads = qkv_lin[:, q_cols + k_cols :].reshape(length, kvs, HD)
+    mixed, sums = attention_forward(
+        query_rot, key_rot, value_heads, documents, 512, scale
+    )
+    hidden = inputs + join(jnp.dot(mixed, out_w, preferred_element_type=f32))
+    inv_two = inverse_rms(hidden)
+    unit_two = hidden * inv_two
+    normed_two = both((unit_two * gains[1]).astype(low))
+    gate = jnp.dot(normed_two, gate_w, preferred_element_type=f32)
+    upward = jnp.dot(normed_two, up_w, preferred_element_type=f32)
+    sigma = jax.nn.sigmoid(gate)
+    activated = (gate * sigma * upward).astype(low)
+    grad_act = back_product(seed_full, down_w)
+    up_low = (grad_act * gate * sigma).astype(low)
+    gate_low = (grad_act * upward * sigma * (1.0 + gate * (1.0 - sigma))).astype(low)
+    grad_down = scatter_all(
+        outer_sum(activated, seed_full).astype(low).reshape(16, -1, width), y, x, z, True
+    )
+
+    def swap_out(block, shape, axis):
+        block = block.reshape(2, rows, -1)
+        got = to_core(pick(block, 1 - core))
+        mine = pick(block, core)
+        return in_order(mine.reshape(shape), got.reshape(shape), core, axis=axis)
+
+    grad_gate = scatter_all(
+        outer_sum(normed_two, gate_low).astype(low).reshape(16, 2 * rows, -1), y, x, z, True
+    )
+    grad_gate = swap_out(grad_gate, (rows, 16, 1, 128), 2).reshape(rows, units)
+    grad_up = scatter_all(
+        outer_sum(normed_two, up_low).astype(low).reshape(16, 2 * rows, -1), y, x, z, False
+    )
+    grad_up = swap_out(grad_up, (rows, 16, 1, 128), 2).reshape(rows, units)
+    output = hidden + join(jnp.dot(activated, down_w, preferred_element_type=f32))
+    output = plane_turn(output.astype(low).reshape(2, quarter, width), x)
+    grad_normed_two = join(back_product(gate_low, gate_w) + back_product(up_low, up_w))
+    gain_two = add_all(jnp.sum(grad_normed_two * unit_two, axis=0))
+    scaled_two = grad_normed_two * gains[1]
+    grad_hidden = seed_low.astype(f32) + inv_two * (
+        scaled_two - unit_two * jnp.mean(scaled_two * unit_two, axis=-1, keepdims=True)
+    )
+    grad_low = both(grad_hidden.astype(low))
+    grad_out_w = outer_sum(mixed, grad_low).astype(low).reshape(8, 2, rows, width)
+    got = to_core(pick(grad_out_w, 1 - core, 1))
+    grad_out_w = in_order(pick(grad_out_w, core, 1), got, core)
+    grad_output = scatter_all(grad_out_w, y, x, z, False)
+    grad_heads = back_product(grad_low, out_w).astype(low).reshape(length, kvs, 2, HD)
+    grad_query_rot, grad_key_rot, grad_values = attention_backward(
+        query_rot, key_rot, value_heads, documents, sums, grad_heads, 512, scale
+    )
+    grad_qkv = jnp.concatenate(
+        [
+            rotate_behind(grad_query_rot, cosine, sine).reshape(length, q_cols),
+            rotate_behind(grad_key_rot, cosine, sine).reshape(length, k_cols),
+            grad_values.reshape(length, k_cols),
+        ],
+        axis=1,
+    ).astype(low)
+    grad_normed = join(back_product(grad_qkv, qkv))
+    gain_one = add_all(jnp.sum(grad_normed * unit_one, axis=0))
+    scaled_one = grad_normed * gains[0]
+    grad_input = grad_hidden + inv_one * (
+        scaled_one - unit_one * jnp.mean(scaled_one * unit_one, axis=-1, keepdims=True)
+    )
+    grad_input = plane_turn(grad_input.astype(low).reshape(2, quarter, width), x)
+    grad_w = scatter_all(
+        outer_sum(normed, grad_qkv).astype(low).reshape(16, 2 * rows, -1), y, x, z, True
+    )
+    grad_w = swap_out(grad_w, (rows, 1, 2 * k_cols + q_cols), 1)
+    q_grad = grad_w[:, :, :q_cols].reshape(rows, -1)
+    k_grad = grad_w[:, :, q_cols : q_cols + k_cols].reshape(rows, -1)
+    v_grad = grad_w[:, :, q_cols + k_cols :].reshape(rows, -1)
+
+    def shard_of(total):
+        return lax.dynamic_slice_in_dim(total, device * rows, rows, 0)
+
+    return (
+        output,
+        grad_input,
+        shard_of(gain_one),
+        q_grad,
+        k_grad,
+        v_grad,
+        grad_output,
+        shard_of(gain_two),
+        grad_gate,
+        grad_up,
+        grad_down,
+    )
+
+
 def solution(mesh):
-    placed = (
-        P("batch", "seq", None),
-        P("batch", "seq", None),
-        P("batch", "seq"),
-        P("batch", None),
-        P(("seq", "batch")),
-        P(("seq", "batch"), None),
-        P(("seq", "batch"), None),
-        P(("seq", "batch"), None),
-        P(("seq", "batch"), None),
-        P(("seq", "batch")),
-        P(("seq", "batch"), None),
-        P(("seq", "batch"), None),
-        P(("seq", "batch"), None),
-    )
+    fast = dict(mesh.shape) == {"seq": 4, "batch": 8}
+    if fast:
+        grid = Mesh(mesh.devices.reshape(SIZES), AXES)
+        seq, batch = ("y", "x"), ("z", "core")
+    else:
+        grid, seq, batch = mesh, ("seq",), ("batch",)
+    weight = P(seq + batch, None)
+    gain = P(seq + batch)
+    token = P(batch, seq, None)
     return jax.shard_map(
-        body,
-        mesh=mesh,
-        in_specs=placed,
-        out_specs=(
-            P("batch", "seq", None),
-            P("batch", "seq", None),
-            P(("seq", "batch")),
-            P(("seq", "batch"), None),
-            P(("seq", "batch"), None),
-            P(("seq", "batch"), None),
-            P(("seq", "batch"), None),
-            P(("seq", "batch")),
-            P(("seq", "batch"), None),
-            P(("seq", "batch"), None),
-            P(("seq", "batch"), None),
-        ),
+        fast_body if fast else body,
+        mesh=grid,
+        in_specs=(token, token, P(batch, seq), P(batch, None), gain)
+        + (weight,) * 4
+        + (gain,)
+        + (weight,) * 3,
+        out_specs=(token, token, gain) + (weight,) * 4 + (gain,) + (weight,) * 3,
         check_vma=False,
     )

time: 2170 us -> 1230 us (0.57)
  waiting for transfers between devices: 1450 us -> 566 us
  matrix products: 308 us -> 223 us
  other arithmetic: 74.4 us -> 158 us
  blocking collectives: 82 us -> 0 us
  starting transfers between devices: 47.6 us -> 117 us
  local copies, waits for them, and re-layouts: 170 us -> 148 us
    reduce_scatter x7 -> x0, waiting for transfers between devices: 1070 us -> none  [the longest x1 253 us: body(): lax.psum_scatter(outer_sum(rows['normed_two'], rows['up_low']), ('seq', '...]
    ppermute x0 -> x96, waiting for transfers between devices: none -> 566 us  [send(): return lax.ppermute(value, AXES, route(move))]
    all_gather x7 -> x0, waiting for transfers between devices: 307 us -> none  [the longest x1 87.9 us: fetch_feedforward(): lax.all_gather(w_down, ('seq', 'batch'), axis=0, tiled=True)]
    ppermute x0 -> x96, starting transfers between devices: none -> 117 us  [send(): return lax.ppermute(value, AXES, route(move))]
    unnamed x2 -> x0, blocking collectives: 82 us -> none
    all_to_all x12 -> x0, waiting for transfers between devices: 68.2 us -> none  [the longest x2 22.1 us: body(): lax.all_to_all(grad_query_heads, 'seq', split_axis=0, concat_axis=1, tile...]
    dynamic_update_slice x8 -> x0, local copies, waits for them, and re-layouts: 63 us -> none  [attention_backward(): lax.scan(one_block, (empty, empty), (jnp.arange(count, dtype=jnp.int32),...]
    all_to_all x12 -> x0, starting transfers between devices: 47 us -> none  [the longest x2 8.61 us: body(): lax.all_to_all(attended.reshape(length, 1, heads_here * HD), 'seq', split...]
  transfers between devices with their start and end apart: 26 -> 96, of which waited for: 22 -> 35; matrix products, arithmetic and copies ran while one was open for 16% -> 35% of each run, Pallas kernels for 0% -> 0%
where the time goes in v1:
time: 1230 us; the launch traced here: 1220 us
  waiting for transfers between devices  566 us (46%)
  matrix products  223 us (18%)
  other arithmetic  158 us (13%)
  local copies, waits for them, and re-layouts  148 us (12%)
  starting transfers between devices  117 us (10%)
    ppermute x96, waiting for transfers between devices, send(): return lax.ppermute(value, AXES, route(move))  566 us
    ppermute x96, starting transfers between devices, send(): return lax.ppermute(value, AXES, route(move))  117 us
    dot_general x5, matrix products, back_product(): lax.dot_general(left, right, (((1,), (1,)), ((), ())), preferred_element_...  41.8 us
    dot_general x5, matrix products, outer_sum(): lax.dot_general(left, right, (((0,), (0,)), ((), ())), preferred_element_...  35.1 us
    dot_general x4, matrix products, block_scores(): jnp.einsum('qjhd,kjd->jhqk', query_block, keys, preferred_element_type=jn...  31.8 us
    unnamed x231, local copies, waits for them, and re-layouts  31.4 us
  transfers between devices with their start and end apart: 96, of which 35 were waited for; matrix products, arithmetic and copies ran while one was open for 35% of the time, Pallas kernels for 0%

profile of v1, /device:TPU:0, one launch (start us, length us, event | category | flops | bytes accessed | tf_op | source)
XLA Modules:
  0.0 1219.0 jit_solution(15767883899193668748)
XLA Ops:
  58.6 7.6 collective-permute-done.36
  73.6 6.3 collective-permute-done.41
  97.8 15.6 %collective-permute-done.12 = bf16[96,1536]{1,0:T(8,128)(2,1)S(1)} collective-permute-done((bf16[96,1536]{1,0:T(8,128)(2,1)S(1)}, bf16[96,1536]{1,0:T(8,128)(2,1)S(1)}, u32[]{:S(2)}, u32[]{:S(2)}) %collective-permute-start.12) | collective-permute-done | bytes 294944 | tf_op jit(solution)/shard_map/ppermute | solution.py:420
  113.4 15.4 %collective-permute-start.25 = (bf16[96,2048]{1,0:T(8,128)(2,1)S(1)}, bf16[96,2048]{1,0:T(8,128)(2,1)S(1)}, u32[]{:S(2)}, u32[]{:S(2)}) collective-permute-start(bf16[96,2048]{1,0:T(8,128)(2,1)S(1)} %bitcast.692), channel_id=1, source_target_pairs={{0,2},{1,3},{2,0},{3,1},{4,6},{5,7},{6,4},{7,5},{8,10},{9,11},{10,... | collective-permute-start | bytes 1179656 | tf_op jit(solution)/shard_map/ppermute | solution.py:420
  129.1 16.5 %collective-permute-done.25 = bf16[96,2048]{1,0:T(8,128)(2,1)S(1)} collective-permute-done((bf16[96,2048]{1,0:T(8,128)(2,1)S(1)}, bf16[96,2048]{1,0:T(8,128)(2,1)S(1)}, u32[]{:S(2)}, u32[]{:S(2)}) %collective-permute-start.25) | collective-permute-done | bytes 393248 | tf_op jit(solution)/shard_map/ppermute | solution.py:420
  145.7 11.0 collective-permute-done.31
  159.2 11.5 collective-permute-done.27
  173.0 29.3 %collective-permute-done.32 = bf16[96,2048]{1,0:T(8,128)(2,1)S(1)} collective-permute-done((bf16[96,2048]{1,0:T(8,128)(2,1)S(1)}, bf16[96,2048]{1,0:T(8,128)(2,1)S(1)}, u32[]{:S(2)}, u32[]{:S(2)}) %collective-permute-start.32) | collective-permute-done | bytes 393248 | tf_op jit(solution)/shard_map/ppermute | solution.py:420
  203.0 20.3 %collective-permute-done.19 = bf16[4,48,1536]{2,1,0:T(8,128)(2,1)S(1)} collective-permute-done((bf16[4,48,1536]{2,1,0:T(8,128)(2,1)S(1)}, bf16[4,48,1536]{2,1,0:T(8,128)(2,1)S(1)}, u32[]{:S(2)}, u32[]{:S(2)}) %collective-permute-start.19) | collective-permute-done | bytes 589856 | tf_op jit(solution)/shard_map/ppermute | solution.py:420
  230.1 13.6 %collective-permute-done.39 = bf16[4,128,768]{2,1,0:T(8,128)(2,1)S(1)} collective-permute-done((bf16[4,128,768]{2,1,0:T(8,128)(2,1)S(1)}, bf16[4,128,768]{2,1,0:T(8,128)(2,1)S(1)}, u32[]{:S(2)}, u32[]{:S(2)}) %collective-permute-start.39) | collective-permute-done | bytes 786464 | tf_op jit(solution)/shard_map/ppermute | solution.py:420
  246.8 22.1 %collective-permute-done.14 = bf16[4,96,1536]{2,1,0:T(8,128)(2,1)S(1)} collective-permute-done((bf16[4,96,1536]{2,1,0:T(8,128)(2,1)S(1)}, bf16[4,96,1536]{2,1,0:T(8,128)(2,1)S(1)}, u32[]{:S(2)}, u32[]{:S(2)}) %collective-permute-start.14) | collective-permute-done | bytes 1179680 | tf_op jit(solution)/shard_map/ppermute | solution.py:420
  269.4 56.1 %collective-permute-done.20 = bf16[2,4,48,1536]{3,2,1,0:T(8,128)(2,1)S(1)} collective-permute-done((bf16[2,4,48,1536]{3,2,1,0:T(8,128)(2,1)S(1)}, bf16[2,4,48,1536]{3,2,1,0:T(8,128)(2,1)S(1)}, u32[]{:S(2)}, u32[]{:S(2)}) %collective-permute-start.20) | collective-permute-done | bytes 1179680 | tf_op jit(solution)/shard_map/ppermute | solution.py:420
  336.8 76.8 %collective-permute-done.15 = bf16[2,4,96,1536]{3,2,1,0:T(8,128)(2,1)S(1)} collective-permute-done((bf16[2,4,96,1536]{3,2,1,0:T(8,128)(2,1)S(1)}, bf16[2,4,96,1536]{3,2,1,0:T(8,128)(2,1)S(1)}, u32[]{:S(2)}, u32[]{:S(2)}) %collective-permute-start.15) | collective-permute-done | bytes 2359328 | tf_op jit(solution)/shard_map/ppermute | solution.py:420
  414.4 6.3 convolution_convert_fusion.4
  438.8 31.6 %while.27 = (s32[]{:T(128)}, bf16[2,512,768]{1,2,0:T(8,128)(2,1)}, f32[2,4,2,512]{3,2,1,0:T(2,128)}, s32[2]{0:T(128)S(1)}, s32[1024]{0:T(1024)S(1)}, /*index=5*/...) while((s32[]{:T(128)}, bf16[2,512,768]{1,2,0:T(8,128)(2,1)}, ...), condition=%wide.region_4.5_spmd, body=%wide.region_1.4_spmd.sunk | while | flops 1662906880 | bytes 57555700 | solution.py:105
  492.5 8.9 fusion.33
  516.0 37.3 %collective-permute-done.35 = bf16[2,4,96,2048]{3,2,1,0:T(8,128)(2,1)} collective-permute-done((bf16[2,4,96,2048]{3,2,1,0:T(8,128)(2,1)}, bf16[2,4,96,2048]{3,2,1,0:T(8,128)(2,1)}, u32[]{:S(2)}, u32[]{:S(2)}) %collective-permute-start.35) | collective-permute-done | bytes 3145760 | tf_op jit(solution)/shard_map/ppermute | solution.py:420
  561.8 10.0 fusion.129
  571.9 18.2 %multiply_convert_fusion.1 = (bf16[1024,2048]{1,0:T(8,128)(2,1)}, bf16[1024,2048]{1,0:T(8,128)(2,1)}, bf16[1024,2048]{1,0:T(8,128)(2,1)}) fusion(f32[1024,2048]{1,0:T(8,128)} %fusion.33, f32[1024,2048]{1,0:T(8,128)} %fusion.129, bf16[1536,2048]{1,0:T(8,128)(2,1)} %bitcast.647, bf16[512,1536]{1,0:T(8,128)(2,1)S(1)} %get-tuple-element.266, ...), kind=kOutput, calls=%fused_computation.50 | convolution fusion | flops 6482296832 | bytes 38797312 | tf_op jit(solution)/shard_map/dot_general | solution.py:594
  590.1 9.5 convolution_convert_fusion.2
  599.7 10.7 fusion.135
  610.4 7.4 convolution_convert_fusion.1
  625.7 10.1 convolution_add_fusion
  639.9 7.2 convolution_convert_fusion.3
  652.2 8.7 fusion.34
  666.0 26.8 %collective-permute-done.91 = bf16[2,4,128,1536]{3,2,1,0:T(8,128)(2,1)} collective-permute-done((bf16[2,4,128,1536]{3,2,1,0:T(8,128)(2,1)}, bf16[2,4,128,1536]{3,2,1,0:T(8,128)(2,1)}, u32[]{:S(2)}, u32[]{:S(2)}) %collective-permute-start.91) | collective-permute-done | bytes 3145760 | tf_op jit(solution)/shard_map/ppermute | solution.py:420
  707.6 52.6 %collective-permute-done.79 = bf16[2,4,96,2048]{3,2,1,0:T(8,128)(2,1)} collective-permute-done((bf16[2,4,96,2048]{3,2,1,0:T(8,128)(2,1)S(1)}, bf16[2,4,96,2048]{3,2,1,0:T(8,128)(2,1)}, u32[]{:S(2)}, u32[]{:S(2)}) %collective-permute-start.79) | collective-permute-done | bytes 3145760 | tf_op jit(solution)/shard_map/ppermute | solution.py:420
  765.9 26.8 %collective-permute-done.76 = f32[1536]{0:T(1024)S(1)} collective-permute-done((f32[1536]{0:T(1024)S(1)}, f32[1536]{0:T(1024)S(1)}, u32[]{:S(2)}, u32[]{:S(2)}) %collective-permute-start.76) | collective-permute-done | bytes 6176 | tf_op jit(solution)/shard_map/ppermute | solution.py:420
  824.7 113.6 %while.28 = (s32[]{:T(128)}, f32[1024,4,96]{0,2,1:T(8,128)S(1)}, f32[1024,4,96]{0,2,1:T(8,128)}, f32[2,512,4,2,96]{1,4,3,2,0:T(8,128)}, s32[2]{0:T(128)S(1)}, /*...) while((s32[]{:T(128)}, f32[1024,4,96]{0,2,1:T(8,128)S(1)}, ...), condition=%wide.region_9.10_spmd.clone, body=%wide.region_7.9_spmd.clone.sunk | while | flops 4068209152 | bytes 186481488 | solution.py:146
  827.0 9.5 fusion.182
  836.5 12.7 %fusion.184 = (f32[4,2,512]{2,1,0:T(2,128)S(1)}, f32[4,2,512,1024]{3,2,1,0:T(8,128)}) fusion(f32[4,512,2,1024]{3,1,2,0:T(8,128)} %fusion.182, f32[4,2,512]{2,1,0:T(2,128)S(1)} %dynamic-slice_bitcast_fusion.24, bf16[1024,4,96]{0,2,1:T(8,128)(2,1)S(1)} %get-tuple-element.585, bf16[1024,4,2,96]{0,3,2,1:T(8,128)(2,1)S(1)} %copy-done.7, ...), kind=kOutput, calls=%fused_computation.22.clone.1 | convolution fusion | flops 826273792 | bytes 35684356 | tf_op jit(solution)/shard_map/while/body/eval_jaxpr/qjhd,kjd->jhqk/dot_general | solution.py:78
  849.1 11.3 fusion.185
  873.1 8.4 bitcast_add_fusion.21
  883.3 9.5 fusion.182
  892.8 12.7 %fusion.184 = (f32[4,2,512]{2,1,0:T(2,128)S(1)}, f32[4,2,512,1024]{3,2,1,0:T(8,128)}) fusion(f32[4,512,2,1024]{3,1,2,0:T(8,128)} %fusion.182, f32[4,2,512]{2,1,0:T(2,128)S(1)} %dynamic-slice_bitcast_fusion.24, bf16[1024,4,96]{0,2,1:T(8,128)(2,1)S(1)} %get-tuple-element.585, bf16[1024,4,2,96]{0,3,2,1:T(8,128)(2,1)S(1)} %copy-done.7, ...), kind=kOutput, calls=%fused_computation.22.clone.1 | convolution fusion | flops 826273792 | bytes 35684356 | tf_op jit(solution)/shard_map/while/body/eval_jaxpr/qjhd,kjd->jhqk/dot_general | solution.py:78
  905.4 11.3 fusion.185
  929.3 8.9 bitcast_add_fusion.21
  975.9 7.0 convolution_convert_fusion
  1004.1 7.4 fusion.37
  1022.0 22.1 %collective-permute-done.82 = bf16[96,2048]{1,0:T(8,128)(2,1)} collective-permute-done((bf16[96,2048]{1,0:T(8,128)(2,1)}, bf16[96,2048]{1,0:T(8,128)(2,1)}, u32[]{:S(2)}, u32[]{:S(2)}) %collective-permute-start.82) | collective-permute-done | bytes 393248 | tf_op jit(solution)/shard_map/ppermute | solution.py:420
  1052.6 25.2 %collective-permute-done.94 = bf16[128,1536]{1,0:T(8,128)(2,1)} collective-permute-done((bf16[128,1536]{1,0:T(8,128)(2,1)}, bf16[128,1536]{1,0:T(8,128)(2,1)}, u32[]{:S(2)}, u32[]{:S(2)}) %collective-permute-start.94) | collective-permute-done | bytes 393248 | tf_op jit(solution)/shard_map/ppermute | solution.py:420
  1089.5 17.0 %collective-permute-done.69 = bf16[2,4,48,1536]{3,2,1,0:T(8,128)(2,1)} collective-permute-done((bf16[2,4,48,1536]{3,2,1,0:T(8,128)(2,1)}, bf16[2,4,48,1536]{3,2,1,0:T(8,128)(2,1)}, u32[]{:S(2)}, u32[]{:S(2)}) %collective-permute-start.69) | collective-permute-done | bytes 1179680 | tf_op jit(solution)/shard_map/ppermute | solution.py:420
  1114.3 8.9 collective-permute-done.70
  1123.4 16.5 %collective-permute-start.71 = (bf16[48,1536]{1,0:T(8,128)(2,1)S(1)}, bf16[48,1536]{1,0:T(8,128)(2,1)S(1)}, u32[]{:S(2)}, u32[]{:S(2)}) collective-permute-start(bf16[48,1536]{1,0:T(8,128)(2,1)S(1)} %get-tuple-element.310), channel_id=1, source_target_pairs={{0,2},{1,3},{2,0},{3,1},{4,6},{5,7},{6,4},{7,5},{8,10},{9,11},{10,... | collective-permute-start | bytes 442376 | tf_op jit(solution)/shard_map/ppermute | solution.py:420
  1145.9 6.9 collective-permute-done.72
  1177.9 7.3 collective-permute-done.64
  1185.9 9.0 collective-permute-done.65
  1196.6 17.0 %collective-permute-done.48 = bf16[256,1536]{1,0:T(8,128)(2,1)S(1)} collective-permute-done((bf16[256,1536]{1,0:T(8,128)(2,1)S(1)}, bf16[256,1536]{1,0:T(8,128)(2,1)S(1)}, u32[]{:S(2)}, u32[]{:S(2)}) %collective-permute-start.48) | collective-permute-done | bytes 786464 | tf_op jit(solution)/shard_map/ppermute | solution.py:420
  (676 shorter events, 440.8 us)
Async XLA Ops:
  0.7 55.6 %collective-permute-start.17 = (bf16[48,1536]{1,0:T(8,128)(2,1)}, bf16[48,1536]{1,0:T(8,128)(2,1)}, u32[]{:S(2)}, u32[]{:S(2)}) collective-permute-start(bf16[48,1536]{1,0:T(8,128)(2,1)} %param.25), channel_id=1, source_target_pairs={{0,4},{1,5},{2,6},{3,7},{4,0},{5,1},{6,2},{7,3},{8,12},{9,13},{10,... | collective-permute-start | bytes 442376 | tf_op jit(solution)/shard_map/ppermute | solution.py:420
  4.8 51.6 %collective-permute-start.18 = (bf16[48,1536]{1,0:T(8,128)(2,1)}, bf16[48,1536]{1,0:T(8,128)(2,1)}, u32[]{:S(2)}, u32[]{:S(2)}) collective-permute-start(bf16[48,1536]{1,0:T(8,128)(2,1)} %param.25), channel_id=1, source_target_pairs={{0,6},{1,7},{2,4},{3,5},{4,2},{5,3},{6,0},{7,1},{8,14},{9,15},{10,... | collective-permute-start | bytes 442376 | tf_op jit(solution)/shard_map/ppermute | solution.py:420
  6.1 48.3 %collective-permute-start.16 = (bf16[48,1536]{1,0:T(8,128)(2,1)}, bf16[48,1536]{1,0:T(8,128)(2,1)}, u32[]{:S(2)}, u32[]{:S(2)}) collective-permute-start(bf16[48,1536]{1,0:T(8,128)(2,1)} %param.25), channel_id=1, source_target_pairs={{0,2},{1,3},{2,0},{3,1},{4,6},{5,7},{6,4},{7,5},{8,10},{9,11},{10,... | collective-permute-start | bytes 442376 | tf_op jit(solution)/shard_map/ppermute | solution.py:420
  66.2 157.3 %collective-permute-start = (bf16[256,1536]{1,0:T(8,128)(2,1)S(1)}, bf16[256,1536]{1,0:T(8,128)(2,1)S(1)}, u32[]{:S(2)}, u32[]{:S(2)}) collective-permute-start(bf16[256,1536]{1,0:T(8,128)(2,1)S(1)} %copy-done.82), channel_id=1, source_target_pairs={{0,0},{1,16},{2,2},{3,18},{4,4},{5,20},{6,6},{7,22},{8,8},{9,24},{... | collective-permute-start | bytes 2359304 | tf_op jit(solution)/shard_map/ppermute | solution.py:420
  67.1 156.5 %collective-permute-start.1 = (bf16[256,1536]{1,0:T(8,128)(2,1)S(1)}, bf16[256,1536]{1,0:T(8,128)(2,1)S(1)}, u32[]{:S(2)}, u32[]{:S(2)}) collective-permute-start(bf16[256,1536]{1,0:T(8,128)(2,1)S(1)} %copy-done.81), channel_id=1, source_target_pairs={{0,8},{1,24},{2,10},{3,26},{4,12},{5,28},{6,14},{7,30},{8,0},{9,16... | collective-permute-start | bytes 2359304 | tf_op jit(solution)/shard_map/ppermute | solution.py:420
  67.7 158.4 %collective-permute-start.49 = (bf16[256,1536]{1,0:T(8,128)(2,1)S(1)}, bf16[256,1536]{1,0:T(8,128)(2,1)S(1)}, u32[]{:S(2)}, u32[]{:S(2)}) collective-permute-start(bf16[256,1536]{1,0:T(8,128)(2,1)S(1)} %copy-done.80), channel_id=1, source_target_pairs={{0,0},{1,16},{2,2},{3,18},{4,4},{5,20},{6,6},{7,22},{8,8},{9,24},{... | collective-permute-start | bytes 2359304 | tf_op jit(solution)/shard_map/ppermute | solution.py:420
  87.4 26.0 %collective-permute-start.12 = (bf16[96,1536]{1,0:T(8,128)(2,1)S(1)}, bf16[96,1536]{1,0:T(8,128)(2,1)S(1)}, u32[]{:S(2)}, u32[]{:S(2)}) collective-permute-start(bf16[96,1536]{1,0:T(8,128)(2,1)S(1)} %bitcast.703), channel_id=1, source_target_pairs={{0,4},{1,5},{2,6},{3,7},{4,0},{5,1},{6,2},{7,3},{8,12},{9,13},{10,... | collective-permute-start | bytes 884744 | tf_op jit(solution)/shard_map/ppermute | solution.py:420
  113.4 45.7 %collective-permute-start.26 = (bf16[96,2048]{1,0:T(8,128)(2,1)S(1)}, bf16[96,2048]{1,0:T(8,128)(2,1)S(1)}, u32[]{:S(2)}, u32[]{:S(2)}) collective-permute-start(bf16[96,2048]{1,0:T(8,128)(2,1)S(1)} %bitcast.691), channel_id=1, source_target_pairs={{0,4},{1,5},{2,6},{3,7},{4,0},{5,1},{6,2},{7,3},{8,12},{9,13},{10,... | collective-permute-start | bytes 1179656 | tf_op jit(solution)/shard_map/ppermute | solution.py:420
  113.4 32.2 %collective-permute-start.25 = (bf16[96,2048]{1,0:T(8,128)(2,1)S(1)}, bf16[96,2048]{1,0:T(8,128)(2,1)S(1)}, u32[]{:S(2)}, u32[]{:S(2)}) collective-permute-start(bf16[96,2048]{1,0:T(8,128)(2,1)S(1)} %bitcast.692), channel_id=1, source_target_pairs={{0,2},{1,3},{2,0},{3,1},{4,6},{5,7},{6,4},{7,5},{8,10},{9,11},{10,... | collective-permute-start | bytes 1179656 | tf_op jit(solution)/shard_map/ppermute | solution.py:420
  159.1 43.1 %collective-permute-start.32 = (bf16[96,2048]{1,0:T(8,128)(2,1)S(1)}, bf16[96,2048]{1,0:T(8,128)(2,1)S(1)}, u32[]{:S(2)}, u32[]{:S(2)}) collective-permute-start(bf16[96,2048]{1,0:T(8,128)(2,1)S(1)} %bitcast.689), channel_id=1, source_target_pairs={{0,4},{1,5},{2,6},{3,7},{4,0},{5,1},{6,2},{7,3},{8,12},{9,13},{10,... | collective-permute-start | bytes 1179656 | tf_op jit(solution)/shard_map/ppermute | solution.py:420
  170.7 31.6 %collective-permute-start.33 = (bf16[96,2048]{1,0:T(8,128)(2,1)S(1)}, bf16[96,2048]{1,0:T(8,128)(2,1)S(1)}, u32[]{:S(2)}, u32[]{:S(2)}) collective-permute-start(bf16[96,2048]{1,0:T(8,128)(2,1)S(1)} %bitcast.690), channel_id=1, source_target_pairs={{0,6},{1,7},{2,4},{3,5},{4,2},{5,3},{6,0},{7,1},{8,14},{9,15},{10,... | collective-permute-start | bytes 1179656 | tf_op jit(solution)/shard_map/ppermute | solution.py:420
  223.6 45.4 %collective-permute-start.14 = (bf16[4,96,1536]{2,1,0:T(8,128)(2,1)S(1)}, bf16[4,96,1536]{2,1,0:T(8,128)(2,1)S(1)}, u32[]{:S(2)}, u32[]{:S(2)}) collective-permute-start(bf16[4,96,1536]{2,1,0:T(8,128)(2,1)S(1)} %pad_maximum_fusion.34), channel_id=1, source_target_pairs={{0,8},{1,9},{2,10},{3,11},{4,12},{5,13},{6,14},{7,15},{8,0},{9,1},... | collective-permute-start | bytes 3538952 | tf_op jit(solution)/shard_map/ppermute | solution.py:420
  226.2 100.8 %collective-permute-start.28 = (bf16[4,96,2048]{2,1,0:T(8,128)(2,1)S(1)}, bf16[4,96,2048]{2,1,0:T(8,128)(2,1)S(1)}, u32[]{:S(2)}, u32[]{:S(2)}) collective-permute-start(bf16[4,96,2048]{2,1,0:T(8,128)(2,1)S(1)} %pad_maximum_fusion.27), channel_id=1, source_target_pairs={{0,8},{1,9},{2,10},{3,11},{4,12},{5,13},{6,14},{7,15},{8,0},{9,1},... | collective-permute-start | bytes 4718600 | tf_op jit(solution)/shard_map/ppermute | solution.py:420
  226.2 104.8 %collective-permute-start.34 = (bf16[4,96,2048]{2,1,0:T(8,128)(2,1)S(1)}, bf16[4,96,2048]{2,1,0:T(8,128)(2,1)S(1)}, u32[]{:S(2)}, u32[]{:S(2)}) collective-permute-start(bf16[4,96,2048]{2,1,0:T(8,128)(2,1)S(1)} %pad_maximum_fusion.28), channel_id=1, source_target_pairs={{0,16},{1,17},{2,18},{3,19},{4,20},{5,21},{6,22},{7,23},{8,24},{9,... | collective-permute-start | bytes 4718600 | tf_op jit(solution)/shard_map/ppermute | solution.py:420
  243.7 81.8 %collective-permute-start.20 = (bf16[2,4,48,1536]{3,2,1,0:T(8,128)(2,1)S(1)}, bf16[2,4,48,1536]{3,2,1,0:T(8,128)(2,1)S(1)}, u32[]{:S(2)}, u32[]{:S(2)}) collective-permute-start(bf16[2,4,48,1536]{3,2,1,0:T(8,128)(2,1)S(1)} %pad_maximum_fusion.35), channel_id=1, source_target_pairs={{0,8},{1,9},{2,10},{3,11},{4,12},{5,13},{6,14},{7,15},{8,0},{9,1},... | collective-permute-start | bytes 3538952 | tf_op jit(solution)/shard_map/ppermute | solution.py:420
  245.3 87.8 %collective-permute-start.9 = (bf16[512,1536]{1,0:T(8,128)(2,1)S(1)}, bf16[512,1536]{1,0:T(8,128)(2,1)S(1)}, u32[]{:S(2)}, u32[]{:S(2)}) collective-permute-start(bf16[512,1536]{1,0:T(8,128)(2,1)S(1)} %fusion.56), channel_id=1, source_target_pairs={{0,1},{1,0},{2,3},{3,2},{4,5},{5,4},{6,7},{7,6},{8,9},{9,8},{10,11... | collective-permute-start | bytes 4718600 | tf_op jit(solution)/shard_map/ppermute | solution.py:420
  269.0 213.5 %collective-permute-start.51 = (bf16[512,1536]{1,0:T(8,128)(2,1)}, bf16[512,1536]{1,0:T(8,128)(2,1)}, u32[]{:S(2)}, u32[]{:S(2)}) collective-permute-start(bf16[512,1536]{1,0:T(8,128)(2,1)} %bitcast.120), channel_id=1, source_target_pairs={{0,1},{1,0},{2,3},{3,2},{4,5},{5,4},{6,7},{7,6},{8,9},{9,8},{10,11... | collective-permute-start | bytes 4718600 | tf_op jit(solution)/shard_map/ppermute | solution.py:420
  325.5 159.5 %collective-permute-start.40 = (bf16[2,4,128,768]{3,2,1,0:T(8,128)(2,1)}, bf16[2,4,128,768]{3,2,1,0:T(8,128)(2,1)}, u32[]{:S(2)}, u32[]{:S(2)}) collective-permute-start(bf16[2,4,128,768]{3,2,1,0:T(8,128)(2,1)} %pad_maximum_fusion.29), channel_id=1, source_target_pairs={{0,16},{1,17},{2,18},{3,19},{4,20},{5,21},{6,22},{7,23},{8,24},{9,... | collective-permute-start | bytes 4718600 | tf_op jit(solution)/shard_map/ppermute | solution.py:420
  326.9 86.7 %collective-permute-start.15 = (bf16[2,4,96,1536]{3,2,1,0:T(8,128)(2,1)S(1)}, bf16[2,4,96,1536]{3,2,1,0:T(8,128)(2,1)S(1)}, u32[]{:S(2)}, u32[]{:S(2)}) collective-permute-start(bf16[2,4,96,1536]{3,2,1,0:T(8,128)(2,1)S(1)} %pad_maximum_fusion.14), channel_id=1, source_target_pairs={{0,16},{1,17},{2,18},{3,19},{4,20},{5,21},{6,22},{7,23},{8,24},{9,... | collective-permute-start | bytes 7077896 | tf_op jit(solution)/shard_map/ppermute | solution.py:420
  333.1 154.4 %collective-permute-start.45 = (bf16[2,4,128,768]{3,2,1,0:T(8,128)(2,1)}, bf16[2,4,128,768]{3,2,1,0:T(8,128)(2,1)}, u32[]{:S(2)}, u32[]{:S(2)}) collective-permute-start(bf16[2,4,128,768]{3,2,1,0:T(8,128)(2,1)} %pad_maximum_fusion.30), channel_id=1, source_target_pairs={{0,8},{1,9},{2,10},{3,11},{4,12},{5,13},{6,14},{7,15},{8,0},{9,1},... | collective-permute-start | bytes 4718600 | tf_op jit(solution)/shard_map/ppermute | solution.py:420
  333.9 174.4 %collective-permute-start.29 = (bf16[2,4,96,2048]{3,2,1,0:T(8,128)(2,1)}, bf16[2,4,96,2048]{3,2,1,0:T(8,128)(2,1)}, u32[]{:S(2)}, u32[]{:S(2)}) collective-permute-start(bf16[2,4,96,2048]{3,2,1,0:T(8,128)(2,1)} %pad_maximum_fusion.8), channel_id=1, source_target_pairs={{0,16},{1,17},{2,18},{3,19},{4,20},{5,21},{6,22},{7,23},{8,24},{9,... | collective-permute-start | bytes 9437192 | tf_op jit(solution)/shard_map/ppermute | solution.py:420
  482.5 70.8 %collective-permute-start.35 = (bf16[2,4,96,2048]{3,2,1,0:T(8,128)(2,1)}, bf16[2,4,96,2048]{3,2,1,0:T(8,128)(2,1)}, u32[]{:S(2)}, u32[]{:S(2)}) collective-permute-start(bf16[2,4,96,2048]{3,2,1,0:T(8,128)(2,1)} %pad_maximum_fusion.9), channel_id=1, source_target_pairs={{0,8},{1,9},{2,10},{3,11},{4,12},{5,13},{6,14},{7,15},{8,0},{9,1},... | collective-permute-start | bytes 9437192 | tf_op jit(solution)/shard_map/ppermute | solution.py:420
  508.0 50.6 %collective-permute-start.23 = (bf16[512,1536]{1,0:T(8,128)(2,1)S(1)}, bf16[512,1536]{1,0:T(8,128)(2,1)}, u32[]{:S(2)}, u32[]{:S(2)}) collective-permute-start(bf16[512,1536]{1,0:T(8,128)(2,1)S(1)} %multiply_convert_fusion.3), channel_id=1, source_target_pairs={{0,1},{1,0},{2,3},{3,2},{4,5},{5,4},{6,7},{7,6},{8,9},{9,8},{10,11... | collective-permute-start | bytes 4718600 | tf_op jit(solution)/shard_map/ppermute | solution.py:420
  621.4 71.3 %collective-permute-start.91 = (bf16[2,4,128,1536]{3,2,1,0:T(8,128)(2,1)}, bf16[2,4,128,1536]{3,2,1,0:T(8,128)(2,1)}, u32[]{:S(2)}, u32[]{:S(2)}) collective-permute-start(bf16[2,4,128,1536]{3,2,1,0:T(8,128)(2,1)} %dynamic-slice_bitcast_fusion.1), channel_id=1, source_target_pairs={{0,16},{1,17},{2,18},{3,19},{4,20},{5,21},{6,22},{7,23},{8,24},{9,... | collective-permute-start | bytes 9437192 | tf_op jit(solution)/shard_map/ppermute | solution.py:420
  624.4 76.0 %collective-permute-start.85 = (bf16[2,4,96,2048]{3,2,1,0:T(8,128)(2,1)}, bf16[2,4,96,2048]{3,2,1,0:T(8,128)(2,1)}, u32[]{:S(2)}, u32[]{:S(2)}) collective-permute-start(bf16[2,4,96,2048]{3,2,1,0:T(8,128)(2,1)} %dynamic-slice_bitcast_fusion.2), channel_id=1, source_target_pairs={{0,8},{1,9},{2,10},{3,11},{4,12},{5,13},{6,14},{7,15},{8,0},{9,1},... | collective-permute-start | bytes 9437192 | tf_op jit(solution)/shard_map/ppermute | solution.py:420
  639.9 57.2 %collective-permute-start.52 = (f32[512,1536]{1,0:T(8,128)}, f32[512,1536]{1,0:T(8,128)}, u32[]{:S(2)}, u32[]{:S(2)}) collective-permute-start(f32[512,1536]{1,0:T(8,128)} %dynamic-slice_bitcast_fusion.5), channel_id=1, source_target_pairs={{0,1},{1,0},{2,3},{3,2},{4,5},{5,4},{6,7},{7,6},{8,9},{9,8},{10,11... | collective-permute-start | bytes 9437192 | tf_op jit(solution)/shard_map/ppermute | solution.py:420
  650.2 109.9 %collective-permute-start.79 = (bf16[2,4,96,2048]{3,2,1,0:T(8,128)(2,1)S(1)}, bf16[2,4,96,2048]{3,2,1,0:T(8,128)(2,1)}, u32[]{:S(2)}, u32[]{:S(2)}) collective-permute-start(bf16[2,4,96,2048]{3,2,1,0:T(8,128)(2,1)S(1)} %dynamic-slice_bitcast_fusion.3), channel_id=1, source_target_pairs={{0,16},{1,17},{2,18},{3,19},{4,20},{5,21},{6,22},{7,23},{8,24},{9,... | collective-permute-start | bytes 9437192 | tf_op jit(solution)/shard_map/ppermute | solution.py:420
  665.4 492.6 %collective-permute-start.46 = (f32[512,1536]{1,0:T(8,128)}, f32[512,1536]{1,0:T(8,128)}, u32[]{:S(2)}, u32[]{:S(2)}) collective-permute-start(f32[512,1536]{1,0:T(8,128)} %dynamic-slice_bitcast_fusion.6), channel_id=1, source_target_pairs={{0,1},{1,0},{2,3},{3,2},{4,5},{5,4},{6,7},{7,6},{8,9},{9,8},{10,11... | collective-permute-start | bytes 9437192 | tf_op jit(solution)/shard_map/ppermute | solution.py:420
  696.7 112.5 %collective-permute-start.92 = (bf16[4,128,1536]{2,1,0:T(8,128)(2,1)S(1)}, bf16[4,128,1536]{2,1,0:T(8,128)(2,1)}, u32[]{:S(2)}, u32[]{:S(2)}) collective-permute-start(bf16[4,128,1536]{2,1,0:T(8,128)(2,1)S(1)} %fusion.68), channel_id=1, source_target_pairs={{0,8},{1,9},{2,10},{3,11},{4,12},{5,13},{6,14},{7,15},{8,0},{9,1},... | collective-permute-start | bytes 4718600 | tf_op jit(solution)/shard_map/ppermute | solution.py:420
  704.8 96.7 %collective-permute-start.86 = (bf16[4,96,2048]{2,1,0:T(8,128)(2,1)S(1)}, bf16[4,96,2048]{2,1,0:T(8,128)(2,1)}, u32[]{:S(2)}, u32[]{:S(2)}) collective-permute-start(bf16[4,96,2048]{2,1,0:T(8,128)(2,1)S(1)} %fusion.67), channel_id=1, source_target_pairs={{0,16},{1,17},{2,18},{3,19},{4,20},{5,21},{6,22},{7,23},{8,24},{9,... | collective-permute-start | bytes 4718600 | tf_op jit(solution)/shard_map/ppermute | solution.py:420
  705.8 58.5 %collective-permute-start.75 = (f32[1536]{0:T(1024)S(1)}, f32[1536]{0:T(1024)S(1)}, u32[]{:S(2)}, u32[]{:S(2)}) collective-permute-start(f32[1536]{0:T(1024)S(1)} %add.396), channel_id=1, source_target_pairs={{0,8},{1,9},{2,10},{3,11},{4,12},{5,13},{6,14},{7,15},{8,0},{9,1},... | collective-permute-start | bytes 18440 | tf_op jit(solution)/shard_map/ppermute | solution.py:420
  764.3 28.3 %collective-permute-start.76 = (f32[1536]{0:T(1024)S(1)}, f32[1536]{0:T(1024)S(1)}, u32[]{:S(2)}, u32[]{:S(2)}) collective-permute-start(f32[1536]{0:T(1024)S(1)} %add.397), channel_id=1, source_target_pairs={{0,16},{1,17},{2,18},{3,19},{4,20},{5,21},{6,22},{7,23},{8,24},{9,... | collective-permute-start | bytes 18440 | tf_op jit(solution)/shard_map/ppermute | solution.py:420
  765.6 39.7 %collective-permute-start.80 = (bf16[4,96,2048]{2,1,0:T(8,128)(2,1)S(1)}, bf16[4,96,2048]{2,1,0:T(8,128)(2,1)S(1)}, u32[]{:S(2)}, u32[]{:S(2)}) collective-permute-start(bf16[4,96,2048]{2,1,0:T(8,128)(2,1)S(1)} %fusion.66), channel_id=1, source_target_pairs={{0,8},{1,9},{2,10},{3,11},{4,12},{5,13},{6,14},{7,15},{8,0},{9,1},... | collective-permute-start | bytes 4718600 | tf_op jit(solution)/shard_map/ppermute | solution.py:420
  804.8 210.7 %collective-permute-start.87 = (bf16[96,2048]{1,0:T(8,128)(2,1)}, bf16[96,2048]{1,0:T(8,128)(2,1)}, u32[]{:S(2)}, u32[]{:S(2)}) collective-permute-start(bf16[96,2048]{1,0:T(8,128)(2,1)} %get-tuple-element.245), channel_id=1, source_target_pairs={{0,2},{1,3},{2,0},{3,1},{4,6},{5,7},{6,4},{7,5},{8,10},{9,11},{10,... | collective-permute-start | bytes 1179656 | tf_op jit(solution)/shard_map/ppermute | solution.py:420
  805.3 211.2 %collective-permute-start.88 = (bf16[96,2048]{1,0:T(8,128)(2,1)}, bf16[96,2048]{1,0:T(8,128)(2,1)}, u32[]{:S(2)}, u32[]{:S(2)}) collective-permute-start(bf16[96,2048]{1,0:T(8,128)(2,1)} %get-tuple-element.247), channel_id=1, source_target_pairs={{0,4},{1,5},{2,6},{3,7},{4,0},{5,1},{6,2},{7,3},{8,12},{9,13},{10,... | collective-permute-start | bytes 1179656 | tf_op jit(solution)/shard_map/ppermute | solution.py:420
  809.2 209.2 %collective-permute-start.89 = (bf16[96,2048]{1,0:T(8,128)(2,1)}, bf16[96,2048]{1,0:T(8,128)(2,1)}, u32[]{:S(2)}, u32[]{:S(2)}) collective-permute-start(bf16[96,2048]{1,0:T(8,128)(2,1)} %get-tuple-element.246), channel_id=1, source_target_pairs={{0,6},{1,7},{2,4},{3,5},{4,2},{5,3},{6,0},{7,1},{8,14},{9,15},{10,... | collective-permute-start | bytes 1179656 | tf_op jit(solution)/shard_map/ppermute | solution.py:420
  814.2 207.2 %collective-permute-start.81 = (bf16[96,2048]{1,0:T(8,128)(2,1)}, bf16[96,2048]{1,0:T(8,128)(2,1)}, u32[]{:S(2)}, u32[]{:S(2)}) collective-permute-start(bf16[96,2048]{1,0:T(8,128)(2,1)} %get-tuple-element.248), channel_id=1, source_target_pairs={{0,2},{1,3},{2,0},{3,1},{4,6},{5,7},{6,4},{7,5},{8,10},{9,11},{10,... | collective-permute-start | bytes 1179656 | tf_op jit(solution)/shard_map/ppermute | solution.py:420
  1015.5 28.6 %collective-permute-start.82 = (bf16[96,2048]{1,0:T(8,128)(2,1)}, bf16[96,2048]{1,0:T(8,128)(2,1)}, u32[]{:S(2)}, u32[]{:S(2)}) collective-permute-start(bf16[96,2048]{1,0:T(8,128)(2,1)} %get-tuple-element.250), channel_id=1, source_target_pairs={{0,4},{1,5},{2,6},{3,7},{4,0},{5,1},{6,2},{7,3},{8,12},{9,13},{10,... | collective-permute-start | bytes 1179656 | tf_op jit(solution)/shard_map/ppermute | solution.py:420
  1016.5 27.5 %collective-permute-start.83 = (bf16[96,2048]{1,0:T(8,128)(2,1)S(1)}, bf16[96,2048]{1,0:T(8,128)(2,1)}, u32[]{:S(2)}, u32[]{:S(2)}) collective-permute-start(bf16[96,2048]{1,0:T(8,128)(2,1)S(1)} %copy-done.85), channel_id=1, source_target_pairs={{0,6},{1,7},{2,4},{3,5},{4,2},{5,3},{6,0},{7,1},{8,14},{9,15},{10,... | collective-permute-start | bytes 1179656 | tf_op jit(solution)/shard_map/ppermute | solution.py:420
  1018.4 30.6 %collective-permute-start.68 = (bf16[8,48,1536]{2,1,0:T(8,128)(2,1)}, bf16[8,48,1536]{2,1,0:T(8,128)(2,1)}, u32[]{:S(2)}, u32[]{:S(2)}) collective-permute-start(bf16[8,48,1536]{2,1,0:T(8,128)(2,1)} %dynamic-slice_bitcast_fusion.10), channel_id=1, source_target_pairs={{0,1},{1,0},{2,3},{3,2},{4,5},{5,4},{6,7},{7,6},{8,9},{9,8},{10,11... | collective-permute-start | bytes 3538952 | tf_op jit(solution)/shard_map/ppermute | solution.py:420
  1021.3 31.3 %collective-permute-start.93 = (bf16[128,1536]{1,0:T(8,128)(2,1)}, bf16[128,1536]{1,0:T(8,128)(2,1)}, u32[]{:S(2)}, u32[]{:S(2)}) collective-permute-start(bf16[128,1536]{1,0:T(8,128)(2,1)} %get-tuple-element.242), channel_id=1, source_target_pairs={{0,2},{1,3},{2,0},{3,1},{4,6},{5,7},{6,4},{7,5},{8,10},{9,11},{10,... | collective-permute-start | bytes 1179656 | tf_op jit(solution)/shard_map/ppermute | solution.py:420
  1044.1 33.7 %collective-permute-start.94 = (bf16[128,1536]{1,0:T(8,128)(2,1)}, bf16[128,1536]{1,0:T(8,128)(2,1)}, u32[]{:S(2)}, u32[]{:S(2)}) collective-permute-start(bf16[128,1536]{1,0:T(8,128)(2,1)} %get-tuple-element.244), channel_id=1, source_target_pairs={{0,4},{1,5},{2,6},{3,7},{4,0},{5,1},{6,2},{7,3},{8,12},{9,13},{10,... | collective-permute-start | bytes 1179656 | tf_op jit(solution)/shard_map/ppermute | solution.py:420
  1044.1 33.7 %collective-permute-start.95 = (bf16[128,1536]{1,0:T(8,128)(2,1)}, bf16[128,1536]{1,0:T(8,128)(2,1)}, u32[]{:S(2)}, u32[]{:S(2)}) collective-permute-start(bf16[128,1536]{1,0:T(8,128)(2,1)} %get-tuple-element.243), channel_id=1, source_target_pairs={{0,6},{1,7},{2,4},{3,5},{4,2},{5,3},{6,0},{7,1},{8,14},{9,15},{10,... | collective-permute-start | bytes 1179656 | tf_op jit(solution)/shard_map/ppermute | solution.py:420
  1049.0 60.3 %collective-permute-start.62 = (bf16[2,4,96,1536]{3,2,1,0:T(8,128)(2,1)}, bf16[2,4,96,1536]{3,2,1,0:T(8,128)(2,1)}, u32[]{:S(2)}, u32[]{:S(2)}) collective-permute-start(bf16[2,4,96,1536]{3,2,1,0:T(8,128)(2,1)} %dynamic-slice_bitcast_fusion.8), channel_id=1, source_target_pairs={{0,16},{1,17},{2,18},{3,19},{4,20},{5,21},{6,22},{7,23},{8,24},{9,... | collective-permute-start | bytes 7077896 | tf_op jit(solution)/shard_map/ppermute | solution.py:420
  1052.6 87.8 %collective-permute-start.54 = (f32[512,1536]{1,0:T(8,128)}, f32[512,1536]{1,0:T(8,128)}, u32[]{:S(2)}, u32[]{:S(2)}) collective-permute-start(f32[512,1536]{1,0:T(8,128)} %dynamic-slice_bitcast_fusion.4), channel_id=1, source_target_pairs={{0,1},{1,0},{2,3},{3,2},{4,5},{5,4},{6,7},{7,6},{8,9},{9,8},{10,11... | collective-permute-start | bytes 9437192 | tf_op jit(solution)/shard_map/ppermute | solution.py:420
  1077.8 28.7 %collective-permute-start.69 = (bf16[2,4,48,1536]{3,2,1,0:T(8,128)(2,1)}, bf16[2,4,48,1536]{3,2,1,0:T(8,128)(2,1)}, u32[]{:S(2)}, u32[]{:S(2)}) collective-permute-start(bf16[2,4,48,1536]{3,2,1,0:T(8,128)(2,1)} %dynamic-slice_bitcast_fusion.9), channel_id=1, source_target_pairs={{0,8},{1,9},{2,10},{3,11},{4,12},{5,13},{6,14},{7,15},{8,0},{9,1},... | collective-permute-start | bytes 3538952 | tf_op jit(solution)/shard_map/ppermute | solution.py:420
  1112.7 56.9 %collective-permute-start.63 = (bf16[4,96,1536]{2,1,0:T(8,128)(2,1)S(1)}, bf16[4,96,1536]{2,1,0:T(8,128)(2,1)}, u32[]{:S(2)}, u32[]{:S(2)}) collective-permute-start(bf16[4,96,1536]{2,1,0:T(8,128)(2,1)S(1)} %fusion.73), channel_id=1, source_target_pairs={{0,8},{1,9},{2,10},{3,11},{4,12},{5,13},{6,14},{7,15},{8,0},{9,1},... | collective-permute-start | bytes 3538952 | tf_op jit(solution)/shard_map/ppermute | solution.py:420
  1165.6 30.9 %collective-permute-start.55 = (bf16[256,1536]{1,0:T(8,128)(2,1)S(1)}, bf16[256,1536]{1,0:T(8,128)(2,1)S(1)}, u32[]{:S(2)}, u32[]{:S(2)}) collective-permute-start(bf16[256,1536]{1,0:T(8,128)(2,1)S(1)} %get-tuple-element.284), channel_id=1, source_target_pairs={{0,0},{1,16},{2,2},{3,18},{4,4},{5,20},{6,6},{7,22},{8,8},{9,24},{... | collective-permute-start | bytes 2359304 | tf_op jit(solution)/shard_map/ppermute | solution.py:420
  (170 other events, 3264.0 us)

commit v2 on v0

--- a/solution.py
+++ b/solution.py
@@ -1,8 +1,12 @@
+import functools
 import math
 
 import jax
 import jax.numpy as jnp
 from jax import lax
+from jax.experimental import pallas as pl
+from jax.experimental.pallas import tpu as pltpu
+from jax.sharding import Mesh
 from jax.sharding import PartitionSpec as P
 
 HEADS = 16
@@ -398,38 +402,508 @@
     )
 
 
+QB = 256
+SPAN = 768
+
+
+def turned(field, back):
+    middle = HD // 2
+    left, right = field[:, :middle], field[:, middle:]
+    if back:
+        return jnp.concatenate([right, -left], axis=1)
+    return jnp.concatenate([-right, left], axis=1)
+
+
+def spun(field, cosine, sine, back=False):
+    field = field.astype(jnp.float32)
+    return field * cosine + turned(field, back) * sine
+
+
+def nt(left, right):
+    return lax.dot_general(left, right, (((1,), (1,)), ((), ())), preferred_element_type=jnp.float32)
+
+
+def nn(left, right):
+    return jnp.dot(left, right, preferred_element_type=jnp.float32)
+
+
+def tn(left, right):
+    return lax.dot_general(left, right, (((0,), (0,)), ((), ())), preferred_element_type=jnp.float32)
+
+
+def head(ref, rows, number):
+    return ref[rows, HD * number : HD * (number + 1)]
+
+
+def ahead_kernel(heads, kvs, q_ref, kv_ref, cos_ref, sin_ref, row_ref, col_ref, out_ref, keys):
+    low, f32 = jnp.bfloat16, jnp.float32
+    step = pl.program_id(0)
+    everything = pl.ds(0, kv_ref.shape[0])
+
+    @pl.when(step == 0)
+    def _():
+        for j in range(kvs):
+            keys[j] = spun(head(kv_ref, everything, j), cos_ref[...], sin_ref[...]).astype(low)
+
+    start = pl.multiple_of(step * QB, QB)
+    base = pl.multiple_of(jnp.maximum(start + QB - SPAN, 0), QB)
+    here, span = pl.ds(start, QB), pl.ds(base, SPAN)
+    place = start + lax.broadcasted_iota(jnp.int32, (QB, SPAN), 0)
+    key_place = base + lax.broadcasted_iota(jnp.int32, (QB, SPAN), 1)
+    allowed = (key_place <= place) & (col_ref[here, :] == row_ref[:, span])
+    bias = jnp.where(allowed, 0.0, -1e30).astype(f32)
+    scale = (1.0 / math.sqrt(HD)) * math.log2(math.e)
+    cosine, sine = cos_ref[here, :], sin_ref[here, :]
+    results = []
+    for h in range(heads):
+        j = h * kvs // heads
+        query = spun(head(q_ref, here, h), cosine, sine).astype(low)
+        scores = nt(query, keys[j, span, :]) * scale + bias
+        peak = jnp.max(scores, axis=1, keepdims=True)
+        weights = jnp.exp2(scores - peak)
+        total = jnp.sum(weights, axis=1, keepdims=True)
+        probs = (weights * (1.0 / total)).astype(low)
+        results.append(nn(probs, head(kv_ref, span, kvs + j)).astype(low))
+    out_ref[...] = jnp.concatenate(results, axis=1)
+
+
+def behind_kernel(
+    heads, kvs, q_ref, kv_ref, grad_ref, cos_ref, sin_ref, row_ref, col_ref, gq_ref, gkv_ref, keys, gks, gvs
+):
+    low, f32 = jnp.bfloat16, jnp.float32
+    step = pl.program_id(0)
+    everything = pl.ds(0, kv_ref.shape[0])
+
+    @pl.when(step == 0)
+    def _():
+        for j in range(kvs):
+            keys[j] = spun(head(kv_ref, everything, j), cos_ref[...], sin_ref[...]).astype(low)
+        gks[...] = jnp.zeros_like(gks)
+        gvs[...] = jnp.zeros_like(gvs)
+
+    start = pl.multiple_of(step * QB, QB)
+    base = pl.multiple_of(jnp.maximum(start + QB - SPAN, 0), QB)
+    here, span = pl.ds(start, QB), pl.ds(base, SPAN)
+    key_place = base + lax.broadcasted_iota(jnp.int32, (SPAN, QB), 0)
+    place = start + lax.broadcasted_iota(jnp.int32, (SPAN, QB), 1)
+    allowed = (key_place <= place) & (col_ref[span, :] == row_ref[:, here])
+    bias = jnp.where(allowed, 0.0, -1e30).astype(f32)
+    width = 1.0 / math.sqrt(HD)
+    scale = width * math.log2(math.e)
+    cosine, sine = cos_ref[here, :], sin_ref[here, :]
+    results = []
+    for h in range(heads):
+        j = h * kvs // heads
+        query = spun(head(q_ref, here, h), cosine, sine).astype(low)
+        key, value = keys[j, span, :], head(kv_ref, span, kvs + j)
+        grad = head(grad_ref, here, h)
+        scores = nt(key, query) * scale + bias
+        peak = jnp.max(scores, axis=0, keepdims=True)
+        weights = jnp.exp2(scores - peak)
+        total = jnp.sum(weights, axis=0, keepdims=True)
+        probs = weights * (1.0 / total)
+        slope = nt(value, grad)
+        centre = jnp.sum(probs * slope, axis=0, keepdims=True)
+        gs = (probs * (slope - centre)).astype(low)
+        gvs[j, span, :] += nn(probs.astype(low), grad)
+        gks[j, span, :] += nn(gs, query)
+        results.append(spun(tn(gs, key) * width, cosine, sine, True).astype(low))
+    gq_ref[...] = jnp.concatenate(results, axis=1)
+
+    @pl.when(step == pl.num_programs(0) - 1)
+    def _():
+        gk = [spun(gks[j] * width, cos_ref[...], sin_ref[...], True).astype(low) for j in range(kvs)]
+        gv = [gvs[j].astype(low) for j in range(kvs)]
+        gkv_ref[...] = jnp.concatenate(gk + gv, axis=1)
+
+
+def whole(shape):
+    return pl.BlockSpec(shape, lambda i: (0,) * len(shape))
+
+
+def attend_ahead(heads, kvs, q, kv, cosine, sine, row, col):
+    length = q.shape[0]
+    return pl.pallas_call(
+        functools.partial(ahead_kernel, heads, kvs),
+        grid=(length // QB,),
+        in_specs=[whole(v.shape) for v in (q, kv, cosine, sine, row, col)],
+        out_specs=pl.BlockSpec((QB, heads * HD), lambda i: (i, 0)),
+        out_shape=jax.ShapeDtypeStruct((length, heads * HD), jnp.bfloat16),
+        scratch_shapes=[pltpu.VMEM((kvs, length, HD), jnp.bfloat16)],
+        compiler_params=pltpu.CompilerParams(vmem_limit_bytes=48 << 20),
+        cost_estimate=pl.CostEstimate(flops=4 * heads * length * SPAN * HD, bytes_accessed=6 << 20, transcendentals=heads * length * SPAN),
+    )(q, kv, cosine, sine, row, col)
+
+
+def attend_behind(heads, kvs, q, kv, grad, cosine, sine, row, col):
+    length = q.shape[0]
+    return pl.pallas_call(
+        functools.partial(behind_kernel, heads, kvs),
+        grid=(length // QB,),
+        in_specs=[whole(v.shape) for v in (q, kv, grad, cosine, sine, row, col)],
+        out_specs=[
+            pl.BlockSpec((QB, heads * HD), lambda i: (i, 0)),
+            pl.BlockSpec((length, 2 * kvs * HD), lambda i: (0, 0)),
+        ],
+        out_shape=[
+            jax.ShapeDtypeStruct((length, heads * HD), jnp.bfloat16),
+            jax.ShapeDtypeStruct((length, 2 * kvs * HD), jnp.bfloat16),
+        ],
+        scratch_shapes=[
+            pltpu.VMEM((kvs, length, HD), jnp.bfloat16),
+            pltpu.VMEM((kvs, length, HD), jnp.float32),
+            pltpu.VMEM((kvs, length, HD), jnp.float32),
+        ],
+        compiler_params=pltpu.CompilerParams(vmem_limit_bytes=48 << 20),
+        cost_estimate=pl.CostEstimate(flops=10 * heads * length * SPAN * HD, bytes_accessed=9 << 20, transcendentals=heads * length * SPAN),
+    )(q, kv, grad, cosine, sine, row, col)
+
+
+AXES = ("y", "x", "zh", "zl", "core")
+BITS = {"y": 16, "x": 8, "zh": 4, "zl": 2, "core": 1}
+
+
+def hop(value, *names):
+    flip = sum(BITS[name] for name in names)
+    return lax.ppermute(value, AXES, [(i, i ^ flip) for i in range(32)])
+
+
+def after(value, *others):
+    return lax.optimization_barrier((value,) + others)[0]
+
+
+def in_order(mine, other, place, axis=0):
+    first = jnp.where(place == 0, mine, other)
+    second = jnp.where(place == 0, other, mine)
+    return jnp.concatenate([first, second], axis=axis)
+
+
+def pick(value, place, axis=0):
+    return lax.dynamic_index_in_dim(value, place, axis, keepdims=False)
+
+
+def plane_turn(tokens, x):
+    got = []
+    for flip in range(2):
+        pairs = []
+        for i in range(32):
+            y_i, x_i, z_i, core_i = i // 16, i // 8 % 2, i // 2 % 4, i % 2
+            pairs.append((i, core_i * 16 + (x_i ^ flip) * 8 + z_i * 2 + y_i))
+        got.append(lax.ppermute(pick(tokens, x ^ flip), AXES, pairs)[None])
+    return in_order(got[0], got[1], x)
+
+
+def gather_line(block, zh, zl):
+    got = [block[None]] + [hop(block, *names)[None] for names in (("zl",), ("zh",), ("zh", "zl"))]
+    return in_order(in_order(got[0], got[1], zl), in_order(got[2], got[3], zl), zh)
+
+
+def plane_out(line, x_first):
+    return hop(line, "x" if x_first else "y")
+
+
+def plane_pair(line, got, y, x, x_first):
+    if x_first:
+        return in_order(line[None], got[None], x)[None]
+    return in_order(line[None], got[None], y)[:, None]
+
+
+def plane_rest(pair, y, x, x_first):
+    if x_first:
+        done = in_order(pair, hop(pair, "y"), y)
+    else:
+        done = in_order(pair, hop(pair, "x"), x, axis=1)
+    return done.reshape((4,) + done.shape[2:])
+
+
+def gather_plane(line, y, x, x_first):
+    pair = plane_pair(line, plane_out(line, x_first), y, x, x_first)
+    return plane_rest(pair, y, x, x_first)
+
+
+def plane_send(total, y, x, y_first):
+    total = total.reshape((2, 2) + total.shape[1:])
+    if y_first:
+        return pick(total, y), hop(pick(total, 1 - y), "y")
+    return pick(total, x, 1), hop(pick(total, 1 - x, 1), "x")
+
+
+def plane_sum(kept, got, y, x, y_first):
+    f32, low = jnp.float32, jnp.bfloat16
+    half = kept.astype(f32) + got.astype(f32)
+    if y_first:
+        return pick(half, x) + hop(pick(half, 1 - x).astype(low), "x").astype(f32)
+    return pick(half, y) + hop(pick(half, 1 - y).astype(low), "y").astype(f32)
+
+
+def scatter_line(line, zh, zl):
+    f32, low = jnp.float32, jnp.bfloat16
+    place = zh * 2 + zl
+    result = pick(line, place)
+    for k, names in ((1, ("zl",)), (2, ("zh",)), (3, ("zh", "zl"))):
+        result = result + hop(pick(line, place ^ k).astype(low), *names).astype(f32)
+    return result
+
+
+def scatter_pairs(line, zh):
+    return pick(line, zh) + hop(pick(line, 1 - zh).astype(jnp.bfloat16), "zh").astype(jnp.float32)
+
+
+def add_all(value):
+    for name in ("core", "x", "y", "zl", "zh"):
+        value = value + hop(value, name)
+    return value
+
+
+def fast_body(
+    layer_input,
+    cotangent,
+    token_mask,
+    document_ids,
+    attn_gain,
+    w_query,
+    w_key,
+    w_value,
+    w_output,
+    mlp_gain,
+    w_gate,
+    w_up,
+    w_down,
+):
+    f32, low = jnp.float32, jnp.bfloat16
+    y, x, zh, zl, core = (lax.axis_index(name) for name in AXES)
+    device = sum(lax.axis_index(name) * BITS[name] for name in AXES)
+    quarter, width = layer_input.shape[1:]
+    half_len = 2 * quarter
+    length = 2 * half_len
+    rows = w_query.shape[0]
+    units = w_gate.shape[1]
+    heads, kvs = HEADS // 2, KV // 2
+    cosine, sine = rope_tables(length, HD)
+
+    def swap_in(mine, sent):
+        return in_order(mine[None], hop(sent, "core")[None], core)
+
+    def halves(weight):
+        return weight.reshape(rows, 2, -1)
+
+    def both(mine):
+        return in_order(mine, hop(mine, "core"), core)
+
+    def join(part):
+        part = part.reshape(2, half_len, width)
+        return pick(part, core) + hop(pick(part, 1 - core), "core")
+
+    query_w = halves(w_query)
+    pair_w = jnp.concatenate([halves(w_key), halves(w_value)], axis=2)
+    query_w, pair_w = (
+        swap_in(pick(w, core, 1), pick(w, 1 - core, 1)).reshape(2 * rows, -1)
+        for w in (query_w, pair_w)
+    )
+    own = plane_turn(layer_input, x).reshape(half_len, width)
+    masked = cotangent * token_mask.astype(low)[:, :, None]
+    masked = after(masked, own)
+    seed_low = plane_turn(masked, x).reshape(half_len, width)
+    gains = jnp.stack([attn_gain, mlp_gain])[:, None]
+    gains = in_order(gains, hop(gains, "core"), core, axis=1).reshape(1, -1)
+    gains = gather_plane(gather_line(gains, zh, zl), y, x, True).reshape(16, 2, 2 * rows)
+    gains = jnp.moveaxis(gains, 1, 0).reshape(2, width).astype(f32)
+    documents = pick(jnp.where(core == y, document_ids, hop(document_ids, "core")), x)
+    row, col = documents[None, :], documents[:, None]
+    query_w = gather_line(query_w, zh, zl)
+    pair_w = gather_line(pair_w, zh, zl)
+
+    hidden_ws = []
+    for weight in (w_gate, w_up):
+        weight = weight.reshape(rows, units // 512, 2, 2, 128)
+        mine, sent = (
+            jnp.moveaxis(pick(weight, place, 3), 2, 0).reshape(2, rows, -1)
+            for place in (core, 1 - core)
+        )
+        block = jnp.stack([mine, hop(sent, "core")])
+        block = jnp.where(core == 0, block, block[::-1])
+        block = after(jnp.moveaxis(block, 0, 1), query_w, pair_w)
+        block = in_order(pick(block, zl)[None], hop(pick(block, 1 - zl), "zl")[None], zl)
+        block = block.reshape(4 * rows, -1)
+        hidden_ws.append(in_order(block, hop(block, "zh"), zh))
+    down_ws = []
+    for columns in (slice(0, width // 2), slice(width // 2, width)):
+        block = after(w_down[:, columns], query_w, pair_w)
+        down_ws.append(in_order(block, hop(block, "zh"), zh))
+    out_w = gather_line(after(w_output, query_w, pair_w), zh, zl)
+
+    query_w = gather_plane(query_w, y, x, True).reshape(width, -1)
+    pair_w = gather_plane(pair_w, y, x, False).reshape(width, -1)
+    lines = [out_w] + hidden_ws + down_ws
+    ways = [True, True, False, True, False]
+    lines = [after(line, query_w, pair_w) for line in lines]
+    outs = [plane_out(line, way) for line, way in zip(lines, ways)]
+
+    inputs = own.astype(f32)
+    inv_one = inverse_rms(inputs)
+    unit_one = inputs * inv_one
+    normed = both((unit_one * gains[0]).astype(low))
+    query = nn(normed, query_w).astype(low)
+    pair = nn(normed, pair_w).astype(low)
+    mixed = attend_ahead(heads, kvs, query, pair, cosine, sine, row, col)
+
+    pairs = [
+        plane_pair(line, after(got, mixed), y, x, way)
+        for line, got, way in zip(lines, outs, ways)
+    ]
+    out_w = plane_rest(pairs[0], y, x, True).reshape(2, 8, rows, width)
+    out_got = hop(pick(out_w, 1 - core), "core")
+    out_w = in_order(pick(out_w, core)[:, None], out_got[:, None], core, axis=1).reshape(-1, width)
+    gate_w, up_w, down_l, down_r = (
+        plane_rest(pair_, y, x, way) for pair_, way in zip(pairs[1:], ways[1:])
+    )
+    gate_w, up_w = gate_w.reshape(width, -1), up_w.reshape(width, -1)
+    down_w = jnp.concatenate([down_l, down_r], axis=-1).reshape(-1, width)
+
+    hidden = inputs + join(nn(mixed, out_w))
+    inv_two = inverse_rms(hidden)
+    unit_two = hidden * inv_two
+
+    def spread(mine):
+        far = hop(mine, "zl")
+        return (
+            jnp.concatenate([mine, hop(mine, "core")]),
+            jnp.concatenate([far, hop(far, "core")]),
+        )
+
+    seeds = spread(after(seed_low, query_w, pair_w))
+    normed_two = spread((unit_two * gains[1]).astype(low))
+
+    def ahead_and_back(tokens, seed):
+        gate, upward, grad_act = nn(tokens, gate_w), nn(tokens, up_w), nt(seed, down_w)
+        sigma = jax.nn.sigmoid(gate)
+        activated = (gate * sigma * upward).astype(low)
+        up_low = (grad_act * gate * sigma).astype(low)
+        gate_low = (grad_act * upward * sigma * (1.0 + gate * (1.0 - sigma))).astype(low)
+        back = nt(gate_low, gate_w) + nt(up_low, up_w)
+        return activated, gate_low, up_low, nn(activated, down_w), back
+
+    near = ahead_and_back(normed_two[0], seeds[0])
+    far_tokens = after(normed_two[1], near[4])
+    far = ahead_and_back(far_tokens, seeds[1])
+
+    def fold(part):
+        return part[:half_len] + hop(part[half_len:], "core")
+
+    theirs = fold(far[4]).astype(low)
+    back = hop(theirs, "zl")
+    near_low, far_low = (
+        tuple(after(v, theirs) for v in parts[:3]) for parts in (near, far)
+    )
+    grad_down = (tn(near_low[0], seeds[0]) + tn(far_low[0], seeds[1])).astype(low)
+    grad_gate = (tn(normed_two[0], near_low[1]) + tn(far_tokens, far_low[1])).astype(low)
+    grad_up = (tn(normed_two[0], near_low[2]) + tn(far_tokens, far_low[2])).astype(low)
+    totals = [
+        grad_gate.reshape(4, 2, 2, 2 * rows, -1),
+        grad_up.reshape(4, 2, 2, 2 * rows, -1),
+        grad_down[:, : width // 2].reshape(4, 2, -1, width // 2),
+        grad_down[:, width // 2 :].reshape(4, 2, -1, width // 2),
+    ]
+    kepts = [plane_send(total, y, x, way) for total, way in zip(totals, ways[1:])]
+
+    grad_normed_two = fold(near[4]) + back.astype(f32)
+    scaled_two = grad_normed_two * gains[1]
+    grad_hidden = seed_low.astype(f32) + inv_two * (
+        scaled_two - unit_two * jnp.mean(scaled_two * unit_two, axis=-1, keepdims=True)
+    )
+    grad_low = both(grad_hidden.astype(low))
+    grad_heads = nt(grad_low, out_w).astype(low)
+    grad_heads = after(grad_heads, *totals)
+
+    ahead_low = after(fold(far[3]).astype(low), back)
+    output = hidden + fold(near[3]) + hop(ahead_low, "zl").astype(f32)
+    gain_two = jnp.sum(grad_normed_two * unit_two, axis=0)
+
+    grad_query, grad_pair = attend_behind(
+        heads, kvs, query, pair, grad_heads, cosine, sine, row, col
+    )
+    output = after(output.astype(low), grad_query)
+    output = plane_turn(output.reshape(2, quarter, width), x)
+    part = nt(grad_query, query_w) + nt(grad_pair, pair_w)
+    grad_out_w = tn(mixed, grad_low).astype(low).reshape(8, 2, rows, width)
+    got = hop(pick(grad_out_w, 1 - core, 1), "core")
+    grad_out_w = in_order(pick(grad_out_w, core, 1), got, core).reshape(4, 4, rows, width)
+    tails = [
+        tn(normed, grad_query).astype(low).reshape(4, 4, 2 * rows, -1),
+        tn(normed, grad_pair).astype(low).reshape(4, 4, 2 * rows, -1),
+        grad_out_w[..., : width // 2],
+        grad_out_w[..., width // 2 :],
+    ]
+    tail_ways = [True, False, True, False]
+    tail_kepts = [plane_send(total, y, x, way) for total, way in zip(tails, tail_ways)]
+    sums = [
+        scatter_pairs(plane_sum(kept, after(got, part), y, x, way), zh)
+        for (kept, got), way in zip(kepts, ways[1:])
+    ]
+    grad_normed = join(part)
+    scaled_one = grad_normed * gains[0]
+    grad_input = grad_hidden + inv_one * (
+        scaled_one - unit_one * jnp.mean(scaled_one * unit_one, axis=-1, keepdims=True)
+    )
+    grad_input = plane_turn(grad_input.astype(low).reshape(2, quarter, width), x)
+    gain_one = add_all(jnp.stack([jnp.sum(grad_normed * unit_one, axis=0), gain_two]))
+    tail_sums = [
+        scatter_line(plane_sum(kept, got, y, x, way), zh, zl)
+        for (kept, got), way in zip(tail_kepts, tail_ways)
+    ]
+
+    hidden_grads = []
+    for total in sums[:2]:
+        total = in_order(pick(total, zl)[None], hop(pick(total, 1 - zl), "zl")[None], zl)
+        total = total.reshape(2, 2, rows, -1)
+        total = swap_in(pick(total, core, 1), pick(total, 1 - core, 1))
+        total = jnp.transpose(total.reshape(2, 2, rows, -1, 128), (2, 3, 1, 0, 4))
+        hidden_grads.append(total.reshape(rows, units))
+    grad_down = jnp.concatenate(sums[2:], axis=1)
+    grad_output = jnp.concatenate(tail_sums[2:], axis=1)
+    moved = []
+    for total in tail_sums[:2]:
+        total = total.reshape(2, rows, -1)
+        moved.append(swap_in(pick(total, core), pick(total, 1 - core)))
+    q_grad = jnp.moveaxis(moved[0], 0, 1).reshape(rows, -1)
+    k_grad, v_grad = (
+        jnp.moveaxis(part_, 0, 1).reshape(rows, -1)
+        for part_ in (moved[1][:, :, : kvs * HD], moved[1][:, :, kvs * HD :])
+    )
+    gain_one = lax.dynamic_slice_in_dim(gain_one, device * rows, rows, 1)
+
+    return (
+        output,
+        grad_input,
+        gain_one[0],
+        q_grad,
+        k_grad,
+        v_grad,
+        grad_output,
+        gain_one[1],
+        hidden_grads[0],
+        hidden_grads[1],
+        grad_down,
+    )
+
+
 def solution(mesh):
-    placed = (
-        P("batch", "seq", None),
-        P("batch", "seq", None),
-        P("batch", "seq"),
-        P("batch", None),
-        P(("seq", "batch")),
-        P(("seq", "batch"), None),
-        P(("seq", "batch"), None),
-        P(("seq", "batch"), None),
-        P(("seq", "batch"), None),
-        P(("seq", "batch")),
-        P(("seq", "batch"), None),
-        P(("seq", "batch"), None),
-        P(("seq", "batch"), None),
-    )
+    fast = dict(mesh.shape) == {"seq": 4, "batch": 8}
+    if fast:
+        grid = Mesh(mesh.devices.reshape((2,) * 5), AXES)
+        seq, batch = ("y", "x"), ("zh", "zl", "core")
+    else:
+        grid, seq, batch = mesh, ("seq",), ("batch",)
+    weight = P(seq + batch, None)
+    gain = P(seq + batch)
+    token = P(batch, seq, None)
     return jax.shard_map(
-        body,
-        mesh=mesh,
-        in_specs=placed,
-        out_specs=(
-            P("batch", "seq", None),
-            P("batch", "seq", None),
-            P(("seq", "batch")),
-            P(("seq", "batch"), None),
-            P(("seq", "batch"), None),
-            P(("seq", "batch"), None),
-            P(("seq", "batch"), None),
-            P(("seq", "batch")),
-            P(("seq", "batch"), None),
-            P(("seq", "batch"), None),
-            P(("seq", "batch"), None),
-        ),
+        fast_body if fast else body,
+        mesh=grid,
+        in_specs=(token, token, P(batch, seq), P(batch, None), gain)
+        + (weight,) * 4
+        + (gain,)
+        + (weight,) * 3,
+        out_specs=(token, token, gain) + (weight,) * 4 + (gain,) + (weight,) * 3,
         check_vma=False,
     )

time: 2170 us -> 814 us (0.38)
  waiting for transfers between devices: 1450 us -> 354 us
  matrix products: 308 us -> 121 us
  local copies, waits for them, and re-layouts: 170 us -> 68.9 us
  blocking collectives: 82 us -> 0 us
  Pallas kernels: 0 us -> 75.4 us
  starting transfers between devices: 47.6 us -> 114 us
    reduce_scatter x7 -> x0, waiting for transfers between devices: 1070 us -> none  [the longest x1 253 us: body(): lax.psum_scatter(outer_sum(rows['normed_two'], rows['up_low']), ('seq', '...]
    ppermute x0 -> x109, waiting for transfers between devices: none -> 354 us  [the longest x101 331 us: hop(): return lax.ppermute(value, AXES, [(i, i ^ flip) for i in range(32)])]
    all_gather x7 -> x0, waiting for transfers between devices: 307 us -> none  [the longest x1 87.9 us: fetch_feedforward(): lax.all_gather(w_down, ('seq', 'batch'), axis=0, tiled=True)]
    dot_general x63 -> x27, matrix products: 308 us -> 121 us  [the longest x9 42.4 us: tn(): lax.dot_general(left, right, (((0,), (0,)), ((), ())), preferred_element_...]
    ppermute x0 -> x109, starting transfers between devices: none -> 114 us  [the longest x101 93.7 us: hop(): return lax.ppermute(value, AXES, [(i, i ^ flip) for i in range(32)])]
    unnamed x2 -> x0, blocking collectives: 82 us -> none
    pallas_call x0 -> x2, Pallas kernels: none -> 75.4 us  [the longest x1 40.9 us: attend_behind(): pl.pallas_call(functools.partial(behind_kernel, heads, kvs), grid=(length...]
    all_to_all x12 -> x0, waiting for transfers between devices: 68.2 us -> none  [the longest x2 22.1 us: body(): lax.all_to_all(grad_query_heads, 'seq', split_axis=0, concat_axis=1, tile...]
  transfers between devices with their start and end apart: 26 -> 109, of which waited for: 22 -> 42; matrix products, arithmetic and copies ran while one was open for 16% -> 27% of each run, Pallas kernels for 0% -> 9%
where the time goes in v2:
time: 814 us; the launch traced here: 806 us
  waiting for transfers between devices  354 us (43%)
  matrix products  121 us (15%)
  starting transfers between devices  114 us (14%)
  Pallas kernels  75.4 us (9%)
  local copies, waits for them, and re-layouts  68.9 us (8%)
  other arithmetic  68.2 us (8%)
    ppermute x101, waiting for transfers between devices, hop(): return lax.ppermute(value, AXES, [(i, i ^ flip) for i in range(32)])  331 us
    ppermute x101, starting transfers between devices, hop(): return lax.ppermute(value, AXES, [(i, i ^ flip) for i in range(32)])  93.7 us
    dot_general x9, matrix products, tn(): lax.dot_general(left, right, (((0,), (0,)), ((), ())), preferred_element_...  42.4 us
    dot_general x9, matrix products, nn(): return jnp.dot(left, right, preferred_element_type=jnp.float32)  41.3 us
    pallas_call x1, Pallas kernels, attend_behind(): pl.pallas_call(functools.partial(behind_kernel, heads, kvs), grid=(length...  40.9 us
    dot_general x9, matrix products, nt(): lax.dot_general(left, right, (((1,), (1,)), ((), ())), preferred_element_...  37.7 us
    pallas_call x1, Pallas kernels, attend_ahead(): pl.pallas_call(functools.partial(ahead_kernel, heads, kvs), grid=(length...  34.5 us
    unnamed x199, local copies, waits for them, and re-layouts  24.4 us
  transfers between devices with their start and end apart: 109, of which 42 were waited for; matrix products, arithmetic and copies ran while one was open for 27% of the time, Pallas kernels for 9%

profile of v2, /device:TPU:0, one launch (start us, length us, event | category | flops | bytes accessed | tf_op | source)
XLA Modules:
  0.0 805.6 jit_solution(16858294953573202049)
XLA Ops:
  28.8 7.5 collective-permute-start
  48.4 7.6 collective-permute-start.49
  60.2 6.6 collective-permute-done.16
  66.9 7.2 collective-permute-done.10
  75.2 5.9 collective-permute-done.18
  89.4 5.0 collective-permute-start.22
  101.7 4.2 collective-permute-done.24
  106.1 5.5 collective-permute-done.31
  112.9 6.3 collective-permute-done.36
  119.8 11.3 %collective-permute-done.40 = bf16[128,768]{1,0:T(8,128)(2,1)S(1)} collective-permute-done((bf16[128,768]{1,0:T(8,128)(2,1)S(1)}, bf16[128,768]{1,0:T(8,128)(2,1)S(1)}, u32[]{:S(2)}, u32[]{:S(2)}) %collective-permute-start.40) | collective-permute-done | bytes 196640 | tf_op jit(solution)/shard_map/ppermute | solution.py:568
  135.6 11.3 %collective-permute-done.13 = bf16[4,96,768]{2,1,0:T(8,128)(2,1)S(1)} collective-permute-done((bf16[4,96,768]{2,1,0:T(8,128)(2,1)S(1)}, bf16[4,96,768]{2,1,0:T(8,128)(2,1)S(1)}, u32[]{:S(2)}, u32[]{:S(2)}) %collective-permute-start.13) | collective-permute-done | bytes 589856 | tf_op jit(solution)/shard_map/ppermute | solution.py:568
  148.7 17.6 %collective-permute-done.20 = bf16[2,1,4,96,768]{4,3,2,1,0:T(8,128)(2,1)S(1)} collective-permute-done((bf16[2,1,4,96,768]{4,3,2,1,0:T(8,128)(2,1)S(1)}, bf16[2,1,4,96,768]{4,3,2,1,0:T(8,128)(2,1)S(1)}, u32[]{:S(2)}, u32[]{:S(2)}) %collective-permute-start.20) | collective-permute-done | bytes 1179680 | tf_op jit(solution)/shard_map/ppermute | solution.py:568
  166.3 3.9 collective-permute-start.32
  170.6 4.4 collective-permute-done.14
  176.8 4.9 convolution_convert_fusion.3.kv_ref
  184.3 34.5 %shard_map.212 = bf16[1024,768]{1,0:T(8,128)(2,1)S(1)} custom-call(bf16[1024,768]{1,0:T(8,128)(2,1)S(1)} %convolution_convert_fusion.4.q_ref, bf16[1024,768]{1,0:T(8,128)(2,1)} %convolution_convert_fusion.3.kv_ref, f32[1024,96]{1,0:T(8,128)S(1)} %get-tuple-element.243.cos_ref, f32[1024,96]{1,0:T(8,128)S(1)} %get-tuple-element.244.sin_ref, ...), custom_call_target="tpu_custom_call" | custom-call | flops 2415919104 | bytes 6291456 | tf_op jit(solution)/shard_map/pallas_call | solution.py:526
  228.9 12.6 %collective-permute-done.26 = bf16[1,2,4,48,1536]{4,3,2,1,0:T(8,128)(2,1)S(1)} collective-permute-done((bf16[1,2,4,48,1536]{4,3,2,1,0:T(8,128)(2,1)S(1)}, bf16[1,2,4,48,1536]{4,3,2,1,0:T(8,128)(2,1)S(1)}, u32[]{:S(2)}, u32[]{:S(2)}) %collective-permute-start.26) | collective-permute-done | bytes 1179680 | tf_op jit(solution)/shard_map/ppermute | solution.py:568
  249.9 22.0 %collective-permute-done.44 = bf16[256,768]{1,0:T(8,128)(2,1)S(1)} collective-permute-done((bf16[256,768]{1,0:T(8,128)(2,1)S(1)}, bf16[256,768]{1,0:T(8,128)(2,1)S(1)}, u32[]{:S(2)}, u32[]{:S(2)}) %collective-permute-start.44) | collective-permute-done | bytes 393248 | tf_op jit(solution)/shard_map/ppermute | solution.py:568
  278.7 12.0 %collective-permute-done.42 = bf16[1,2,256,768]{3,2,1,0:T(8,128)(2,1)S(1)} collective-permute-done((bf16[1,2,256,768]{3,2,1,0:T(8,128)(2,1)S(1)}, bf16[1,2,256,768]{3,2,1,0:T(8,128)(2,1)S(1)}, u32[]{:S(2)}, u32[]{:S(2)}) %collective-permute-start.42) | collective-permute-done | bytes 786464 | tf_op jit(solution)/shard_map/ppermute | solution.py:568
  296.7 6.9 fusion.72
  303.6 23.5 %collective-permute-done.39 = bf16[2,1,384,1024]{3,2,0,1:T(8,128)(2,1)} collective-permute-done((bf16[2,1,384,1024]{3,2,0,1:T(8,128)(2,1)S(1)}, bf16[2,1,384,1024]{3,2,0,1:T(8,128)(2,1)}, u32[]{:S(2)}, u32[]{:S(2)}) %collective-permute-start.39) | collective-permute-done | bytes 1572896 | tf_op jit(solution)/shard_map/ppermute | solution.py:568
  339.4 5.0 fusion.70
  344.4 25.7 %collective-permute-done.47 = bf16[512,1536]{1,0:T(8,128)(2,1)S(1)} collective-permute-done((bf16[512,1536]{1,0:T(8,128)(2,1)S(1)}, bf16[512,1536]{1,0:T(8,128)(2,1)S(1)}, u32[]{:S(2)}, u32[]{:S(2)}) %collective-permute-start.47) | collective-permute-done | bytes 1572896 | tf_op jit(solution)/shard_map/ppermute | solution.py:568
  370.2 5.9 fusion.74
  376.0 8.4 %multiply_convert_fusion.4 = (bf16[1024,1024]{1,0:T(8,128)(2,1)S(1)}, bf16[1024,1024]{1,0:T(8,128)(2,1)}, bf16[1024,1024]{1,0:T(8,128)(2,1)S(1)}) fusion(f32[1024,1024]{1,0:T(8,128)S(1)} %copy-done.79, f32[1024,1024]{1,0:T(8,128)} %fusion.74, bf16[1536,1024]{1,0:T(8,128)(2,1)S(1)} %bitcast.591, bf16[512,1536]{1,0:T(8,128)(2,1)} %copy-done.76, ...), kind=kOutput, calls=%fused_computation.11 | convolution fusion | flops 3244294144 | bytes 20971520 | tf_op jit(solution)/shard_map/dot_general | solution.py:427
  387.9 5.4 convolution_add_fusion.2
  397.0 6.7 multiply_convert_fusion.1
  440.4 5.6 add_convert_fusion
  449.1 5.4 fusion.87
  454.5 7.5 add_convert_fusion.1
  465.1 5.4 fusion.86
  478.6 5.6 add_convert_fusion.2
  494.1 4.7 fusion.18.grad_ref
  498.8 40.9 %shard_map.213 = (bf16[1024,768]{1,0:T(8,128)(2,1)S(1)}, bf16[1024,768]{1,0:T(8,128)(2,1)S(1)}) custom-call(bf16[1024,768]{1,0:T(8,128)(2,1)} %copy-done.2, bf16[1024,768]{1,0:T(8,128)(2,1)} %convolution_convert_fusion.3.kv_ref, bf16[1024,768]{1,0:T(8,128)(2,1)} %fusion.18.grad_ref, f32[1024,96]{1,0:T(8,128)S(1)} %get-tuple-element.243.cos_ref, ...), custom_call_target="tpu_custom_call" | custom-call | flops 6039797760 | bytes 9437184 | tf_op jit(solution)/shard_map/pallas_call | solution.py:540
  570.5 11.7 %collective-permute-done.105 = bf16[128,768]{1,0:T(8,128)(2,1)S(1)} collective-permute-done((bf16[128,768]{1,0:T(8,128)(2,1)S(1)}, bf16[128,768]{1,0:T(8,128)(2,1)S(1)}, u32[]{:S(2)}, u32[]{:S(2)}) %collective-permute-start.105) | collective-permute-done | bytes 196640 | tf_op jit(solution)/shard_map/ppermute | solution.py:568
  582.3 9.2 %collective-permute-done.108 = bf16[128,768]{1,0:T(8,128)(2,1)S(1)} collective-permute-done((bf16[128,768]{1,0:T(8,128)(2,1)S(1)}, bf16[128,768]{1,0:T(8,128)(2,1)S(1)}, u32[]{:S(2)}, u32[]{:S(2)}) %collective-permute-start.108) | collective-permute-done | bytes 196640 | tf_op jit(solution)/shard_map/ppermute | solution.py:568
  597.7 24.1 %collective-permute-done.100 = bf16[2,96,1024]{2,1,0:T(8,128)(2,1)S(1)} collective-permute-done((bf16[2,96,1024]{2,1,0:T(8,128)(2,1)S(1)}, bf16[2,96,1024]{2,1,0:T(8,128)(2,1)S(1)}, u32[]{:S(2)}, u32[]{:S(2)}) %collective-permute-start.100) | collective-permute-done | bytes 393248 | tf_op jit(solution)/shard_map/ppermute | solution.py:568
  622.0 8.2 %collective-permute-done.95 = bf16[2,96,1024]{2,1,0:T(8,128)(2,1)S(1)} collective-permute-done((bf16[2,96,1024]{2,1,0:T(8,128)(2,1)S(1)}, bf16[2,96,1024]{2,1,0:T(8,128)(2,1)S(1)}, u32[]{:S(2)}, u32[]{:S(2)}) %collective-permute-start.95) | collective-permute-done | bytes 393248 | tf_op jit(solution)/shard_map/ppermute | solution.py:568
  634.9 7.2 collective-permute-done.101
  642.6 7.0 collective-permute-done.96
  650.6 10.0 %collective-permute-done.77 = bf16[4,96,768]{2,1,0:T(8,128)(2,1)S(1)} collective-permute-done((bf16[4,96,768]{2,1,0:T(8,128)(2,1)S(1)}, bf16[4,96,768]{2,1,0:T(8,128)(2,1)S(1)}, u32[]{:S(2)}, u32[]{:S(2)}) %collective-permute-start.77) | collective-permute-done | bytes 589856 | tf_op jit(solution)/shard_map/ppermute | solution.py:568
  668.3 8.0 collective-permute-done.79
  678.5 10.4 %collective-permute-done.73 = bf16[96,768]{1,0:T(8,128)(2,1)S(1)} collective-permute-done((bf16[96,768]{1,0:T(8,128)(2,1)S(1)}, bf16[96,768]{1,0:T(8,128)(2,1)S(1)}, u32[]{:S(2)}, u32[]{:S(2)}) %collective-permute-start.73) | collective-permute-done | bytes 147488 | tf_op jit(solution)/shard_map/ppermute | solution.py:568
  719.3 31.8 %collective-permute-done.91 = bf16[48,768]{1,0:T(8,128)(2,1)S(1)} collective-permute-done((bf16[48,768]{1,0:T(8,128)(2,1)S(1)}, bf16[48,768]{1,0:T(8,128)(2,1)S(1)}, u32[]{:S(2)}, u32[]{:S(2)}) %collective-permute-start.91) | collective-permute-done | bytes 73760 | tf_op jit(solution)/shard_map/ppermute | solution.py:568
  754.2 4.2 fusion.10
  761.0 4.8 fusion.9
  778.7 8.3 %collective-permute-done.64 = bf16[256,1536]{1,0:T(8,128)(2,1)S(1)} collective-permute-done((bf16[256,1536]{1,0:T(8,128)(2,1)S(1)}, bf16[256,1536]{1,0:T(8,128)(2,1)S(1)}, u32[]{:S(2)}, u32[]{:S(2)}) %collective-permute-start.64) | collective-permute-done | bytes 786464 | tf_op jit(solution)/shard_map/ppermute | solution.py:592
  788.4 15.5 %collective-permute-done.61 = bf16[256,1536]{1,0:T(8,128)(2,1)S(1)} collective-permute-done((bf16[256,1536]{1,0:T(8,128)(2,1)S(1)}, bf16[256,1536]{1,0:T(8,128)(2,1)S(1)}, u32[]{:S(2)}, u32[]{:S(2)}) %collective-permute-start.61) | collective-permute-done | bytes 786464 | tf_op jit(solution)/shard_map/ppermute | solution.py:592
  (632 shorter events, 288.6 us)
Async XLA Ops:
  4.3 42.3 %collective-permute-start.15 = (bf16[48,768]{1,0:T(8,128)(2,1)}, bf16[48,768]{1,0:T(8,128)(2,1)}, u32[]{:S(2)}, u32[]{:S(2)}) collective-permute-start(bf16[48,768]{1,0:T(8,128)(2,1)} %bitcast.561), channel_id=1, source_target_pairs={{0,1},{1,0},{2,3},{3,2},{4,5},{5,4},{6,7},{7,6},{8,9},{9,8},{10,11... | collective-permute-start | bytes 221192 | tf_op jit(solution)/shard_map/ppermute | solution.py:568
  7.3 41.1 %collective-permute-start.9 = (bf16[48,768]{1,0:T(8,128)(2,1)}, bf16[48,768]{1,0:T(8,128)(2,1)}, u32[]{:S(2)}, u32[]{:S(2)}) collective-permute-start(bf16[48,768]{1,0:T(8,128)(2,1)} %bitcast.562), channel_id=1, source_target_pairs={{0,1},{1,0},{2,3},{3,2},{4,5},{5,4},{6,7},{7,6},{8,9},{9,8},{10,11... | collective-permute-start | bytes 221192 | tf_op jit(solution)/shard_map/ppermute | solution.py:568
  11.3 45.7 %collective-permute-start.30 = (bf16[2,48,1024]{2,1,0:T(8,128)(2,1)}, bf16[2,48,1024]{2,1,0:T(8,128)(2,1)}, u32[]{:S(2)}, u32[]{:S(2)}) collective-permute-start(bf16[2,48,1024]{2,1,0:T(8,128)(2,1)} %reshape.477), channel_id=1, source_target_pairs={{0,1},{1,0},{2,3},{3,2},{4,5},{5,4},{6,7},{7,6},{8,9},{9,8},{10,11... | collective-permute-start | bytes 589832 | tf_op jit(solution)/shard_map/ppermute | solution.py:568
  28.8 102.3 %collective-permute-start = (bf16[256,1536]{1,0:T(8,128)(2,1)}, bf16[256,1536]{1,0:T(8,128)(2,1)}, u32[]{:S(2)}, u32[]{:S(2)}) collective-permute-start(bf16[256,1536]{1,0:T(8,128)(2,1)} %get-tuple-element.137), channel_id=1, source_target_pairs={{0,0},{1,16},{2,2},{3,18},{4,4},{5,20},{6,6},{7,22},{8,8},{9,24},{... | collective-permute-start | bytes 2359304 | tf_op jit(solution)/shard_map/ppermute | solution.py:592
  44.9 86.4 %collective-permute-start.1 = (bf16[256,1536]{1,0:T(8,128)(2,1)S(1)}, bf16[256,1536]{1,0:T(8,128)(2,1)}, u32[]{:S(2)}, u32[]{:S(2)}) collective-permute-start(bf16[256,1536]{1,0:T(8,128)(2,1)S(1)} %copy-done.52), channel_id=1, source_target_pairs={{0,8},{1,24},{2,10},{3,26},{4,12},{5,28},{6,14},{7,30},{8,0},{9,16... | collective-permute-start | bytes 2359304 | tf_op jit(solution)/shard_map/ppermute | solution.py:592
  48.4 174.6 %collective-permute-start.49 = (bf16[256,1536]{1,0:T(8,128)(2,1)}, bf16[256,1536]{1,0:T(8,128)(2,1)}, u32[]{:S(2)}, u32[]{:S(2)}) collective-permute-start(bf16[256,1536]{1,0:T(8,128)(2,1)} %get-tuple-element.125), channel_id=1, source_target_pairs={{0,0},{1,16},{2,2},{3,18},{4,4},{5,20},{6,6},{7,22},{8,8},{9,24},{... | collective-permute-start | bytes 2359304 | tf_op jit(solution)/shard_map/ppermute | solution.py:592
  101.7 31.7 %collective-permute-start.19 = (bf16[4,96,768]{2,1,0:T(8,128)(2,1)S(1)}, bf16[4,96,768]{2,1,0:T(8,128)(2,1)S(1)}, u32[]{:S(2)}, u32[]{:S(2)}) collective-permute-start(bf16[4,96,768]{2,1,0:T(8,128)(2,1)S(1)} %pad_maximum_fusion.28), channel_id=1, source_target_pairs={{0,16},{1,17},{2,18},{3,19},{4,20},{5,21},{6,22},{7,23},{8,24},{9,... | collective-permute-start | bytes 1769480 | tf_op jit(solution)/shard_map/ppermute | solution.py:568
  133.5 32.7 %collective-permute-start.20 = (bf16[2,1,4,96,768]{4,3,2,1,0:T(8,128)(2,1)S(1)}, bf16[2,1,4,96,768]{4,3,2,1,0:T(8,128)(2,1)S(1)}, u32[]{:S(2)}, u32[]{:S(2)}) collective-permute-start(bf16[2,1,4,96,768]{4,3,2,1,0:T(8,128)(2,1)S(1)} %maximum_bitcast_fusion.3), channel_id=1, source_target_pairs={{0,8},{1,9},{2,10},{3,11},{4,12},{5,13},{6,14},{7,15},{8,0},{9,1},... | collective-permute-start | bytes 3538952 | tf_op jit(solution)/shard_map/ppermute | solution.py:568
  147.1 27.9 %collective-permute-start.14 = (bf16[1,2,4,96,768]{4,3,2,1,0:T(8,128)(2,1)S(1)}, bf16[1,2,4,96,768]{4,3,2,1,0:T(8,128)(2,1)S(1)}, u32[]{:S(2)}, u32[]{:S(2)}) collective-permute-start(bf16[1,2,4,96,768]{4,3,2,1,0:T(8,128)(2,1)S(1)} %maximum_bitcast_fusion.2), channel_id=1, source_target_pairs={{0,16},{1,17},{2,18},{3,19},{4,20},{5,21},{6,22},{7,23},{8,24},{9,... | collective-permute-start | bytes 3538952 | tf_op jit(solution)/shard_map/ppermute | solution.py:568
  147.7 27.8 %collective-permute-start.8 = (bf16[512,1536]{1,0:T(8,128)(2,1)S(1)}, bf16[512,1536]{1,0:T(8,128)(2,1)S(1)}, u32[]{:S(2)}, u32[]{:S(2)}) collective-permute-start(bf16[512,1536]{1,0:T(8,128)(2,1)S(1)} %fusion.4), channel_id=1, source_target_pairs={{0,1},{1,0},{2,3},{3,2},{4,5},{5,4},{6,7},{7,6},{8,9},{9,8},{10,11... | collective-permute-start | bytes 4718600 | tf_op jit(solution)/shard_map/ppermute | solution.py:568
  148.3 74.8 %collective-permute-start.50 = (bf16[256,1536]{1,0:T(8,128)(2,1)S(1)}, bf16[256,1536]{1,0:T(8,128)(2,1)S(1)}, u32[]{:S(2)}, u32[]{:S(2)}) collective-permute-start(bf16[256,1536]{1,0:T(8,128)(2,1)S(1)} %copy-done.51), channel_id=1, source_target_pairs={{0,8},{1,24},{2,10},{3,26},{4,12},{5,28},{6,14},{7,30},{8,0},{9,16... | collective-permute-start | bytes 2359304 | tf_op jit(solution)/shard_map/ppermute | solution.py:592
  166.3 58.3 %collective-permute-start.32 = (bf16[192,1024]{1,0:T(8,128)(2,1)S(1)}, bf16[192,1024]{1,0:T(8,128)(2,1)}, u32[]{:S(2)}, u32[]{:S(2)}) collective-permute-start(bf16[192,1024]{1,0:T(8,128)(2,1)S(1)} %bitcast.623), channel_id=1, source_target_pairs={{0,4},{1,5},{2,6},{3,7},{4,0},{5,1},{6,2},{7,3},{8,12},{9,13},{10,... | collective-permute-start | bytes 1179656 | tf_op jit(solution)/shard_map/ppermute | solution.py:568
  175.0 51.0 %collective-permute-start.37 = (bf16[192,1024]{1,0:T(8,128)(2,1)S(1)}, bf16[192,1024]{1,0:T(8,128)(2,1)}, u32[]{:S(2)}, u32[]{:S(2)}) collective-permute-start(bf16[192,1024]{1,0:T(8,128)(2,1)S(1)} %bitcast.624), channel_id=1, source_target_pairs={{0,4},{1,5},{2,6},{3,7},{4,0},{5,1},{6,2},{7,3},{8,12},{9,13},{10,... | collective-permute-start | bytes 1179656 | tf_op jit(solution)/shard_map/ppermute | solution.py:568
  175.4 43.4 %collective-permute-start.25 = (bf16[4,48,1536]{2,1,0:T(8,128)(2,1)S(1)}, bf16[4,48,1536]{2,1,0:T(8,128)(2,1)}, u32[]{:S(2)}, u32[]{:S(2)}) collective-permute-start(bf16[4,48,1536]{2,1,0:T(8,128)(2,1)S(1)} %pad_maximum_fusion.29), channel_id=1, source_target_pairs={{0,8},{1,9},{2,10},{3,11},{4,12},{5,13},{6,14},{7,15},{8,0},{9,1},... | collective-permute-start | bytes 1769480 | tf_op jit(solution)/shard_map/ppermute | solution.py:568
  241.9 32.3 %collective-permute-start.27 = (bf16[8,48,1536]{2,1,0:T(8,128)(2,1)S(1)}, bf16[8,48,1536]{2,1,0:T(8,128)(2,1)S(1)}, u32[]{:S(2)}, u32[]{:S(2)}) collective-permute-start(bf16[8,48,1536]{2,1,0:T(8,128)(2,1)S(1)} %dynamic-slice_bitcast_fusion.7), channel_id=1, source_target_pairs={{0,1},{1,0},{2,3},{3,2},{4,5},{5,4},{6,7},{7,6},{8,9},{9,8},{10,11... | collective-permute-start | bytes 3538952 | tf_op jit(solution)/shard_map/ppermute | solution.py:568
  242.1 31.6 %collective-permute-start.33 = (bf16[384,1024]{1,0:T(8,128)(2,1)S(1)}, bf16[384,1024]{1,0:T(8,128)(2,1)S(1)}, u32[]{:S(2)}, u32[]{:S(2)}) collective-permute-start(bf16[384,1024]{1,0:T(8,128)(2,1)S(1)} %pad_maximum_fusion.22), channel_id=1, source_target_pairs={{0,8},{1,9},{2,10},{3,11},{4,12},{5,13},{6,14},{7,15},{8,0},{9,1},... | collective-permute-start | bytes 2359304 | tf_op jit(solution)/shard_map/ppermute | solution.py:568
  243.7 34.1 %collective-permute-start.38 = (bf16[384,1024]{1,0:T(8,128)(2,1)S(1)}, bf16[384,1024]{1,0:T(8,128)(2,1)S(1)}, u32[]{:S(2)}, u32[]{:S(2)}) collective-permute-start(bf16[384,1024]{1,0:T(8,128)(2,1)S(1)} %pad_maximum_fusion.23), channel_id=1, source_target_pairs={{0,16},{1,17},{2,18},{3,19},{4,20},{5,21},{6,22},{7,23},{8,24},{9,... | collective-permute-start | bytes 2359304 | tf_op jit(solution)/shard_map/ppermute | solution.py:568
  245.5 48.0 %collective-permute-start.53 = (bf16[512,1536]{1,0:T(8,128)(2,1)S(1)}, bf16[512,1536]{1,0:T(8,128)(2,1)S(1)}, u32[]{:S(2)}, u32[]{:S(2)}) collective-permute-start(bf16[512,1536]{1,0:T(8,128)(2,1)S(1)} %bitcast.565), channel_id=1, source_target_pairs={{0,2},{1,3},{2,0},{3,1},{4,6},{5,7},{6,4},{7,5},{8,10},{9,11},{10,... | collective-permute-start | bytes 4718600 | tf_op jit(solution)/shard_map/ppermute | solution.py:568
  277.5 51.4 %collective-permute-start.28 = (f32[512,1536]{1,0:T(8,128)S(1)}, f32[512,1536]{1,0:T(8,128)S(1)}, u32[]{:S(2)}, u32[]{:S(2)}) collective-permute-start(f32[512,1536]{1,0:T(8,128)S(1)} %dynamic-slice_bitcast_fusion.1), channel_id=1, source_target_pairs={{0,1},{1,0},{2,3},{3,2},{4,5},{5,4},{6,7},{7,6},{8,9},{9,8},{10,11... | collective-permute-start | bytes 9437192 | tf_op jit(solution)/shard_map/ppermute | solution.py:568
  290.7 45.1 %collective-permute-start.34 = (bf16[1,2,384,1024]{3,2,1,0:T(8,128)(2,1)S(1)}, bf16[1,2,384,1024]{3,2,1,0:T(8,128)(2,1)}, u32[]{:S(2)}, u32[]{:S(2)}) collective-permute-start(bf16[1,2,384,1024]{3,2,1,0:T(8,128)(2,1)S(1)} %maximum_bitcast_fusion), channel_id=1, source_target_pairs={{0,16},{1,17},{2,18},{3,19},{4,20},{5,21},{6,22},{7,23},{8,24},{9,... | collective-permute-start | bytes 4718600 | tf_op jit(solution)/shard_map/ppermute | solution.py:568
  292.5 34.7 %collective-permute-start.39 = (bf16[2,1,384,1024]{3,2,0,1:T(8,128)(2,1)S(1)}, bf16[2,1,384,1024]{3,2,0,1:T(8,128)(2,1)}, u32[]{:S(2)}, u32[]{:S(2)}) collective-permute-start(bf16[2,1,384,1024]{3,2,0,1:T(8,128)(2,1)S(1)} %maximum_bitcast_fusion.1), channel_id=1, source_target_pairs={{0,8},{1,9},{2,10},{3,11},{4,12},{5,13},{6,14},{7,15},{8,0},{9,1},... | collective-permute-start | bytes 4718600 | tf_op jit(solution)/shard_map/ppermute | solution.py:568
  293.5 44.2 %collective-permute-start.54 = (bf16[512,1536]{1,0:T(8,128)(2,1)S(1)}, bf16[512,1536]{1,0:T(8,128)(2,1)S(1)}, u32[]{:S(2)}, u32[]{:S(2)}) collective-permute-start(bf16[512,1536]{1,0:T(8,128)(2,1)S(1)} %collective-permute-done.53), channel_id=1, source_target_pairs={{0,1},{1,0},{2,3},{3,2},{4,5},{5,4},{6,7},{7,6},{8,9},{9,8},{10,11... | collective-permute-start | bytes 4718600 | tf_op jit(solution)/shard_map/ppermute | solution.py:568
  331.3 38.8 %collective-permute-start.29 = (bf16[512,1536]{1,0:T(8,128)(2,1)S(1)}, bf16[512,1536]{1,0:T(8,128)(2,1)S(1)}, u32[]{:S(2)}, u32[]{:S(2)}) collective-permute-start(bf16[512,1536]{1,0:T(8,128)(2,1)S(1)} %multiply_convert_fusion.6), channel_id=1, source_target_pairs={{0,1},{1,0},{2,3},{3,2},{4,5},{5,4},{6,7},{7,6},{8,9},{9,8},{10,11... | collective-permute-start | bytes 4718600 | tf_op jit(solution)/shard_map/ppermute | solution.py:568
  331.3 38.8 %collective-permute-start.47 = (bf16[512,1536]{1,0:T(8,128)(2,1)S(1)}, bf16[512,1536]{1,0:T(8,128)(2,1)S(1)}, u32[]{:S(2)}, u32[]{:S(2)}) collective-permute-start(bf16[512,1536]{1,0:T(8,128)(2,1)S(1)} %multiply_convert_fusion.6), channel_id=1, source_target_pairs={{0,2},{1,3},{2,0},{3,1},{4,6},{5,7},{6,4},{7,5},{8,10},{9,11},{10,... | collective-permute-start | bytes 4718600 | tf_op jit(solution)/shard_map/ppermute | solution.py:568
  370.1 23.2 %collective-permute-start.48 = (bf16[512,1536]{1,0:T(8,128)(2,1)S(1)}, bf16[512,1536]{1,0:T(8,128)(2,1)S(1)}, u32[]{:S(2)}, u32[]{:S(2)}) collective-permute-start(bf16[512,1536]{1,0:T(8,128)(2,1)S(1)} %collective-permute-done.47), channel_id=1, source_target_pairs={{0,1},{1,0},{2,3},{3,2},{4,5},{5,4},{6,7},{7,6},{8,9},{9,8},{10,11... | collective-permute-start | bytes 4718600 | tf_op jit(solution)/shard_map/ppermute | solution.py:568
  417.2 53.3 %collective-permute-start.58 = (f32[512,1536]{1,0:T(8,128)S(1)}, f32[512,1536]{1,0:T(8,128)}, u32[]{:S(2)}, u32[]{:S(2)}) collective-permute-start(f32[512,1536]{1,0:T(8,128)S(1)} %slice.93), channel_id=1, source_target_pairs={{0,1},{1,0},{2,3},{3,2},{4,5},{5,4},{6,7},{7,6},{8,9},{9,8},{10,11... | collective-permute-start | bytes 9437192 | tf_op jit(solution)/shard_map/ppermute | solution.py:568
  431.2 54.5 %collective-permute-start.52 = (f32[512,1536]{1,0:T(8,128)}, f32[512,1536]{1,0:T(8,128)}, u32[]{:S(2)}, u32[]{:S(2)}) collective-permute-start(f32[512,1536]{1,0:T(8,128)} %slice.89), channel_id=1, source_target_pairs={{0,1},{1,0},{2,3},{3,2},{4,5},{5,4},{6,7},{7,6},{8,9},{9,8},{10,11... | collective-permute-start | bytes 9437192 | tf_op jit(solution)/shard_map/ppermute | solution.py:568
  434.8 37.1 %collective-permute-start.56 = (bf16[512,1536]{1,0:T(8,128)(2,1)}, bf16[512,1536]{1,0:T(8,128)(2,1)S(1)}, u32[]{:S(2)}, u32[]{:S(2)}) collective-permute-start(bf16[512,1536]{1,0:T(8,128)(2,1)} %fusion.12), channel_id=1, source_target_pairs={{0,2},{1,3},{2,0},{3,1},{4,6},{5,7},{6,4},{7,5},{8,10},{9,11},{10,... | collective-permute-start | bytes 4718600 | tf_op jit(solution)/shard_map/ppermute | solution.py:568
  447.1 98.0 %collective-permute-start.103 = (bf16[2,2,128,768]{3,2,1,0:T(8,128)(2,1)}, bf16[2,2,128,768]{3,2,1,0:T(8,128)(2,1)}, u32[]{:S(2)}, u32[]{:S(2)}) collective-permute-start(bf16[2,2,128,768]{3,2,1,0:T(8,128)(2,1)} %dynamic-slice_bitcast_fusion.9), channel_id=1, source_target_pairs={{0,16},{1,17},{2,18},{3,19},{4,20},{5,21},{6,22},{7,23},{8,24},{9,... | collective-permute-start | bytes 2359304 | tf_op jit(solution)/shard_map/ppermute | solution.py:568
  448.3 99.3 %collective-permute-start.106 = (bf16[2,2,128,768]{3,2,1,0:T(8,128)(2,1)}, bf16[2,2,128,768]{3,2,1,0:T(8,128)(2,1)}, u32[]{:S(2)}, u32[]{:S(2)}) collective-permute-start(bf16[2,2,128,768]{3,2,1,0:T(8,128)(2,1)} %dynamic-slice_bitcast_fusion.8), channel_id=1, source_target_pairs={{0,8},{1,9},{2,10},{3,11},{4,12},{5,13},{6,14},{7,15},{8,0},{9,1},... | collective-permute-start | bytes 2359304 | tf_op jit(solution)/shard_map/ppermute | solution.py:568
  470.5 79.9 %collective-permute-start.98 = (bf16[2,2,2,96,1024]{4,3,2,1,0:T(8,128)(2,1)}, bf16[2,2,2,96,1024]{4,3,2,1,0:T(8,128)(2,1)}, u32[]{:S(2)}, u32[]{:S(2)}) collective-permute-start(bf16[2,2,2,96,1024]{4,3,2,1,0:T(8,128)(2,1)} %dynamic-slice_bitcast_fusion.2), channel_id=1, source_target_pairs={{0,8},{1,9},{2,10},{3,11},{4,12},{5,13},{6,14},{7,15},{8,0},{9,1},... | collective-permute-start | bytes 4718600 | tf_op jit(solution)/shard_map/ppermute | solution.py:568
  485.7 77.6 %collective-permute-start.93 = (bf16[2,2,2,96,1024]{4,3,2,1,0:T(8,128)(2,1)}, bf16[2,2,2,96,1024]{4,3,2,1,0:T(8,128)(2,1)}, u32[]{:S(2)}, u32[]{:S(2)}) collective-permute-start(bf16[2,2,2,96,1024]{4,3,2,1,0:T(8,128)(2,1)} %dynamic-slice_bitcast_fusion.3), channel_id=1, source_target_pairs={{0,16},{1,17},{2,18},{3,19},{4,20},{5,21},{6,22},{7,23},{8,24},{9,... | collective-permute-start | bytes 4718600 | tf_op jit(solution)/shard_map/ppermute | solution.py:568
  552.8 40.3 %collective-permute-start.99 = (bf16[2,2,96,1024]{3,2,1,0:T(8,128)(2,1)S(1)}, bf16[2,2,96,1024]{3,2,1,0:T(8,128)(2,1)S(1)}, u32[]{:S(2)}, u32[]{:S(2)}) collective-permute-start(bf16[2,2,96,1024]{3,2,1,0:T(8,128)(2,1)S(1)} %fusion.22), channel_id=1, source_target_pairs={{0,16},{1,17},{2,18},{3,19},{4,20},{5,21},{6,22},{7,23},{8,24},{9,... | collective-permute-start | bytes 2359304 | tf_op jit(solution)/shard_map/ppermute | solution.py:568
  565.5 28.0 %collective-permute-start.94 = (bf16[2,2,96,1024]{3,2,1,0:T(8,128)(2,1)S(1)}, bf16[2,2,96,1024]{3,2,1,0:T(8,128)(2,1)S(1)}, u32[]{:S(2)}, u32[]{:S(2)}) collective-permute-start(bf16[2,2,96,1024]{3,2,1,0:T(8,128)(2,1)S(1)} %fusion.21), channel_id=1, source_target_pairs={{0,8},{1,9},{2,10},{3,11},{4,12},{5,13},{6,14},{7,15},{8,0},{9,1},... | collective-permute-start | bytes 2359304 | tf_op jit(solution)/shard_map/ppermute | solution.py:568
  566.4 63.9 %collective-permute-start.82 = (bf16[8,48,1536]{2,1,0:T(8,128)(2,1)S(1)}, bf16[8,48,1536]{2,1,0:T(8,128)(2,1)S(1)}, u32[]{:S(2)}, u32[]{:S(2)}) collective-permute-start(bf16[8,48,1536]{2,1,0:T(8,128)(2,1)S(1)} %dynamic-slice_bitcast_fusion.4), channel_id=1, source_target_pairs={{0,1},{1,0},{2,3},{3,2},{4,5},{5,4},{6,7},{7,6},{8,9},{9,8},{10,11... | collective-permute-start | bytes 3538952 | tf_op jit(solution)/shard_map/ppermute | solution.py:568
  568.5 64.6 %collective-permute-start.76 = (bf16[2,4,96,768]{3,2,1,0:T(8,128)(2,1)S(1)}, bf16[2,4,96,768]{3,2,1,0:T(8,128)(2,1)S(1)}, u32[]{:S(2)}, u32[]{:S(2)}) collective-permute-start(bf16[2,4,96,768]{3,2,1,0:T(8,128)(2,1)S(1)} %dynamic-slice_bitcast_fusion.5), channel_id=1, source_target_pairs={{0,8},{1,9},{2,10},{3,11},{4,12},{5,13},{6,14},{7,15},{8,0},{9,1},... | collective-permute-start | bytes 3538952 | tf_op jit(solution)/shard_map/ppermute | solution.py:568
  591.4 42.4 %collective-permute-start.70 = (bf16[2,4,96,768]{3,2,1,0:T(8,128)(2,1)S(1)}, bf16[2,4,96,768]{3,2,1,0:T(8,128)(2,1)S(1)}, u32[]{:S(2)}, u32[]{:S(2)}) collective-permute-start(bf16[2,4,96,768]{3,2,1,0:T(8,128)(2,1)S(1)} %dynamic-slice_bitcast_fusion.6), channel_id=1, source_target_pairs={{0,16},{1,17},{2,18},{3,19},{4,20},{5,21},{6,22},{7,23},{8,24},{9,... | collective-permute-start | bytes 3538952 | tf_op jit(solution)/shard_map/ppermute | solution.py:568
  593.4 28.4 %collective-permute-start.100 = (bf16[2,96,1024]{2,1,0:T(8,128)(2,1)S(1)}, bf16[2,96,1024]{2,1,0:T(8,128)(2,1)S(1)}, u32[]{:S(2)}, u32[]{:S(2)}) collective-permute-start(bf16[2,96,1024]{2,1,0:T(8,128)(2,1)S(1)} %fusion.30), channel_id=1, source_target_pairs={{0,4},{1,5},{2,6},{3,7},{4,0},{5,1},{6,2},{7,3},{8,12},{9,13},{10,... | collective-permute-start | bytes 1179656 | tf_op jit(solution)/shard_map/ppermute | solution.py:568
  593.8 36.4 %collective-permute-start.95 = (bf16[2,96,1024]{2,1,0:T(8,128)(2,1)S(1)}, bf16[2,96,1024]{2,1,0:T(8,128)(2,1)S(1)}, u32[]{:S(2)}, u32[]{:S(2)}) collective-permute-start(bf16[2,96,1024]{2,1,0:T(8,128)(2,1)S(1)} %fusion.29), channel_id=1, source_target_pairs={{0,4},{1,5},{2,6},{3,7},{4,0},{5,1},{6,2},{7,3},{8,12},{9,13},{10,... | collective-permute-start | bytes 1179656 | tf_op jit(solution)/shard_map/ppermute | solution.py:568
  621.8 132.4 %collective-permute-start.62 = (f32[512,1536]{1,0:T(8,128)}, f32[512,1536]{1,0:T(8,128)}, u32[]{:S(2)}, u32[]{:S(2)}) collective-permute-start(f32[512,1536]{1,0:T(8,128)} %dynamic-slice_bitcast_fusion), channel_id=1, source_target_pairs={{0,1},{1,0},{2,3},{3,2},{4,5},{5,4},{6,7},{7,6},{8,9},{9,8},{10,11... | collective-permute-start | bytes 9437192 | tf_op jit(solution)/shard_map/ppermute | solution.py:568
  633.1 27.6 %collective-permute-start.83 = (bf16[2,4,48,768]{3,2,1,0:T(8,128)(2,1)S(1)}, bf16[2,4,48,768]{3,2,1,0:T(8,128)(2,1)S(1)}, u32[]{:S(2)}, u32[]{:S(2)}) collective-permute-start(bf16[2,4,48,768]{3,2,1,0:T(8,128)(2,1)S(1)} %dynamic-slice_bitcast_fusion.19), channel_id=1, source_target_pairs={{0,16},{1,17},{2,18},{3,19},{4,20},{5,21},{6,22},{7,23},{8,24},{9,... | collective-permute-start | bytes 1769480 | tf_op jit(solution)/shard_map/ppermute | solution.py:568
  633.8 27.5 %collective-permute-start.88 = (bf16[2,4,48,768]{3,2,1,0:T(8,128)(2,1)S(1)}, bf16[2,4,48,768]{3,2,1,0:T(8,128)(2,1)S(1)}, u32[]{:S(2)}, u32[]{:S(2)}) collective-permute-start(bf16[2,4,48,768]{3,2,1,0:T(8,128)(2,1)S(1)} %dynamic-slice_bitcast_fusion.18), channel_id=1, source_target_pairs={{0,8},{1,9},{2,10},{3,11},{4,12},{5,13},{6,14},{7,15},{8,0},{9,1},... | collective-permute-start | bytes 1769480 | tf_op jit(solution)/shard_map/ppermute | solution.py:568
  660.5 29.8 %collective-permute-start.102 = (f32[2,48,1024]{2,1,0:T(8,128)S(1)}, f32[2,48,1024]{2,1,0:T(8,128)S(1)}, u32[]{:S(2)}, u32[]{:S(2)}) collective-permute-start(f32[2,48,1024]{2,1,0:T(8,128)S(1)} %dynamic-slice_bitcast_fusion.20), channel_id=1, source_target_pairs={{0,1},{1,0},{2,3},{3,2},{4,5},{5,4},{6,7},{7,6},{8,9},{9,8},{10,11... | collective-permute-start | bytes 1179656 | tf_op jit(solution)/shard_map/ppermute | solution.py:568
  678.5 82.5 %collective-permute-start.46 = (f32[512,1536]{1,0:T(8,128)}, f32[512,1536]{1,0:T(8,128)}, u32[]{:S(2)}, u32[]{:S(2)}) collective-permute-start(f32[512,1536]{1,0:T(8,128)} %slice.87), channel_id=1, source_target_pairs={{0,1},{1,0},{2,3},{3,2},{4,5},{5,4},{6,7},{7,6},{8,9},{9,8},{10,11... | collective-permute-start | bytes 9437192 | tf_op jit(solution)/shard_map/ppermute | solution.py:568
  714.8 46.1 %collective-permute-start.57 = (bf16[512,1536]{1,0:T(8,128)(2,1)S(1)}, bf16[512,1536]{1,0:T(8,128)(2,1)S(1)}, u32[]{:S(2)}, u32[]{:S(2)}) collective-permute-start(bf16[512,1536]{1,0:T(8,128)(2,1)S(1)} %copy-done.45), channel_id=1, source_target_pairs={{0,2},{1,3},{2,0},{3,1},{4,6},{5,7},{6,4},{7,5},{8,10},{9,11},{10,... | collective-permute-start | bytes 4718600 | tf_op jit(solution)/shard_map/ppermute | solution.py:568
  714.8 36.2 %collective-permute-start.91 = (bf16[48,768]{1,0:T(8,128)(2,1)S(1)}, bf16[48,768]{1,0:T(8,128)(2,1)S(1)}, u32[]{:S(2)}, u32[]{:S(2)}) collective-permute-start(bf16[48,768]{1,0:T(8,128)(2,1)S(1)} %get-tuple-element.172), channel_id=1, source_target_pairs={{0,4},{1,5},{2,6},{3,7},{4,0},{5,1},{6,2},{7,3},{8,12},{9,13},{10,... | collective-permute-start | bytes 221192 | tf_op jit(solution)/shard_map/ppermute | solution.py:568
  717.2 37.0 %collective-permute-start.92 = (bf16[48,768]{1,0:T(8,128)(2,1)S(1)}, bf16[48,768]{1,0:T(8,128)(2,1)S(1)}, u32[]{:S(2)}, u32[]{:S(2)}) collective-permute-start(bf16[48,768]{1,0:T(8,128)(2,1)S(1)} %get-tuple-element.171), channel_id=1, source_target_pairs={{0,6},{1,7},{2,4},{3,5},{4,2},{5,3},{6,0},{7,1},{8,14},{9,15},{10,... | collective-permute-start | bytes 221192 | tf_op jit(solution)/shard_map/ppermute | solution.py:568
  775.0 28.9 %collective-permute-start.61 = (bf16[256,1536]{1,0:T(8,128)(2,1)S(1)}, bf16[256,1536]{1,0:T(8,128)(2,1)S(1)}, u32[]{:S(2)}, u32[]{:S(2)}) collective-permute-start(bf16[256,1536]{1,0:T(8,128)(2,1)S(1)} %get-tuple-element.122), channel_id=1, source_target_pairs={{0,8},{1,24},{2,10},{3,26},{4,12},{5,28},{6,14},{7,30},{8,0},{9,16... | collective-permute-start | bytes 2359304 | tf_op jit(solution)/shard_map/ppermute | solution.py:592
  (154 other events, 1949.9 us)

commit v3 on v2

--- a/solution.py
+++ b/solution.py
@@ -402,6 +402,260 @@
     )
 
 
+AXES = ("y", "x", "zh", "zl", "core")
+BITS = {"y": 16, "x": 8, "zh": 4, "zl": 2, "core": 1}
+MESH = pl.DeviceIdType.MESH
+
+
+def coordinates():
+    return tuple(lax.axis_index(name) for name in AXES)
+
+
+def peer(me, *names):
+    return tuple(1 - at if name in names else at for name, at in zip(AXES, me))
+
+
+def greet(me, groups):
+    barrier = pltpu.get_barrier_semaphore()
+    for names in groups:
+        pl.semaphore_signal(barrier, 1, device_id=peer(me, *names), device_id_type=MESH)
+    pl.semaphore_wait(barrier, len(groups))
+
+
+class Mover:
+    def __init__(self, me, sends, recvs):
+        self.me, self.sends, self.recvs, self.used = me, sends, recvs, 0
+        self.started = []
+
+    def next(self):
+        number = self.used
+        self.used += 1
+        assert number < self.sends.shape[0]
+        return number
+
+    def copy(self, src, dst, *names, device=None):
+        number = self.next()
+        return pltpu.make_async_remote_copy(
+            src_ref=src,
+            dst_ref=dst,
+            send_sem=self.sends.at[number],
+            recv_sem=self.recvs.at[number],
+            device_id=peer(self.me, *names) if device is None else device,
+            device_id_type=MESH,
+        )
+
+    def send(self, src, dst, *names):
+        made = self.copy(src, dst, *names)
+        made.start()
+        self.started.append(made)
+        return made
+
+    def local(self, src, dst):
+        made = self.quiet(src, dst)
+        made.start()
+        return made
+
+    def quiet(self, src, dst):
+        number = self.next()
+        return pltpu.make_async_copy(src, dst, self.recvs.at[number])
+
+    def finish(self):
+        for made in self.started:
+            made.wait_send()
+
+
+HEAD_GROUPS = (
+    ("core",),
+    ("zl",),
+    ("zh",),
+    ("zh", "zl"),
+    ("zl", "core"),
+    ("x",),
+    ("y",),
+    ("y", "core"),
+    ("y", "core", "x"),
+)
+LINE = (("zl",), ("zh",), ("zh", "zl"))
+
+
+def turn_start(move, me, src, dst):
+    y, x, zh, zl, core = me
+    stays = y == core
+    made = []
+    for flip in (1, 0):
+        place = x if flip == 0 else 1 - x
+        from_, to = src.at[place], dst.at[x]
+        copy = move.copy(from_, to, device=(core, place, zh, zl, y))
+        if flip == 0:
+            own = move.quiet(from_, to)
+            pl.when(stays)(own.start)
+            pl.when(jnp.logical_not(stays))(copy.start)
+            made.append((copy, own))
+        else:
+            copy.start()
+            made.append((copy, None))
+    return made
+
+
+def turn_end(me, made):
+    stays = me[0] == me[4]
+    for copy, own in made:
+        if own is None:
+            copy.wait()
+        else:
+            pl.when(stays)(own.wait)
+            pl.when(jnp.logical_not(stays))(copy.wait)
+
+
+def head_kernel(
+    x_in,
+    g_in,
+    qkv_in,
+    gate_in,
+    up_in,
+    down_in,
+    out_in,
+    gain_in,
+    docs_in,
+    x_out,
+    g_out,
+    qkv_w,
+    gate_w,
+    up_w,
+    down_w,
+    out_w,
+    gains,
+    docs_out,
+    sends,
+    recvs,
+):
+    me = coordinates()
+    y, x, zh, zl, core = me
+    s, z = y * 2 + x, zh * 2 + zl
+    half = qkv_w.shape[-1] // 2
+    left, right = pl.ds(0, half), pl.ds(half, half)
+    greet(me, HEAD_GROUPS)
+    move = Mover(me, sends, recvs)
+
+    own = [
+        move.local(qkv_in.at[core], qkv_w.at[s, z, core]),
+        move.local(gain_in, gains.at[s, z, core]),
+        move.local(gate_in.at[zl, core], gate_w.at[s, zh, zl, core]),
+        move.local(up_in.at[zl, core], up_w.at[s, zh, zl, core]),
+        move.local(down_in, down_w.at[s, zh]),
+    ]
+    first = [
+        move.send(qkv_in.at[1 - core], qkv_w.at[s, z, core], "core"),
+        move.send(gain_in, gains.at[s, z, core], "core"),
+    ]
+    docs = move.send(docs_in, docs_out, "core")
+    x_turn = turn_start(move, me, x_in, x_out)
+    own[0].wait()
+    own[1].wait()
+    first[0].wait_recv()
+    first[1].wait_recv()
+    line = [move.send(qkv_w.at[s, z], qkv_w.at[s, z], *names) for names in LINE]
+    line += [move.send(gains.at[s, z], gains.at[s, z], *names) for names in LINE]
+    g_turn = turn_start(move, me, g_in, g_out)
+
+    spread = []
+    for src, dst in ((gate_in, gate_w), (up_in, up_w)):
+        for names in (("core",), ("zl",), ("zl", "core")):
+            to_zl = 1 - zl if "zl" in names else zl
+            to_core = 1 - core if "core" in names else core
+            spread.append(move.send(src.at[to_zl, to_core], dst.at[s, zh, zl, core], *names))
+    mine = y == core
+    other = jnp.logical_not(mine)
+    out_own = move.quiet(out_in, out_w.at[x, z, core])
+    out_sent = move.copy(out_in, out_w.at[x, z, core], "core")
+    pl.when(mine)(out_own.start)
+    pl.when(other)(out_sent.start)
+
+    for made in line:
+        made.wait_recv()
+    hops = plane_start(move, qkv_w, s, (left, right))
+    hops += [move.send(gains.at[s], gains.at[s], "x")]
+    for made in own[2:]:
+        made.wait()
+    for made in spread:
+        made.wait_recv()
+    pairs = [
+        move.send(ref.at[s, zh], ref.at[s, zh], "zh") for ref in (gate_w, up_w, down_w)
+    ]
+    out_line = [move.copy(out_w.at[x, z], out_w.at[x, z], *names) for names in LINE]
+    pl.when(other)(out_sent.wait_send)
+
+    @pl.when(mine)
+    def _():
+        out_own.wait()
+        out_sent.wait_recv()
+        for made in out_line:
+            made.start()
+
+    rest = plane_pass(move, hops[:4], qkv_w, y, x, (left, right))
+    hops[4].wait_recv()
+    xs = pl.ds(2 * y, 2)
+    rest.append(move.send(gains.at[xs], gains.at[xs], "y"))
+    turn_end(me, x_turn)
+    turn_end(me, g_turn)
+    docs.wait_recv()
+    for made in rest + pairs:
+        made.wait_recv()
+
+    @pl.when(mine)
+    def _():
+        for made in out_line:
+            made.wait()
+
+    move.finish()
+
+
+def plane_start(move, ref, s, parts):
+    made = []
+    for part in parts:
+        piece = ref.at[s] if part is None else ref.at[s, ..., part]
+        made += [move.send(piece, piece, "x"), move.send(piece, piece, "y")]
+    return made
+
+
+def plane_pass(move, made, ref, y, x, parts):
+    made[0].wait_recv()
+    first = ref.at[2 * y + 1 - x, ..., parts[0]]
+    rest = [move.send(first, first, "y")]
+    made[3].wait_recv()
+    second = ref.at[2 * (1 - y) + x, ..., parts[1]]
+    rest.append(move.send(second, second, "x"))
+    made[1].wait_recv()
+    made[2].wait_recv()
+    return rest
+
+
+def fetch_head(x_in, g_in, qkv, gate, up, down, out, gain, docs):
+    low = jnp.bfloat16
+    rows = qkv.shape[1]
+    shapes = [
+        jax.ShapeDtypeStruct(x_in.shape, low),
+        jax.ShapeDtypeStruct(g_in.shape, low),
+        jax.ShapeDtypeStruct((4, 4, 2) + qkv.shape[1:], low),
+        jax.ShapeDtypeStruct((4, 2, 2, 2) + gate.shape[2:], low),
+        jax.ShapeDtypeStruct((4, 2, 2, 2) + up.shape[2:], low),
+        jax.ShapeDtypeStruct((4, 2) + down.shape, low),
+        jax.ShapeDtypeStruct((2, 4, 2) + out.shape, low),
+        jax.ShapeDtypeStruct((4, 4, 2) + gain.shape, gain.dtype),
+        jax.ShapeDtypeStruct(docs.shape, docs.dtype),
+    ]
+    hbm = pl.BlockSpec(memory_space=pl.ANY)
+    return pl.pallas_call(
+        head_kernel,
+        in_specs=[hbm] * 9,
+        out_specs=[hbm] * 9,
+        out_shape=shapes,
+        scratch_shapes=[pltpu.SemaphoreType.DMA((48,)), pltpu.SemaphoreType.DMA((48,))],
+        compiler_params=pltpu.CompilerParams(collective_id=1, has_side_effects=True),
+        name="head",
+    )(x_in, g_in, qkv, gate, up, down, out, gain, docs)
+
+
 QB = 256
 SPAN = 768
 
@@ -435,49 +689,138 @@
     return ref[rows, HD * number : HD * (number + 1)]
 
 
-def ahead_kernel(heads, kvs, q_ref, kv_ref, cos_ref, sin_ref, row_ref, col_ref, out_ref, keys):
+def ahead_block(heads, kvs, step, qkv_ref, cos_ref, sin_ref, row_ref, col_ref, out_ref, keys):
     low, f32 = jnp.bfloat16, jnp.float32
-    step = pl.program_id(0)
-    everything = pl.ds(0, kv_ref.shape[0])
-
-    @pl.when(step == 0)
-    def _():
-        for j in range(kvs):
-            keys[j] = spun(head(kv_ref, everything, j), cos_ref[...], sin_ref[...]).astype(low)
-
     start = pl.multiple_of(step * QB, QB)
     base = pl.multiple_of(jnp.maximum(start + QB - SPAN, 0), QB)
     here, span = pl.ds(start, QB), pl.ds(base, SPAN)
-    place = start + lax.broadcasted_iota(jnp.int32, (QB, SPAN), 0)
-    key_place = base + lax.broadcasted_iota(jnp.int32, (QB, SPAN), 1)
-    allowed = (key_place <= place) & (col_ref[here, :] == row_ref[:, span])
+    key_place = base + lax.broadcasted_iota(jnp.int32, (SPAN, QB), 0)
+    place = start + lax.broadcasted_iota(jnp.int32, (SPAN, QB), 1)
+    allowed = (key_place <= place) & (col_ref[span, :] == row_ref[:, here])
     bias = jnp.where(allowed, 0.0, -1e30).astype(f32)
     scale = (1.0 / math.sqrt(HD)) * math.log2(math.e)
     cosine, sine = cos_ref[here, :], sin_ref[here, :]
     results = []
     for h in range(heads):
         j = h * kvs // heads
-        query = spun(head(q_ref, here, h), cosine, sine).astype(low)
-        scores = nt(query, keys[j, span, :]) * scale + bias
-        peak = jnp.max(scores, axis=1, keepdims=True)
+        query = spun(head(qkv_ref, here, h), cosine, sine).astype(low)
+        scores = nt(keys[j, span, :], query) * scale + bias
+        peak = jnp.max(scores, axis=0, keepdims=True)
         weights = jnp.exp2(scores - peak)
-        total = jnp.sum(weights, axis=1, keepdims=True)
+        total = jnp.sum(weights, axis=0, keepdims=True)
         probs = (weights * (1.0 / total)).astype(low)
-        results.append(nn(probs, head(kv_ref, span, kvs + j)).astype(low))
-    out_ref[...] = jnp.concatenate(results, axis=1)
+        results.append(tn(probs, head(qkv_ref, span, heads + kvs + j)).astype(low))
+    out_ref[here, :] = jnp.concatenate(results, axis=1)
+
+
+def ahead_kernel(
+    heads,
+    kvs,
+    qkv_ref,
+    cos_ref,
+    sin_ref,
+    row_ref,
+    col_ref,
+    out_in,
+    gate_in,
+    up_in,
+    down_in,
+    seed_in,
+    mixed_ref,
+    out_w,
+    gate_w,
+    up_w,
+    down_w,
+    seeds,
+    keys,
+    sends,
+    recvs,
+):
+    me = coordinates()
+    y, x, zh, zl, core = me
+    s = 2 * y + x
+    mine = y == core
+    other = jnp.logical_not(mine)
+    greet(me, (("x",), ("y",), ("core",), ("zl",)))
+    move = Mover(me, sends, recvs)
+    seed_own = move.local(seed_in, seeds.at[0])
+    seed_moves = [
+        move.send(seed_in, seeds.at[1], "core"),
+        move.send(seed_in, seeds.at[2], "zl"),
+    ]
+    out_x = move.copy(out_w.at[x], out_w.at[x], "x")
+    out_y = [move.copy(out_w.at[at], out_w.at[at], "y") for at in (x, 1 - x)]
+
+    @pl.when(mine)
+    def _():
+        out_x.start()
+        out_y[0].start()
+
+    wide = gate_w.shape[-1]
+    gate_hops = plane_start(move, gate_w, s, (pl.ds(0, wide // 2), pl.ds(wide // 2, wide // 2)))
+    up_hops = plane_start(move, up_w, s, (pl.ds(0, wide // 2), pl.ds(wide // 2, wide // 2)))
+    deep = down_w.shape[-1]
+    down_hops = plane_start(move, down_w, s, (pl.ds(0, deep // 2), pl.ds(deep // 2, deep // 2)))
+    everything = pl.ds(0, qkv_ref.shape[0])
+    for j in range(kvs):
+        keys[j] = spun(head(qkv_ref, everything, heads + j), cos_ref[...], sin_ref[...]).astype(
+            jnp.bfloat16
+        )
+
+    def block(step, carry):
+        ahead_block(
+            heads, kvs, step, qkv_ref, cos_ref, sin_ref, row_ref, col_ref, mixed_ref, keys
+        )
+
+        @pl.when(step == 1)
+        def _():
+            @pl.when(mine)
+            def _():
+                out_x.wait_recv()
+                out_y[1].start()
+
+        return carry
+
+    lax.fori_loop(0, qkv_ref.shape[0] // QB, block, 0)
+    seed_moves[1].wait_recv()
+    seed_moves.append(move.send(seeds.at[2], seeds.at[3], "core"))
+    rest = []
+    for made, ref, size in (
+        (gate_hops, gate_w, wide), (up_hops, up_w, wide), (down_hops, down_w, deep)
+    ):
+        parts = (pl.ds(0, size // 2), pl.ds(size // 2, size // 2))
+        rest += plane_pass(move, made, ref, y, x, parts)
+
+    @pl.when(mine)
+    def _():
+        out_x.wait_send()
+        for made in out_y:
+            made.wait_send()
+
+    @pl.when(other)
+    def _():
+        for made in out_y:
+            made.wait_recv()
+
+    seed_own.wait()
+    seed_moves[0].wait_recv()
+    seed_moves[2].wait_recv()
+    for made in rest:
+        made.wait_recv()
+    move.finish()
 
 
 def behind_kernel(
-    heads, kvs, q_ref, kv_ref, grad_ref, cos_ref, sin_ref, row_ref, col_ref, gq_ref, gkv_ref, keys, gks, gvs
+    heads, kvs, qkv_ref, grad_ref, cos_ref, sin_ref, row_ref, col_ref, gq_ref, gkv_ref, keys, gks, gvs
 ):
     low, f32 = jnp.bfloat16, jnp.float32
     step = pl.program_id(0)
-    everything = pl.ds(0, kv_ref.shape[0])
+    everything = pl.ds(0, qkv_ref.shape[0])
 
     @pl.when(step == 0)
     def _():
         for j in range(kvs):
-            keys[j] = spun(head(kv_ref, everything, j), cos_ref[...], sin_ref[...]).astype(low)
+            keys[j] = spun(head(qkv_ref, everything, heads + j), cos_ref[...], sin_ref[...]).astype(low)
         gks[...] = jnp.zeros_like(gks)
         gvs[...] = jnp.zeros_like(gvs)
 
@@ -494,8 +837,8 @@
     results = []
     for h in range(heads):
         j = h * kvs // heads
-        query = spun(head(q_ref, here, h), cosine, sine).astype(low)
-        key, value = keys[j, span, :], head(kv_ref, span, kvs + j)
+        query = spun(head(qkv_ref, here, h), cosine, sine).astype(low)
+        key, value = keys[j, span, :], head(qkv_ref, span, heads + kvs + j)
         grad = head(grad_ref, here, h)
         scores = nt(key, query) * scale + bias
         peak = jnp.max(scores, axis=0, keepdims=True)
@@ -521,26 +864,42 @@
     return pl.BlockSpec(shape, lambda i: (0,) * len(shape))
 
 
-def attend_ahead(heads, kvs, q, kv, cosine, sine, row, col):
-    length = q.shape[0]
+def attend_ahead(heads, kvs, qkv, cosine, sine, row, col, seed, out_w, gate_w, up_w, down_w):
+    length = qkv.shape[0]
+    hbm = pl.BlockSpec(memory_space=pl.ANY)
+    vmem = pl.BlockSpec(memory_space=pltpu.VMEM)
+    weights = (out_w, gate_w, up_w, down_w)
     return pl.pallas_call(
         functools.partial(ahead_kernel, heads, kvs),
-        grid=(length // QB,),
-        in_specs=[whole(v.shape) for v in (q, kv, cosine, sine, row, col)],
-        out_specs=pl.BlockSpec((QB, heads * HD), lambda i: (i, 0)),
-        out_shape=jax.ShapeDtypeStruct((length, heads * HD), jnp.bfloat16),
-        scratch_shapes=[pltpu.VMEM((kvs, length, HD), jnp.bfloat16)],
-        compiler_params=pltpu.CompilerParams(vmem_limit_bytes=48 << 20),
-        cost_estimate=pl.CostEstimate(flops=4 * heads * length * SPAN * HD, bytes_accessed=6 << 20, transcendentals=heads * length * SPAN),
-    )(q, kv, cosine, sine, row, col)
-
-
-def attend_behind(heads, kvs, q, kv, grad, cosine, sine, row, col):
-    length = q.shape[0]
+        in_specs=[vmem] * 5 + [hbm] * 5,
+        out_specs=[vmem] + [hbm] * 5,
+        out_shape=[jax.ShapeDtypeStruct((length, heads * HD), jnp.bfloat16)]
+        + [jax.ShapeDtypeStruct(w.shape, w.dtype) for w in weights]
+        + [jax.ShapeDtypeStruct((4,) + seed.shape, seed.dtype)],
+        input_output_aliases={5: 1, 6: 2, 7: 3, 8: 4},
+        scratch_shapes=[
+            pltpu.VMEM((kvs, length, HD), jnp.bfloat16),
+            pltpu.SemaphoreType.DMA((32,)),
+            pltpu.SemaphoreType.DMA((32,)),
+        ],
+        compiler_params=pltpu.CompilerParams(
+            collective_id=2, has_side_effects=True, vmem_limit_bytes=48 << 20
+        ),
+        cost_estimate=pl.CostEstimate(
+            flops=4 * heads * length * SPAN * HD,
+            bytes_accessed=6 << 20,
+            transcendentals=heads * length * SPAN,
+        ),
+        name="ahead",
+    )(qkv, cosine, sine, row, col, *weights, seed)
+
+
+def attend_behind(heads, kvs, qkv, grad, cosine, sine, row, col):
+    length = qkv.shape[0]
     return pl.pallas_call(
         functools.partial(behind_kernel, heads, kvs),
         grid=(length // QB,),
-        in_specs=[whole(v.shape) for v in (q, kv, grad, cosine, sine, row, col)],
+        in_specs=[whole(v.shape) for v in (qkv, grad, cosine, sine, row, col)],
         out_specs=[
             pl.BlockSpec((QB, heads * HD), lambda i: (i, 0)),
             pl.BlockSpec((length, 2 * kvs * HD), lambda i: (0, 0)),
@@ -556,11 +915,7 @@
         ],
         compiler_params=pltpu.CompilerParams(vmem_limit_bytes=48 << 20),
         cost_estimate=pl.CostEstimate(flops=10 * heads * length * SPAN * HD, bytes_accessed=9 << 20, transcendentals=heads * length * SPAN),
-    )(q, kv, grad, cosine, sine, row, col)
-
-
-AXES = ("y", "x", "zh", "zl", "core")
-BITS = {"y": 16, "x": 8, "zh": 4, "zl": 2, "core": 1}
+    )(qkv, grad, cosine, sine, row, col)
 
 
 def hop(value, *names):
@@ -694,71 +1049,37 @@
         part = part.reshape(2, half_len, width)
         return pick(part, core) + hop(pick(part, 1 - core), "core")
 
-    query_w = halves(w_query)
-    pair_w = jnp.concatenate([halves(w_key), halves(w_value)], axis=2)
-    query_w, pair_w = (
-        swap_in(pick(w, core, 1), pick(w, 1 - core, 1)).reshape(2 * rows, -1)
-        for w in (query_w, pair_w)
-    )
-    own = plane_turn(layer_input, x).reshape(half_len, width)
     masked = cotangent * token_mask.astype(low)[:, :, None]
-    masked = after(masked, own)
-    seed_low = plane_turn(masked, x).reshape(half_len, width)
-    gains = jnp.stack([attn_gain, mlp_gain])[:, None]
-    gains = in_order(gains, hop(gains, "core"), core, axis=1).reshape(1, -1)
-    gains = gather_plane(gather_line(gains, zh, zl), y, x, True).reshape(16, 2, 2 * rows)
-    gains = jnp.moveaxis(gains, 1, 0).reshape(2, width).astype(f32)
-    documents = pick(jnp.where(core == y, document_ids, hop(document_ids, "core")), x)
+    qkv = jnp.concatenate([halves(w) for w in (w_query, w_key, w_value)], axis=2)
+    qkv = jnp.moveaxis(qkv, 1, 0)
+    gate_in, up_in = (
+        jnp.transpose(w.reshape(rows, units // 512, 2, 2, 128), (2, 3, 0, 1, 4)).reshape(
+            2, 2, rows, -1
+        )
+        for w in (w_gate, w_up)
+    )
+    gain = jnp.concatenate([attn_gain, mlp_gain]).astype(f32)
+    gain = jnp.broadcast_to(jnp.pad(gain, (0, 128 - 2 * rows)), (8, 128))
+    own, seed_low, qkv_w, gate_w, up_w, down_w, out_w, gains, docs = fetch_head(
+        layer_input, masked, qkv, gate_in, up_in, w_down, w_output, gain, document_ids
+    )
+    own, seed_low = own.reshape(half_len, width), seed_low.reshape(half_len, width)
+    gains = gains[..., 0, : 2 * rows].reshape(32, 2, rows)
+    gains = jnp.moveaxis(gains, 1, 0).reshape(2, width)
+    documents = pick(jnp.where(core == y, document_ids, docs), x)
     row, col = documents[None, :], documents[:, None]
-    query_w = gather_line(query_w, zh, zl)
-    pair_w = gather_line(pair_w, zh, zl)
-
-    hidden_ws = []
-    for weight in (w_gate, w_up):
-        weight = weight.reshape(rows, units // 512, 2, 2, 128)
-        mine, sent = (
-            jnp.moveaxis(pick(weight, place, 3), 2, 0).reshape(2, rows, -1)
-            for place in (core, 1 - core)
-        )
-        block = jnp.stack([mine, hop(sent, "core")])
-        block = jnp.where(core == 0, block, block[::-1])
-        block = after(jnp.moveaxis(block, 0, 1), query_w, pair_w)
-        block = in_order(pick(block, zl)[None], hop(pick(block, 1 - zl), "zl")[None], zl)
-        block = block.reshape(4 * rows, -1)
-        hidden_ws.append(in_order(block, hop(block, "zh"), zh))
-    down_ws = []
-    for columns in (slice(0, width // 2), slice(width // 2, width)):
-        block = after(w_down[:, columns], query_w, pair_w)
-        down_ws.append(in_order(block, hop(block, "zh"), zh))
-    out_w = gather_line(after(w_output, query_w, pair_w), zh, zl)
-
-    query_w = gather_plane(query_w, y, x, True).reshape(width, -1)
-    pair_w = gather_plane(pair_w, y, x, False).reshape(width, -1)
-    lines = [out_w] + hidden_ws + down_ws
-    ways = [True, True, False, True, False]
-    lines = [after(line, query_w, pair_w) for line in lines]
-    outs = [plane_out(line, way) for line, way in zip(lines, ways)]
+    qkv_w = qkv_w.reshape(width, -1)
 
     inputs = own.astype(f32)
     inv_one = inverse_rms(inputs)
     unit_one = inputs * inv_one
     normed = both((unit_one * gains[0]).astype(low))
-    query = nn(normed, query_w).astype(low)
-    pair = nn(normed, pair_w).astype(low)
-    mixed = attend_ahead(heads, kvs, query, pair, cosine, sine, row, col)
-
-    pairs = [
-        plane_pair(line, after(got, mixed), y, x, way)
-        for line, got, way in zip(lines, outs, ways)
-    ]
-    out_w = plane_rest(pairs[0], y, x, True).reshape(2, 8, rows, width)
-    out_got = hop(pick(out_w, 1 - core), "core")
-    out_w = in_order(pick(out_w, core)[:, None], out_got[:, None], core, axis=1).reshape(-1, width)
-    gate_w, up_w, down_l, down_r = (
-        plane_rest(pair_, y, x, way) for pair_, way in zip(pairs[1:], ways[1:])
-    )
+    pair = nn(normed, qkv_w).astype(low)
+    mixed, out_w, gate_w, up_w, down_w, seeds = attend_ahead(
+        heads, kvs, pair, cosine, sine, row, col, seed_low, out_w, gate_w, up_w, down_w
+    )
+    out_w, down_w = out_w.reshape(-1, width), down_w.reshape(-1, width)
     gate_w, up_w = gate_w.reshape(width, -1), up_w.reshape(width, -1)
-    down_w = jnp.concatenate([down_l, down_r], axis=-1).reshape(-1, width)
 
     hidden = inputs + join(nn(mixed, out_w))
     inv_two = inverse_rms(hidden)
@@ -771,7 +1092,7 @@
             jnp.concatenate([far, hop(far, "core")]),
         )
 
-    seeds = spread(after(seed_low, query_w, pair_w))
+    seeds = seeds.reshape(2, length, width)
     normed_two = spread((unit_two * gains[1]).astype(low))
 
     def ahead_and_back(tokens, seed):
@@ -804,7 +1125,8 @@
         grad_down[:, : width // 2].reshape(4, 2, -1, width // 2),
         grad_down[:, width // 2 :].reshape(4, 2, -1, width // 2),
     ]
-    kepts = [plane_send(total, y, x, way) for total, way in zip(totals, ways[1:])]
+    ways = [True, False, True, False]
+    kepts = [plane_send(total, y, x, way) for total, way in zip(totals, ways)]
 
     grad_normed_two = fold(near[4]) + back.astype(f32)
     scaled_two = grad_normed_two * gains[1]
@@ -820,11 +1142,12 @@
     gain_two = jnp.sum(grad_normed_two * unit_two, axis=0)
 
     grad_query, grad_pair = attend_behind(
-        heads, kvs, query, pair, grad_heads, cosine, sine, row, col
+        heads, kvs, pair, grad_heads, cosine, sine, row, col
     )
     output = after(output.astype(low), grad_query)
     output = plane_turn(output.reshape(2, quarter, width), x)
-    part = nt(grad_query, query_w) + nt(grad_pair, pair_w)
+    cols = heads * HD
+    part = nt(grad_query, qkv_w[:, :cols]) + nt(grad_pair, qkv_w[:, cols:])
     grad_out_w = tn(mixed, grad_low).astype(low).reshape(8, 2, rows, width)
     got = hop(pick(grad_out_w, 1 - core, 1), "core")
     grad_out_w = in_order(pick(grad_out_w, core, 1), got, core).reshape(4, 4, rows, width)
@@ -838,7 +1161,7 @@
     tail_kepts = [plane_send(total, y, x, way) for total, way in zip(tails, tail_ways)]
     sums = [
         scatter_pairs(plane_sum(kept, after(got, part), y, x, way), zh)
-        for (kept, got), way in zip(kepts, ways[1:])
+        for (kept, got), way in zip(kepts, ways)
     ]
     grad_normed = join(part)
     scaled_one = grad_normed * gains[0]

time: 814 us -> 741 us (0.910)
  Pallas kernels: 75.4 us -> 253 us
  waiting for transfers between devices: 354 us -> 184 us
  starting transfers between devices: 114 us -> 55.3 us
  local copies, waits for them, and re-layouts: 68.9 us -> 55.5 us
  other arithmetic: 68.2 us -> 56.9 us
    pallas_call x1 -> x2, Pallas kernels: 34.5 us -> 213 us  [the longest x1 108 us: attend_ahead(): pl.pallas_call(functools.partial(ahead_kernel, heads, kvs), in_specs=[vme...]
    ppermute x101 -> x57, waiting for transfers between devices: 331 us -> 160 us  [hop(): return lax.ppermute(value, AXES, [(i, i ^ flip) for i in range(32)])]
    ppermute x101 -> x57, starting transfers between devices: 93.7 us -> 50.7 us  [hop(): return lax.ppermute(value, AXES, [(i, i ^ flip) for i in range(32)])]
    ppermute x8 -> x4, starting transfers between devices: 20 us -> 4.62 us  [plane_turn(): got.append(lax.ppermute(pick(tokens, x ^ flip), AXES, pairs)[None])]
    select_n x47 -> x10, other arithmetic: 17 us -> 4.48 us  [in_order(): first = jnp.where(place == 0, mine, other)]
    dot_general x9 -> x8, matrix products: 41.3 us -> 47 us  [nn(): return jnp.dot(left, right, preferred_element_type=jnp.float32)]
    unnamed x199 -> x188, local copies, waits for them, and re-layouts: 24.4 us -> 18.7 us
    ppermute x8 -> x4, waiting for transfers between devices: 23.8 us -> 23.7 us  [plane_turn(): got.append(lax.ppermute(pick(tokens, x ^ flip), AXES, pairs)[None])]
  transfers between devices with their start and end apart: 109 -> 61, of which waited for: 42 -> 25; matrix products, arithmetic and copies ran while one was open for 27% -> 22% of each run, Pallas kernels for 9% -> 6%
where the time goes in v3:
time: 741 us; the launch traced here: 734 us
  Pallas kernels  253 us (34%)
  waiting for transfers between devices  184 us (25%)
  matrix products  126 us (17%)
  other arithmetic  56.9 us (8%)
  local copies, waits for them, and re-layouts  55.5 us (7%)
  starting transfers between devices  55.3 us (7%)
    ppermute x57, waiting for transfers between devices, hop(): return lax.ppermute(value, AXES, [(i, i ^ flip) for i in range(32)])  160 us
    pallas_call x1, Pallas kernels, attend_ahead(): pl.pallas_call(functools.partial(ahead_kernel, heads, kvs), in_specs=[vme...  108 us
    pallas_call x1, Pallas kernels, fetch_head(): pl.pallas_call(head_kernel, in_specs=[hbm] * 9, out_specs=[hbm] * 9, out_...  105 us
    ppermute x57, starting transfers between devices, hop(): return lax.ppermute(value, AXES, [(i, i ^ flip) for i in range(32)])  50.7 us
    dot_general x8, matrix products, nn(): return jnp.dot(left, right, preferred_element_type=jnp.float32)  47 us
    pallas_call x1, Pallas kernels, attend_behind(): pl.pallas_call(functools.partial(behind_kernel, heads, kvs), grid=(length...  40.5 us
    dot_general x9, matrix products, tn(): lax.dot_general(left, right, (((0,), (0,)), ((), ())), preferred_element_...  39.8 us
    dot_general x9, matrix products, nt(): lax.dot_general(left, right, (((1,), (1,)), ((), ())), preferred_element_...  39.6 us
  transfers between devices with their start and end apart: 61, of which 25 were waited for; matrix products, arithmetic and copies ran while one was open for 22% of the time, Pallas kernels for 6%

profile of v3, /device:TPU:0, one launch (start us, length us, event | category | flops | bytes accessed | tf_op | source)
XLA Modules:
  0.0 734.1 jit_solution(13300116982701213402)
XLA Ops:
  9.7 105.0 %head.1 = (bf16[2,256,1536]{2,1,0:T(8,128)(2,1)}, bf16[2,256,1536]{2,1,0:T(8,128)(2,1)}, bf16[4,4,2,48,1536]{4,3,2,1,0:T(8,128)(2,1)}, bf16[4,2,2,2,48,1024]{5,4...) custom-call(bf16[2,256,1536]{2,1,0:T(8,128)(2,1)} %x_in.1, ...), custom_call_target="tpu_custom_call" | custom-call | tf_op jit(solution)/shard_map/head/pallas_call | solution.py:648
  117.8 3.1 fusion.11
  126.9 10.9 %convolution_convert_fusion.qkv_ref = bf16[1024,1536]{1,0:T(8,128)(2,1)} fusion(bf16[1536,1536]{1,0:T(8,128)(2,1)} %bitcast.446, bf16[512,1536]{1,0:T(8,128)(2,1)S(1)} %get-tuple-element.98, bf16[512,1536]{1,0:T(8,128)(2,1)S(1)} %get-tuple-element.97), kind=kOutput, calls=%fused_computation.14 | convolution fusion | flops 4839702528 | bytes 11010048 | tf_op jit(solution)/shard_map/dot_general | solution.py:681
  137.9 107.9 %ahead.1 = (bf16[1024,768]{1,0:T(8,128)(2,1)S(1)}, bf16[2,4,2,48,1536]{4,3,2,1,0:T(8,128)(2,1)}, bf16[4,2,2,2,48,1024]{5,4,3,2,1,0:T(8,128)(2,1)}, bf16[4,2,2,2,...) custom-call(bf16[1024,1536]{1,0:T(8,128)(2,1)} %convolution_convert_, ...), custom_call_target="tpu_custom_call", output_to_operand_aliasing={{1}: (5, {}), {2}: (6, {}), {3}: (7, {}), {4}: (8, {})} | custom-call | flops 2415919104 | bytes 6291456 | tf_op jit(solution)/shard_map/ahead/pallas_call | solution.py:872
  245.8 4.8 fusion.76
  255.1 3.4 fusion.73
  267.0 5.5 fusion.78
  272.5 5.0 fusion.82
  277.5 23.5 %collective-permute-done.4 = bf16[512,1536]{1,0:T(8,128)(2,1)S(1)} collective-permute-done((bf16[512,1536]{1,0:T(8,128)(2,1)S(1)}, bf16[512,1536]{1,0:T(8,128)(2,1)S(1)}, u32[]{:S(2)}, u32[]{:S(2)}) %collective-permute-start.4) | collective-permute-done | bytes 1572896 | tf_op jit(solution)/shard_map/ppermute | solution.py:923
  301.1 5.7 fusion.68
  306.8 8.8 %multiply_convert_fusion.3 = (bf16[1024,1024]{1,0:T(8,128)(2,1)S(1)}, bf16[1024,1024]{1,0:T(8,128)(2,1)S(1)}, bf16[1024,1024]{1,0:T(8,128)(2,1)}) fusion(f32[1024,1024]{1,0:T(8,128)S(1)} %copy-done.82, f32[1024,1024]{1,0:T(8,128)} %fusion.68, bf16[1536,1024]{1,0:T(8,128)(2,1)S(1)} %bitcast.387, bf16[512,1536]{1,0:T(8,128)(2,1)S(1)} %collective-permute-done.2, ...), kind=kOutput, calls=%fused_computation.10 | convolution fusion | flops 3244294144 | bytes 20971520 | tf_op jit(solution)/shard_map/dot_general | solution.py:681
  315.6 3.4 fusion.79
  319.0 5.5 convolution_add_fusion.2
  324.7 3.4 fusion.80
  328.2 6.6 multiply_convert_fusion
  334.8 3.5 fusion.83
  338.3 3.5 convolution_add_fusion.1
  348.4 3.4 fusion.77
  356.4 3.4 fusion.81
  362.0 3.6 fusion.1
  367.2 4.0 fusion.86
  371.2 4.0 add_convert_fusion
  379.6 5.4 fusion.85
  385.0 6.4 add_convert_fusion.1
  394.4 5.4 fusion.84
  409.7 5.3 add_convert_fusion.2
  417.2 3.5 fusion.2
  423.5 4.7 fusion.23.grad_ref
  428.2 40.5 %shard_map.212 = (bf16[1024,768]{1,0:T(8,128)(2,1)S(1)}, bf16[1024,768]{1,0:T(8,128)(2,1)S(1)}) custom-call(bf16[1024,1536]{1,0:T(8,128)(2,1)} %convolution_convert_fusion.qkv_ref, bf16[1024,768]{1,0:T(8,128)(2,1)} %fusion.23.grad_ref, f32[1024,96]{1,0:T(8,128)S(1)} %copy-done.5, f32[1024,96]{1,0:T(8,128)S(1)} %copy-done.7, s32[1,1024]{1,0:T(1,128)S(1)} %copy-done.9, ...), custom_call_target="tpu_custom_call" | custom-call | flops 6039797760 | bytes 9437184 | tf_op jit(solution)/shard_map/pallas_call | solution.py:899
  468.7 4.3 fusion.20
  473.0 4.3 convolution_add_fusion
  492.6 3.3 convolution_convert_fusion.3
  503.6 11.3 %collective-permute-done.57 = bf16[128,768]{1,0:T(8,128)(2,1)S(1)} collective-permute-done((bf16[128,768]{1,0:T(8,128)(2,1)S(1)}, bf16[128,768]{1,0:T(8,128)(2,1)S(1)}, u32[]{:S(2)}, u32[]{:S(2)}) %collective-permute-start.57) | collective-permute-done | bytes 196640 | tf_op jit(solution)/shard_map/ppermute | solution.py:923
  514.9 9.5 %collective-permute-done.60 = bf16[128,768]{1,0:T(8,128)(2,1)S(1)} collective-permute-done((bf16[128,768]{1,0:T(8,128)(2,1)S(1)}, bf16[128,768]{1,0:T(8,128)(2,1)S(1)}, u32[]{:S(2)}, u32[]{:S(2)}) %collective-permute-start.60) | collective-permute-done | bytes 196640 | tf_op jit(solution)/shard_map/ppermute | solution.py:923
  526.2 3.0 collective-permute-start.47
  530.1 23.4 %collective-permute-done.52 = bf16[2,96,1024]{2,1,0:T(8,128)(2,1)S(1)} collective-permute-done((bf16[2,96,1024]{2,1,0:T(8,128)(2,1)S(1)}, bf16[2,96,1024]{2,1,0:T(8,128)(2,1)S(1)}, u32[]{:S(2)}, u32[]{:S(2)}) %collective-permute-start.52) | collective-permute-done | bytes 393248 | tf_op jit(solution)/shard_map/ppermute | solution.py:923
  553.7 8.2 %collective-permute-done.47 = bf16[2,96,1024]{2,1,0:T(8,128)(2,1)S(1)} collective-permute-done((bf16[2,96,1024]{2,1,0:T(8,128)(2,1)S(1)}, bf16[2,96,1024]{2,1,0:T(8,128)(2,1)S(1)}, u32[]{:S(2)}, u32[]{:S(2)}) %collective-permute-start.47) | collective-permute-done | bytes 393248 | tf_op jit(solution)/shard_map/ppermute | solution.py:923
  568.5 5.3 collective-permute-done.53
  575.2 6.2 collective-permute-done.48
  585.3 7.0 collective-permute-done.29
  600.5 7.2 collective-permute-done.31
  610.7 9.6 %collective-permute-done.25 = bf16[96,768]{1,0:T(8,128)(2,1)S(1)} collective-permute-done((bf16[96,768]{1,0:T(8,128)(2,1)S(1)}, bf16[96,768]{1,0:T(8,128)(2,1)S(1)}, u32[]{:S(2)}, u32[]{:S(2)}) %collective-permute-start.25) | collective-permute-done | bytes 147488 | tf_op jit(solution)/shard_map/ppermute | solution.py:923
  648.6 32.1 %collective-permute-done.43 = bf16[48,768]{1,0:T(8,128)(2,1)S(1)} collective-permute-done((bf16[48,768]{1,0:T(8,128)(2,1)S(1)}, bf16[48,768]{1,0:T(8,128)(2,1)S(1)}, u32[]{:S(2)}, u32[]{:S(2)}) %collective-permute-start.43) | collective-permute-done | bytes 73760 | tf_op jit(solution)/shard_map/ppermute | solution.py:923
  683.7 4.1 fusion.17
  689.8 4.7 fusion.16
  699.1 2.9 collective-permute-done.20
  707.4 8.3 %collective-permute-done.16 = bf16[256,1536]{1,0:T(8,128)(2,1)S(1)} collective-permute-done((bf16[256,1536]{1,0:T(8,128)(2,1)S(1)}, bf16[256,1536]{1,0:T(8,128)(2,1)S(1)}, u32[]{:S(2)}, u32[]{:S(2)}) %collective-permute-start.16) | collective-permute-done | bytes 786464 | tf_op jit(solution)/shard_map/ppermute | solution.py:947
  717.0 15.5 %collective-permute-done.13 = bf16[256,1536]{1,0:T(8,128)(2,1)S(1)} collective-permute-done((bf16[256,1536]{1,0:T(8,128)(2,1)S(1)}, bf16[256,1536]{1,0:T(8,128)(2,1)S(1)}, u32[]{:S(2)}, u32[]{:S(2)}) %collective-permute-start.13) | collective-permute-done | bytes 786464 | tf_op jit(solution)/shard_map/ppermute | solution.py:947
  (432 shorter events, 162.0 us)
Async XLA Ops:
  264.2 36.8 %collective-permute-start.2 = (bf16[512,1536]{1,0:T(8,128)(2,1)S(1)}, bf16[512,1536]{1,0:T(8,128)(2,1)S(1)}, u32[]{:S(2)}, u32[]{:S(2)}) collective-permute-start(bf16[512,1536]{1,0:T(8,128)(2,1)S(1)} %multiply_convert_fusion.6), channel_id=1, source_target_pairs={{0,1},{1,0},{2,3},{3,2},{4,5},{5,4},{6,7},{7,6},{8,9},{9,8},{10,11... | collective-permute-start | bytes 4718600 | tf_op jit(solution)/shard_map/ppermute | solution.py:923
  264.3 36.7 %collective-permute-start.4 = (bf16[512,1536]{1,0:T(8,128)(2,1)S(1)}, bf16[512,1536]{1,0:T(8,128)(2,1)S(1)}, u32[]{:S(2)}, u32[]{:S(2)}) collective-permute-start(bf16[512,1536]{1,0:T(8,128)(2,1)S(1)} %multiply_convert_fusion.6), channel_id=1, source_target_pairs={{0,2},{1,3},{2,0},{3,1},{4,6},{5,7},{6,4},{7,5},{8,10},{9,11},{10,... | collective-permute-start | bytes 4718600 | tf_op jit(solution)/shard_map/ppermute | solution.py:923
  301.0 23.4 %collective-permute-start.5 = (bf16[512,1536]{1,0:T(8,128)(2,1)S(1)}, bf16[512,1536]{1,0:T(8,128)(2,1)S(1)}, u32[]{:S(2)}, u32[]{:S(2)}) collective-permute-start(bf16[512,1536]{1,0:T(8,128)(2,1)S(1)} %collective-permute-done.4), channel_id=1, source_target_pairs={{0,1},{1,0},{2,3},{3,2},{4,5},{5,4},{6,7},{7,6},{8,9},{9,8},{10,11... | collective-permute-start | bytes 4718600 | tf_op jit(solution)/shard_map/ppermute | solution.py:923
  345.3 16.6 %collective-permute-start.7 = (f32[512,1536]{1,0:T(8,128)}, f32[512,1536]{1,0:T(8,128)}, u32[]{:S(2)}, u32[]{:S(2)}) collective-permute-start(f32[512,1536]{1,0:T(8,128)} %slice.107), channel_id=1, source_target_pairs={{0,1},{1,0},{2,3},{3,2},{4,5},{5,4},{6,7},{7,6},{8,9},{9,8},{10,11... | collective-permute-start | bytes 9437192 | tf_op jit(solution)/shard_map/ppermute | solution.py:923
  348.1 51.7 %collective-permute-start.10 = (f32[512,1536]{1,0:T(8,128)S(1)}, f32[512,1536]{1,0:T(8,128)}, u32[]{:S(2)}, u32[]{:S(2)}) collective-permute-start(f32[512,1536]{1,0:T(8,128)S(1)} %slice.109), channel_id=1, source_target_pairs={{0,1},{1,0},{2,3},{3,2},{4,5},{5,4},{6,7},{7,6},{8,9},{9,8},{10,11... | collective-permute-start | bytes 9437192 | tf_op jit(solution)/shard_map/ppermute | solution.py:923
  361.7 53.6 %collective-permute-start.6 = (f32[512,1536]{1,0:T(8,128)}, f32[512,1536]{1,0:T(8,128)}, u32[]{:S(2)}, u32[]{:S(2)}) collective-permute-start(f32[512,1536]{1,0:T(8,128)} %slice.105), channel_id=1, source_target_pairs={{0,1},{1,0},{2,3},{3,2},{4,5},{5,4},{6,7},{7,6},{8,9},{9,8},{10,11... | collective-permute-start | bytes 9437192 | tf_op jit(solution)/shard_map/ppermute | solution.py:923
  365.6 36.7 %collective-permute-start.8 = (bf16[512,1536]{1,0:T(8,128)(2,1)}, bf16[512,1536]{1,0:T(8,128)(2,1)S(1)}, u32[]{:S(2)}, u32[]{:S(2)}) collective-permute-start(bf16[512,1536]{1,0:T(8,128)(2,1)} %fusion.1), channel_id=1, source_target_pairs={{0,2},{1,3},{2,0},{3,1},{4,6},{5,7},{6,4},{7,5},{8,10},{9,11},{10,... | collective-permute-start | bytes 4718600 | tf_op jit(solution)/shard_map/ppermute | solution.py:923
  376.4 101.0 %collective-permute-start.55 = (bf16[2,2,128,768]{3,2,1,0:T(8,128)(2,1)}, bf16[2,2,128,768]{3,2,1,0:T(8,128)(2,1)}, u32[]{:S(2)}, u32[]{:S(2)}) collective-permute-start(bf16[2,2,128,768]{3,2,1,0:T(8,128)(2,1)} %dynamic-slice_bitcast_fusion.8), channel_id=1, source_target_pairs={{0,16},{1,17},{2,18},{3,19},{4,20},{5,21},{6,22},{7,23},{8,24},{9,... | collective-permute-start | bytes 2359304 | tf_op jit(solution)/shard_map/ppermute | solution.py:923
  378.3 101.8 %collective-permute-start.58 = (bf16[2,2,128,768]{3,2,1,0:T(8,128)(2,1)}, bf16[2,2,128,768]{3,2,1,0:T(8,128)(2,1)}, u32[]{:S(2)}, u32[]{:S(2)}) collective-permute-start(bf16[2,2,128,768]{3,2,1,0:T(8,128)(2,1)} %dynamic-slice_bitcast_fusion.7), channel_id=1, source_target_pairs={{0,8},{1,9},{2,10},{3,11},{4,12},{5,13},{6,14},{7,15},{8,0},{9,1},... | collective-permute-start | bytes 2359304 | tf_op jit(solution)/shard_map/ppermute | solution.py:923
  399.8 83.2 %collective-permute-start.50 = (bf16[2,2,2,96,1024]{4,3,2,1,0:T(8,128)(2,1)}, bf16[2,2,2,96,1024]{4,3,2,1,0:T(8,128)(2,1)}, u32[]{:S(2)}, u32[]{:S(2)}) collective-permute-start(bf16[2,2,2,96,1024]{4,3,2,1,0:T(8,128)(2,1)} %dynamic-slice_bitcast_fusion.2), channel_id=1, source_target_pairs={{0,8},{1,9},{2,10},{3,11},{4,12},{5,13},{6,14},{7,15},{8,0},{9,1},... | collective-permute-start | bytes 4718600 | tf_op jit(solution)/shard_map/ppermute | solution.py:923
  407.0 13.7 %collective-permute-start.11 = (bf16[512,1536]{1,0:T(8,128)(2,1)S(1)}, bf16[512,1536]{1,0:T(8,128)(2,1)S(1)}, u32[]{:S(2)}, u32[]{:S(2)}) collective-permute-start(bf16[512,1536]{1,0:T(8,128)(2,1)S(1)} %fusion.70), channel_id=1, source_target_pairs={{0,1},{1,0},{2,3},{3,2},{4,5},{5,4},{6,7},{7,6},{8,9},{9,8},{10,11... | collective-permute-start | bytes 4718600 | tf_op jit(solution)/shard_map/ppermute | solution.py:923
  415.3 80.7 %collective-permute-start.45 = (bf16[2,2,2,96,1024]{4,3,2,1,0:T(8,128)(2,1)S(1)}, bf16[2,2,2,96,1024]{4,3,2,1,0:T(8,128)(2,1)}, u32[]{:S(2)}, u32[]{:S(2)}) collective-permute-start(bf16[2,2,2,96,1024]{4,3,2,1,0:T(8,128)(2,1)S(1)} %dynamic-slice_bitcast_fusion.3), channel_id=1, source_target_pairs={{0,16},{1,17},{2,18},{3,19},{4,20},{5,21},{6,22},{7,23},{8,24},{9,... | collective-permute-start | bytes 4718600 | tf_op jit(solution)/shard_map/ppermute | solution.py:923
  479.4 21.8 %collective-permute-start.56 = (bf16[2,128,768]{2,1,0:T(8,128)(2,1)S(1)}, bf16[2,128,768]{2,1,0:T(8,128)(2,1)S(1)}, u32[]{:S(2)}, u32[]{:S(2)}) collective-permute-start(bf16[2,128,768]{2,1,0:T(8,128)(2,1)S(1)} %fusion.32), channel_id=1, source_target_pairs={{0,8},{1,9},{2,10},{3,11},{4,12},{5,13},{6,14},{7,15},{8,0},{9,1},... | collective-permute-start | bytes 1179656 | tf_op jit(solution)/shard_map/ppermute | solution.py:923
  482.1 20.5 %collective-permute-start.59 = (bf16[2,128,768]{2,1,0:T(8,128)(2,1)S(1)}, bf16[2,128,768]{2,1,0:T(8,128)(2,1)S(1)}, u32[]{:S(2)}, u32[]{:S(2)}) collective-permute-start(bf16[2,128,768]{2,1,0:T(8,128)(2,1)S(1)} %fusion.33), channel_id=1, source_target_pairs={{0,16},{1,17},{2,18},{3,19},{4,20},{5,21},{6,22},{7,23},{8,24},{9,... | collective-permute-start | bytes 1179656 | tf_op jit(solution)/shard_map/ppermute | solution.py:923
  485.7 39.8 %collective-permute-start.51 = (bf16[2,2,96,1024]{3,2,1,0:T(8,128)(2,1)S(1)}, bf16[2,2,96,1024]{3,2,1,0:T(8,128)(2,1)S(1)}, u32[]{:S(2)}, u32[]{:S(2)}) collective-permute-start(bf16[2,2,96,1024]{3,2,1,0:T(8,128)(2,1)S(1)} %fusion.25), channel_id=1, source_target_pairs={{0,16},{1,17},{2,18},{3,19},{4,20},{5,21},{6,22},{7,23},{8,24},{9,... | collective-permute-start | bytes 2359304 | tf_op jit(solution)/shard_map/ppermute | solution.py:923
  498.1 27.8 %collective-permute-start.46 = (bf16[2,2,96,1024]{3,2,1,0:T(8,128)(2,1)S(1)}, bf16[2,2,96,1024]{3,2,1,0:T(8,128)(2,1)S(1)}, u32[]{:S(2)}, u32[]{:S(2)}) collective-permute-start(bf16[2,2,96,1024]{3,2,1,0:T(8,128)(2,1)S(1)} %fusion.24), channel_id=1, source_target_pairs={{0,8},{1,9},{2,10},{3,11},{4,12},{5,13},{6,14},{7,15},{8,0},{9,1},... | collective-permute-start | bytes 2359304 | tf_op jit(solution)/shard_map/ppermute | solution.py:923
  499.0 63.1 %collective-permute-start.34 = (bf16[8,48,1536]{2,1,0:T(8,128)(2,1)S(1)}, bf16[8,48,1536]{2,1,0:T(8,128)(2,1)S(1)}, u32[]{:S(2)}, u32[]{:S(2)}) collective-permute-start(bf16[8,48,1536]{2,1,0:T(8,128)(2,1)S(1)} %dynamic-slice_bitcast_fusion.4), channel_id=1, source_target_pairs={{0,1},{1,0},{2,3},{3,2},{4,5},{5,4},{6,7},{7,6},{8,9},{9,8},{10,11... | collective-permute-start | bytes 3538952 | tf_op jit(solution)/shard_map/ppermute | solution.py:923
  501.1 63.7 %collective-permute-start.28 = (bf16[2,4,96,768]{3,2,1,0:T(8,128)(2,1)S(1)}, bf16[2,4,96,768]{3,2,1,0:T(8,128)(2,1)S(1)}, u32[]{:S(2)}, u32[]{:S(2)}) collective-permute-start(bf16[2,4,96,768]{3,2,1,0:T(8,128)(2,1)S(1)} %dynamic-slice_bitcast_fusion.5), channel_id=1, source_target_pairs={{0,8},{1,9},{2,10},{3,11},{4,12},{5,13},{6,14},{7,15},{8,0},{9,1},... | collective-permute-start | bytes 3538952 | tf_op jit(solution)/shard_map/ppermute | solution.py:923
  502.6 12.2 %collective-permute-start.57 = (bf16[128,768]{1,0:T(8,128)(2,1)S(1)}, bf16[128,768]{1,0:T(8,128)(2,1)S(1)}, u32[]{:S(2)}, u32[]{:S(2)}) collective-permute-start(bf16[128,768]{1,0:T(8,128)(2,1)S(1)} %fusion.40), channel_id=1, source_target_pairs={{0,4},{1,5},{2,6},{3,7},{4,0},{5,1},{6,2},{7,3},{8,12},{9,13},{10,... | collective-permute-start | bytes 589832 | tf_op jit(solution)/shard_map/ppermute | solution.py:923
  514.8 9.5 %collective-permute-start.60 = (bf16[128,768]{1,0:T(8,128)(2,1)S(1)}, bf16[128,768]{1,0:T(8,128)(2,1)S(1)}, u32[]{:S(2)}, u32[]{:S(2)}) collective-permute-start(bf16[128,768]{1,0:T(8,128)(2,1)S(1)} %fusion.41), channel_id=1, source_target_pairs={{0,4},{1,5},{2,6},{3,7},{4,0},{5,1},{6,2},{7,3},{8,12},{9,13},{10,... | collective-permute-start | bytes 589832 | tf_op jit(solution)/shard_map/ppermute | solution.py:923
  524.3 42.0 %collective-permute-start.22 = (bf16[2,4,96,768]{3,2,1,0:T(8,128)(2,1)S(1)}, bf16[2,4,96,768]{3,2,1,0:T(8,128)(2,1)S(1)}, u32[]{:S(2)}, u32[]{:S(2)}) collective-permute-start(bf16[2,4,96,768]{3,2,1,0:T(8,128)(2,1)S(1)} %dynamic-slice_bitcast_fusion.6), channel_id=1, source_target_pairs={{0,16},{1,17},{2,18},{3,19},{4,20},{5,21},{6,22},{7,23},{8,24},{9,... | collective-permute-start | bytes 3538952 | tf_op jit(solution)/shard_map/ppermute | solution.py:923
  525.8 27.7 %collective-permute-start.52 = (bf16[2,96,1024]{2,1,0:T(8,128)(2,1)S(1)}, bf16[2,96,1024]{2,1,0:T(8,128)(2,1)S(1)}, u32[]{:S(2)}, u32[]{:S(2)}) collective-permute-start(bf16[2,96,1024]{2,1,0:T(8,128)(2,1)S(1)} %fusion.31), channel_id=1, source_target_pairs={{0,4},{1,5},{2,6},{3,7},{4,0},{5,1},{6,2},{7,3},{8,12},{9,13},{10,... | collective-permute-start | bytes 1179656 | tf_op jit(solution)/shard_map/ppermute | solution.py:923
  526.2 35.7 %collective-permute-start.47 = (bf16[2,96,1024]{2,1,0:T(8,128)(2,1)S(1)}, bf16[2,96,1024]{2,1,0:T(8,128)(2,1)S(1)}, u32[]{:S(2)}, u32[]{:S(2)}) collective-permute-start(bf16[2,96,1024]{2,1,0:T(8,128)(2,1)S(1)} %fusion.30), channel_id=1, source_target_pairs={{0,4},{1,5},{2,6},{3,7},{4,0},{5,1},{6,2},{7,3},{8,12},{9,13},{10,... | collective-permute-start | bytes 1179656 | tf_op jit(solution)/shard_map/ppermute | solution.py:923
  553.6 130.1 %collective-permute-start.14 = (f32[512,1536]{1,0:T(8,128)}, f32[512,1536]{1,0:T(8,128)}, u32[]{:S(2)}, u32[]{:S(2)}) collective-permute-start(f32[512,1536]{1,0:T(8,128)} %dynamic-slice_bitcast_fusion), channel_id=1, source_target_pairs={{0,1},{1,0},{2,3},{3,2},{4,5},{5,4},{6,7},{7,6},{8,9},{9,8},{10,11... | collective-permute-start | bytes 9437192 | tf_op jit(solution)/shard_map/ppermute | solution.py:923
  561.9 12.0 %collective-permute-start.53 = (f32[96,1024]{1,0:T(8,128)S(1)}, f32[96,1024]{1,0:T(8,128)S(1)}, u32[]{:S(2)}, u32[]{:S(2)}) collective-permute-start(f32[96,1024]{1,0:T(8,128)S(1)} %dynamic-slice_bitcast_fusion.16), channel_id=1, source_target_pairs={{0,2},{1,3},{2,0},{3,1},{4,6},{5,7},{6,4},{7,5},{8,10},{9,11},{10,... | collective-permute-start | bytes 1179656 | tf_op jit(solution)/shard_map/ppermute | solution.py:923
  562.1 19.3 %collective-permute-start.48 = (f32[96,1024]{1,0:T(8,128)S(1)}, f32[96,1024]{1,0:T(8,128)S(1)}, u32[]{:S(2)}, u32[]{:S(2)}) collective-permute-start(f32[96,1024]{1,0:T(8,128)S(1)} %dynamic-slice_bitcast_fusion.18), channel_id=1, source_target_pairs={{0,2},{1,3},{2,0},{3,1},{4,6},{5,7},{6,4},{7,5},{8,10},{9,11},{10,... | collective-permute-start | bytes 1179656 | tf_op jit(solution)/shard_map/ppermute | solution.py:923
  564.8 27.6 %collective-permute-start.35 = (bf16[2,4,48,768]{3,2,1,0:T(8,128)(2,1)S(1)}, bf16[2,4,48,768]{3,2,1,0:T(8,128)(2,1)S(1)}, u32[]{:S(2)}, u32[]{:S(2)}) collective-permute-start(bf16[2,4,48,768]{3,2,1,0:T(8,128)(2,1)S(1)} %dynamic-slice_bitcast_fusion.14), channel_id=1, source_target_pairs={{0,16},{1,17},{2,18},{3,19},{4,20},{5,21},{6,22},{7,23},{8,24},{9,... | collective-permute-start | bytes 1769480 | tf_op jit(solution)/shard_map/ppermute | solution.py:923
  566.4 27.4 %collective-permute-start.40 = (bf16[2,4,48,768]{3,2,1,0:T(8,128)(2,1)S(1)}, bf16[2,4,48,768]{3,2,1,0:T(8,128)(2,1)S(1)}, u32[]{:S(2)}, u32[]{:S(2)}) collective-permute-start(bf16[2,4,48,768]{3,2,1,0:T(8,128)(2,1)S(1)} %dynamic-slice_bitcast_fusion.13), channel_id=1, source_target_pairs={{0,8},{1,9},{2,10},{3,11},{4,12},{5,13},{6,14},{7,15},{8,0},{9,1},... | collective-permute-start | bytes 1769480 | tf_op jit(solution)/shard_map/ppermute | solution.py:923
  573.9 18.4 %collective-permute-start.29 = (bf16[4,96,768]{2,1,0:T(8,128)(2,1)S(1)}, bf16[4,96,768]{2,1,0:T(8,128)(2,1)S(1)}, u32[]{:S(2)}, u32[]{:S(2)}) collective-permute-start(bf16[4,96,768]{2,1,0:T(8,128)(2,1)S(1)} %fusion.27), channel_id=1, source_target_pairs={{0,16},{1,17},{2,18},{3,19},{4,20},{5,21},{6,22},{7,23},{8,24},{9,... | collective-permute-start | bytes 1769480 | tf_op jit(solution)/shard_map/ppermute | solution.py:923
  581.4 14.9 %collective-permute-start.23 = (bf16[4,96,768]{2,1,0:T(8,128)(2,1)S(1)}, bf16[4,96,768]{2,1,0:T(8,128)(2,1)S(1)}, u32[]{:S(2)}, u32[]{:S(2)}) collective-permute-start(bf16[4,96,768]{2,1,0:T(8,128)(2,1)S(1)} %fusion.26), channel_id=1, source_target_pairs={{0,8},{1,9},{2,10},{3,11},{4,12},{5,13},{6,14},{7,15},{8,0},{9,1},... | collective-permute-start | bytes 1769480 | tf_op jit(solution)/shard_map/ppermute | solution.py:923
  592.2 31.0 %collective-permute-start.54 = (f32[2,48,1024]{2,1,0:T(8,128)S(1)}, f32[2,48,1024]{2,1,0:T(8,128)S(1)}, u32[]{:S(2)}, u32[]{:S(2)}) collective-permute-start(f32[2,48,1024]{2,1,0:T(8,128)S(1)} %dynamic-slice_bitcast_fusion.15), channel_id=1, source_target_pairs={{0,1},{1,0},{2,3},{3,2},{4,5},{5,4},{6,7},{7,6},{8,9},{9,8},{10,11... | collective-permute-start | bytes 1179656 | tf_op jit(solution)/shard_map/ppermute | solution.py:923
  593.8 14.0 %collective-permute-start.31 = (bf16[96,768]{1,0:T(8,128)(2,1)S(1)}, bf16[96,768]{1,0:T(8,128)(2,1)S(1)}, u32[]{:S(2)}, u32[]{:S(2)}) collective-permute-start(bf16[96,768]{1,0:T(8,128)(2,1)S(1)} %get-tuple-element.119), channel_id=1, source_target_pairs={{0,4},{1,5},{2,6},{3,7},{4,0},{5,1},{6,2},{7,3},{8,12},{9,13},{10,... | collective-permute-start | bytes 442376 | tf_op jit(solution)/shard_map/ppermute | solution.py:923
  596.3 11.5 %collective-permute-start.32 = (bf16[96,768]{1,0:T(8,128)(2,1)S(1)}, bf16[96,768]{1,0:T(8,128)(2,1)S(1)}, u32[]{:S(2)}, u32[]{:S(2)}) collective-permute-start(bf16[96,768]{1,0:T(8,128)(2,1)S(1)} %get-tuple-element.118), channel_id=1, source_target_pairs={{0,6},{1,7},{2,4},{3,5},{4,2},{5,3},{6,0},{7,1},{8,14},{9,15},{10,... | collective-permute-start | bytes 442376 | tf_op jit(solution)/shard_map/ppermute | solution.py:923
  600.5 10.2 %collective-permute-start.24 = (bf16[96,768]{1,0:T(8,128)(2,1)S(1)}, bf16[96,768]{1,0:T(8,128)(2,1)S(1)}, u32[]{:S(2)}, u32[]{:S(2)}) collective-permute-start(bf16[96,768]{1,0:T(8,128)(2,1)S(1)} %get-tuple-element.120), channel_id=1, source_target_pairs={{0,2},{1,3},{2,0},{3,1},{4,6},{5,7},{6,4},{7,5},{8,10},{9,11},{10,... | collective-permute-start | bytes 442376 | tf_op jit(solution)/shard_map/ppermute | solution.py:923
  607.8 12.6 %collective-permute-start.25 = (bf16[96,768]{1,0:T(8,128)(2,1)S(1)}, bf16[96,768]{1,0:T(8,128)(2,1)S(1)}, u32[]{:S(2)}, u32[]{:S(2)}) collective-permute-start(bf16[96,768]{1,0:T(8,128)(2,1)S(1)} %get-tuple-element.122), channel_id=1, source_target_pairs={{0,4},{1,5},{2,6},{3,7},{4,0},{5,1},{6,2},{7,3},{8,12},{9,13},{10,... | collective-permute-start | bytes 442376 | tf_op jit(solution)/shard_map/ppermute | solution.py:923
  607.8 12.6 %collective-permute-start.26 = (bf16[96,768]{1,0:T(8,128)(2,1)S(1)}, bf16[96,768]{1,0:T(8,128)(2,1)S(1)}, u32[]{:S(2)}, u32[]{:S(2)}) collective-permute-start(bf16[96,768]{1,0:T(8,128)(2,1)S(1)} %get-tuple-element.121), channel_id=1, source_target_pairs={{0,6},{1,7},{2,4},{3,5},{4,2},{5,3},{6,0},{7,1},{8,14},{9,15},{10,... | collective-permute-start | bytes 442376 | tf_op jit(solution)/shard_map/ppermute | solution.py:923
  610.7 79.0 %collective-permute-start.3 = (f32[512,1536]{1,0:T(8,128)}, f32[512,1536]{1,0:T(8,128)}, u32[]{:S(2)}, u32[]{:S(2)}) collective-permute-start(f32[512,1536]{1,0:T(8,128)} %slice.103), channel_id=1, source_target_pairs={{0,1},{1,0},{2,3},{3,2},{4,5},{5,4},{6,7},{7,6},{8,9},{9,8},{10,11... | collective-permute-start | bytes 9437192 | tf_op jit(solution)/shard_map/ppermute | solution.py:923
  620.3 10.1 %collective-permute-start.36 = (bf16[4,48,768]{2,1,0:T(8,128)(2,1)}, bf16[4,48,768]{2,1,0:T(8,128)(2,1)}, u32[]{:S(2)}, u32[]{:S(2)}) collective-permute-start(bf16[4,48,768]{2,1,0:T(8,128)(2,1)} %fusion.34), channel_id=1, source_target_pairs={{0,8},{1,9},{2,10},{3,11},{4,12},{5,13},{6,14},{7,15},{8,0},{9,1},... | collective-permute-start | bytes 884744 | tf_op jit(solution)/shard_map/ppermute | solution.py:923
  623.3 9.5 %collective-permute-start.41 = (bf16[4,48,768]{2,1,0:T(8,128)(2,1)}, bf16[4,48,768]{2,1,0:T(8,128)(2,1)}, u32[]{:S(2)}, u32[]{:S(2)}) collective-permute-start(bf16[4,48,768]{2,1,0:T(8,128)(2,1)} %fusion.35), channel_id=1, source_target_pairs={{0,16},{1,17},{2,18},{3,19},{4,20},{5,21},{6,22},{7,23},{8,24},{9,... | collective-permute-start | bytes 884744 | tf_op jit(solution)/shard_map/ppermute | solution.py:923
  626.6 9.5 %collective-permute-start.33 = (f32[48,768]{1,0:T(8,128)}, f32[48,768]{1,0:T(8,128)}, u32[]{:S(2)}, u32[]{:S(2)}) collective-permute-start(f32[48,768]{1,0:T(8,128)} %get-tuple-element.134), channel_id=1, source_target_pairs={{0,1},{1,0},{2,3},{3,2},{4,5},{5,4},{6,7},{7,6},{8,9},{9,8},{10,11... | collective-permute-start | bytes 442376 | tf_op jit(solution)/shard_map/ppermute | solution.py:923
  632.7 9.0 %collective-permute-start.37 = (bf16[48,768]{1,0:T(8,128)(2,1)S(1)}, bf16[48,768]{1,0:T(8,128)(2,1)S(1)}, u32[]{:S(2)}, u32[]{:S(2)}) collective-permute-start(bf16[48,768]{1,0:T(8,128)(2,1)S(1)} %get-tuple-element.123), channel_id=1, source_target_pairs={{0,2},{1,3},{2,0},{3,1},{4,6},{5,7},{6,4},{7,5},{8,10},{9,11},{10,... | collective-permute-start | bytes 221192 | tf_op jit(solution)/shard_map/ppermute | solution.py:923
  644.1 45.6 %collective-permute-start.9 = (bf16[512,1536]{1,0:T(8,128)(2,1)S(1)}, bf16[512,1536]{1,0:T(8,128)(2,1)S(1)}, u32[]{:S(2)}, u32[]{:S(2)}) collective-permute-start(bf16[512,1536]{1,0:T(8,128)(2,1)S(1)} %copy-done.51), channel_id=1, source_target_pairs={{0,2},{1,3},{2,0},{3,1},{4,6},{5,7},{6,4},{7,5},{8,10},{9,11},{10,... | collective-permute-start | bytes 4718600 | tf_op jit(solution)/shard_map/ppermute | solution.py:923
  645.0 35.7 %collective-permute-start.43 = (bf16[48,768]{1,0:T(8,128)(2,1)S(1)}, bf16[48,768]{1,0:T(8,128)(2,1)S(1)}, u32[]{:S(2)}, u32[]{:S(2)}) collective-permute-start(bf16[48,768]{1,0:T(8,128)(2,1)S(1)} %get-tuple-element.128), channel_id=1, source_target_pairs={{0,4},{1,5},{2,6},{3,7},{4,0},{5,1},{6,2},{7,3},{8,12},{9,13},{10,... | collective-permute-start | bytes 221192 | tf_op jit(solution)/shard_map/ppermute | solution.py:923
  646.3 37.2 %collective-permute-start.44 = (bf16[48,768]{1,0:T(8,128)(2,1)S(1)}, bf16[48,768]{1,0:T(8,128)(2,1)S(1)}, u32[]{:S(2)}, u32[]{:S(2)}) collective-permute-start(bf16[48,768]{1,0:T(8,128)(2,1)S(1)} %get-tuple-element.127), channel_id=1, source_target_pairs={{0,6},{1,7},{2,4},{3,5},{4,2},{5,3},{6,0},{7,1},{8,14},{9,15},{10,... | collective-permute-start | bytes 221192 | tf_op jit(solution)/shard_map/ppermute | solution.py:923
  695.8 11.6 %collective-permute-start.15 = (bf16[256,1536]{1,0:T(8,128)(2,1)S(1)}, bf16[256,1536]{1,0:T(8,128)(2,1)S(1)}, u32[]{:S(2)}, u32[]{:S(2)}) collective-permute-start(bf16[256,1536]{1,0:T(8,128)(2,1)S(1)} %get-tuple-element.103), channel_id=1, source_target_pairs={{0,0},{1,16},{2,2},{3,18},{4,4},{5,20},{6,6},{7,22},{8,8},{9,24},{... | collective-permute-start | bytes 2359304 | tf_op jit(solution)/shard_map/ppermute | solution.py:947
  696.5 19.1 %collective-permute-start.16 = (bf16[256,1536]{1,0:T(8,128)(2,1)S(1)}, bf16[256,1536]{1,0:T(8,128)(2,1)S(1)}, u32[]{:S(2)}, u32[]{:S(2)}) collective-permute-start(bf16[256,1536]{1,0:T(8,128)(2,1)S(1)} %get-tuple-element.104), channel_id=1, source_target_pairs={{0,8},{1,24},{2,10},{3,26},{4,12},{5,28},{6,14},{7,30},{8,0},{9,16... | collective-permute-start | bytes 2359304 | tf_op jit(solution)/shard_map/ppermute | solution.py:947
  703.0 14.1 %collective-permute-start.12 = (bf16[256,1536]{1,0:T(8,128)(2,1)S(1)}, bf16[256,1536]{1,0:T(8,128)(2,1)S(1)}, u32[]{:S(2)}, u32[]{:S(2)}) collective-permute-start(bf16[256,1536]{1,0:T(8,128)(2,1)S(1)} %get-tuple-element.107), channel_id=1, source_target_pairs={{0,0},{1,16},{2,2},{3,18},{4,4},{5,20},{6,6},{7,22},{8,8},{9,24},{... | collective-permute-start | bytes 2359304 | tf_op jit(solution)/shard_map/ppermute | solution.py:947
  703.7 28.8 %collective-permute-start.13 = (bf16[256,1536]{1,0:T(8,128)(2,1)S(1)}, bf16[256,1536]{1,0:T(8,128)(2,1)S(1)}, u32[]{:S(2)}, u32[]{:S(2)}) collective-permute-start(bf16[256,1536]{1,0:T(8,128)(2,1)S(1)} %get-tuple-element.108), channel_id=1, source_target_pairs={{0,8},{1,24},{2,10},{3,26},{4,12},{5,28},{6,14},{7,30},{8,0},{9,16... | collective-permute-start | bytes 2359304 | tf_op jit(solution)/shard_map/ppermute | solution.py:947
  (103 other events, 846.4 us)

commit v4 on v0

--- a/solution.py
+++ b/solution.py
@@ -1,8 +1,12 @@
+import functools
 import math
 
 import jax
 import jax.numpy as jnp
 from jax import lax
+from jax.experimental import pallas as pl
+from jax.experimental.pallas import tpu as pltpu
+from jax.sharding import Mesh
 from jax.sharding import PartitionSpec as P
 
 HEADS = 16
@@ -398,38 +402,1219 @@
     )
 
 
+AXES = ("y", "x", "zh", "zl", "core")
+BITS = {"y": 16, "x": 8, "zh": 4, "zl": 2, "core": 1}
+MESH = pl.DeviceIdType.MESH
+
+
+def coordinates():
+    return tuple(lax.axis_index(name) for name in AXES)
+
+
+def peer(me, *names):
+    return tuple(1 - at if name in names else at for name, at in zip(AXES, me))
+
+
+def greet(me, groups):
+    barrier = pltpu.get_barrier_semaphore()
+    for names in groups:
+        pl.semaphore_signal(barrier, 1, device_id=peer(me, *names), device_id_type=MESH)
+    pl.semaphore_wait(barrier, len(groups))
+
+
+class Mover:
+    def __init__(self, me, sends, recvs):
+        self.me, self.sends, self.recvs, self.used = me, sends, recvs, 0
+        self.started = []
+
+    def next(self):
+        number = self.used
+        self.used += 1
+        assert number < self.sends.shape[0]
+        return number
+
+    def copy(self, src, dst, *names, device=None):
+        number = self.next()
+        return pltpu.make_async_remote_copy(
+            src_ref=src,
+            dst_ref=dst,
+            send_sem=self.sends.at[number],
+            recv_sem=self.recvs.at[number],
+            device_id=peer(self.me, *names) if device is None else device,
+            device_id_type=MESH,
+        )
+
+    def later(self, src, dst, *names):
+        made = self.copy(src, dst, *names)
+        self.started.append(made)
+        return made
+
+    def send(self, src, dst, *names):
+        made = self.later(src, dst, *names)
+        made.start()
+        return made
+
+    def local(self, src, dst):
+        made = self.quiet(src, dst)
+        made.start()
+        return made
+
+    def quiet(self, src, dst):
+        number = self.next()
+        return pltpu.make_async_copy(src, dst, self.recvs.at[number])
+
+    def finish(self):
+        for made in self.started:
+            made.wait_send()
+
+
+HEAD_GROUPS = (
+    ("core",),
+    ("zl",),
+    ("zh",),
+    ("zh", "zl"),
+    ("zl", "core"),
+    ("x",),
+    ("y",),
+    ("y", "core"),
+    ("y", "core", "x"),
+)
+LINE = (("zl",), ("zh",), ("zh", "zl"))
+
+
+def turn_start(move, me, src, dst):
+    y, x, zh, zl, core = me
+    stays = y == core
+    made = []
+    for flip in (1, 0):
+        place = x if flip == 0 else 1 - x
+        from_, to = src.at[place], dst.at[x]
+        copy = move.copy(from_, to, device=(core, place, zh, zl, y))
+        if flip == 0:
+            own = move.quiet(from_, to)
+            pl.when(stays)(own.start)
+            pl.when(jnp.logical_not(stays))(copy.start)
+            made.append((copy, own))
+        else:
+            copy.start()
+            made.append((copy, None))
+    return made
+
+
+def turn_end(me, made):
+    stays = me[0] == me[4]
+    for copy, own in made:
+        if own is None:
+            copy.wait()
+        else:
+            pl.when(stays)(own.wait)
+            pl.when(jnp.logical_not(stays))(copy.wait)
+
+
+def plane_make(move, ref, s, parts):
+    made = []
+    for part in parts:
+        piece = ref.at[s, ..., part]
+        made += [move.later(piece, piece, "x"), move.later(piece, piece, "y")]
+    return made
+
+
+def plane_start(move, ref, s, parts):
+    made = plane_make(move, ref, s, parts)
+    for one in made:
+        one.start()
+    return made
+
+
+def plane_pass(move, made, ref, y, x, parts):
+    made[0].wait_recv()
+    first = ref.at[2 * y + 1 - x, ..., parts[0]]
+    rest = [move.send(first, first, "y")]
+    made[3].wait_recv()
+    second = ref.at[2 * (1 - y) + x, ..., parts[1]]
+    rest.append(move.send(second, second, "x"))
+    made[1].wait_recv()
+    made[2].wait_recv()
+    return rest
+
+
+def by_rows(count, chunk, work):
+    def step(i, carry):
+        work(pl.ds(pl.multiple_of(i * chunk, chunk), chunk))
+        return carry
+
+    lax.fori_loop(0, count // chunk, step, 0)
+
+
+class PlaneSum:
+    def __init__(self, move, total, held, y, x):
+        self.move, self.total = move, total
+        self.own, self.mid, self.far, self.near, self.last = (held.at[i] for i in range(5))
+        half = total.shape[-1] // 2
+        self.left, self.right = pl.ds(0, half), pl.ds(half, half)
+        self.at = (2 * y + x, 2 * y + 1 - x, 2 * (1 - y) + x, 2 * (1 - y) + 1 - x)
+
+    def start(self):
+        move, total, left, right = self.move, self.total, self.left, self.right
+        s, sx, sy, sd = self.at
+        self.far_moves = [
+            move.send(total.at[sd, :, left], self.far.at[:, left], "y"),
+            move.send(total.at[sd, :, right], self.far.at[:, right], "x"),
+        ]
+        self.loads = [
+            move.local(total.at[s], self.own),
+            move.local(total.at[sx, :, left], self.mid.at[:, left]),
+            move.local(total.at[sy, :, right], self.mid.at[:, right]),
+        ]
+        self.near_moves = [
+            move.copy(total.at[sy, :, left], self.near.at[:, left], "y"),
+            move.copy(total.at[sx, :, right], self.near.at[:, right], "x"),
+        ]
+        self.last_moves = [
+            move.copy(self.mid.at[:, left], self.last.at[:, left], "x"),
+            move.copy(self.mid.at[:, right], self.last.at[:, right], "y"),
+        ]
+
+    def start_near(self):
+        for made in self.near_moves:
+            made.start()
+
+    def pass_on(self):
+        for made in self.loads[1:]:
+            made.wait()
+        for made in self.far_moves:
+            made.wait_recv()
+        rows = self.mid.shape[0]
+        mid, far = self.mid, self.far
+
+        def work(at):
+            added = mid[at, :].astype(jnp.float32) + far[at, :].astype(jnp.float32)
+            mid[at, :] = added.astype(jnp.bfloat16)
+
+        by_rows(rows, 16, work)
+        for made in self.last_moves:
+            made.start()
+
+    def end(self, write):
+        self.loads[0].wait()
+        for made in self.near_moves + self.last_moves:
+            made.wait()
+        own, near, last = self.own, self.near, self.last
+
+        def work(at):
+            value = own[at, :].astype(jnp.float32) + near[at, :].astype(jnp.float32)
+            write(at, value + last[at, :].astype(jnp.float32))
+
+        by_rows(own.shape[0], 16, work)
+
+
+def tail_kernel(
+    gate_in,
+    up_in,
+    down_in,
+    qkv_in,
+    out_in,
+    y_in,
+    x_in,
+    gain_in,
+    gate_out,
+    up_out,
+    down_out,
+    qkv_out,
+    out_out,
+    y_out,
+    x_out,
+    gain_out,
+    pair_low,
+    pair_got,
+    down_low,
+    down_got,
+    quarter,
+    qkv_held,
+    qkv_sum,
+    qkv_low,
+    qkv_got,
+    out_got,
+    out_low,
+    out_x,
+    out_line,
+    out_line_got,
+    rows_sent,
+    gain_got,
+    sends,
+    recvs,
+):
+    f32, low = jnp.float32, jnp.bfloat16
+    me = coordinates()
+    y, x, zh, zl, core = me
+    z = 2 * zh + zl
+    mine = y == core
+    other = jnp.logical_not(mine)
+    greet(me, HEAD_GROUPS)
+    move = Mover(me, sends, recvs)
+    qkv = PlaneSum(move, qkv_in, qkv_held, y, x)
+    qkv.start()
+    out_y = move.copy(out_in, out_got, "y")
+    pl.when(other)(out_y.start)
+    qkv.start_near()
+
+    pair_rows = pair_got.shape[1]
+
+    def lower(src, dst, skip, count):
+        def work(at):
+            dst[at, :] = src[skip, at, :].astype(low)
+
+        by_rows(count, 32, work)
+
+    pairs = []
+    for i, src in enumerate((gate_in, up_in)):
+        lower(src, pair_low.at[i], 1 - zh, pair_rows)
+        pairs.append(move.send(pair_low.at[i], pair_got.at[i], "zh"))
+    lower(down_in, down_low, 1 - zh, down_low.shape[0])
+    pairs.append(move.send(down_low, down_got, "zh"))
+
+    gain_out[...] = gain_in[...]
+    for turn, name in enumerate(("core", "x", "y", "zl", "zh")):
+        made = move.copy(gain_out, gain_got.at[turn], name)
+        made.start()
+        made.wait()
+        gain_out[...] = gain_out[...] + gain_got[turn]
+
+    qkv.pass_on()
+    out_shape = out_in.shape
+    blocks = [(a, b) for a in range(out_shape[1]) for b in range(out_shape[2])]
+
+    out_x_move = move.copy(out_low.at[1 - x], out_x, "x")
+
+    @pl.when(mine)
+    def _():
+        out_y.wait_recv()
+
+        def half(at_x):
+            def work(i, carry):
+                a, b = i // out_shape[2], i % out_shape[2]
+                value = out_in[at_x, a, b].astype(f32) + out_got[at_x, a, b].astype(f32)
+                out_low[at_x, a, b] = value.astype(low)
+                return carry
+
+            lax.fori_loop(0, len(blocks), work, 0)
+
+        half(1 - x)
+        out_x_move.start()
+        half(x)
+
+    y_turn = turn_start(move, me, y_in, y_out)
+    x_turn = turn_start(move, me, x_in, x_out)
+
+    spread = []
+    for i, (src, dst) in enumerate(((gate_in, gate_out), (up_in, up_out))):
+        pairs[i].wait_recv()
+        got, full = pair_got.at[i], quarter.at[i]
+
+        def work(at, src=src, got=got, full=full):
+            full[at, :] = src[zh, at, :] + got[at, :].astype(f32)
+
+        by_rows(pair_rows, 32, work)
+        count = pair_rows // 4
+        for names in (("core",), ("zl",), ("zl", "core")):
+            to_zl = 1 - zl if "zl" in names else zl
+            to_core = 1 - core if "core" in names else core
+            start = pl.multiple_of((2 * to_zl + to_core) * count, count)
+            spread.append(move.send(full.at[pl.ds(start, count)], dst.at[zl, core], *names))
+        start = pl.multiple_of((2 * zl + core) * count, count)
+        dst[zl, core] = full[pl.ds(start, count), :]
+    pairs[2].wait_recv()
+
+    def work(at):
+        down_out[at, :] = down_in[zh, at, :] + down_got[at, :].astype(f32)
+
+    by_rows(down_out.shape[0], 32, work)
+
+    def keep(at, value):
+        qkv_sum[at, :] = value
+        qkv_low[at, :] = value.astype(low)
+
+    qkv.end(keep)
+    count = qkv_got.shape[1]
+    line = []
+    for k, names in enumerate(LINE):
+        to = z ^ (1, 2, 3)[k]
+        start = pl.multiple_of(to * count, count)
+        line.append(move.send(qkv_low.at[pl.ds(start, count)], qkv_got.at[k], *names))
+
+    out_moves = []
+    for k, names in enumerate(LINE):
+        to = z ^ (1, 2, 3)[k]
+        out_moves.append(move.copy(out_line.at[to], out_line_got.at[k], *names))
+
+    @pl.when(mine)
+    def _():
+        out_x_move.wait()
+
+        def work(i, carry):
+            a, b = i // out_shape[2], i % out_shape[2]
+            value = out_low[x, a, b].astype(f32) + out_x[a, b].astype(f32)
+            out_line[a, b] = value.astype(low)
+            return carry
+
+        lax.fori_loop(0, len(blocks), work, 0)
+        for made in out_moves:
+            made.start()
+
+    for made in line:
+        made.wait_recv()
+    start = pl.multiple_of(z * count, count)
+    total = qkv_sum[pl.ds(start, count), :]
+    for k in range(3):
+        total = total + qkv_got[k].astype(f32)
+    rows = count // 2
+    qkv_sum[pl.ds(0, count), :] = total
+    theirs = pl.multiple_of((1 - core) * rows, rows)
+    swap = move.send(qkv_sum.at[pl.ds(theirs, rows)], qkv_out.at[core], "core")
+    qkv_out[core] = qkv_sum[pl.ds(pl.multiple_of(core * rows, rows), rows), :]
+
+    out_swap = move.copy(rows_sent, out_out, "core")
+
+    @pl.when(mine)
+    def _():
+        for made in out_moves:
+            made.wait()
+        for at in range(2):
+            total = out_line[z, at].astype(f32)
+            for k in range(3):
+                total = total + out_line_got[k, at].astype(f32)
+
+            @pl.when(core == at)
+            def _(total=total):
+                out_out[...] = total
+
+            @pl.when(core != at)
+            def _(total=total):
+                rows_sent[...] = total
+
+        out_swap.start()
+        out_swap.wait_send()
+
+    @pl.when(other)
+    def _():
+        out_y.wait_send()
+        out_swap.wait_recv()
+
+    turn_end(me, y_turn)
+    turn_end(me, x_turn)
+    swap.wait_recv()
+    for made in spread:
+        made.wait_recv()
+    move.finish()
+
+
+def sum_tail(gate, up, down, qkv, out, y_in, x_in, gain):
+    f32, low = jnp.float32, jnp.bfloat16
+    hbm = pl.BlockSpec(memory_space=pl.ANY)
+    vmem = pl.BlockSpec(memory_space=pltpu.VMEM)
+    wide, width = gate.shape[-1], qkv.shape[-1]
+    rows = qkv.shape[1] // 8
+    pair_rows, down_rows = gate.shape[1], down.shape[1]
+    return pl.pallas_call(
+        tail_kernel,
+        in_specs=[vmem, vmem, vmem, hbm, vmem, hbm, hbm, vmem],
+        out_specs=[vmem] * 5 + [hbm, hbm, vmem],
+        out_shape=[
+            jax.ShapeDtypeStruct((2, 2, rows, wide), f32),
+            jax.ShapeDtypeStruct((2, 2, rows, wide), f32),
+            jax.ShapeDtypeStruct((down_rows, width), f32),
+            jax.ShapeDtypeStruct((2, rows, width), f32),
+            jax.ShapeDtypeStruct((rows, width), f32),
+            jax.ShapeDtypeStruct(y_in.shape, low),
+            jax.ShapeDtypeStruct(x_in.shape, low),
+            jax.ShapeDtypeStruct(gain.shape, f32),
+        ],
+        scratch_shapes=[
+            pltpu.VMEM((2, pair_rows, wide), low),
+            pltpu.VMEM((2, pair_rows, wide), low),
+            pltpu.VMEM((down_rows, width), low),
+            pltpu.VMEM((down_rows, width), low),
+            pltpu.VMEM((2, pair_rows, wide), f32),
+            pltpu.VMEM((5,) + qkv.shape[1:], low),
+            pltpu.VMEM(qkv.shape[1:], f32),
+            pltpu.VMEM(qkv.shape[1:], low),
+            pltpu.VMEM((3, 2 * rows, width), low),
+            pltpu.VMEM(out.shape, low),
+            pltpu.VMEM(out.shape, low),
+            pltpu.VMEM(out.shape[1:], low),
+            pltpu.VMEM(out.shape[1:], low),
+            pltpu.VMEM((3,) + out.shape[2:], low),
+            pltpu.VMEM((rows, width), f32),
+            pltpu.VMEM((5,) + gain.shape, f32),
+            pltpu.SemaphoreType.DMA((48,)),
+            pltpu.SemaphoreType.DMA((48,)),
+        ],
+        compiler_params=pltpu.CompilerParams(
+            collective_id=4, has_side_effects=True, vmem_limit_bytes=56 << 20
+        ),
+        name="tail",
+    )(gate, up, down, qkv, out, y_in, x_in, gain)
+
+
+QB = 256
+SPAN = 768
+
+
+def turned(field, back):
+    middle = HD // 2
+    left, right = field[:, :middle], field[:, middle:]
+    if back:
+        return jnp.concatenate([right, -left], axis=1)
+    return jnp.concatenate([-right, left], axis=1)
+
+
+def spun(field, cosine, sine, back=False):
+    field = field.astype(jnp.float32)
+    return field * cosine + turned(field, back) * sine
+
+
+def nt(left, right):
+    return lax.dot_general(left, right, (((1,), (1,)), ((), ())), preferred_element_type=jnp.float32)
+
+
+def nn(left, right):
+    return jnp.dot(left, right, preferred_element_type=jnp.float32)
+
+
+def tn(left, right):
+    return lax.dot_general(left, right, (((0,), (0,)), ((), ())), preferred_element_type=jnp.float32)
+
+
+def head(ref, rows, number):
+    return ref[rows, HD * number : HD * (number + 1)]
+
+
+def ahead_block(
+    heads, kvs, step, size, qkv_ref, cos_ref, sin_ref, row_ref, col_ref, out_ref, keys
+):
+    low, f32 = jnp.bfloat16, jnp.float32
+    start, base = step * QB, (step + 1) * QB - size
+    if not isinstance(step, int):
+        start, base = pl.multiple_of(start, QB), pl.multiple_of(base, QB)
+    here, span = pl.ds(start, QB), pl.ds(base, size)
+    key_place = base + lax.broadcasted_iota(jnp.int32, (size, QB), 0)
+    place = start + lax.broadcasted_iota(jnp.int32, (size, QB), 1)
+    allowed = (key_place <= place) & (col_ref[span, :] == row_ref[:, here])
+    bias = jnp.where(allowed, 0.0, -1e30).astype(f32)
+    scale = (1.0 / math.sqrt(HD)) * math.log2(math.e)
+    cosine, sine = cos_ref[here, :], sin_ref[here, :]
+    results = []
+    for h in range(heads):
+        j = h * kvs // heads
+        query = spun(head(qkv_ref, here, h), cosine, sine).astype(low)
+        scores = nt(keys[j, span, :], query) * scale + bias
+        peak = jnp.max(scores, axis=0, keepdims=True)
+        weights = jnp.exp2(scores - peak)
+        total = jnp.sum(weights, axis=0, keepdims=True)
+        probs = (weights * (1.0 / total)).astype(low)
+        results.append(tn(probs, head(qkv_ref, span, heads + kvs + j)).astype(low))
+    out_ref[here, :] = jnp.concatenate(results, axis=1)
+
+
+def behind_block(
+    heads,
+    kvs,
+    step,
+    size,
+    qkv_ref,
+    grad_ref,
+    cos_ref,
+    sin_ref,
+    row_ref,
+    col_ref,
+    gq_ref,
+    keys,
+    gks,
+    gvs,
+):
+    low, f32 = jnp.bfloat16, jnp.float32
+    start, base = step * QB, (step + 1) * QB - size
+    if not isinstance(step, int):
+        start, base = pl.multiple_of(start, QB), pl.multiple_of(base, QB)
+    here, span = pl.ds(start, QB), pl.ds(base, size)
+    key_place = base + lax.broadcasted_iota(jnp.int32, (size, QB), 0)
+    place = start + lax.broadcasted_iota(jnp.int32, (size, QB), 1)
+    allowed = (key_place <= place) & (col_ref[span, :] == row_ref[:, here])
+    bias = jnp.where(allowed, 0.0, -1e30).astype(f32)
+    width = 1.0 / math.sqrt(HD)
+    scale = width * math.log2(math.e)
+    cosine, sine = cos_ref[here, :], sin_ref[here, :]
+    results = []
+    for h in range(heads):
+        j = h * kvs // heads
+        query = spun(head(qkv_ref, here, h), cosine, sine).astype(low)
+        key, value = keys[j, span, :], head(qkv_ref, span, heads + kvs + j)
+        grad = head(grad_ref, here, h)
+        scores = nt(key, query) * scale + bias
+        peak = jnp.max(scores, axis=0, keepdims=True)
+        weights = jnp.exp2(scores - peak)
+        total = jnp.sum(weights, axis=0, keepdims=True)
+        probs = weights * (1.0 / total)
+        slope = nt(value, grad)
+        centre = jnp.sum(probs * slope, axis=0, keepdims=True)
+        gs = (probs * (slope - centre)).astype(low)
+        gvs[j, span, :] += nn(probs.astype(low), grad)
+        gks[j, span, :] += nn(gs, query)
+        results.append(spun(tn(gs, key) * width, cosine, sine, True).astype(low))
+    gq_ref[here, :] = jnp.concatenate(results, axis=1)
+
+
+def behind_kernel(
+    heads,
+    kvs,
+    qkv_ref,
+    grad_ref,
+    cos_ref,
+    sin_ref,
+    row_ref,
+    col_ref,
+    gate_in,
+    up_in,
+    down_in,
+    gq_ref,
+    gkv_ref,
+    gate_out,
+    up_out,
+    down_out,
+    keys,
+    gks,
+    gvs,
+    gate_held,
+    up_held,
+    down_held,
+    sends,
+    recvs,
+):
+    low = jnp.bfloat16
+    me = coordinates()
+    y, x = me[0], me[1]
+    greet(me, (("x",), ("y",)))
+    move = Mover(me, sends, recvs)
+    sums = [
+        PlaneSum(move, total, held, y, x)
+        for total, held in ((gate_in, gate_held), (up_in, up_held), (down_in, down_held))
+    ]
+    for plane in sums:
+        plane.start()
+    everything = pl.ds(0, qkv_ref.shape[0])
+    for j in range(kvs):
+        keys[j] = spun(head(qkv_ref, everything, heads + j), cos_ref[...], sin_ref[...]).astype(low)
+    gks[...] = jnp.zeros_like(gks)
+    gvs[...] = jnp.zeros_like(gvs)
+
+    def block(step, carry):
+        @pl.when(step == 2)
+        def _():
+            for plane in sums:
+                plane.start_near()
+
+        @pl.when(step == 3)
+        def _():
+            for plane in sums:
+                plane.pass_on()
+
+        work(step, SPAN)
+        return carry
+
+    def work(step, size):
+        behind_block(
+            heads, kvs, step, size, qkv_ref, grad_ref, cos_ref, sin_ref, row_ref, col_ref, gq_ref,
+            keys, gks, gvs,
+        )
+
+    for step in range(SPAN // QB - 1):
+        work(step, (step + 1) * QB)
+    lax.fori_loop(SPAN // QB - 1, qkv_ref.shape[0] // QB, block, 0)
+    width = 1.0 / math.sqrt(HD)
+    gk = [
+        spun(gks[j] * width, cos_ref[...], sin_ref[...], True).astype(low) for j in range(kvs)
+    ]
+    gv = [gvs[j].astype(low) for j in range(kvs)]
+    gkv_ref[...] = jnp.concatenate(gk + gv, axis=1)
+    for plane, out in zip(sums, (gate_out, up_out, down_out)):
+
+        def write(at, value, out=out):
+            out[at, :] = value
+
+        plane.end(write)
+    move.finish()
+
+
+def attend_behind(heads, kvs, qkv, grad, cosine, sine, row, col, gate, up, down):
+    low, f32 = jnp.bfloat16, jnp.float32
+    length = qkv.shape[0]
+    hbm = pl.BlockSpec(memory_space=pl.ANY)
+    vmem = pl.BlockSpec(memory_space=pltpu.VMEM)
+    totals = (gate, up, down)
+    return pl.pallas_call(
+        functools.partial(behind_kernel, heads, kvs),
+        in_specs=[vmem] * 6 + [hbm] * 3,
+        out_specs=[vmem] * 5,
+        out_shape=[
+            jax.ShapeDtypeStruct((length, heads * HD), low),
+            jax.ShapeDtypeStruct((length, 2 * kvs * HD), low),
+        ]
+        + [jax.ShapeDtypeStruct(total.shape[1:], f32) for total in totals],
+        scratch_shapes=[
+            pltpu.VMEM((kvs, length, HD), low),
+            pltpu.VMEM((kvs, length, HD), f32),
+            pltpu.VMEM((kvs, length, HD), f32),
+        ]
+        + [pltpu.VMEM((5,) + total.shape[1:], low) for total in totals]
+        + [pltpu.SemaphoreType.DMA((32,)), pltpu.SemaphoreType.DMA((32,))],
+        compiler_params=pltpu.CompilerParams(
+            collective_id=3, has_side_effects=True, vmem_limit_bytes=56 << 20
+        ),
+        cost_estimate=pl.CostEstimate(
+            flops=10 * heads * length * SPAN * HD,
+            bytes_accessed=9 << 20,
+            transcendentals=heads * length * SPAN,
+        ),
+        name="behind",
+    )(qkv, grad, cosine, sine, row, col, *totals)
+
+
+def bands(size):
+    return (pl.ds(0, size // 2), pl.ds(size // 2, size // 2))
+
+
+def first_kernel(
+    heads,
+    kvs,
+    x_in,
+    g_in,
+    qkv_in,
+    gate_in,
+    up_in,
+    down_in,
+    out_in,
+    gain_in,
+    docs_in,
+    cos_ref,
+    sin_ref,
+    x_own,
+    normed,
+    qkv,
+    mixed,
+    hidden,
+    qkv_w,
+    out_w,
+    gain_rows,
+    seeds,
+    tokens,
+    gate_w,
+    up_w,
+    down_w,
+    docs,
+    row,
+    col,
+    gains,
+    keys,
+    part,
+    part_got,
+    sends,
+    recvs,
+):
+    f32, low = jnp.float32, jnp.bfloat16
+    me = coordinates()
+    y, x, zh, zl, core = me
+    s, z = y * 2 + x, zh * 2 + zl
+    mine = y == core
+    other = jnp.logical_not(mine)
+    width = qkv_w.shape[-1]
+    length = qkv.shape[0]
+    half_len = length // 2
+    greet(me, HEAD_GROUPS)
+    move = Mover(me, sends, recvs)
+
+    own = [
+        move.local(qkv_in.at[core], qkv_w.at[s, z, core]),
+        move.local(gain_in, gains.at[s, z, core]),
+    ]
+    first = [
+        move.send(qkv_in.at[1 - core], qkv_w.at[s, z, core], "core"),
+        move.send(gain_in, gains.at[s, z, core], "core"),
+    ]
+    docs_move = move.send(docs_in, docs, "core")
+    x_turn = turn_start(move, me, x_in, x_own)
+    for made in own:
+        made.wait()
+    for made in first:
+        made.wait_recv()
+    line = [move.send(gains.at[s, z], gains.at[s, z], *names) for names in LINE]
+    line += [move.send(qkv_w.at[s, z], qkv_w.at[s, z], *names) for names in LINE]
+
+    own = [
+        move.local(gate_in.at[zl, core], gate_w.at[s, zh, zl, core]),
+        move.local(up_in.at[zl, core], up_w.at[s, zh, zl, core]),
+        move.local(down_in, down_w.at[s, zh]),
+    ]
+    spread = []
+    for src, dst in ((gate_in, gate_w), (up_in, up_w)):
+        for names in (("core",), ("zl",), ("zl", "core")):
+            to_zl = 1 - zl if "zl" in names else zl
+            to_core = 1 - core if "core" in names else core
+            spread.append(move.send(src.at[to_zl, to_core], dst.at[s, zh, zl, core], *names))
+    out_own = move.quiet(out_in, out_w.at[x, z, core])
+    out_sent = move.copy(out_in, out_w.at[x, z, core], "core")
+    pl.when(mine)(out_own.start)
+    pl.when(other)(out_sent.start)
+
+    for made in line[:3]:
+        made.wait_recv()
+    gain_hops = [move.send(gains.at[s], gains.at[s], *names) for names in (("x",), ("y",))]
+    turn_end(me, x_turn)
+    gain_hops[0].wait_recv()
+    sx = 2 * y + 1 - x
+    gain_hops.append(move.send(gains.at[sx], gains.at[sx], "y"))
+    for made in line[3:]:
+        made.wait_recv()
+    qkv_hops = plane_start(move, qkv_w, s, bands(width))
+
+    out_line = [move.copy(out_w.at[x, z], out_w.at[x, z], *names) for names in LINE]
+    pl.when(other)(out_sent.wait_send)
+
+    @pl.when(mine)
+    def _():
+        out_own.wait()
+        out_sent.wait_recv()
+        for made in out_line:
+            made.start()
+
+    for made in own:
+        made.wait()
+    for made in spread:
+        made.wait_recv()
+    pairs = [
+        move.send(ref.at[s, zh], ref.at[s, zh], "zh") for ref in (gate_w, up_w, down_w)
+    ]
+
+    for made in gain_hops[1:]:
+        made.wait_recv()
+    count = out_in.shape[0]
+    for i in range(2):
+        gain_rows[pl.ds(i, 1), :] = jnp.concatenate(
+            [
+                gains[a, b, c, 0:1, i * count : (i + 1) * count]
+                for a in range(4)
+                for b in range(4)
+                for c in range(2)
+            ],
+            axis=1,
+        )
+
+    quarter = half_len // 2
+    for q in range(2):
+
+        def norm(at, q=q):
+            field = x_own[q, at, :].astype(f32)
+            inverse = lax.rsqrt(jnp.mean(field * field, axis=1, keepdims=True) + EPSILON)
+            rows = pl.ds(pl.multiple_of(q * quarter + at.start, 16), at.size)
+            normed[core, rows, :] = (field * inverse * gain_rows[0:1, :]).astype(low)
+
+        by_rows(quarter, 16, norm)
+    normed_move = move.send(normed.at[core], normed.at[core], "core")
+    docs_move.wait_recv()
+    row[...] = jnp.where(mine, docs_in[x], docs[x])
+    col[...] = jnp.transpose(jnp.broadcast_to(row[...], (8, length)))[:, 0:1]
+
+    qkv_rest = plane_pass(move, qkv_hops, qkv_w, y, x, bands(width))
+    out_x = move.copy(out_w.at[x], out_w.at[x], "x")
+    out_y = [move.copy(out_w.at[at], out_w.at[at], "y") for at in (x, 1 - x)]
+
+    @pl.when(mine)
+    def _():
+        for made in out_line:
+            made.wait()
+        out_x.start()
+        out_y[0].start()
+
+    wides = [
+        (ref.at[:, at], bands(ref.shape[-1]))
+        for at in (zh, 1 - zh)
+        for ref in (gate_w, up_w, down_w)
+    ]
+    hops = [plane_make(move, ref, s, parts) for ref, parts in wides]
+
+    def start_some(which):
+        for i in which:
+            for made in hops[i]:
+                made.start()
+
+    normed_move.wait_recv()
+    for made in qkv_rest:
+        made.wait_recv()
+    g_turn = turn_start(move, me, g_in, seeds.at[0])
+    start_some((0,))
+    weight = qkv_w.reshape(width, width)
+    for i in range(length // QB):
+        at = pl.ds(i * QB % half_len, QB)
+        qkv[pl.ds(i * QB, QB), :] = nn(normed[i * QB // half_len, at, :], weight[...]).astype(low)
+    start_some((1, 2))
+    seed_moves = [
+        move.later(seeds.at[0], seeds.at[1], "core"),
+        move.later(seeds.at[0], seeds.at[2], "zl"),
+    ]
+
+    everything = pl.ds(0, length)
+    for j in range(kvs):
+        keys[j] = spun(head(qkv, everything, heads + j), cos_ref[...], sin_ref[...]).astype(low)
+
+    def work(step, size):
+        ahead_block(heads, kvs, step, size, qkv, cos_ref, sin_ref, row, col, mixed, keys)
+
+    def block(step, carry):
+        @pl.when(step == SPAN // QB - 1)
+        def _():
+            turn_end(me, g_turn)
+            for made in seed_moves:
+                made.start()
+            for made in pairs[:2]:
+                made.wait_recv()
+            start_some((3, 4))
+
+        work(step, SPAN)
+        return carry
+
+    work(0, QB)
+
+    @pl.when(mine)
+    def _():
+        out_x.wait_recv()
+        out_y[1].start()
+
+    for step in range(1, SPAN // QB - 1):
+        work(step, (step + 1) * QB)
+    lax.fori_loop(SPAN // QB - 1, length // QB, block, 0)
+    pairs[2].wait_recv()
+    start_some((5,))
+    rest = []
+
+    def pass_some(which):
+        for i in which:
+            rest.extend(plane_pass(move, hops[i], wides[i][0], y, x, wides[i][1]))
+
+    @pl.when(mine)
+    def _():
+        out_x.wait_send()
+        for made in out_y:
+            made.wait_send()
+
+    @pl.when(other)
+    def _():
+        for made in out_y:
+            made.wait_recv()
+
+    out_weight = out_w.reshape(width // 2, width)
+    theirs, ours = (pl.multiple_of(c * half_len, half_len) for c in (1 - core, core))
+
+    def project(start):
+        for i in range(half_len // QB):
+            at = pl.ds(pl.multiple_of(start + i * QB, QB), QB)
+            part[pl.ds(i * QB, QB), :] = nn(mixed[at, :], out_weight[...])
+
+    project(theirs)
+    part_move = move.copy(part, part_got, "core")
+    part_move.start()
+    pass_some((0, 1, 2))
+    for i in range(half_len // QB):
+        at = pl.ds(pl.multiple_of(ours + i * QB, QB), QB)
+        hidden[pl.ds(i * QB, QB), :] = nn(mixed[at, :], out_weight[...])
+    part_move.wait()
+    for q in range(2):
+
+        def norm(at, q=q):
+            rows = pl.ds(pl.multiple_of(q * quarter + at.start, 16), at.size)
+            field = x_own[q, at, :].astype(f32) + (hidden[rows, :] + part_got[rows, :])
+            hidden[rows, :] = field
+            inverse = lax.rsqrt(jnp.mean(field * field, axis=1, keepdims=True) + EPSILON)
+            tokens[0, rows, :] = (field * inverse * gain_rows[1:2, :]).astype(low)
+
+        by_rows(quarter, 16, norm)
+    token_moves = [
+        move.send(tokens.at[0], tokens.at[2], "zl"),
+        move.send(tokens.at[0], tokens.at[1], "core"),
+    ]
+    seed_moves[1].wait_recv()
+    seed_moves.append(move.send(seeds.at[2], seeds.at[3], "core"))
+    pass_some((3, 4, 5))
+    token_moves[0].wait_recv()
+    token_moves.append(move.send(tokens.at[2], tokens.at[3], "core"))
+    for made in rest + seed_moves[::2] + token_moves[1:]:
+        made.wait_recv()
+    move.finish()
+
+
+def first_part(heads, kvs, x_in, g_in, qkv, gate, up, down, out, gain, docs, cosine, sine):
+    f32, low = jnp.float32, jnp.bfloat16
+    rows, width = out.shape
+    half_len = 2 * x_in.shape[1]
+    length = 2 * half_len
+    hbm = pl.BlockSpec(memory_space=pl.ANY)
+    vmem = pl.BlockSpec(memory_space=pltpu.VMEM)
+
+    def made(shape, dtype=low):
+        return jax.ShapeDtypeStruct(shape, dtype)
+
+    return pl.pallas_call(
+        functools.partial(first_kernel, heads, kvs),
+        in_specs=[hbm] * 8 + [vmem] * 3,
+        out_specs=[vmem] * 9 + [vmem] + [hbm] * 3,
+        out_shape=[
+            made(x_in.shape),
+            made((2, half_len, width)),
+            made((length, width)),
+            made((length, heads * HD)),
+            made((half_len, width), f32),
+            made((4, 4, 2) + qkv.shape[1:]),
+            made((2, 4, 2) + out.shape),
+            made((2, width), f32),
+            made((4,) + x_in.shape),
+            made((4, half_len, width)),
+            made((4, 2, 2, 2) + gate.shape[2:]),
+            made((4, 2, 2, 2) + up.shape[2:]),
+            made((4, 2) + down.shape),
+        ],
+        scratch_shapes=[
+            pltpu.VMEM(docs.shape, docs.dtype),
+            pltpu.VMEM(docs.shape[1:], docs.dtype),
+            pltpu.VMEM(docs.shape[:0:-1], docs.dtype),
+            pltpu.VMEM((4, 4, 2) + gain.shape, f32),
+            pltpu.VMEM((kvs, length, HD), low),
+            pltpu.VMEM((half_len, width), f32),
+            pltpu.VMEM((half_len, width), f32),
+            pltpu.SemaphoreType.DMA((96,)),
+            pltpu.SemaphoreType.DMA((96,)),
+        ],
+        compiler_params=pltpu.CompilerParams(
+            collective_id=1, has_side_effects=True, vmem_limit_bytes=60 << 20
+        ),
+        name="first",
+    )(x_in, g_in, qkv, gate, up, down, out, gain, docs, cosine, sine)
+
+
+def hop(value, *names):
+    flip = sum(BITS[name] for name in names)
+    return lax.ppermute(value, AXES, [(i, i ^ flip) for i in range(32)])
+
+
+def after(value, *others):
+    return lax.optimization_barrier((value,) + others)[0]
+
+
+def in_order(mine, other, place, axis=0):
+    first = jnp.where(place == 0, mine, other)
+    second = jnp.where(place == 0, other, mine)
+    return jnp.concatenate([first, second], axis=axis)
+
+
+def pick(value, place, axis=0):
+    return lax.dynamic_index_in_dim(value, place, axis, keepdims=False)
+
+
+def fast_body(
+    layer_input,
+    cotangent,
+    token_mask,
+    document_ids,
+    attn_gain,
+    w_query,
+    w_key,
+    w_value,
+    w_output,
+    mlp_gain,
+    w_gate,
+    w_up,
+    w_down,
+):
+    f32, low = jnp.float32, jnp.bfloat16
+    y, x, zh, zl, core = (lax.axis_index(name) for name in AXES)
+    device = sum(lax.axis_index(name) * BITS[name] for name in AXES)
+    quarter, width = layer_input.shape[1:]
+    half_len = 2 * quarter
+    length = 2 * half_len
+    rows = w_query.shape[0]
+    units = w_gate.shape[1]
+    heads, kvs = HEADS // 2, KV // 2
+    cosine, sine = rope_tables(length, HD)
+
+    def swap_in(mine, sent):
+        return in_order(mine[None], hop(sent, "core")[None], core)
+
+    def halves(weight):
+        return weight.reshape(rows, 2, -1)
+
+    def both(mine):
+        return in_order(mine, hop(mine, "core"), core)
+
+    def join(part):
+        part = part.reshape(2, half_len, width)
+        return pick(part, core) + hop(pick(part, 1 - core), "core")
+
+    masked = cotangent * token_mask.astype(low)[:, :, None]
+    qkv = jnp.concatenate([halves(w) for w in (w_query, w_key, w_value)], axis=2)
+    qkv = jnp.moveaxis(qkv, 1, 0)
+    gate_in, up_in = (
+        jnp.transpose(w.reshape(rows, units // 512, 2, 2, 128), (2, 3, 0, 1, 4)).reshape(
+            2, 2, rows, -1
+        )
+        for w in (w_gate, w_up)
+    )
+    gain = jnp.concatenate([attn_gain, mlp_gain]).astype(f32)
+    gain = jnp.broadcast_to(jnp.pad(gain, (0, 128 - 2 * rows)), (8, 128))
+    own, normed, pair, mixed, hidden, qkv_w, out_w, gains, seeds, tokens, gate_w, up_w, down_w = (
+        first_part(
+            heads,
+            kvs,
+            layer_input,
+            masked,
+            qkv,
+            gate_in,
+            up_in,
+            w_down,
+            w_output,
+            gain,
+            document_ids[:, None],
+            cosine,
+            sine,
+        )
+    )
+    normed = normed.reshape(length, width)
+    qkv_w, out_w = qkv_w.reshape(width, -1), out_w.reshape(-1, width)
+    gate_w, up_w = gate_w.reshape(width, -1), up_w.reshape(width, -1)
+    down_w = down_w.reshape(-1, width)
+    seed_low = seeds[0].reshape(half_len, width)
+    seeds = seeds.reshape(2, length, width)
+    normed_two = tokens.reshape(2, length, width)
+    documents = pick(jnp.where(core == y, document_ids, hop(document_ids, "core")), x)
+    row, col = documents[None, :], documents[:, None]
+    inputs = own.reshape(half_len, width).astype(f32)
+    inv_one = inverse_rms(inputs)
+    unit_one = inputs * inv_one
+    inv_two = inverse_rms(hidden)
+    unit_two = hidden * inv_two
+
+    def ahead_and_back(tokens, seed):
+        gate, upward, grad_act = nn(tokens, gate_w), nn(tokens, up_w), nt(seed, down_w)
+        sigma = jax.nn.sigmoid(gate)
+        activated = (gate * sigma * upward).astype(low)
+        up_low = (grad_act * gate * sigma).astype(low)
+        gate_low = (grad_act * upward * sigma * (1.0 + gate * (1.0 - sigma))).astype(low)
+        back = nt(gate_low, gate_w) + nt(up_low, up_w)
+        return activated, gate_low, up_low, nn(activated, down_w), back
+
+    near = ahead_and_back(normed_two[0], seeds[0])
+    far_tokens = after(normed_two[1], near[4])
+    far = ahead_and_back(far_tokens, seeds[1])
+
+    def fold(part):
+        return part[:half_len] + hop(part[half_len:], "core")
+
+    theirs = fold(far[4]).astype(low)
+    back = hop(theirs, "zl")
+    near_low, far_low = (
+        tuple(after(v, theirs) for v in parts[:3]) for parts in (near, far)
+    )
+    grad_down = (tn(near_low[0], seeds[0]) + tn(far_low[0], seeds[1])).astype(low)
+    grad_gate = (tn(normed_two[0], near_low[1]) + tn(far_tokens, far_low[1])).astype(low)
+    grad_up = (tn(normed_two[0], near_low[2]) + tn(far_tokens, far_low[2])).astype(low)
+    totals = [
+        grad_gate.reshape(4, -1, units // 4),
+        grad_up.reshape(4, -1, units // 4),
+        grad_down.reshape(4, -1, width),
+    ]
+
+    grad_normed_two = fold(near[4]) + back.astype(f32)
+    scaled_two = grad_normed_two * gains[1]
+    grad_hidden = seed_low.astype(f32) + inv_two * (
+        scaled_two - unit_two * jnp.mean(scaled_two * unit_two, axis=-1, keepdims=True)
+    )
+    grad_low = both(grad_hidden.astype(low))
+    grad_heads = nt(grad_low, out_w).astype(low)
+    grad_heads = after(grad_heads, *totals)
+
+    ahead_low = after(fold(far[3]).astype(low), back)
+    output = hidden + fold(near[3]) + hop(ahead_low, "zl").astype(f32)
+    gain_two = jnp.sum(grad_normed_two * unit_two, axis=0)
+
+    grad_query, grad_pair, *sums = attend_behind(
+        heads, kvs, pair, grad_heads, cosine, sine, row, col, *totals
+    )
+    cols = heads * HD
+    part = nt(grad_query, qkv_w[:, :cols]) + nt(grad_pair, qkv_w[:, cols:])
+    grad_out_w = tn(mixed, grad_low).astype(low).reshape(2, 4, 2, rows, width)
+    grad_qkv = jnp.concatenate(
+        [tn(normed, grad_query).astype(low), tn(normed, grad_pair).astype(low)], axis=1
+    )
+    grad_normed = join(part)
+    scaled_one = grad_normed * gains[0]
+    grad_input = grad_hidden + inv_one * (
+        scaled_one - unit_one * jnp.mean(scaled_one * unit_one, axis=-1, keepdims=True)
+    )
+    gain = jnp.stack([jnp.sum(grad_normed * unit_one, axis=0), gain_two])
+    hidden_grads = [None, None]
+    hidden_grads[0], hidden_grads[1], grad_down, grad_qkv, grad_output, output, grad_input, gain = (
+        sum_tail(
+            sums[0].reshape(2, -1, units // 4),
+            sums[1].reshape(2, -1, units // 4),
+            sums[2].reshape(2, -1, width),
+            grad_qkv.reshape(4, -1, width),
+            grad_out_w,
+            output.astype(low).reshape(2, quarter, width),
+            grad_input.astype(low).reshape(2, quarter, width),
+            gain,
+        )
+    )
+    hidden_grads = [
+        jnp.transpose(total.reshape(2, 2, rows, -1, 128), (2, 3, 0, 1, 4)).reshape(rows, units)
+        for total in hidden_grads
+    ]
+
+    def columns(start, size):
+        return jnp.moveaxis(grad_qkv[:, :, start : start + size], 0, 1).reshape(rows, -1)
+
+    q_grad = columns(0, cols)
+    k_grad = columns(cols, kvs * HD)
+    v_grad = columns(cols + kvs * HD, kvs * HD)
+    gain_one = lax.dynamic_slice_in_dim(gain, device * rows, rows, 1)
+
+    return (
+        output,
+        grad_input,
+        gain_one[0],
+        q_grad,
+        k_grad,
+        v_grad,
+        grad_output,
+        gain_one[1],
+        hidden_grads[0],
+        hidden_grads[1],
+        grad_down,
+    )
+
+
 def solution(mesh):
-    placed = (
-        P("batch", "seq", None),
-        P("batch", "seq", None),
-        P("batch", "seq"),
-        P("batch", None),
-        P(("seq", "batch")),
-        P(("seq", "batch"), None),
-        P(("seq", "batch"), None),
-        P(("seq", "batch"), None),
-        P(("seq", "batch"), None),
-        P(("seq", "batch")),
-        P(("seq", "batch"), None),
-        P(("seq", "batch"), None),
-        P(("seq", "batch"), None),
-    )
+    fast = dict(mesh.shape) == {"seq": 4, "batch": 8}
+    if fast:
+        grid = Mesh(mesh.devices.reshape((2,) * 5), AXES)
+        seq, batch = ("y", "x"), ("zh", "zl", "core")
+    else:
+        grid, seq, batch = mesh, ("seq",), ("batch",)
+    weight = P(seq + batch, None)
+    gain = P(seq + batch)
+    token = P(batch, seq, None)
     return jax.shard_map(
-        body,
-        mesh=mesh,
-        in_specs=placed,
-        out_specs=(
-            P("batch", "seq", None),
-            P("batch", "seq", None),
-            P(("seq", "batch")),
-            P(("seq", "batch"), None),
-            P(("seq", "batch"), None),
-            P(("seq", "batch"), None),
-            P(("seq", "batch"), None),
-            P(("seq", "batch")),
-            P(("seq", "batch"), None),
-            P(("seq", "batch"), None),
-            P(("seq", "batch"), None),
-        ),
+        fast_body if fast else body,
+        mesh=grid,
+        in_specs=(token, token, P(batch, seq), P(batch, None), gain)
+        + (weight,) * 4
+        + (gain,)
+        + (weight,) * 3,
+        out_specs=(token, token, gain) + (weight,) * 4 + (gain,) + (weight,) * 3,
         check_vma=False,
     )

time: 2170 us -> 684 us (0.32)
  waiting for transfers between devices: 1450 us -> 28.6 us
  Pallas kernels: 0 us -> 430 us
  matrix products: 308 us -> 118 us
  local copies, waits for them, and re-layouts: 170 us -> 66.9 us
  blocking collectives: 82 us -> 0 us
  starting transfers between devices: 47.6 us -> 2.09 us
  other arithmetic: 74.4 us -> 33.2 us
    reduce_scatter x7 -> x0, waiting for transfers between devices: 1070 us -> none  [the longest x1 253 us: body(): lax.psum_scatter(outer_sum(rows['normed_two'], rows['up_low']), ('seq', '...]
    pallas_call x0 -> x3, Pallas kernels: none -> 430 us  [the longest x1 219 us: first_part(): pl.pallas_call(functools.partial(first_kernel, heads, kvs), in_specs=[hbm...]
    all_gather x7 -> x0, waiting for transfers between devices: 307 us -> none  [the longest x1 87.9 us: fetch_feedforward(): lax.all_gather(w_down, ('seq', 'batch'), axis=0, tiled=True)]
    dot_general x63 -> x24, matrix products: 308 us -> 118 us  [the longest x9 44 us: nt(): lax.dot_general(left, right, (((1,), (1,)), ((), ())), preferred_element_...]
    unnamed x2 -> x0, blocking collectives: 82 us -> none
    all_to_all x12 -> x0, waiting for transfers between devices: 68.2 us -> none  [the longest x2 22.1 us: body(): lax.all_to_all(grad_query_heads, 'seq', split_axis=0, concat_axis=1, tile...]
    dynamic_update_slice x16 -> x0, local copies, waits for them, and re-layouts: 65.6 us -> none  [the longest x8 63 us: attention_backward(): lax.scan(one_block, (empty, empty), (jnp.arange(count, dtype=jnp.int32),...]
    all_to_all x12 -> x0, starting transfers between devices: 47 us -> none  [the longest x2 8.61 us: body(): lax.all_to_all(attended.reshape(length, 1, heads_here * HD), 'seq', split...]
  transfers between devices with their start and end apart: 26 -> 9, of which waited for: 22 -> 2; matrix products, arithmetic and copies ran while one was open for 16% -> 14% of each run, Pallas kernels for 0% -> 13%
where the time goes in v4:
time: 684 us; the launch traced here: 680 us
  Pallas kernels  430 us (63%)
  matrix products  118 us (17%)
  local copies, waits for them, and re-layouts  66.9 us (10%)
  other arithmetic  33.2 us (5%)
  waiting for transfers between devices  28.6 us (4%)
    pallas_call x1, Pallas kernels, first_part(): pl.pallas_call(functools.partial(first_kernel, heads, kvs), in_specs=[hbm...  219 us
    pallas_call x1, Pallas kernels, sum_tail(): pl.pallas_call(tail_kernel, in_specs=[vmem, vmem, vmem, hbm, vmem, hbm, h...  125 us
    pallas_call x1, Pallas kernels, attend_behind(): pl.pallas_call(functools.partial(behind_kernel, heads, kvs), in_specs=[vm...  85.3 us
    dot_general x9, matrix products, nt(): lax.dot_general(left, right, (((1,), (1,)), ((), ())), preferred_element_...  44 us
    dot_general x9, matrix products, tn(): lax.dot_general(left, right, (((0,), (0,)), ((), ())), preferred_element_...  38.4 us
    dot_general x6, matrix products, nn(): return jnp.dot(left, right, preferred_element_type=jnp.float32)  35.5 us
    ppermute x9, waiting for transfers between devices, hop(): return lax.ppermute(value, AXES, [(i, i ^ flip) for i in range(32)])  28.6 us
    unnamed x123, local copies, waits for them, and re-layouts  28.5 us
  transfers between devices with their start and end apart: 9, of which 2 were waited for; matrix products, arithmetic and copies ran while one was open for 14% of the time, Pallas kernels for 13%

profile of v4, /device:TPU:0, one launch (start us, length us, event | category | flops | bytes accessed | tf_op | source)
XLA Modules:
  0.0 680.3 jit_solution(3227367661670319052)
XLA Ops:
  0.7 1.9 fusion.11
  12.8 2.0 broadcast_multiply_fusion.g_in
  16.3 219.3 %first.1 = (bf16[2,256,1536]{2,1,0:T(8,128)(2,1)}, bf16[2,512,1536]{2,1,0:T(8,128)(2,1)}, bf16[1024,1536]{1,0:T(8,128)(2,1)}, bf16[1024,768]{1,0:T(8,128)(2,1)},...) custom-call(bf16[2,256,1536]{2,1,0:T(8,128)(2,1)} %x_in.1, ...), custom_call_target="tpu_custom_call" | custom-call | tf_op jit(solution)/shard_map/first/pallas_call | solution.py:1364
  235.5 3.4 fusion.20
  241.2 3.7 copy-done.35
  244.8 5.0 fusion.22
  249.8 5.1 fusion.21
  254.9 9.0 %multiply_convert_fusion.1 = (bf16[1024,1024]{1,0:T(8,128)(2,1)}, bf16[1024,1024]{1,0:T(8,128)(2,1)S(1)}, bf16[1024,1024]{1,0:T(8,128)(2,1)}) fusion(f32[1024,1024]{1,0:T(8,128)} %fusion.22, f32[1024,1024]{1,0:T(8,128)} %fusion.21, bf16[1024,1536]{1,0:T(8,128)(2,1)S(1)} %bitcast.157, bf16[1536,1024]{1,0:T(8,128)(2,1)S(1)} %bitcast.192), kind=kOutput, calls=%fused_computation.8 | convolution fusion | flops 3238002688 | bytes 20971520 | tf_op jit(solution)/shard_map/dot_general | solution.py:881
  263.9 5.6 fusion.23
  269.5 6.2 convolution_add_fusion.2
  275.8 5.0 fusion.25
  280.8 5.0 fusion.24
  285.9 9.6 %multiply_convert_fusion = (bf16[1024,1024]{1,0:T(8,128)(2,1)}, bf16[1024,1024]{1,0:T(8,128)(2,1)}, bf16[1024,1024]{1,0:T(8,128)(2,1)}) fusion(f32[1024,1024]{1,0:T(8,128)} %fusion.25, f32[1024,1024]{1,0:T(8,128)} %fusion.24, bf16[1024,1536]{1,0:T(8,128)(2,1)S(1)} %bitcast.153, bf16[1536,1024]{1,0:T(8,128)(2,1)S(1)} %bitcast.194), kind=kOutput, calls=%fused_computation.7 | convolution fusion | flops 3238002688 | bytes 20971520 | tf_op jit(solution)/shard_map/dot_general | solution.py:881
  295.5 5.0 fusion.26
  300.6 5.0 convolution_add_fusion.1
  305.7 2.1 slice.99
  309.8 1.9 slice.97
  312.1 3.4 fusion.31
  315.5 1.9 slice.103
  317.4 1.9 copy-done.9
  319.4 3.4 fusion.30
  324.7 2.8 copy-done.8
  331.1 3.6 fusion.4
  335.5 3.5 fusion.29
  339.1 5.2 add_convert_fusion
  344.3 3.5 fusion.28
  347.9 5.2 add_convert_fusion.1
  353.1 18.5 %collective-permute-done.2 = bf16[512,1536]{1,0:T(8,128)(2,1)S(1)} collective-permute-done((bf16[512,1536]{1,0:T(8,128)(2,1)S(1)}, bf16[512,1536]{1,0:T(8,128)(2,1)S(1)}, u32[]{:S(2)}, u32[]{:S(2)}) %collective-permute-start.2) | collective-permute-done | bytes 1572896 | tf_op jit(solution)/shard_map/ppermute | solution.py:1403
  372.7 3.5 multiply_reduce_fusion
  379.0 3.5 fusion.27
  382.5 5.1 add_convert_fusion.2
  387.9 2.6 copy-done.37
  390.4 5.0 fusion.10.grad_ref
  395.5 85.3 %behind.1 = (bf16[1024,768]{1,0:T(8,128)(2,1)}, bf16[1024,768]{1,0:T(8,128)(2,1)}, f32[384,1024]{1,0:T(8,128)}, f32[384,1024]{1,0:T(8,128)}, f32[256,1536]{1,0:T(8,128)}) custom-call(bf16[1024,1536]{1,0:T(8,128)(2,1)} %get-tuple-element.46.qkv_ref, bf16[1024,768]{1,0:T(8,128)(2,1)} %fusion.10.grad_ref, f32[1024,96]{1,0:T(8,128)} %get-tuple-element.111.cos_ref, ...), custom_call_target="tpu_custom_call" | custom-call | flops 6039797760 | bytes 9437184 | tf_op jit(solution)/shard_map/behind/pallas_call | solution.py:1054
  480.9 4.2 fusion.6
  485.1 2.7 convolution_add_fusion
  487.8 2.1 dynamic-slice_bitcast_fusion
  491.3 3.7 fusion
  495.5 2.9 convolution_convert_fusion.2
  498.4 2.9 convolution_convert_fusion.1
  501.4 2.4 pad_maximum_fusion
  503.8 6.7 copy.35
  510.5 6.5 convolution_convert_fusion
  517.0 4.1 multiply_reduce_fusion.1
  521.8 10.2 %collective-permute-done.7 = bf16[512,1536]{1,0:T(8,128)(2,1)} collective-permute-done((bf16[512,1536]{1,0:T(8,128)(2,1)}, bf16[512,1536]{1,0:T(8,128)(2,1)}, u32[]{:S(2)}, u32[]{:S(2)}) %collective-permute-start.7) | collective-permute-done | bytes 1572896 | tf_op jit(solution)/shard_map/ppermute | solution.py:1403
  532.0 6.1 add_convert_fusion.3
  538.1 125.3 %tail.1 = (f32[2,2,48,1024]{3,2,1,0:T(8,128)}, f32[2,2,48,1024]{3,2,1,0:T(8,128)}, f32[128,1536]{1,0:T(8,128)}, f32[2,48,1536]{2,1,0:T(8,128)}, f32[48,1536]{1,0...) custom-call(f32[2,192,1024]{2,1,0:T(8,128)} %bitcast.167, ...), custom_call_target="tpu_custom_call" | custom-call | tf_op jit(solution)/shard_map/tail/pallas_call | solution.py:818
  674.5 2.7 copy.62
  (178 shorter events, 43.1 us)
Async XLA Ops:
  6.0 6.8 copy-start.22
  8.4 6.5 copy-start.38
  8.4 6.5 copy-start.39
  235.5 5.2 copy-start.7
  239.0 15.9 %copy-start.15 = (bf16[2,512,1536]{2,1,0:T(8,128)(2,1)}, bf16[2,512,1536]{2,1,0:T(8,128)(2,1)S(1)}, u32[]{:S(2)}) copy-start(bf16[2,512,1536]{2,1,0:T(8,128)(2,1)S(1)} %get-tuple-element.97) | copy-start | bytes 9437188
  239.0 46.9 %copy-start.13 = (bf16[2,512,1536]{2,1,0:T(8,128)(2,1)}, bf16[2,512,1536]{2,1,0:T(8,128)(2,1)S(1)}, u32[]{:S(2)}) copy-start(bf16[2,512,1536]{2,1,0:T(8,128)(2,1)S(1)} %get-tuple-element.98) | copy-start | bytes 9437188
  241.2 8.7 %copy-start.19 = (bf16[2,2,256,1536]{3,2,1,0:T(8,128)(2,1)}, bf16[2,2,256,1536]{3,2,1,0:T(8,128)(2,1)S(1)}, u32[]{:S(2)}) copy-start(bf16[2,2,256,1536]{3,2,1,0:T(8,128)(2,1)S(1)} %get-tuple-element.96) | copy-start | bytes 9437188
  241.2 39.7 %copy-start.17 = (bf16[2,2,256,1536]{3,2,1,0:T(8,128)(2,1)}, bf16[2,2,256,1536]{3,2,1,0:T(8,128)(2,1)S(1)}, u32[]{:S(2)}) copy-start(bf16[2,2,256,1536]{3,2,1,0:T(8,128)(2,1)S(1)} %get-tuple-element.95) | copy-start | bytes 9437188
  244.8 5.0 copy-start.33
  249.8 5.1 copy-start.34
  254.9 9.0 %copy-start.36 = (bf16[4,2,2,2,48,1024]{5,4,3,2,1,0:T(8,128)(2,1)S(1)}, bf16[4,2,2,2,48,1024]{5,4,3,2,1,0:T(8,128)(2,1)}, u32[]{:S(2)}) copy-start(bf16[4,2,2,2,48,1024]{5,4,3,2,1,0:T(8,128)(2,1)} %get-tuple-element.52) | copy-start | bytes 9437188
  263.9 5.7 copy-start.48
  275.8 34.0 %copy-start.10 = (f32[1024,1536]{1,0:T(8,128)}, f32[1024,1536]{1,0:T(8,128)S(1)}, u32[]{:S(2)}) copy-start(f32[1024,1536]{1,0:T(8,128)S(1)} %convolution_add_fusion.2) | copy-start | bytes 18874372
  309.2 21.9 %collective-permute-start.1 = (f32[512,1536]{1,0:T(8,128)}, f32[512,1536]{1,0:T(8,128)}, u32[]{:S(2)}, u32[]{:S(2)}) collective-permute-start(f32[512,1536]{1,0:T(8,128)} %slice.99), channel_id=1, source_target_pairs={{0,1},{1,0},{2,3},{3,2},{4,5},{5,4},{6,7},{7,6},{8,9},{9,8},{10,11... | collective-permute-start | bytes 9437192 | tf_op jit(solution)/shard_map/ppermute | solution.py:1403
  309.7 20.4 %collective-permute-start.4 = (s32[2,1024]{1,0:T(2,128)S(1)}, s32[2,1024]{1,0:T(2,128)S(1)}, u32[]{:S(2)}, u32[]{:S(2)}) collective-permute-start(s32[2,1024]{1,0:T(2,128)S(1)} %copy-done.29), channel_id=1, source_target_pairs={{0,1},{1,0},{2,3},{3,2},{4,5},{5,4},{6,7},{7,6},{8,9},{9,8},{10,11... | collective-permute-start | bytes 24584 | tf_op jit(solution)/shard_map/ppermute | solution.py:1403
  311.7 41.5 %collective-permute-start = (f32[512,1536]{1,0:T(8,128)}, f32[512,1536]{1,0:T(8,128)}, u32[]{:S(2)}, u32[]{:S(2)}) collective-permute-start(f32[512,1536]{1,0:T(8,128)} %slice.97), channel_id=1, source_target_pairs={{0,1},{1,0},{2,3},{3,2},{4,5},{5,4},{6,7},{7,6},{8,9},{9,8},{10,11... | collective-permute-start | bytes 9437192 | tf_op jit(solution)/shard_map/ppermute | solution.py:1403
  319.3 172.0 %collective-permute-start.6 = (f32[512,1536]{1,0:T(8,128)}, f32[512,1536]{1,0:T(8,128)}, u32[]{:S(2)}, u32[]{:S(2)}) collective-permute-start(f32[512,1536]{1,0:T(8,128)} %slice.103), channel_id=1, source_target_pairs={{0,1},{1,0},{2,3},{3,2},{4,5},{5,4},{6,7},{7,6},{8,9},{9,8},{10,11... | collective-permute-start | bytes 9437192 | tf_op jit(solution)/shard_map/ppermute | solution.py:1403
  322.8 4.7 copy-start.8
  322.8 5.1 copy-start.3
  322.8 5.7 copy-start
  327.5 194.3 %collective-permute-start.5 = (f32[512,1536]{1,0:T(8,128)}, f32[512,1536]{1,0:T(8,128)}, u32[]{:S(2)}, u32[]{:S(2)}) collective-permute-start(f32[512,1536]{1,0:T(8,128)} %slice.101), channel_id=1, source_target_pairs={{0,1},{1,0},{2,3},{3,2},{4,5},{5,4},{6,7},{7,6},{8,9},{9,8},{10,11... | collective-permute-start | bytes 9437192 | tf_op jit(solution)/shard_map/ppermute | solution.py:1403
  330.1 4.7 copy-start.30
  331.1 4.4 copy-start.41
  334.8 4.3 copy-start.18
  334.8 4.3 copy-start.47
  334.8 36.8 %collective-permute-start.2 = (bf16[512,1536]{1,0:T(8,128)(2,1)S(1)}, bf16[512,1536]{1,0:T(8,128)(2,1)S(1)}, u32[]{:S(2)}, u32[]{:S(2)}) collective-permute-start(bf16[512,1536]{1,0:T(8,128)(2,1)S(1)} %fusion.4), channel_id=1, source_target_pairs={{0,2},{1,3},{2,0},{3,1},{4,6},{5,7},{6,4},{7,5},{8,10},{9,11},{10,... | collective-permute-start | bytes 4718600 | tf_op jit(solution)/shard_map/ppermute | solution.py:1403
  339.1 5.2 copy-start.16
  339.1 5.2 copy-start.44
  344.3 28.4 %slice-start.2 = ((s8[6291456]{0:T(1024)(128)(4,1)}), s8[4194304]{0:T(1024)(128)(4,1)S(1)}, s32[]{:S(2)}) async-start(s8[6291456]{0:T(1024)(128)(4,1)} %bitcast.144), calls=%async_computation.2 | async-start | bytes 8388608
  347.8 24.9 %slice-start.3 = ((s8[6291456]{0:T(1024)(128)(4,1)}), s8[2097152]{0:T(1024)(128)(4,1)S(1)}, s32[]{:S(2)}) async-start(s8[6291456]{0:T(1024)(128)(4,1)} %bitcast.144), calls=%async_computation.3 | async-start | bytes 4194304
  377.9 4.6 copy-start.50
  377.9 9.7 %collective-permute-start.3 = (bf16[512,1536]{1,0:T(8,128)(2,1)S(1)}, bf16[512,1536]{1,0:T(8,128)(2,1)S(1)}, u32[]{:S(2)}, u32[]{:S(2)}) collective-permute-start(bf16[512,1536]{1,0:T(8,128)(2,1)S(1)} %fusion.17), channel_id=1, source_target_pairs={{0,1},{1,0},{2,3},{3,2},{4,5},{5,4},{6,7},{7,6},{8,9},{9,8},{10,11... | collective-permute-start | bytes 4718600 | tf_op jit(solution)/shard_map/ppermute | solution.py:1403
  387.6 93.2 %slice-start.4 = ((s8[4718592]{0:T(1024)(128)(4,1)}), s8[4194304]{0:T(1024)(128)(4,1)S(1)}, s32[]{:S(2)}) async-start(s8[4718592]{0:T(1024)(128)(4,1)} %bitcast.182), calls=%async_computation.4 | async-start | bytes 8388608
  387.8 7.6 %copy-start.24 = (bf16[512,1536]{1,0:T(8,128)(2,1)}, bf16[512,1536]{1,0:T(8,128)(2,1)S(1)}, u32[]{:S(2)}) copy-start(bf16[512,1536]{1,0:T(8,128)(2,1)S(1)} %get-tuple-element.101) | copy-start | bytes 4718596
  387.8 7.6 %copy-start.25 = (bf16[512,1536]{1,0:T(8,128)(2,1)}, bf16[512,1536]{1,0:T(8,128)(2,1)S(1)}, u32[]{:S(2)}) copy-start(bf16[512,1536]{1,0:T(8,128)(2,1)S(1)} %get-tuple-element.102) | copy-start | bytes 4718596
  390.4 90.4 %slice-start.5 = ((s8[4718592]{0:T(1024)(128)(4,1)}), s8[524288]{0:T(1024)(128)(4,1)S(1)}, s32[]{:S(2)}) async-start(s8[4718592]{0:T(1024)(128)(4,1)} %bitcast.182), calls=%async_computation.5 | async-start | bytes 1048576
  480.9 4.2 copy-start.42
  480.9 10.4 %slice-start = ((s8[6291456]{0:T(1024)(128)(4,1)}), s8[4194304]{0:T(1024)(128)(4,1)S(1)}, s32[]{:S(2)}) async-start(s8[6291456]{0:T(1024)(128)(4,1)} %bitcast.142), calls=%async_computation | async-start | bytes 8388608
  485.1 6.2 slice-start.1
  491.3 4.2 copy-start.32
  491.3 25.7 %collective-permute-start.8 = (f32[512,1536]{1,0:T(8,128)}, f32[512,1536]{1,0:T(8,128)}, u32[]{:S(2)}, u32[]{:S(2)}) collective-permute-start(f32[512,1536]{1,0:T(8,128)} %dynamic-slice_bitcast_fusion), channel_id=1, source_target_pairs={{0,1},{1,0},{2,3},{3,2},{4,5},{5,4},{6,7},{7,6},{8,9},{9,8},{10,11... | collective-permute-start | bytes 9437192 | tf_op jit(solution)/shard_map/ppermute | solution.py:1403
  495.0 37.0 %collective-permute-start.7 = (bf16[512,1536]{1,0:T(8,128)(2,1)}, bf16[512,1536]{1,0:T(8,128)(2,1)}, u32[]{:S(2)}, u32[]{:S(2)}) collective-permute-start(bf16[512,1536]{1,0:T(8,128)(2,1)} %fusion), channel_id=1, source_target_pairs={{0,2},{1,3},{2,0},{3,1},{4,6},{5,7},{6,4},{7,5},{8,10},{9,11},{10,... | collective-permute-start | bytes 4718600 | tf_op jit(solution)/shard_map/ppermute | solution.py:1403
  510.4 6.6 copy-start.4
  517.0 15.0 %copy-start.2 = (f32[512,1536]{1,0:T(8,128)S(1)}, f32[512,1536]{1,0:T(8,128)}, u32[]{:S(2)}) copy-start(f32[512,1536]{1,0:T(8,128)} %copy-done.1) | copy-start | bytes 9437188
  517.0 15.0 %copy-start.6 = (bf16[1,2,256,1536]{3,2,1,0:T(8,128)(2,1)S(1)}, bf16[1,2,256,1536]{3,2,1,0:T(8,128)(2,1)}, u32[]{:S(2)}) copy-start(bf16[1,2,256,1536]{3,2,1,0:T(8,128)(2,1)} %slice.74) | copy-start | bytes 4718596
  663.4 5.5 copy-start.27
  669.7 7.6 %copy-start.23 = (bf16[2,256,1536]{2,1,0:T(8,128)(2,1)S(1)}, bf16[2,256,1536]{2,1,0:T(8,128)(2,1)}, u32[]{:S(2)}) copy-start(bf16[2,256,1536]{2,1,0:T(8,128)(2,1)} %get-tuple-element.125) | copy-start | bytes 4718596
  674.5 4.6 copy-start.26
  (18 other events, 56.5 us)

commit v5 on v4

--- a/solution.py
+++ b/solution.py
@@ -549,7 +549,8 @@
 class PlaneSum:
     def __init__(self, move, total, held, y, x):
         self.move, self.total = move, total
-        self.own, self.mid, self.far, self.near, self.last = (held.at[i] for i in range(5))
+        self.mid, self.far, self.near, self.last = (held.at[i] for i in range(4))
+        self.own = self.far
         half = total.shape[-1] // 2
         self.left, self.right = pl.ds(0, half), pl.ds(half, half)
         self.at = (2 * y + x, 2 * y + 1 - x, 2 * (1 - y) + x, 2 * (1 - y) + 1 - x)
@@ -562,10 +563,10 @@
             move.send(total.at[sd, :, right], self.far.at[:, right], "x"),
         ]
         self.loads = [
-            move.local(total.at[s], self.own),
             move.local(total.at[sx, :, left], self.mid.at[:, left]),
             move.local(total.at[sy, :, right], self.mid.at[:, right]),
         ]
+        self.own_load = move.quiet(total.at[s], self.own)
         self.near_moves = [
             move.copy(total.at[sy, :, left], self.near.at[:, left], "y"),
             move.copy(total.at[sx, :, right], self.near.at[:, right], "x"),
@@ -580,7 +581,7 @@
             made.start()
 
     def pass_on(self):
-        for made in self.loads[1:]:
+        for made in self.loads:
             made.wait()
         for made in self.far_moves:
             made.wait_recv()
@@ -594,9 +595,11 @@
         by_rows(rows, 16, work)
         for made in self.last_moves:
             made.start()
+        self.own_load.start()
 
     def end(self, write):
-        self.loads[0].wait()
+        if self.own_load is not None:
+            self.own_load.wait()
         for made in self.near_moves + self.last_moves:
             made.wait()
         own, near, last = self.own, self.near, self.last
@@ -606,17 +609,62 @@
             write(at, value + last[at, :].astype(jnp.float32))
 
         by_rows(own.shape[0], 16, work)
+
+
+class PlaneSumHere(PlaneSum):
+    def __init__(self, move, total, held, y, x):
+        self.move, self.total = move, total
+        self.far, self.near, self.last = (held.at[i] for i in range(3))
+        half = total.shape[-1] // 2
+        self.left, self.right = left, right = pl.ds(0, half), pl.ds(half, half)
+        self.at = s, sx, sy, sd = (2 * y + x, 2 * y + 1 - x, 2 * (1 - y) + x, 3 - 2 * y - x)
+        self.own, self.mids = total.at[s], (total.at[sx], total.at[sy])
+        self.far_moves = [
+            move.later(total.at[sd, :, left], self.far.at[:, left], "y"),
+            move.later(total.at[sd, :, right], self.far.at[:, right], "x"),
+        ]
+        self.near_moves = [
+            move.copy(total.at[sy, :, left], self.near.at[:, left], "y"),
+            move.copy(total.at[sx, :, right], self.near.at[:, right], "x"),
+        ]
+        self.last_moves = [
+            move.copy(total.at[sx, :, left], self.last.at[:, left], "x"),
+            move.copy(total.at[sy, :, right], self.last.at[:, right], "y"),
+        ]
+        self.own_load = None
+
+    def start(self):
+        for made in self.far_moves:
+            made.start()
+
+    def pass_on(self):
+        for made in self.far_moves:
+            made.wait_recv()
+        far = self.far
+
+        def work(at):
+            for mid, part in zip(self.mids, (self.left, self.right)):
+                added = mid[at, part].astype(jnp.float32) + far[at, part].astype(jnp.float32)
+                mid[at, part] = added.astype(jnp.bfloat16)
+
+        by_rows(far.shape[0], 16, work)
+        for made in self.last_moves:
+            made.start()
 
 
 def tail_kernel(
     gate_in,
     up_in,
     down_in,
-    qkv_in,
+    grad_in,
+    normed,
+    qkv_w,
+    x_own,
+    steep,
+    gain_rows,
+    gain_two,
     out_in,
     y_in,
-    x_in,
-    gain_in,
     gate_out,
     up_out,
     down_out,
@@ -630,12 +678,15 @@
     down_low,
     down_got,
     quarter,
+    part,
+    part_got,
+    x_low,
+    qkv_in,
     qkv_held,
     qkv_sum,
     qkv_low,
     qkv_got,
     out_got,
-    out_low,
     out_x,
     out_line,
     out_line_got,
@@ -652,10 +703,22 @@
     other = jnp.logical_not(mine)
     greet(me, HEAD_GROUPS)
     move = Mover(me, sends, recvs)
-    qkv = PlaneSum(move, qkv_in, qkv_held, y, x)
+    qkv = PlaneSumHere(move, qkv_in, qkv_held, y, x)
+    out_y = move.copy(out_in, out_got, "y")
+    half_len = part.shape[0]
+    block_rows = qkv_in.shape[1]
+
+    def weigh(at):
+        lanes = pl.ds(pl.multiple_of(at * block_rows, 128), block_rows)
+        total = tn(normed[0, :, lanes], grad_in[pl.ds(0, half_len), :])
+        total = total + tn(normed[1, :, lanes], grad_in[pl.ds(half_len, half_len), :])
+        qkv_in[at] = total.astype(low)
+
+    weigh(qkv.at[3])
     qkv.start()
-    out_y = move.copy(out_in, out_got, "y")
-    pl.when(other)(out_y.start)
+
+    weigh(qkv.at[1])
+    weigh(qkv.at[2])
     qkv.start_near()
 
     pair_rows = pair_got.shape[1]
@@ -673,62 +736,57 @@
     lower(down_in, down_low, 1 - zh, down_low.shape[0])
     pairs.append(move.send(down_low, down_got, "zh"))
 
-    gain_out[...] = gain_in[...]
-    for turn, name in enumerate(("core", "x", "y", "zl", "zh")):
-        made = move.copy(gain_out, gain_got.at[turn], name)
-        made.start()
-        made.wait()
-        gain_out[...] = gain_out[...] + gain_got[turn]
-
+    theirs, ours = (pl.multiple_of(c * half_len, half_len) for c in (1 - core, core))
+
+    def project(start):
+        for i in range(half_len // QB):
+            at = pl.ds(pl.multiple_of(start + i * QB, QB), QB)
+            part[pl.ds(i * QB, QB), :] = nt(grad_in[at, :], qkv_w[...])
+
+    project(theirs)
+    part_move = move.copy(part, part_got, "core")
+    part_move.start()
+    weigh(qkv.at[0])
     qkv.pass_on()
+    pl.when(other)(out_y.start)
+    y_turn = turn_start(move, me, y_in, y_out)
+    part_move.wait()
+    project(ours)
+    gain_out[...] = jnp.zeros_like(gain_out)
+    gain_out[1:2, :] = gain_two[...]
+    piece = half_len // 2
+    for q in range(2):
+
+        def norm_back(at, q=q):
+            every = pl.ds(pl.multiple_of(q * piece + at.start, 16), at.size)
+            grad = part[every, :] + part_got[every, :]
+            field = x_own[q, at, :].astype(f32)
+            inverse = lax.rsqrt(jnp.mean(field * field, axis=1, keepdims=True) + EPSILON)
+            unit = field * inverse
+            gain_out[0:1, :] += jnp.sum(grad * unit, axis=0, keepdims=True)
+            scaled = grad * gain_rows[0:1, :]
+            centre = jnp.mean(scaled * unit, axis=1, keepdims=True)
+            value = steep[every, :] + inverse * (scaled - unit * centre)
+            x_low[q, at, :] = value.astype(low)
+
+        by_rows(piece, 16, norm_back)
+    x_turn = turn_start(move, me, x_low, x_out)
+
+    gain_moves = [
+        move.copy(gain_out, gain_got.at[turn], name)
+        for turn, name in enumerate(("core", "x", "y", "zl", "zh"))
+    ]
+
+    def gain_round(turn):
+        if turn > 0:
+            gain_moves[turn - 1].wait()
+            gain_out[...] = gain_out[...] + gain_got[turn - 1]
+        if turn < len(gain_moves):
+            gain_moves[turn].start()
+
+    gain_round(0)
     out_shape = out_in.shape
     blocks = [(a, b) for a in range(out_shape[1]) for b in range(out_shape[2])]
-
-    out_x_move = move.copy(out_low.at[1 - x], out_x, "x")
-
-    @pl.when(mine)
-    def _():
-        out_y.wait_recv()
-
-        def half(at_x):
-            def work(i, carry):
-                a, b = i // out_shape[2], i % out_shape[2]
-                value = out_in[at_x, a, b].astype(f32) + out_got[at_x, a, b].astype(f32)
-                out_low[at_x, a, b] = value.astype(low)
-                return carry
-
-            lax.fori_loop(0, len(blocks), work, 0)
-
-        half(1 - x)
-        out_x_move.start()
-        half(x)
-
-    y_turn = turn_start(move, me, y_in, y_out)
-    x_turn = turn_start(move, me, x_in, x_out)
-
-    spread = []
-    for i, (src, dst) in enumerate(((gate_in, gate_out), (up_in, up_out))):
-        pairs[i].wait_recv()
-        got, full = pair_got.at[i], quarter.at[i]
-
-        def work(at, src=src, got=got, full=full):
-            full[at, :] = src[zh, at, :] + got[at, :].astype(f32)
-
-        by_rows(pair_rows, 32, work)
-        count = pair_rows // 4
-        for names in (("core",), ("zl",), ("zl", "core")):
-            to_zl = 1 - zl if "zl" in names else zl
-            to_core = 1 - core if "core" in names else core
-            start = pl.multiple_of((2 * to_zl + to_core) * count, count)
-            spread.append(move.send(full.at[pl.ds(start, count)], dst.at[zl, core], *names))
-        start = pl.multiple_of((2 * zl + core) * count, count)
-        dst[zl, core] = full[pl.ds(start, count), :]
-    pairs[2].wait_recv()
-
-    def work(at):
-        down_out[at, :] = down_in[zh, at, :] + down_got[at, :].astype(f32)
-
-    by_rows(down_out.shape[0], 32, work)
 
     def keep(at, value):
         qkv_sum[at, :] = value
@@ -742,6 +800,54 @@
         start = pl.multiple_of(to * count, count)
         line.append(move.send(qkv_low.at[pl.ds(start, count)], qkv_got.at[k], *names))
 
+    gain_round(1)
+
+    out_x_move = move.copy(out_got.at[1 - x], out_x, "x")
+
+    @pl.when(mine)
+    def _():
+        out_y.wait_recv()
+
+        def half(at_x):
+            def work(i, carry):
+                a, b = i // out_shape[2], i % out_shape[2]
+                value = out_in[at_x, a, b].astype(f32) + out_got[at_x, a, b].astype(f32)
+                out_got[at_x, a, b] = value.astype(low)
+                return carry
+
+            lax.fori_loop(0, len(blocks), work, 0)
+
+        half(1 - x)
+        out_x_move.start()
+        half(x)
+
+    gain_round(2)
+
+    spread = []
+    for i, (src, dst) in enumerate(((gate_in, gate_out), (up_in, up_out))):
+        pairs[i].wait_recv()
+        got, full = pair_got.at[i], quarter.at[i]
+
+        def work(at, src=src, got=got, full=full):
+            full[at, :] = src[zh, at, :] + got[at, :].astype(f32)
+
+        by_rows(pair_rows, 32, work)
+        share = pair_rows // 4
+        for names in (("core",), ("zl",), ("zl", "core")):
+            to_zl = 1 - zl if "zl" in names else zl
+            to_core = 1 - core if "core" in names else core
+            start = pl.multiple_of((2 * to_zl + to_core) * share, share)
+            spread.append(move.send(full.at[pl.ds(start, share)], dst.at[zl, core], *names))
+        start = pl.multiple_of((2 * zl + core) * share, share)
+        dst[zl, core] = full[pl.ds(start, share), :]
+    pairs[2].wait_recv()
+
+    def work(at):
+        down_out[at, :] = down_in[zh, at, :] + down_got[at, :].astype(f32)
+
+    by_rows(down_out.shape[0], 32, work)
+
+    gain_round(3)
     out_moves = []
     for k, names in enumerate(LINE):
         to = z ^ (1, 2, 3)[k]
@@ -753,7 +859,7 @@
 
         def work(i, carry):
             a, b = i // out_shape[2], i % out_shape[2]
-            value = out_low[x, a, b].astype(f32) + out_x[a, b].astype(f32)
+            value = out_got[x, a, b].astype(f32) + out_x[a, b].astype(f32)
             out_line[a, b] = value.astype(low)
             return carry
 
@@ -761,6 +867,7 @@
         for made in out_moves:
             made.start()
 
+    gain_round(4)
     for made in line:
         made.wait_recv()
     start = pl.multiple_of(z * count, count)
@@ -800,6 +907,7 @@
         out_y.wait_send()
         out_swap.wait_recv()
 
+    gain_round(5)
     turn_end(me, y_turn)
     turn_end(me, x_turn)
     swap.wait_recv()
@@ -808,16 +916,17 @@
     move.finish()
 
 
-def sum_tail(gate, up, down, qkv, out, y_in, x_in, gain):
+def sum_tail(gate, up, down, grad, normed, qkv_w, x_own, steep, gain_rows, gain_two, out, y_in):
     f32, low = jnp.float32, jnp.bfloat16
     hbm = pl.BlockSpec(memory_space=pl.ANY)
     vmem = pl.BlockSpec(memory_space=pltpu.VMEM)
-    wide, width = gate.shape[-1], qkv.shape[-1]
-    rows = qkv.shape[1] // 8
+    wide, width = gate.shape[-1], grad.shape[-1]
+    rows = out.shape[-2]
+    half_len = steep.shape[0]
     pair_rows, down_rows = gate.shape[1], down.shape[1]
     return pl.pallas_call(
         tail_kernel,
-        in_specs=[vmem, vmem, vmem, hbm, vmem, hbm, hbm, vmem],
+        in_specs=[vmem] * 11 + [hbm],
         out_specs=[vmem] * 5 + [hbm, hbm, vmem],
         out_shape=[
             jax.ShapeDtypeStruct((2, 2, rows, wide), f32),
@@ -826,34 +935,38 @@
             jax.ShapeDtypeStruct((2, rows, width), f32),
             jax.ShapeDtypeStruct((rows, width), f32),
             jax.ShapeDtypeStruct(y_in.shape, low),
-            jax.ShapeDtypeStruct(x_in.shape, low),
-            jax.ShapeDtypeStruct(gain.shape, f32),
+            jax.ShapeDtypeStruct(y_in.shape, low),
+            jax.ShapeDtypeStruct((2, width), f32),
         ],
+        input_output_aliases={},
         scratch_shapes=[
             pltpu.VMEM((2, pair_rows, wide), low),
             pltpu.VMEM((2, pair_rows, wide), low),
             pltpu.VMEM((down_rows, width), low),
             pltpu.VMEM((down_rows, width), low),
             pltpu.VMEM((2, pair_rows, wide), f32),
-            pltpu.VMEM((5,) + qkv.shape[1:], low),
-            pltpu.VMEM(qkv.shape[1:], f32),
-            pltpu.VMEM(qkv.shape[1:], low),
+            pltpu.VMEM((half_len, width), f32),
+            pltpu.VMEM((half_len, width), f32),
+            pltpu.VMEM(y_in.shape, low),
+            pltpu.VMEM((4, 8 * rows, width), low),
+            pltpu.VMEM((3, 8 * rows, width), low),
+            pltpu.VMEM((8 * rows, width), f32),
+            pltpu.VMEM((8 * rows, width), low),
             pltpu.VMEM((3, 2 * rows, width), low),
-            pltpu.VMEM(out.shape, low),
             pltpu.VMEM(out.shape, low),
             pltpu.VMEM(out.shape[1:], low),
             pltpu.VMEM(out.shape[1:], low),
             pltpu.VMEM((3,) + out.shape[2:], low),
             pltpu.VMEM((rows, width), f32),
-            pltpu.VMEM((5,) + gain.shape, f32),
+            pltpu.VMEM((5, 2, width), f32),
             pltpu.SemaphoreType.DMA((48,)),
             pltpu.SemaphoreType.DMA((48,)),
         ],
         compiler_params=pltpu.CompilerParams(
-            collective_id=4, has_side_effects=True, vmem_limit_bytes=56 << 20
+            collective_id=4, has_side_effects=True, vmem_limit_bytes=63 << 20
         ),
         name="tail",
-    )(gate, up, down, qkv, out, y_in, x_in, gain)
+    )(gate, up, down, grad, normed, qkv_w, x_own, steep, gain_rows, gain_two, out, y_in)
 
 
 QB = 256
@@ -961,14 +1074,22 @@
         gvs[j, span, :] += nn(probs.astype(low), grad)
         gks[j, span, :] += nn(gs, query)
         results.append(spun(tn(gs, key) * width, cosine, sine, True).astype(low))
-    gq_ref[here, :] = jnp.concatenate(results, axis=1)
+    gq_ref[here, : HD * heads] = jnp.concatenate(results, axis=1)
 
 
 def behind_kernel(
     heads,
     kvs,
     qkv_ref,
-    grad_ref,
+    mixed,
+    hidden,
+    seed,
+    back_own,
+    back,
+    ahead_own,
+    ahead_far,
+    out_w,
+    gain_rows,
     cos_ref,
     sin_ref,
     row_ref,
@@ -976,11 +1097,16 @@
     gate_in,
     up_in,
     down_in,
-    gq_ref,
-    gkv_ref,
+    grad_ref,
+    steep,
+    steep_low,
+    y_low,
+    out_grad,
+    gain_ref,
     gate_out,
     up_out,
     down_out,
+    ahead_got,
     keys,
     gks,
     gvs,
@@ -990,10 +1116,10 @@
     sends,
     recvs,
 ):
-    low = jnp.bfloat16
+    f32, low = jnp.float32, jnp.bfloat16
     me = coordinates()
-    y, x = me[0], me[1]
-    greet(me, (("x",), ("y",)))
+    y, x, zh, zl, core = me
+    greet(me, (("x",), ("y",), ("core",), ("zl",)))
     move = Mover(me, sends, recvs)
     sums = [
         PlaneSum(move, total, held, y, x)
@@ -1001,19 +1127,39 @@
     ]
     for plane in sums:
         plane.start()
+    ahead_move = move.send(ahead_far, ahead_got, "zl")
+    gain_ref[...] = jnp.zeros_like(gain_ref)
+    half_len = hidden.shape[0]
+
+    def norm_back(at):
+        grad = back_own[at, :] + back[at, :].astype(f32)
+        field = hidden[at, :]
+        inverse = lax.rsqrt(jnp.mean(field * field, axis=1, keepdims=True) + EPSILON)
+        unit = field * inverse
+        gain_ref[...] += jnp.sum(grad * unit, axis=0, keepdims=True)
+        scaled = grad * gain_rows[1:2, :]
+        centre = jnp.mean(scaled * unit, axis=1, keepdims=True)
+        value = seed[at, :].astype(f32) + inverse * (scaled - unit * centre)
+        steep[at, :] = value
+        steep_low[core, at, :] = value.astype(low)
+
+    by_rows(half_len, 16, norm_back)
+    swap = move.send(steep_low.at[core], steep_low.at[core], "core")
     everything = pl.ds(0, qkv_ref.shape[0])
     for j in range(kvs):
         keys[j] = spun(head(qkv_ref, everything, heads + j), cos_ref[...], sin_ref[...]).astype(low)
     gks[...] = jnp.zeros_like(gks)
     gvs[...] = jnp.zeros_like(gvs)
+    swap.wait_recv()
+    per = half_len // QB
+    for i in range(2 * per):
+        at = pl.ds(i % per * QB, QB)
+        grad_ref[pl.ds(i * QB, QB), : heads * HD] = nt(steep_low[i // per, at, :], out_w[...]).astype(low)
+    for plane in sums:
+        plane.start_near()
 
     def block(step, carry):
-        @pl.when(step == 2)
-        def _():
-            for plane in sums:
-                plane.start_near()
-
-        @pl.when(step == 3)
+        @pl.when(step == SPAN // QB - 1)
         def _():
             for plane in sums:
                 plane.pass_on()
@@ -1023,8 +1169,8 @@
 
     def work(step, size):
         behind_block(
-            heads, kvs, step, size, qkv_ref, grad_ref, cos_ref, sin_ref, row_ref, col_ref, gq_ref,
-            keys, gks, gvs,
+            heads, kvs, step, size, qkv_ref, grad_ref, cos_ref, sin_ref, row_ref, col_ref,
+            grad_ref, keys, gks, gvs,
         )
 
     for step in range(SPAN // QB - 1):
@@ -1035,40 +1181,69 @@
         spun(gks[j] * width, cos_ref[...], sin_ref[...], True).astype(low) for j in range(kvs)
     ]
     gv = [gvs[j].astype(low) for j in range(kvs)]
-    gkv_ref[...] = jnp.concatenate(gk + gv, axis=1)
+    grad_ref[:, HD * heads :] = jnp.concatenate(gk + gv, axis=1)
+    rows = mixed.shape[1] // 4
+    for i in range(4):
+        lanes = pl.ds(i * rows, rows)
+        total = tn(mixed[pl.ds(0, half_len), lanes], steep_low[0])
+        total = total + tn(mixed[pl.ds(half_len, half_len), lanes], steep_low[1])
+        out_grad[pl.ds(i * rows, rows), :] = total.astype(low)
+    ahead_move.wait_recv()
+    quarter = half_len // 2
+    for q in range(2):
+
+        def add(at, q=q):
+            every = pl.ds(pl.multiple_of(q * quarter + at.start, 16), at.size)
+            value = hidden[every, :] + ahead_own[every, :] + ahead_got[q, at, :].astype(f32)
+            ahead_got[q, at, :] = value.astype(low)
+
+        by_rows(quarter, 16, add)
+    stored = move.local(ahead_got, y_low)
     for plane, out in zip(sums, (gate_out, up_out, down_out)):
 
         def write(at, value, out=out):
             out[at, :] = value
 
         plane.end(write)
+    stored.wait()
     move.finish()
 
 
-def attend_behind(heads, kvs, qkv, grad, cosine, sine, row, col, gate, up, down):
-    low, f32 = jnp.bfloat16, jnp.float32
-    length = qkv.shape[0]
+def attend_behind(heads, kvs, *operands):
+    f32, low = jnp.float32, jnp.bfloat16
+    qkv, mixed, hidden = operands[:3]
+    totals = operands[-3:]
+    length, width = qkv.shape
+    half_len = length // 2
     hbm = pl.BlockSpec(memory_space=pl.ANY)
     vmem = pl.BlockSpec(memory_space=pltpu.VMEM)
-    totals = (gate, up, down)
+
+    def made(*shape, dtype=low):
+        return jax.ShapeDtypeStruct(shape, dtype)
+
     return pl.pallas_call(
         functools.partial(behind_kernel, heads, kvs),
-        in_specs=[vmem] * 6 + [hbm] * 3,
-        out_specs=[vmem] * 5,
+        in_specs=[vmem] * 7 + [hbm] + [vmem] * 6 + [hbm] * 3,
+        out_specs=[vmem] * 3 + [hbm] + [vmem] * 5,
         out_shape=[
-            jax.ShapeDtypeStruct((length, heads * HD), low),
-            jax.ShapeDtypeStruct((length, 2 * kvs * HD), low),
+            made(length, width),
+            made(half_len, width, dtype=f32),
+            made(2, half_len, width),
+            made(2, half_len // 2, width),
+            made(heads * HD, width),
+            made(1, width, dtype=f32),
         ]
-        + [jax.ShapeDtypeStruct(total.shape[1:], f32) for total in totals],
+        + [made(*total.shape[1:], dtype=f32) for total in totals],
         scratch_shapes=[
+            pltpu.VMEM((2, half_len // 2, width), low),
             pltpu.VMEM((kvs, length, HD), low),
             pltpu.VMEM((kvs, length, HD), f32),
             pltpu.VMEM((kvs, length, HD), f32),
         ]
-        + [pltpu.VMEM((5,) + total.shape[1:], low) for total in totals]
-        + [pltpu.SemaphoreType.DMA((32,)), pltpu.SemaphoreType.DMA((32,))],
+        + [pltpu.VMEM((4,) + total.shape[1:], low) for total in totals]
+        + [pltpu.SemaphoreType.DMA((40,)), pltpu.SemaphoreType.DMA((40,))],
         compiler_params=pltpu.CompilerParams(
-            collective_id=3, has_side_effects=True, vmem_limit_bytes=56 << 20
+            collective_id=3, has_side_effects=True, vmem_limit_bytes=63 << 20
         ),
         cost_estimate=pl.CostEstimate(
             flops=10 * heads * length * SPAN * HD,
@@ -1076,7 +1251,7 @@
             transcendentals=heads * length * SPAN,
         ),
         name="behind",
-    )(qkv, grad, cosine, sine, row, col, *totals)
+    )(*operands)
 
 
 def bands(size):
@@ -1398,6 +1573,131 @@
     )(x_in, g_in, qkv, gate, up, down, out, gain, docs, cosine, sine)
 
 
+def hidden_kernel(
+    tokens,
+    seeds,
+    gate_w,
+    up_w,
+    down_w,
+    act_out,
+    gate_out,
+    up_out,
+    back_own,
+    back_far,
+    ahead_own,
+    ahead_far,
+    backs,
+    aheads,
+    back_got,
+    ahead_got,
+    sends,
+    recvs,
+):
+    f32, low = jnp.float32, jnp.bfloat16
+    me = coordinates()
+    move = Mover(me, sends, recvs)
+
+    @pl.when(pl.program_id(0) == 0)
+    def _():
+        greet(me, (("core",),))
+
+    half_len = backs.shape[1]
+    per = half_len // QB
+    i = pl.program_id(0)
+    moves = [
+        (
+            move.copy(backs.at[1], back_got.at[turn], "core"),
+            move.copy(aheads.at[1], ahead_got.at[turn], "core"),
+        )
+        for turn in range(2)
+    ]
+
+    def fold(turn, back_ref, ahead_ref):
+        for made in moves[turn]:
+            made.wait()
+
+        def work(at):
+            back_ref[at, :] = (backs[0, at, :] + back_got[turn, at, :]).astype(back_ref.dtype)
+            ahead_ref[at, :] = (aheads[0, at, :] + ahead_got[turn, at, :]).astype(ahead_ref.dtype)
+
+        by_rows(half_len, 16, work)
+
+    slot = 3 - i // per
+    rows = pl.ds(pl.multiple_of(i % per * QB, QB), QB)
+    token, seed = tokens[...], seeds[...]
+    gate, upward = nn(token, gate_w[...]), nn(token, up_w[...])
+    sigma = 1.0 / (1.0 + jnp.exp(-gate))
+    silu = gate * sigma
+    activated = (silu * upward).astype(low)
+    act_out[...] = activated
+    grad = nt(seed, down_w[...])
+    up_low = (grad * silu).astype(low)
+    gate_low = (grad * upward * sigma * (1.0 + gate * (1.0 - sigma))).astype(low)
+    up_out[...] = up_low
+    gate_out[...] = gate_low
+    aheads[slot % 2, rows, :] = nn(activated, down_w[...])
+    backs[slot % 2, rows, :] = nt(gate_low, gate_w[...]) + nt(up_low, up_w[...])
+    for turn in range(2):
+
+        @pl.when(i == (2 * turn + 1) * per - 1)
+        def _(turn=turn):
+            for made in moves[turn]:
+                made.start()
+
+    @pl.when(i == 2 * per - 1)
+    def _():
+        fold(0, back_far, ahead_far)
+
+    @pl.when(i == 4 * per - 1)
+    def _():
+        fold(1, back_own, ahead_own)
+
+
+def hidden_part(tokens, seeds, gate_w, up_w, down_w):
+    f32, low = jnp.float32, jnp.bfloat16
+    half_len, width = tokens.shape[1:]
+    wide = gate_w.shape[1]
+    per = half_len // QB
+    vmem = pl.BlockSpec(memory_space=pltpu.VMEM)
+
+    def banded(columns):
+        return pl.BlockSpec((QB, columns), lambda i: ((3 - i // per) * per + i % per, 0))
+
+    def made(rows, columns, dtype=low):
+        return jax.ShapeDtypeStruct((rows, columns), dtype)
+
+    return pl.pallas_call(
+        hidden_kernel,
+        grid=(4 * per,),
+        in_specs=[banded(width)] * 2 + [vmem] * 3,
+        out_specs=[banded(wide)] * 3 + [vmem] * 4,
+        out_shape=[made(4 * half_len, wide)] * 3
+        + [
+            made(half_len, width, f32),
+            made(half_len, width),
+            made(half_len, width, f32),
+            made(half_len, width),
+        ],
+        scratch_shapes=[
+            pltpu.VMEM((2, half_len, width), f32),
+            pltpu.VMEM((2, half_len, width), f32),
+            pltpu.VMEM((2, half_len, width), f32),
+            pltpu.VMEM((2, half_len, width), f32),
+            pltpu.SemaphoreType.DMA((4,)),
+            pltpu.SemaphoreType.DMA((4,)),
+        ],
+        compiler_params=pltpu.CompilerParams(
+            collective_id=2, has_side_effects=True, vmem_limit_bytes=63 << 20
+        ),
+        cost_estimate=pl.CostEstimate(
+            flops=2 * 6 * 4 * half_len * width * wide,
+            bytes_accessed=40 << 20,
+            transcendentals=4 * half_len * wide,
+        ),
+        name="hidden",
+    )(tokens.reshape(-1, width), seeds.reshape(-1, width), gate_w, up_w, down_w)
+
+
 def hop(value, *names):
     flip = sum(BITS[name] for name in names)
     return lax.ppermute(value, AXES, [(i, i ^ flip) for i in range(32)])
@@ -1443,18 +1743,8 @@
     heads, kvs = HEADS // 2, KV // 2
     cosine, sine = rope_tables(length, HD)
 
-    def swap_in(mine, sent):
-        return in_order(mine[None], hop(sent, "core")[None], core)
-
     def halves(weight):
         return weight.reshape(rows, 2, -1)
-
-    def both(mine):
-        return in_order(mine, hop(mine, "core"), core)
-
-    def join(part):
-        part = part.reshape(2, half_len, width)
-        return pick(part, core) + hop(pick(part, 1 - core), "core")
 
     masked = cotangent * token_mask.astype(low)[:, :, None]
     qkv = jnp.concatenate([halves(w) for w in (w_query, w_key, w_value)], axis=2)
@@ -1484,96 +1774,67 @@
             sine,
         )
     )
-    normed = normed.reshape(length, width)
     qkv_w, out_w = qkv_w.reshape(width, -1), out_w.reshape(-1, width)
     gate_w, up_w = gate_w.reshape(width, -1), up_w.reshape(width, -1)
     down_w = down_w.reshape(-1, width)
-    seed_low = seeds[0].reshape(half_len, width)
-    seeds = seeds.reshape(2, length, width)
-    normed_two = tokens.reshape(2, length, width)
+    seeds = seeds.reshape(4, half_len, width)
     documents = pick(jnp.where(core == y, document_ids, hop(document_ids, "core")), x)
     row, col = documents[None, :], documents[:, None]
-    inputs = own.reshape(half_len, width).astype(f32)
-    inv_one = inverse_rms(inputs)
-    unit_one = inputs * inv_one
-    inv_two = inverse_rms(hidden)
-    unit_two = hidden * inv_two
-
-    def ahead_and_back(tokens, seed):
-        gate, upward, grad_act = nn(tokens, gate_w), nn(tokens, up_w), nt(seed, down_w)
-        sigma = jax.nn.sigmoid(gate)
-        activated = (gate * sigma * upward).astype(low)
-        up_low = (grad_act * gate * sigma).astype(low)
-        gate_low = (grad_act * upward * sigma * (1.0 + gate * (1.0 - sigma))).astype(low)
-        back = nt(gate_low, gate_w) + nt(up_low, up_w)
-        return activated, gate_low, up_low, nn(activated, down_w), back
-
-    near = ahead_and_back(normed_two[0], seeds[0])
-    far_tokens = after(normed_two[1], near[4])
-    far = ahead_and_back(far_tokens, seeds[1])
-
-    def fold(part):
-        return part[:half_len] + hop(part[half_len:], "core")
-
-    theirs = fold(far[4]).astype(low)
-    back = hop(theirs, "zl")
-    near_low, far_low = (
-        tuple(after(v, theirs) for v in parts[:3]) for parts in (near, far)
+    activated, gate_low, up_low, back_own, back_far, ahead_own, ahead_far = hidden_part(
+        tokens, seeds, gate_w, up_w, down_w
     )
-    grad_down = (tn(near_low[0], seeds[0]) + tn(far_low[0], seeds[1])).astype(low)
-    grad_gate = (tn(normed_two[0], near_low[1]) + tn(far_tokens, far_low[1])).astype(low)
-    grad_up = (tn(normed_two[0], near_low[2]) + tn(far_tokens, far_low[2])).astype(low)
+    back = hop(back_far, "zl")
+    flat_tokens, flat_seeds = tokens.reshape(-1, width), seeds.reshape(-1, width)
+    grad_gate = tn(flat_tokens, gate_low).astype(low)
+    grad_up = tn(flat_tokens, up_low).astype(low)
+    grad_down = tn(activated, flat_seeds).astype(low)
     totals = [
         grad_gate.reshape(4, -1, units // 4),
         grad_up.reshape(4, -1, units // 4),
         grad_down.reshape(4, -1, width),
     ]
-
-    grad_normed_two = fold(near[4]) + back.astype(f32)
-    scaled_two = grad_normed_two * gains[1]
-    grad_hidden = seed_low.astype(f32) + inv_two * (
-        scaled_two - unit_two * jnp.mean(scaled_two * unit_two, axis=-1, keepdims=True)
+    back = after(back, *totals)
+    grad_qkv, steep, _, y_low, grad_out_w, gain_two, *sums = attend_behind(
+        heads,
+        kvs,
+        pair,
+        mixed,
+        hidden,
+        seeds[0],
+        back_own,
+        back,
+        ahead_own,
+        ahead_far.reshape(2, quarter, width),
+        out_w,
+        gains,
+        cosine,
+        sine,
+        row,
+        col,
+        *totals,
     )
-    grad_low = both(grad_hidden.astype(low))
-    grad_heads = nt(grad_low, out_w).astype(low)
-    grad_heads = after(grad_heads, *totals)
-
-    ahead_low = after(fold(far[3]).astype(low), back)
-    output = hidden + fold(near[3]) + hop(ahead_low, "zl").astype(f32)
-    gain_two = jnp.sum(grad_normed_two * unit_two, axis=0)
-
-    grad_query, grad_pair, *sums = attend_behind(
-        heads, kvs, pair, grad_heads, cosine, sine, row, col, *totals
-    )
-    cols = heads * HD
-    part = nt(grad_query, qkv_w[:, :cols]) + nt(grad_pair, qkv_w[:, cols:])
-    grad_out_w = tn(mixed, grad_low).astype(low).reshape(2, 4, 2, rows, width)
-    grad_qkv = jnp.concatenate(
-        [tn(normed, grad_query).astype(low), tn(normed, grad_pair).astype(low)], axis=1
-    )
-    grad_normed = join(part)
-    scaled_one = grad_normed * gains[0]
-    grad_input = grad_hidden + inv_one * (
-        scaled_one - unit_one * jnp.mean(scaled_one * unit_one, axis=-1, keepdims=True)
-    )
-    gain = jnp.stack([jnp.sum(grad_normed * unit_one, axis=0), gain_two])
     hidden_grads = [None, None]
     hidden_grads[0], hidden_grads[1], grad_down, grad_qkv, grad_output, output, grad_input, gain = (
         sum_tail(
             sums[0].reshape(2, -1, units // 4),
             sums[1].reshape(2, -1, units // 4),
             sums[2].reshape(2, -1, width),
-            grad_qkv.reshape(4, -1, width),
-            grad_out_w,
-            output.astype(low).reshape(2, quarter, width),
-            grad_input.astype(low).reshape(2, quarter, width),
-            gain,
+            grad_qkv,
+            normed,
+            qkv_w,
+            own,
+            steep,
+            gains,
+            gain_two,
+            grad_out_w.reshape(2, 4, 2, rows, width),
+            y_low,
         )
     )
     hidden_grads = [
         jnp.transpose(total.reshape(2, 2, rows, -1, 128), (2, 3, 0, 1, 4)).reshape(rows, units)
         for total in hidden_grads
     ]
+    cols = heads * HD
 
     def columns(start, size):
         return jnp.moveaxis(grad_qkv[:, :, start : start + size], 0, 1).reshape(rows, -1)

time: 684 us -> 568 us (0.83)
  matrix products: 118 us -> 28.2 us
  Pallas kernels: 430 us -> 494 us
  local copies, waits for them, and re-layouts: 66.9 us -> 28.4 us
  other arithmetic: 33.2 us -> 8.02 us
  waiting for transfers between devices: 28.6 us -> 3.98 us
    dot_general x15 -> x0, matrix products: 79.4 us -> none  [the longest x9 44 us: nt(): lax.dot_general(left, right, (((1,), (1,)), ((), ())), preferred_element_...]
    pallas_call x1 -> x2, Pallas kernels: 125 us -> 181 us  [the longest x1 128 us: sum_tail(): pl.pallas_call(tail_kernel, in_specs=[vmem] * 11 + [hbm], out_specs=[vmem...]
    ppermute x9 -> x2, waiting for transfers between devices: 28.6 us -> 3.98 us  [hop(): return lax.ppermute(value, AXES, [(i, i ^ flip) for i in range(32)])]
    unnamed x123 -> x32, local copies, waits for them, and re-layouts: 28.5 us -> 9.02 us
    convert_element_type x4 -> x0, other arithmetic: 14.2 us -> none  [the longest x1 6.08 us: fast_body(): grad_input.astype(low).reshape(2, quarter, width)]
    dot_general x9 -> x3, matrix products: 38.4 us -> 28.2 us  [tn(): lax.dot_general(left, right, (((0,), (0,)), ((), ())), preferred_element_...]
    slice x8 -> x1, local copies, waits for them, and re-layouts: 12.8 us -> 2.66 us  [fast_body(): seeds[0]]
    reduce_sum x4 -> x0, other arithmetic: 8.33 us -> none  [the longest x1 4.15 us: fast_body(): gain = jnp.stack([jnp.sum(grad_normed * unit_one, axis=0), gain_two])]
  transfers between devices with their start and end apart: 9 -> 2, of which waited for: 2 -> 1; matrix products, arithmetic and copies ran while one was open for 14% -> 9% of each run, Pallas kernels for 13% -> 48%
where the time goes in v5:
time: 568 us; the launch traced here: 564 us
  Pallas kernels  494 us (87%)
  local copies, waits for them, and re-layouts  28.4 us (5%)
  matrix products  28.2 us (5%)
  other arithmetic  8.02 us (1%)
    pallas_call x1, Pallas kernels, first_part(): pl.pallas_call(functools.partial(first_kernel, heads, kvs), in_specs=[hbm...  220 us
    pallas_call x1, Pallas kernels, sum_tail(): pl.pallas_call(tail_kernel, in_specs=[vmem] * 11 + [hbm], out_specs=[vmem...  128 us
    pallas_call x1, Pallas kernels, attend_behind(): pl.pallas_call(functools.partial(behind_kernel, heads, kvs), in_specs=[vm...  92.8 us
    pallas_call x1, Pallas kernels, hidden_part(): pl.pallas_call(hidden_kernel, grid=(4 * per,), in_specs=[banded(width)] *...  53.4 us
    dot_general x3, matrix products, tn(): lax.dot_general(left, right, (((0,), (0,)), ((), ())), preferred_element_...  28.2 us
  transfers between devices with their start and end apart: 2, of which 1 were waited for; matrix products, arithmetic and copies ran while one was open for 9% of the time, Pallas kernels for 48%

profile of v5, /device:TPU:0, one launch (start us, length us, event | category | flops | bytes accessed | tf_op | source)
XLA Modules:
  0.0 564.4 jit_solution(811425177614162553)
XLA Ops:
  0.6 0.5 collective-permute-start.1
  1.2 1.3 broadcast_in_dim.14.docs_in
  2.5 1.9 fusion
  4.4 0.9 copy.54
  5.3 1.2 convert_element_type.15
  6.6 1.3 reshape.120
  7.9 0.0 copy-start
  7.9 0.1 copy.53
  7.9 0.9 reshape.121.gate_in
  8.8 1.3 reshape.122
  10.1 0.1 copy.52
  10.2 0.0 copy-start.9
  10.2 0.9 reshape.123.up_in
  11.1 1.3 pad_maximum_fusion
  12.4 0.9 copy_bitcast_fusion.3
  13.4 2.0 broadcast_multiply_fusion.g_in
  15.4 0.1 fusion.3
  15.4 0.7 maximum_bitcast_fusion.qkv_in
  16.2 0.6 broadcast_in_dim.6.gain_in
  16.8 219.9 %first.1 = (bf16[2,256,1536]{2,1,0:T(8,128)(2,1)}, bf16[2,512,1536]{2,1,0:T(8,128)(2,1)}, bf16[1024,1536]{1,0:T(8,128)(2,1)}, bf16[1024,768]{1,0:T(8,128)(2,1)},...) custom-call(bf16[2,256,1536]{2,1,0:T(8,128)(2,1)} %x_in.1, ...), custom_call_target="tpu_custom_call" | custom-call | tf_op jit(solution)/shard_map/first/pallas_call | solution.py:1539
  236.7 53.4 %hidden.1 = (bf16[2048,1024]{1,0:T(8,128)(2,1)}, bf16[2048,1024]{1,0:T(8,128)(2,1)}, bf16[2048,1024]{1,0:T(8,128)(2,1)}, f32[512,1536]{1,0:T(8,128)}, bf16[512,1...) custom-call(bf16[2048,1536]{1,0:T(8,128)(2,1)} %bitcast.102, bf16[2048,1536]{1,0:T(8,128)(2,1)} %bitcast.93, ...), custom_call_target="tpu_custom_call" | custom-call | flops 38654705664 | bytes 41943040 | tf_op jit(solution)/shard_map/hidden/pallas_call | solution.py:1669
  290.1 0.1 collective-permute-start
  290.2 11.8 %convolution_convert_fusion = bf16[1024,1536]{1,0:T(8,128)(2,1)} fusion(bf16[2048,1024]{1,0:T(8,128)(2,1)} %get-tuple-element.60, bf16[2048,1536]{1,0:T(8,128)(2,1)} %bitcast.94), kind=kOutput, calls=%fused_computation | convolution fusion | flops 6444023808 | bytes 13631488 | tf_op jit(solution)/shard_map/dot_general | solution.py:998
  302.0 8.2 %convolution_convert_fusion.1 = bf16[1536,1024]{1,0:T(8,128)(2,1)} fusion(bf16[2048,1536]{1,0:T(8,128)(2,1)S(1)} %bitcast.103, bf16[2048,1024]{1,0:T(8,128)(2,1)S(1)} %copy-done.11), kind=kOutput, calls=%fused_computation.1 | convolution fusion | flops 6444023808 | bytes 13631488 | tf_op jit(solution)/shard_map/dot_general | solution.py:998
  310.2 8.2 %convolution_convert_fusion.2 = bf16[1536,1024]{1,0:T(8,128)(2,1)} fusion(bf16[2048,1536]{1,0:T(8,128)(2,1)S(1)} %bitcast.104, bf16[2048,1024]{1,0:T(8,128)(2,1)S(1)} %copy-done.10), kind=kOutput, calls=%fused_computation.2 | convolution fusion | flops 6444023808 | bytes 13631488 | tf_op jit(solution)/shard_map/dot_general | solution.py:998
  318.4 2.7 slice.19
  321.1 0.7 broadcast_select_fusion.row_ref
  321.8 1.0 copy.33.col_ref
  322.8 4.0 collective-permute-done.back
  326.8 92.8 %behind.1 = (bf16[1024,1536]{1,0:T(8,128)(2,1)}, f32[512,1536]{1,0:T(8,128)}, bf16[2,512,1536]{2,1,0:T(8,128)(2,1)}, bf16[2,256,1536]{2,1,0:T(8,128)(2,1)}, bf16...) custom-call(bf16[1024,1536]{1,0:T(8,128)(2,1)} %get-tuple-element.48, ...), custom_call_target="tpu_custom_call" | custom-call | flops 6039797760 | bytes 9437184 | tf_op jit(solution)/shard_map/behind/pallas_call | solution.py:1224
  419.6 127.9 %tail.1 = (f32[2,2,48,1024]{3,2,1,0:T(8,128)}, f32[2,2,48,1024]{3,2,1,0:T(8,128)}, f32[128,1536]{1,0:T(8,128)}, f32[2,48,1536]{2,1,0:T(8,128)}, f32[48,1536]{1,0...) custom-call(f32[2,192,1024]{2,1,0:T(8,128)} %bitcast.87, ...), custom_call_target="tpu_custom_call" | custom-call | tf_op jit(solution)/shard_map/tail/pallas_call | solution.py:927
  547.6 1.1 slice_bitcast_fusion
  548.6 1.0 slice_bitcast_fusion.1
  549.6 1.3 copy.45
  550.9 0.6 copy.37
  551.5 1.5 reshape.142
  553.1 0.1 copy.46
  553.2 0.6 copy.38
  553.8 1.5 reshape.144
  555.3 0.7 copy.42
  556.1 0.7 copy.43
  556.7 0.7 copy.44
  557.4 0.7 constant_dynamic-slice_fusion
  558.1 0.5 slice_bitcast_fusion.3
  558.6 2.7 copy.59
  561.4 1.1 copy.60
  562.5 0.7 copy.61
  563.2 0.9 copy.62
  (24 shorter events, 0.1 us)
Async XLA Ops:
  0.6 320.4 %collective-permute-start.1 = (s32[2,1024]{1,0:T(2,128)}, s32[2,1024]{1,0:T(2,128)}, u32[]{:S(2)}, u32[]{:S(2)}) collective-permute-start(s32[2,1024]{1,0:T(2,128)} %param.16), channel_id=1, source_target_pairs={{0,1},{1,0},{2,3},{3,2},{4,5},{5,4},{6,7},{7,6},{8,9},{9,8},{10,11... | collective-permute-start | bytes 24584 | tf_op jit(solution)/shard_map/ppermute | solution.py:1703
  7.9 5.5 copy-start
  10.2 5.2 copy-start.8
  10.2 5.2 copy-start.9
  290.1 36.7 %collective-permute-start = (bf16[512,1536]{1,0:T(8,128)(2,1)}, bf16[512,1536]{1,0:T(8,128)(2,1)}, u32[]{:S(2)}, u32[]{:S(2)}) collective-permute-start(bf16[512,1536]{1,0:T(8,128)(2,1)} %get-tuple-element.57), channel_id=1, source_target_pairs={{0,2},{1,3},{2,0},{3,1},{4,6},{5,7},{6,4},{7,5},{8,10},{9,11},{10,... | collective-permute-start | bytes 4718600 | tf_op jit(solution)/shard_map/ppermute | solution.py:1703
  290.2 11.8 %copy-start.7 = (bf16[4,512,1536]{2,1,0:T(8,128)(2,1)S(1)}, bf16[4,512,1536]{2,1,0:T(8,128)(2,1)}, u32[]{:S(2)}) copy-start(bf16[4,512,1536]{2,1,0:T(8,128)(2,1)} %get-tuple-element.52) | copy-start | bytes 18874372
  290.2 11.8 %copy-start.11 = (bf16[2048,1024]{1,0:T(8,128)(2,1)S(1)}, bf16[2048,1024]{1,0:T(8,128)(2,1)}, u32[]{:S(2)}) copy-start(bf16[2048,1024]{1,0:T(8,128)(2,1)} %get-tuple-element.59) | copy-start | bytes 12582916
  302.0 8.2 %copy-start.10 = (bf16[2048,1024]{1,0:T(8,128)(2,1)S(1)}, bf16[2048,1024]{1,0:T(8,128)(2,1)}, u32[]{:S(2)}) copy-start(bf16[2048,1024]{1,0:T(8,128)(2,1)} %get-tuple-element.58) | copy-start | bytes 12582916
  318.4 2.7 copy-start.6
  321.8 5.0 copy-start.5
  547.6 5.5 copy-start.3
  553.8 7.5 %copy-start.1 = (bf16[2,256,1536]{2,1,0:T(8,128)(2,1)S(1)}, bf16[2,256,1536]{2,1,0:T(8,128)(2,1)}, u32[]{:S(2)}) copy-start(bf16[2,256,1536]{2,1,0:T(8,128)(2,1)} %get-tuple-element.107) | copy-start | bytes 4718596
  558.6 3.9 copy-start.4
  558.6 4.6 copy-start.2

commit v6 on v5

--- a/solution.py
+++ b/solution.py
@@ -1080,36 +1080,39 @@
 def behind_kernel(
     heads,
     kvs,
-    qkv_ref,
-    mixed,
     hidden,
     seed,
     back_own,
-    back,
-    ahead_own,
-    ahead_far,
-    out_w,
     gain_rows,
     cos_ref,
     sin_ref,
     row_ref,
     col_ref,
+    qkv_in,
+    mixed_in,
+    out_in,
+    back_far,
+    ahead_own,
+    ahead_far,
+    tokens,
+    seeds,
+    act_in,
     gate_in,
     up_in,
-    down_in,
     grad_ref,
     steep,
-    steep_low,
+    gain_ref,
     y_low,
     out_grad,
-    gain_ref,
     gate_out,
     up_out,
     down_out,
+    steep_low,
+    back_got,
     ahead_got,
-    keys,
-    gks,
-    gvs,
+    gate_sum,
+    up_sum,
+    down_sum,
     gate_held,
     up_held,
     down_held,
@@ -1121,127 +1124,225 @@
     y, x, zh, zl, core = me
     greet(me, (("x",), ("y",), ("core",), ("zl",)))
     move = Mover(me, sends, recvs)
-    sums = [
-        PlaneSum(move, total, held, y, x)
-        for total, held in ((gate_in, gate_held), (up_in, up_held), (down_in, down_held))
+    back_move = move.send(back_far, back_got, "zl")
+    ahead_move = move.later(ahead_far, ahead_got, "zl")
+    swap = move.later(steep_low.at[core], steep_low.at[core], "core")
+    gate, up, down = sums = [
+        PlaneSumHere(move, total, held, y, x)
+        for total, held in (
+            (gate_sum, gate_held), (up_sum, up_held), (down_sum, down_held)
+        )
     ]
-    for plane in sums:
-        plane.start()
-    ahead_move = move.send(ahead_far, ahead_got, "zl")
-    gain_ref[...] = jnp.zeros_like(gain_ref)
-    half_len = hidden.shape[0]
-
-    def norm_back(at):
-        grad = back_own[at, :] + back[at, :].astype(f32)
-        field = hidden[at, :]
-        inverse = lax.rsqrt(jnp.mean(field * field, axis=1, keepdims=True) + EPSILON)
-        unit = field * inverse
-        gain_ref[...] += jnp.sum(grad * unit, axis=0, keepdims=True)
-        scaled = grad * gain_rows[1:2, :]
-        centre = jnp.mean(scaled * unit, axis=1, keepdims=True)
-        value = seed[at, :].astype(f32) + inverse * (scaled - unit * centre)
-        steep[at, :] = value
-        steep_low[core, at, :] = value.astype(low)
-
-    by_rows(half_len, 16, norm_back)
-    swap = move.send(steep_low.at[core], steep_low.at[core], "core")
-    everything = pl.ds(0, qkv_ref.shape[0])
-    for j in range(kvs):
-        keys[j] = spun(head(qkv_ref, everything, heads + j), cos_ref[...], sin_ref[...]).astype(low)
-    gks[...] = jnp.zeros_like(gks)
-    gvs[...] = jnp.zeros_like(gvs)
-    swap.wait_recv()
-    per = half_len // QB
-    for i in range(2 * per):
-        at = pl.ds(i % per * QB, QB)
-        grad_ref[pl.ds(i * QB, QB), : heads * HD] = nt(steep_low[i // per, at, :], out_w[...]).astype(low)
-    for plane in sums:
-        plane.start_near()
-
-    def block(step, carry):
-        @pl.when(step == SPAN // QB - 1)
-        def _():
-            for plane in sums:
-                plane.pass_on()
-
-        work(step, SPAN)
-        return carry
-
-    def work(step, size):
-        behind_block(
-            heads, kvs, step, size, qkv_ref, grad_ref, cos_ref, sin_ref, row_ref, col_ref,
-            grad_ref, keys, gks, gvs,
-        )
-
-    for step in range(SPAN // QB - 1):
-        work(step, (step + 1) * QB)
-    lax.fori_loop(SPAN // QB - 1, qkv_ref.shape[0] // QB, block, 0)
-    width = 1.0 / math.sqrt(HD)
-    gk = [
-        spun(gks[j] * width, cos_ref[...], sin_ref[...], True).astype(low) for j in range(kvs)
-    ]
-    gv = [gvs[j].astype(low) for j in range(kvs)]
-    grad_ref[:, HD * heads :] = jnp.concatenate(gk + gv, axis=1)
-    rows = mixed.shape[1] // 4
-    for i in range(4):
-        lanes = pl.ds(i * rows, rows)
-        total = tn(mixed[pl.ds(0, half_len), lanes], steep_low[0])
-        total = total + tn(mixed[pl.ds(half_len, half_len), lanes], steep_low[1])
-        out_grad[pl.ds(i * rows, rows), :] = total.astype(low)
-    ahead_move.wait_recv()
-    quarter = half_len // 2
-    for q in range(2):
-
-        def add(at, q=q):
-            every = pl.ds(pl.multiple_of(q * quarter + at.start, 16), at.size)
-            value = hidden[every, :] + ahead_own[every, :] + ahead_got[q, at, :].astype(f32)
-            ahead_got[q, at, :] = value.astype(low)
-
-        by_rows(quarter, 16, add)
-    stored = move.local(ahead_got, y_low)
-    for plane, out in zip(sums, (gate_out, up_out, down_out)):
-
-        def write(at, value, out=out):
-            out[at, :] = value
-
-        plane.end(write)
-    stored.wait()
+    s, sx, sy, sd = gate.at
+    order = (sd, sx, sy, s)
+    half_len, width = hidden.shape
+    count, wide = gate_in.shape
+    block = gate_sum.shape[1]
+
+    def wide_part(gates, ups, pieces):
+        def column(i):
+            lanes = pl.ds(pl.multiple_of(order[i] * block, 128), block)
+            return move.quiet(tokens.at[:, lanes], pieces.at[i % 2])
+
+        columns = [column(i) for i in range(4)]
+        columns[0].start()
+        loads = [move.local(gate_in, gates), move.local(up_in, ups)]
+        for i in range(4):
+            columns[i].wait()
+            if i < 3:
+                columns[i + 1].start()
+            if i == 0:
+                loads[0].wait()
+            gate_sum[order[i]] = tn(pieces[i % 2], gates[...]).astype(low)
+            if i == 0:
+                gate.start()
+                loads[1].wait()
+            up_sum[order[i]] = tn(pieces[i % 2], ups[...]).astype(low)
+            if i == 0:
+                up.start()
+            if i == 2:
+                gate.start_near()
+                up.start_near()
+
+    pl.run_scoped(
+        wide_part,
+        pltpu.VMEM((count, wide), low),
+        pltpu.VMEM((count, wide), low),
+        pltpu.VMEM((2, count, block), low),
+    )
+    deep = down_sum.shape[1]
+
+    def deep_part(rows, pieces):
+        def column(i):
+            lanes = pl.ds(pl.multiple_of(order[i] * deep, 128), deep)
+            return move.quiet(act_in.at[:, lanes], pieces.at[i % 2])
+
+        columns = [column(i) for i in range(4)]
+        columns[0].start()
+        move.local(seeds, rows).wait()
+        for i in range(4):
+            columns[i].wait()
+            if i < 3:
+                columns[i + 1].start()
+            down_sum[order[i]] = tn(pieces[i % 2], rows[...]).astype(low)
+            if i == 0:
+                down.start()
+            if i == 2:
+                down.start_near()
+
+    pl.run_scoped(
+        deep_part,
+        pltpu.VMEM((count, width), low),
+        pltpu.VMEM((2, count, deep), low),
+    )
+    gate.pass_on()
+    up.pass_on()
+
+    def heads_part(qkv_ref, out_w, keys, gks, gvs):
+        loads = [move.local(qkv_in, qkv_ref), move.local(out_in, out_w)]
+        gain_ref[...] = jnp.zeros_like(gain_ref)
+        back_move.wait_recv()
+        ahead_move.start()
+
+        def norm_back(at):
+            grad = back_own[at, :] + back_got[at, :].astype(f32)
+            field = hidden[at, :]
+            inverse = lax.rsqrt(jnp.mean(field * field, axis=1, keepdims=True) + EPSILON)
+            unit = field * inverse
+            gain_ref[...] += jnp.sum(grad * unit, axis=0, keepdims=True)
+            scaled = grad * gain_rows[1:2, :]
+            centre = jnp.mean(scaled * unit, axis=1, keepdims=True)
+            value = seed[at, :].astype(f32) + inverse * (scaled - unit * centre)
+            steep[at, :] = value
+            steep_low[core, at, :] = value.astype(low)
+
+        by_rows(half_len, 16, norm_back)
+        swap.start()
+        for made in loads:
+            made.wait()
+        everything = pl.ds(0, 2 * half_len)
+        for j in range(kvs):
+            keys[j] = spun(
+                head(qkv_ref, everything, heads + j), cos_ref[...], sin_ref[...]
+            ).astype(low)
+        gks[...] = jnp.zeros_like(gks)
+        gvs[...] = jnp.zeros_like(gvs)
+        swap.wait_recv()
+        per = half_len // QB
+        for i in range(2 * per):
+            at = pl.ds(i % per * QB, QB)
+            part = nt(steep_low[i // per, at, :], out_w[...]).astype(low)
+            grad_ref[pl.ds(i * QB, QB), : heads * HD] = part
+        down.pass_on()
+
+        def work(step, size):
+            behind_block(
+                heads, kvs, step, size, qkv_ref, grad_ref, cos_ref, sin_ref, row_ref, col_ref,
+                grad_ref, keys, gks, gvs,
+            )
+
+        def one(step, carry):
+            work(step, SPAN)
+            return carry
+
+        for step in range(SPAN // QB - 1):
+            work(step, (step + 1) * QB)
+        lax.fori_loop(SPAN // QB - 1, 2 * half_len // QB, one, 0)
+        scale = 1.0 / math.sqrt(HD)
+        gk = [
+            spun(gks[j] * scale, cos_ref[...], sin_ref[...], True).astype(low)
+            for j in range(kvs)
+        ]
+        gv = [gvs[j].astype(low) for j in range(kvs)]
+        grad_ref[:, HD * heads :] = jnp.concatenate(gk + gv, axis=1)
+
+    pl.run_scoped(
+        heads_part,
+        pltpu.VMEM(qkv_in.shape, low),
+        pltpu.VMEM(out_in.shape, low),
+        pltpu.VMEM((kvs, 2 * half_len, HD), low),
+        pltpu.VMEM((kvs, 2 * half_len, HD), f32),
+        pltpu.VMEM((kvs, 2 * half_len, HD), f32),
+    )
+
+    def last_part(mixed, own, out_made, gate_made, up_made, down_made):
+        loads = [move.local(mixed_in, mixed), move.local(ahead_own, own)]
+        loads[0].wait()
+        rows = mixed.shape[1] // 4
+        for i in range(4):
+            lanes = pl.ds(i * rows, rows)
+            total = tn(mixed[pl.ds(0, half_len), lanes], steep_low[0])
+            total = total + tn(mixed[pl.ds(half_len, half_len), lanes], steep_low[1])
+            out_made[pl.ds(i * rows, rows), :] = total.astype(low)
+        stores = [move.local(out_made, out_grad)]
+        ahead_move.wait_recv()
+        loads[1].wait()
+        quarter = half_len // 2
+        for q in range(2):
+
+            def add(at, q=q):
+                every = pl.ds(pl.multiple_of(q * quarter + at.start, 16), at.size)
+                value = hidden[every, :] + own[every, :] + ahead_got[q, at, :].astype(f32)
+                ahead_got[q, at, :] = value.astype(low)
+
+            by_rows(quarter, 16, add)
+        stores.append(move.local(ahead_got, y_low))
+        for plane, made, out in zip(
+            sums, (gate_made, up_made, down_made), (gate_out, up_out, down_out)
+        ):
+
+            def write(at, value, made=made):
+                made[at, :] = value
+
+            plane.end(write)
+            stores.append(move.local(made, out))
+        for made in stores:
+            made.wait()
+
+    pl.run_scoped(
+        last_part,
+        pltpu.VMEM(mixed_in.shape, low),
+        pltpu.VMEM((half_len, width), f32),
+        pltpu.VMEM(out_grad.shape, low),
+        pltpu.VMEM(gate_out.shape, f32),
+        pltpu.VMEM(up_out.shape, f32),
+        pltpu.VMEM(down_out.shape, f32),
+    )
     move.finish()
 
 
 def attend_behind(heads, kvs, *operands):
     f32, low = jnp.float32, jnp.bfloat16
-    qkv, mixed, hidden = operands[:3]
-    totals = operands[-3:]
-    length, width = qkv.shape
-    half_len = length // 2
+    half_len, width = operands[0].shape
+    length = 2 * half_len
+    wide = operands[-1].shape[1]
     hbm = pl.BlockSpec(memory_space=pl.ANY)
     vmem = pl.BlockSpec(memory_space=pltpu.VMEM)
+    shapes = [(width // 4, wide), (width // 4, wide), (wide // 4, width)]
 
     def made(*shape, dtype=low):
         return jax.ShapeDtypeStruct(shape, dtype)
 
     return pl.pallas_call(
         functools.partial(behind_kernel, heads, kvs),
-        in_specs=[vmem] * 7 + [hbm] + [vmem] * 6 + [hbm] * 3,
-        out_specs=[vmem] * 3 + [hbm] + [vmem] * 5,
+        in_specs=[vmem] * 8 + [hbm] * 11,
+        out_specs=[vmem] * 3 + [hbm] * 5,
         out_shape=[
             made(length, width),
             made(half_len, width, dtype=f32),
-            made(2, half_len, width),
+            made(1, width, dtype=f32),
             made(2, half_len // 2, width),
             made(heads * HD, width),
-            made(1, width, dtype=f32),
         ]
-        + [made(*total.shape[1:], dtype=f32) for total in totals],
+        + [made(*shape, dtype=f32) for shape in shapes],
         scratch_shapes=[
+            pltpu.VMEM((2, half_len, width), low),
+            pltpu.VMEM((half_len, width), low),
             pltpu.VMEM((2, half_len // 2, width), low),
-            pltpu.VMEM((kvs, length, HD), low),
-            pltpu.VMEM((kvs, length, HD), f32),
-            pltpu.VMEM((kvs, length, HD), f32),
         ]
-        + [pltpu.VMEM((4,) + total.shape[1:], low) for total in totals]
-        + [pltpu.SemaphoreType.DMA((40,)), pltpu.SemaphoreType.DMA((40,))],
+        + [pltpu.VMEM((4,) + shape, low) for shape in shapes]
+        + [pltpu.VMEM((3,) + shape, low) for shape in shapes]
+        + [pltpu.SemaphoreType.DMA((64,)), pltpu.SemaphoreType.DMA((64,))],
         compiler_params=pltpu.CompilerParams(
             collective_id=3, has_side_effects=True, vmem_limit_bytes=63 << 20
         ),
@@ -1307,6 +1408,24 @@
     greet(me, HEAD_GROUPS)
     move = Mover(me, sends, recvs)
 
+    wides = [
+        (ref.at[:, at], bands(ref.shape[-1]))
+        for at in (zh, 1 - zh)
+        for ref in (gate_w, up_w, down_w)
+    ]
+    hops = [plane_make(move, ref, s, parts) for ref, parts in wides]
+    rest = []
+
+    def start_some(which):
+        for i in which:
+            for made in hops[i]:
+                made.start()
+
+    def pass_some(which):
+        for i in which:
+            rest.extend(plane_pass(move, hops[i], wides[i][0], y, x, wides[i][1]))
+
+    down_own = move.local(down_in, down_w.at[s, zh])
     own = [
         move.local(qkv_in.at[core], qkv_w.at[s, z, core]),
         move.local(gain_in, gains.at[s, z, core]),
@@ -1323,11 +1442,12 @@
         made.wait_recv()
     line = [move.send(gains.at[s, z], gains.at[s, z], *names) for names in LINE]
     line += [move.send(qkv_w.at[s, z], qkv_w.at[s, z], *names) for names in LINE]
+    down_own.wait()
+    start_some((2,))
 
     own = [
         move.local(gate_in.at[zl, core], gate_w.at[s, zh, zl, core]),
         move.local(up_in.at[zl, core], up_w.at[s, zh, zl, core]),
-        move.local(down_in, down_w.at[s, zh]),
     ]
     spread = []
     for src, dst in ((gate_in, gate_w), (up_in, up_w)):
@@ -1350,6 +1470,7 @@
     for made in line[3:]:
         made.wait_recv()
     qkv_hops = plane_start(move, qkv_w, s, bands(width))
+    pass_some((2,))
 
     out_line = [move.copy(out_w.at[x, z], out_w.at[x, z], *names) for names in LINE]
     pl.when(other)(out_sent.wait_send)
@@ -1409,28 +1530,15 @@
         out_x.start()
         out_y[0].start()
 
-    wides = [
-        (ref.at[:, at], bands(ref.shape[-1]))
-        for at in (zh, 1 - zh)
-        for ref in (gate_w, up_w, down_w)
-    ]
-    hops = [plane_make(move, ref, s, parts) for ref, parts in wides]
-
-    def start_some(which):
-        for i in which:
-            for made in hops[i]:
-                made.start()
-
+    g_turn = turn_start(move, me, g_in, seeds.at[0])
     normed_move.wait_recv()
     for made in qkv_rest:
         made.wait_recv()
-    g_turn = turn_start(move, me, g_in, seeds.at[0])
-    start_some((0,))
     weight = qkv_w.reshape(width, width)
     for i in range(length // QB):
         at = pl.ds(i * QB % half_len, QB)
         qkv[pl.ds(i * QB, QB), :] = nn(normed[i * QB // half_len, at, :], weight[...]).astype(low)
-    start_some((1, 2))
+    start_some((0,))
     seed_moves = [
         move.later(seeds.at[0], seeds.at[1], "core"),
         move.later(seeds.at[0], seeds.at[2], "zl"),
@@ -1449,9 +1557,12 @@
             turn_end(me, g_turn)
             for made in seed_moves:
                 made.start()
-            for made in pairs[:2]:
-                made.wait_recv()
-            start_some((3, 4))
+            start_some((1,))
+
+        @pl.when(step == SPAN // QB)
+        def _():
+            pairs[0].wait_recv()
+            start_some((3,))
 
         work(step, SPAN)
         return carry
@@ -1466,13 +1577,9 @@
     for step in range(1, SPAN // QB - 1):
         work(step, (step + 1) * QB)
     lax.fori_loop(SPAN // QB - 1, length // QB, block, 0)
-    pairs[2].wait_recv()
-    start_some((5,))
-    rest = []
-
-    def pass_some(which):
-        for i in which:
-            rest.extend(plane_pass(move, hops[i], wides[i][0], y, x, wides[i][1]))
+    for made in pairs[1:]:
+        made.wait_recv()
+    start_some((4, 5))
 
     @pl.when(mine)
     def _():
@@ -1496,7 +1603,6 @@
     project(theirs)
     part_move = move.copy(part, part_got, "core")
     part_move.start()
-    pass_some((0, 1, 2))
     for i in range(half_len // QB):
         at = pl.ds(pl.multiple_of(ours + i * QB, QB), QB)
         hidden[pl.ds(i * QB, QB), :] = nn(mixed[at, :], out_weight[...])
@@ -1515,6 +1621,7 @@
         move.send(tokens.at[0], tokens.at[2], "zl"),
         move.send(tokens.at[0], tokens.at[1], "core"),
     ]
+    pass_some((0, 1))
     seed_moves[1].wait_recv()
     seed_moves.append(move.send(seeds.at[2], seeds.at[3], "core"))
     pass_some((3, 4, 5))
@@ -1783,35 +1890,28 @@
     activated, gate_low, up_low, back_own, back_far, ahead_own, ahead_far = hidden_part(
         tokens, seeds, gate_w, up_w, down_w
     )
-    back = hop(back_far, "zl")
-    flat_tokens, flat_seeds = tokens.reshape(-1, width), seeds.reshape(-1, width)
-    grad_gate = tn(flat_tokens, gate_low).astype(low)
-    grad_up = tn(flat_tokens, up_low).astype(low)
-    grad_down = tn(activated, flat_seeds).astype(low)
-    totals = [
-        grad_gate.reshape(4, -1, units // 4),
-        grad_up.reshape(4, -1, units // 4),
-        grad_down.reshape(4, -1, width),
-    ]
-    back = after(back, *totals)
-    grad_qkv, steep, _, y_low, grad_out_w, gain_two, *sums = attend_behind(
+    grad_qkv, steep, gain_two, y_low, grad_out_w, *sums = attend_behind(
         heads,
         kvs,
-        pair,
-        mixed,
         hidden,
         seeds[0],
         back_own,
-        back,
-        ahead_own,
-        ahead_far.reshape(2, quarter, width),
-        out_w,
         gains,
         cosine,
         sine,
         row,
         col,
-        *totals,
+        pair,
+        mixed,
+        out_w,
+        back_far,
+        ahead_own,
+        ahead_far.reshape(2, quarter, width),
+        tokens.reshape(-1, width),
+        seeds.reshape(-1, width),
+        activated,
+        gate_low,
+        up_low,
     )
     hidden_grads = [None, None]
     hidden_grads[0], hidden_grads[1], grad_down, grad_qkv, grad_output, output, grad_input, gain = (

time: 568 us -> 522 us (0.919)
  matrix products: 28.2 us -> 0 us
  Pallas kernels: 494 us -> 485 us
    dot_general x3 -> x0, matrix products: 28.2 us -> none  [tn(): lax.dot_general(left, right, (((0,), (0,)), ((), ())), preferred_element_...]
    pallas_call x1, Pallas kernels: 220 us -> 208 us  [first_part(): pl.pallas_call(functools.partial(first_kernel, heads, kvs), in_specs=[hbm...]
  transfers between devices with their start and end apart: 2 -> 1, of which waited for: 1 -> 0; matrix products, arithmetic and copies ran while one was open for 9% -> 3% of each run, Pallas kernels for 48% -> 51%
where the time goes in v6:
time: 522 us; the launch traced here: 518 us
  Pallas kernels  485 us (93%)
  local copies, waits for them, and re-layouts  24.7 us (5%)
  other arithmetic  6.08 us (1%)
    pallas_call x1, Pallas kernels, first_part(): pl.pallas_call(functools.partial(first_kernel, heads, kvs), in_specs=[hbm...  208 us
    pallas_call x1, Pallas kernels, sum_tail(): pl.pallas_call(tail_kernel, in_specs=[vmem] * 11 + [hbm], out_specs=[vmem...  129 us
    pallas_call x1, Pallas kernels, attend_behind(): pl.pallas_call(functools.partial(behind_kernel, heads, kvs), in_specs=[vm...  94.7 us
    pallas_call x1, Pallas kernels, hidden_part(): pl.pallas_call(hidden_kernel, grid=(4 * per,), in_specs=[banded(width)] *...  53.6 us
  transfers between devices with their start and end apart: 1, of which 0 were waited for; matrix products, arithmetic and copies ran while one was open for 3% of the time, Pallas kernels for 51%

profile of v6, /device:TPU:0, one launch (start us, length us, event | category | flops | bytes accessed | tf_op | source)
XLA Modules:
  0.0 517.6 jit_solution(1392410339810761223)
XLA Ops:
  0.6 0.0 copy-start.6
  0.7 0.5 collective-permute-start
  1.2 1.3 broadcast_in_dim.14.docs_in
  2.5 0.7 convert_element_type.6
  3.2 0.9 copy.54
  4.1 1.3 reshape.111
  5.4 0.1 copy.53
  5.4 0.9 reshape.112.gate_in
  6.3 0.0 copy-start.9
  6.4 0.3 reshape.113
  6.6 0.1 copy.52
  6.7 0.9 reshape.114.up_in
  7.6 1.9 fusion
  9.6 0.1 fusion.3
  9.7 0.0 copy-done.9
  9.7 1.3 pad_maximum_fusion
  11.0 1.3 broadcast_multiply_fusion.g_in
  12.3 0.7 maximum_bitcast_fusion.qkv_in
  13.0 0.6 broadcast_in_dim.6.gain_in
  13.6 208.1 %first.1 = (bf16[2,256,1536]{2,1,0:T(8,128)(2,1)}, bf16[2,512,1536]{2,1,0:T(8,128)(2,1)}, bf16[1024,1536]{1,0:T(8,128)(2,1)}, bf16[1024,768]{1,0:T(8,128)(2,1)},...) custom-call(bf16[2,256,1536]{2,1,0:T(8,128)(2,1)} %x_in.1, ...), custom_call_target="tpu_custom_call" | custom-call | tf_op jit(solution)/shard_map/first/pallas_call | solution.py:1646
  221.7 53.6 %hidden.1 = (bf16[2048,1024]{1,0:T(8,128)(2,1)}, bf16[2048,1024]{1,0:T(8,128)(2,1)}, bf16[2048,1024]{1,0:T(8,128)(2,1)}, f32[512,1536]{1,0:T(8,128)}, bf16[512,1...) custom-call(bf16[2048,1536]{1,0:T(8,128)(2,1)} %bitcast.69, bf16[2048,1536]{1,0:T(8,128)(2,1)} %bitcast.66, ...), custom_call_target="tpu_custom_call" | custom-call | flops 38654705664 | bytes 41943040 | tf_op jit(solution)/shard_map/hidden/pallas_call | solution.py:1776
  275.3 0.0 copy-start.11
  275.4 2.7 slice.19
  278.0 0.0 collective-permute-done
  278.0 0.0 copy-start.10
  278.0 1.0 copy.33.col_ref
  279.1 94.7 %behind.1 = (bf16[1024,1536]{1,0:T(8,128)(2,1)}, f32[512,1536]{1,0:T(8,128)}, f32[1,1536]{1,0:T(1,128)}, bf16[2,256,1536]{2,1,0:T(8,128)(2,1)}, bf16[768,1536]{1...) custom-call(f32[512,1536]{1,0:T(8,128)} %get-tuple-element.47.hidden, ...), custom_call_target="tpu_custom_call" | custom-call | flops 6039797760 | bytes 9437184 | tf_op jit(solution)/shard_map/behind/pallas_call | solution.py:1326
  373.8 128.8 %tail.1 = (f32[2,2,48,1024]{3,2,1,0:T(8,128)}, f32[2,2,48,1024]{3,2,1,0:T(8,128)}, f32[128,1536]{1,0:T(8,128)}, f32[2,48,1536]{2,1,0:T(8,128)}, f32[48,1536]{1,0...) custom-call(f32[2,192,1024]{2,1,0:T(8,128)} %bitcast.79, ...), custom_call_target="tpu_custom_call" | custom-call | tf_op jit(solution)/shard_map/tail/pallas_call | solution.py:927
  502.7 1.1 slice_bitcast_fusion
  503.7 1.0 slice_bitcast_fusion.1
  504.7 0.8 constant_dynamic-slice_fusion
  505.5 0.5 slice_bitcast_fusion.3
  506.0 0.7 copy.44
  506.7 0.7 copy.42
  507.4 0.7 copy.43
  508.1 0.1 copy.45
  508.2 0.6 copy.37
  508.9 1.5 reshape.130
  510.4 0.0 copy-done.4
  510.4 0.1 copy.46
  510.5 0.0 copy-start.2
  510.5 0.6 copy.38
  511.1 1.5 reshape.132
  512.7 1.1 copy.59
  513.8 0.8 copy-done.1
  514.6 1.1 copy.60
  515.8 0.7 copy.61
  516.5 0.9 copy.62
  (23 shorter events, 0.1 us)
Async XLA Ops:
  0.6 5.7 %copy-start.6 = (bf16[48,4096]{1,0:T(8,128)(2,1)S(1)}, bf16[48,4096]{1,0:T(8,128)(2,1)}, u32[]{:S(2)}) copy-start(bf16[48,4096]{1,0:T(8,128)(2,1)} %param.24) | copy-start | bytes 1179652
  0.7 277.4 %collective-permute-start = (s32[2,1024]{1,0:T(2,128)}, s32[2,1024]{1,0:T(2,128)S(1)}, u32[]{:S(2)}, u32[]{:S(2)}) collective-permute-start(s32[2,1024]{1,0:T(2,128)} %param.16), channel_id=1, source_target_pairs={{0,1},{1,0},{2,3},{3,2},{4,5},{5,4},{6,7},{7,6},{8,9},{9,8},{10,11... | collective-permute-start | bytes 24584 | tf_op jit(solution)/shard_map/ppermute | solution.py:1810
  6.3 3.2 copy-start.12
  6.3 3.2 copy-start.13
  6.3 3.3 copy-start.8
  6.3 3.3 copy-start.9
  7.6 3.4 copy-start
  275.3 2.7 copy-start.11
  278.0 1.0 copy-start.10
  502.6 5.4 %copy-start.5 = (f32[2,2,48,1024]{3,2,1,0:T(8,128)S(1)}, f32[2,2,48,1024]{3,2,1,0:T(8,128)}, u32[]{:S(2)}) copy-start(f32[2,2,48,1024]{3,2,1,0:T(8,128)} %get-tuple-element.80) | copy-start | bytes 2359300
  508.2 2.1 copy-start.4
  510.5 2.1 copy-start.2
  512.7 2.0 copy-start.1
  514.6 1.1 copy-start.7
  514.6 1.9 copy-start.3

commit v7 on v6

--- a/solution.py
+++ b/solution.py
@@ -3,6 +3,7 @@
 
 import jax
 import jax.numpy as jnp
+import numpy as np
 from jax import lax
 from jax.experimental import pallas as pl
 from jax.experimental.pallas import tpu as pltpu
@@ -653,6 +654,28 @@
 
 
 def tail_kernel(
+    gate_hbm,
+    up_hbm,
+    down_hbm,
+    grad_hbm,
+    normed_hbm,
+    qkv_hbm,
+    x_hbm,
+    steep_hbm,
+    gain_rows,
+    gain_two,
+    out_hbm,
+    y_in,
+    gate_grad,
+    up_grad,
+    down_out,
+    query_grad,
+    key_grad,
+    value_grad,
+    out_out,
+    y_out,
+    x_out,
+    gain_out,
     gate_in,
     up_in,
     down_in,
@@ -661,18 +684,10 @@
     qkv_w,
     x_own,
     steep,
-    gain_rows,
-    gain_two,
     out_in,
-    y_in,
     gate_out,
     up_out,
-    down_out,
     qkv_out,
-    out_out,
-    y_out,
-    x_out,
-    gain_out,
     pair_low,
     pair_got,
     down_low,
@@ -701,8 +716,22 @@
     z = 2 * zh + zl
     mine = y == core
     other = jnp.logical_not(mine)
+    move = Mover(me, sends, recvs)
+    loads = [
+        move.local(src, dst)
+        for src, dst in (
+            (normed_hbm, normed),
+            (grad_hbm, grad_in),
+            (qkv_hbm, qkv_w),
+            (gate_hbm, gate_in),
+            (up_hbm, up_in),
+            (down_hbm, down_in),
+            (x_hbm, x_own),
+            (steep_hbm, steep),
+            (out_hbm, out_in),
+        )
+    ]
     greet(me, HEAD_GROUPS)
-    move = Mover(me, sends, recvs)
     qkv = PlaneSumHere(move, qkv_in, qkv_held, y, x)
     out_y = move.copy(out_in, out_got, "y")
     half_len = part.shape[0]
@@ -714,6 +743,8 @@
         total = total + tn(normed[1, :, lanes], grad_in[pl.ds(half_len, half_len), :])
         qkv_in[at] = total.astype(low)
 
+    for made in loads[:2]:
+        made.wait()
     weigh(qkv.at[3])
     qkv.start()
 
@@ -721,6 +752,8 @@
     weigh(qkv.at[2])
     qkv.start_near()
 
+    for made in loads[2:6]:
+        made.wait()
     pair_rows = pair_got.shape[1]
 
     def lower(src, dst, skip, count):
@@ -748,6 +781,8 @@
     part_move.start()
     weigh(qkv.at[0])
     qkv.pass_on()
+    for made in loads[6:]:
+        made.wait()
     pl.when(other)(out_y.start)
     y_turn = turn_start(move, me, y_in, y_out)
     part_move.wait()
@@ -913,6 +948,16 @@
     swap.wait_recv()
     for made in spread:
         made.wait_recv()
+    for parts, grad in ((gate_out, gate_grad), (up_out, up_grad)):
+        for i in range(grad.shape[1] // 128):
+            lanes = slice(i // 4 * 128, i // 4 * 128 + 128)
+            grad[:, i * 128 : (i + 1) * 128] = parts[i // 2 % 2, i % 2, :, lanes]
+    at = 0
+    for grad in (query_grad, key_grad, value_grad):
+        size = grad.shape[1] // 2
+        for c in range(2):
+            grad[:, c * size : (c + 1) * size] = qkv_out[c, :, at : at + size]
+        at += size
     move.finish()
 
 
@@ -926,20 +971,28 @@
     pair_rows, down_rows = gate.shape[1], down.shape[1]
     return pl.pallas_call(
         tail_kernel,
-        in_specs=[vmem] * 11 + [hbm],
-        out_specs=[vmem] * 5 + [hbm, hbm, vmem],
+        in_specs=[hbm] * 8 + [vmem] * 2 + [hbm] * 2,
+        out_specs=[vmem] * 7 + [hbm, hbm, vmem],
         out_shape=[
-            jax.ShapeDtypeStruct((2, 2, rows, wide), f32),
-            jax.ShapeDtypeStruct((2, 2, rows, wide), f32),
+            jax.ShapeDtypeStruct((rows, 4 * wide), f32),
+            jax.ShapeDtypeStruct((rows, 4 * wide), f32),
             jax.ShapeDtypeStruct((down_rows, width), f32),
-            jax.ShapeDtypeStruct((2, rows, width), f32),
+            jax.ShapeDtypeStruct((rows, width), f32),
+            jax.ShapeDtypeStruct((rows, width // 2), f32),
+            jax.ShapeDtypeStruct((rows, width // 2), f32),
             jax.ShapeDtypeStruct((rows, width), f32),
             jax.ShapeDtypeStruct(y_in.shape, low),
             jax.ShapeDtypeStruct(y_in.shape, low),
             jax.ShapeDtypeStruct((2, width), f32),
         ],
-        input_output_aliases={},
         scratch_shapes=[
+            pltpu.VMEM(one.shape, one.dtype)
+            for one in (gate, up, down, grad, normed, qkv_w, x_own, steep, out)
+        ]
+        + [
+            pltpu.VMEM((2, 2, rows, wide), f32),
+            pltpu.VMEM((2, 2, rows, wide), f32),
+            pltpu.VMEM((2, rows, width), f32),
             pltpu.VMEM((2, pair_rows, wide), low),
             pltpu.VMEM((2, pair_rows, wide), low),
             pltpu.VMEM((down_rows, width), low),
@@ -959,8 +1012,8 @@
             pltpu.VMEM((3,) + out.shape[2:], low),
             pltpu.VMEM((rows, width), f32),
             pltpu.VMEM((5, 2, width), f32),
-            pltpu.SemaphoreType.DMA((48,)),
-            pltpu.SemaphoreType.DMA((48,)),
+            pltpu.SemaphoreType.DMA((64,)),
+            pltpu.SemaphoreType.DMA((64,)),
         ],
         compiler_params=pltpu.CompilerParams(
             collective_id=4, has_side_effects=True, vmem_limit_bytes=63 << 20
@@ -1080,14 +1133,13 @@
 def behind_kernel(
     heads,
     kvs,
-    hidden,
-    seed,
-    back_own,
     gain_rows,
     cos_ref,
     sin_ref,
     row_ref,
     col_ref,
+    hidden_in,
+    back_in,
     qkv_in,
     mixed_in,
     out_in,
@@ -1099,14 +1151,19 @@
     act_in,
     gate_in,
     up_in,
-    grad_ref,
-    steep,
     gain_ref,
+    grad_out,
+    steep_out,
     y_low,
     out_grad,
     gate_out,
     up_out,
     down_out,
+    hidden,
+    seed,
+    back_own,
+    grad_ref,
+    steep,
     steep_low,
     back_got,
     ahead_got,
@@ -1164,12 +1221,20 @@
                 gate.start_near()
                 up.start_near()
 
+    half_loads = [
+        move.quiet(hidden_in, hidden),
+        move.quiet(back_in, back_own),
+        move.quiet(seeds.at[pl.ds(0, half_len)], seed),
+    ]
+    half_stores = [move.quiet(steep, steep_out), move.quiet(grad_ref, grad_out)]
     pl.run_scoped(
         wide_part,
         pltpu.VMEM((count, wide), low),
         pltpu.VMEM((count, wide), low),
         pltpu.VMEM((2, count, block), low),
     )
+    for made in half_loads:
+        made.start()
     deep = down_sum.shape[1]
 
     def deep_part(rows, pieces):
@@ -1201,6 +1266,8 @@
     def heads_part(qkv_ref, out_w, keys, gks, gvs):
         loads = [move.local(qkv_in, qkv_ref), move.local(out_in, out_w)]
         gain_ref[...] = jnp.zeros_like(gain_ref)
+        for made in half_loads:
+            made.wait()
         back_move.wait_recv()
         ahead_move.start()
 
@@ -1218,6 +1285,7 @@
 
         by_rows(half_len, 16, norm_back)
         swap.start()
+        half_stores[0].start()
         for made in loads:
             made.wait()
         everything = pl.ds(0, 2 * half_len)
@@ -1255,6 +1323,7 @@
         ]
         gv = [gvs[j].astype(low) for j in range(kvs)]
         grad_ref[:, HD * heads :] = jnp.concatenate(gk + gv, axis=1)
+        half_stores[1].start()
 
     pl.run_scoped(
         heads_part,
@@ -1296,7 +1365,7 @@
 
             plane.end(write)
             stores.append(move.local(made, out))
-        for made in stores:
+        for made in half_stores + stores:
             made.wait()
 
     pl.run_scoped(
@@ -1313,7 +1382,7 @@
 
 def attend_behind(heads, kvs, *operands):
     f32, low = jnp.float32, jnp.bfloat16
-    half_len, width = operands[0].shape
+    half_len, width = operands[5].shape
     length = 2 * half_len
     wide = operands[-1].shape[1]
     hbm = pl.BlockSpec(memory_space=pl.ANY)
@@ -1325,17 +1394,22 @@
 
     return pl.pallas_call(
         functools.partial(behind_kernel, heads, kvs),
-        in_specs=[vmem] * 8 + [hbm] * 11,
-        out_specs=[vmem] * 3 + [hbm] * 5,
+        in_specs=[vmem] * 5 + [hbm] * 13,
+        out_specs=[vmem] + [hbm] * 7,
         out_shape=[
+            made(1, width, dtype=f32),
             made(length, width),
             made(half_len, width, dtype=f32),
-            made(1, width, dtype=f32),
             made(2, half_len // 2, width),
             made(heads * HD, width),
         ]
         + [made(*shape, dtype=f32) for shape in shapes],
         scratch_shapes=[
+            pltpu.VMEM((half_len, width), f32),
+            pltpu.VMEM((half_len, width), low),
+            pltpu.VMEM((half_len, width), f32),
+            pltpu.VMEM((length, width), low),
+            pltpu.VMEM((half_len, width), f32),
             pltpu.VMEM((2, half_len, width), low),
             pltpu.VMEM((half_len, width), low),
             pltpu.VMEM((2, half_len // 2, width), low),
@@ -1364,15 +1438,32 @@
     kvs,
     x_in,
     g_in,
-    qkv_in,
-    gate_in,
-    up_in,
+    query_in,
+    key_in,
+    value_in,
+    gate_raw,
+    up_raw,
     down_in,
     out_in,
     gain_in,
     docs_in,
     cos_ref,
     sin_ref,
+    x_out,
+    normed_out,
+    qkv_out,
+    mixed_out,
+    hidden_out,
+    qkv_w_out,
+    out_w_out,
+    gain_rows,
+    row,
+    col,
+    seeds,
+    tokens,
+    gate_w,
+    up_w,
+    down_w,
     x_own,
     normed,
     qkv,
@@ -1380,15 +1471,11 @@
     hidden,
     qkv_w,
     out_w,
-    gain_rows,
-    seeds,
-    tokens,
-    gate_w,
-    up_w,
-    down_w,
+    token,
+    qkv_in,
+    gate_in,
+    up_in,
     docs,
-    row,
-    col,
     gains,
     keys,
     part,
@@ -1405,8 +1492,19 @@
     width = qkv_w.shape[-1]
     length = qkv.shape[0]
     half_len = length // 2
+    at = 0
+    for ref in (query_in, key_in, value_in):
+        size = ref.shape[1] // 2
+        for c in range(2):
+            qkv_in[c, :, at : at + size] = ref[:, c * size : (c + 1) * size]
+        at += size
+    for raw, parts in ((gate_raw, gate_in), (up_raw, up_in)):
+        for i in range(raw.shape[1] // 128):
+            lanes = slice(i // 4 * 128, i // 4 * 128 + 128)
+            parts[i // 2 % 2, i % 2, :, lanes] = raw[:, i * 128 : (i + 1) * 128]
     greet(me, HEAD_GROUPS)
     move = Mover(me, sends, recvs)
+    stores = []
 
     wides = [
         (ref.at[:, at], bands(ref.shape[-1]))
@@ -1464,6 +1562,7 @@
         made.wait_recv()
     gain_hops = [move.send(gains.at[s], gains.at[s], *names) for names in (("x",), ("y",))]
     turn_end(me, x_turn)
+    stores.append(move.local(x_own, x_out))
     gain_hops[0].wait_recv()
     sx = 2 * y + 1 - x
     gain_hops.append(move.send(gains.at[sx], gains.at[sx], "y"))
@@ -1534,10 +1633,12 @@
     normed_move.wait_recv()
     for made in qkv_rest:
         made.wait_recv()
+    stores += [move.local(normed, normed_out), move.local(qkv_w, qkv_w_out)]
     weight = qkv_w.reshape(width, width)
     for i in range(length // QB):
         at = pl.ds(i * QB % half_len, QB)
         qkv[pl.ds(i * QB, QB), :] = nn(normed[i * QB // half_len, at, :], weight[...]).astype(low)
+    stores.append(move.local(qkv, qkv_out))
     start_some((0,))
     seed_moves = [
         move.later(seeds.at[0], seeds.at[1], "core"),
@@ -1577,6 +1678,7 @@
     for step in range(1, SPAN // QB - 1):
         work(step, (step + 1) * QB)
     lax.fori_loop(SPAN // QB - 1, length // QB, block, 0)
+    stores.append(move.local(mixed, mixed_out))
     for made in pairs[1:]:
         made.wait_recv()
     start_some((4, 5))
@@ -1591,6 +1693,8 @@
     def _():
         for made in out_y:
             made.wait_recv()
+
+    stores.append(move.local(out_w, out_w_out))
 
     out_weight = out_w.reshape(width // 2, width)
     theirs, ours = (pl.multiple_of(c * half_len, half_len) for c in (1 - core, core))
@@ -1614,13 +1718,14 @@
             field = x_own[q, at, :].astype(f32) + (hidden[rows, :] + part_got[rows, :])
             hidden[rows, :] = field
             inverse = lax.rsqrt(jnp.mean(field * field, axis=1, keepdims=True) + EPSILON)
-            tokens[0, rows, :] = (field * inverse * gain_rows[1:2, :]).astype(low)
+            token[rows, :] = (field * inverse * gain_rows[1:2, :]).astype(low)
 
         by_rows(quarter, 16, norm)
     token_moves = [
-        move.send(tokens.at[0], tokens.at[2], "zl"),
-        move.send(tokens.at[0], tokens.at[1], "core"),
+        move.send(token, tokens.at[2], "zl"),
+        move.send(token, tokens.at[1], "core"),
     ]
+    stores += [move.local(token, tokens.at[0]), move.local(hidden, hidden_out)]
     pass_some((0, 1))
     seed_moves[1].wait_recv()
     seed_moves.append(move.send(seeds.at[2], seeds.at[3], "core"))
@@ -1629,10 +1734,14 @@
     token_moves.append(move.send(tokens.at[2], tokens.at[3], "core"))
     for made in rest + seed_moves[::2] + token_moves[1:]:
         made.wait_recv()
+    for made in stores:
+        made.wait()
     move.finish()
 
 
-def first_part(heads, kvs, x_in, g_in, qkv, gate, up, down, out, gain, docs, cosine, sine):
+def first_part(
+    heads, kvs, x_in, g_in, query, key, value, gate, up, down, out, gain, docs, cosine, sine
+):
     f32, low = jnp.float32, jnp.bfloat16
     rows, width = out.shape
     half_len = 2 * x_in.shape[1]
@@ -1643,41 +1752,51 @@
     def made(shape, dtype=low):
         return jax.ShapeDtypeStruct(shape, dtype)
 
+    qkv_shape = (2, rows, width)
+    quarter = (2, 2, rows, gate.shape[1] // 4)
+    kept = [
+        made(x_in.shape),
+        made((2, half_len, width)),
+        made((length, width)),
+        made((length, heads * HD)),
+        made((half_len, width), f32),
+        made((4, 4) + qkv_shape),
+        made((2, 4, 2) + out.shape),
+    ]
     return pl.pallas_call(
         functools.partial(first_kernel, heads, kvs),
-        in_specs=[hbm] * 8 + [vmem] * 3,
-        out_specs=[vmem] * 9 + [vmem] + [hbm] * 3,
-        out_shape=[
-            made(x_in.shape),
-            made((2, half_len, width)),
-            made((length, width)),
-            made((length, heads * HD)),
-            made((half_len, width), f32),
-            made((4, 4, 2) + qkv.shape[1:]),
-            made((2, 4, 2) + out.shape),
+        in_specs=[hbm] * 2 + [vmem] * 5 + [hbm] * 3 + [vmem] * 3,
+        out_specs=[hbm] * 7 + [vmem] * 3 + [hbm] * 5,
+        out_shape=kept
+        + [
             made((2, width), f32),
+            made((1, length), docs.dtype),
+            made((length, 1), docs.dtype),
             made((4,) + x_in.shape),
             made((4, half_len, width)),
-            made((4, 2, 2, 2) + gate.shape[2:]),
-            made((4, 2, 2, 2) + up.shape[2:]),
+            made((4, 2) + quarter),
+            made((4, 2) + quarter),
             made((4, 2) + down.shape),
         ],
-        scratch_shapes=[
+        scratch_shapes=[pltpu.VMEM(one.shape, one.dtype) for one in kept]
+        + [
+            pltpu.VMEM((half_len, width), low),
+            pltpu.VMEM(qkv_shape, low),
+            pltpu.VMEM(quarter, low),
+            pltpu.VMEM(quarter, low),
             pltpu.VMEM(docs.shape, docs.dtype),
-            pltpu.VMEM(docs.shape[1:], docs.dtype),
-            pltpu.VMEM(docs.shape[:0:-1], docs.dtype),
             pltpu.VMEM((4, 4, 2) + gain.shape, f32),
             pltpu.VMEM((kvs, length, HD), low),
             pltpu.VMEM((half_len, width), f32),
             pltpu.VMEM((half_len, width), f32),
-            pltpu.SemaphoreType.DMA((96,)),
-            pltpu.SemaphoreType.DMA((96,)),
+            pltpu.SemaphoreType.DMA((112,)),
+            pltpu.SemaphoreType.DMA((112,)),
         ],
         compiler_params=pltpu.CompilerParams(
             collective_id=1, has_side_effects=True, vmem_limit_bytes=60 << 20
         ),
         name="first",
-    )(x_in, g_in, qkv, gate, up, down, out, gain, docs, cosine, sine)
+    )(x_in, g_in, query, key, value, gate, up, down, out, gain, docs, cosine, sine)
 
 
 def hidden_kernel(
@@ -1805,23 +1924,10 @@
     )(tokens.reshape(-1, width), seeds.reshape(-1, width), gate_w, up_w, down_w)
 
 
-def hop(value, *names):
-    flip = sum(BITS[name] for name in names)
-    return lax.ppermute(value, AXES, [(i, i ^ flip) for i in range(32)])
-
-
-def after(value, *others):
-    return lax.optimization_barrier((value,) + others)[0]
-
-
-def in_order(mine, other, place, axis=0):
-    first = jnp.where(place == 0, mine, other)
-    second = jnp.where(place == 0, other, mine)
-    return jnp.concatenate([first, second], axis=axis)
-
-
-def pick(value, place, axis=0):
-    return lax.dynamic_index_in_dim(value, place, axis, keepdims=False)
+def rope_constants(length, width):
+    freqs = ROPE_BASE ** (-2.0 * np.arange(width // 2) / width)
+    angles = np.tile(np.arange(length)[:, None] * freqs[None, :], 2)
+    return np.cos(angles).astype(np.float32), np.sin(angles).astype(np.float32)
 
 
 def fast_body(
@@ -1848,59 +1954,61 @@
     rows = w_query.shape[0]
     units = w_gate.shape[1]
     heads, kvs = HEADS // 2, KV // 2
-    cosine, sine = rope_tables(length, HD)
-
-    def halves(weight):
-        return weight.reshape(rows, 2, -1)
+    cosine, sine = (jnp.asarray(table) for table in rope_constants(length, HD))
 
     masked = cotangent * token_mask.astype(low)[:, :, None]
-    qkv = jnp.concatenate([halves(w) for w in (w_query, w_key, w_value)], axis=2)
-    qkv = jnp.moveaxis(qkv, 1, 0)
-    gate_in, up_in = (
-        jnp.transpose(w.reshape(rows, units // 512, 2, 2, 128), (2, 3, 0, 1, 4)).reshape(
-            2, 2, rows, -1
-        )
-        for w in (w_gate, w_up)
-    )
     gain = jnp.concatenate([attn_gain, mlp_gain]).astype(f32)
     gain = jnp.broadcast_to(jnp.pad(gain, (0, 128 - 2 * rows)), (8, 128))
-    own, normed, pair, mixed, hidden, qkv_w, out_w, gains, seeds, tokens, gate_w, up_w, down_w = (
-        first_part(
-            heads,
-            kvs,
-            layer_input,
-            masked,
-            qkv,
-            gate_in,
-            up_in,
-            w_down,
-            w_output,
-            gain,
-            document_ids[:, None],
-            cosine,
-            sine,
-        )
+    (
+        own,
+        normed,
+        pair,
+        mixed,
+        hidden,
+        qkv_w,
+        out_w,
+        gains,
+        row,
+        col,
+        seeds,
+        tokens,
+        gate_w,
+        up_w,
+        down_w,
+    ) = first_part(
+        heads,
+        kvs,
+        layer_input,
+        masked,
+        w_query,
+        w_key,
+        w_value,
+        w_gate,
+        w_up,
+        w_down,
+        w_output,
+        gain,
+        document_ids[:, None],
+        cosine,
+        sine,
     )
     qkv_w, out_w = qkv_w.reshape(width, -1), out_w.reshape(-1, width)
     gate_w, up_w = gate_w.reshape(width, -1), up_w.reshape(width, -1)
     down_w = down_w.reshape(-1, width)
     seeds = seeds.reshape(4, half_len, width)
-    documents = pick(jnp.where(core == y, document_ids, hop(document_ids, "core")), x)
-    row, col = documents[None, :], documents[:, None]
     activated, gate_low, up_low, back_own, back_far, ahead_own, ahead_far = hidden_part(
         tokens, seeds, gate_w, up_w, down_w
     )
-    grad_qkv, steep, gain_two, y_low, grad_out_w, *sums = attend_behind(
+    gain_two, grad_qkv, steep, y_low, grad_out_w, *sums = attend_behind(
         heads,
         kvs,
-        hidden,
-        seeds[0],
-        back_own,
         gains,
         cosine,
         sine,
         row,
         col,
+        hidden,
+        back_own,
         pair,
         mixed,
         out_w,
@@ -1913,49 +2021,45 @@
         gate_low,
         up_low,
     )
-    hidden_grads = [None, None]
-    hidden_grads[0], hidden_grads[1], grad_down, grad_qkv, grad_output, output, grad_input, gain = (
-        sum_tail(
-            sums[0].reshape(2, -1, units // 4),
-            sums[1].reshape(2, -1, units // 4),
-            sums[2].reshape(2, -1, width),
-            grad_qkv,
-            normed,
-            qkv_w,
-            own,
-            steep,
-            gains,
-            gain_two,
-            grad_out_w.reshape(2, 4, 2, rows, width),
-            y_low,
-        )
+    (
+        gate_grad,
+        up_grad,
+        down_grad,
+        query_grad,
+        key_grad,
+        value_grad,
+        out_grad,
+        output,
+        grad_input,
+        gain,
+    ) = sum_tail(
+        sums[0].reshape(2, -1, units // 4),
+        sums[1].reshape(2, -1, units // 4),
+        sums[2].reshape(2, -1, width),
+        grad_qkv,
+        normed,
+        qkv_w,
+        own,
+        steep,
+        gains,
+        gain_two,
+        grad_out_w.reshape(2, 4, 2, rows, width),
+        y_low,
     )
-    hidden_grads = [
-        jnp.transpose(total.reshape(2, 2, rows, -1, 128), (2, 3, 0, 1, 4)).reshape(rows, units)
-        for total in hidden_grads
-    ]
-    cols = heads * HD
-
-    def columns(start, size):
-        return jnp.moveaxis(grad_qkv[:, :, start : start + size], 0, 1).reshape(rows, -1)
-
-    q_grad = columns(0, cols)
-    k_grad = columns(cols, kvs * HD)
-    v_grad = columns(cols + kvs * HD, kvs * HD)
     gain_one = lax.dynamic_slice_in_dim(gain, device * rows, rows, 1)
 
     return (
         output,
         grad_input,
         gain_one[0],
-        q_grad,
-        k_grad,
-        v_grad,
-        grad_output,
+        query_grad,
+        key_grad,
+        value_grad,
+        out_grad,
         gain_one[1],
-        hidden_grads[0],
-        hidden_grads[1],
-        grad_down,
+        gate_grad,
+        up_grad,
+        down_grad,
     )
 
 

time: 522 us -> 493 us (0.944)
  Pallas kernels: 485 us -> 468 us
  local copies, waits for them, and re-layouts: 24.7 us -> 11.9 us
    reshape x13 -> x0, local copies, waits for them, and re-layouts: 9.5 us -> none  [the longest x2 3.02 us: fast_body(): jnp.transpose(total.reshape(2, 2, rows, -1, 128), (2, 3, 0, 1, 4))]
    pallas_call x1, Pallas kernels: 208 us -> 200 us  [first_part(): pl.pallas_call(functools.partial(first_kernel, heads, kvs), in_specs=[hbm...]
    pallas_call x1, Pallas kernels: 129 us -> 123 us  [sum_tail(): pl.pallas_call(tail_kernel, in_specs=[hbm] * 8 + [vmem] * 2 + [hbm] * 2,...]
  transfers between devices with their start and end apart: 1 -> 0, of which waited for: 0 -> 0; matrix products, arithmetic and copies ran while one was open for 3% -> 0% of each run, Pallas kernels for 51% -> 0%
where the time goes in v7:
time: 493 us; the launch traced here: 485 us
  Pallas kernels  468 us (95%)
  local copies, waits for them, and re-layouts  11.9 us (2%)
    pallas_call x1, Pallas kernels, first_part(): pl.pallas_call(functools.partial(first_kernel, heads, kvs), in_specs=[hbm...  200 us
    pallas_call x1, Pallas kernels, sum_tail(): pl.pallas_call(tail_kernel, in_specs=[hbm] * 8 + [vmem] * 2 + [hbm] * 2,...  123 us
    pallas_call x1, Pallas kernels, attend_behind(): pl.pallas_call(functools.partial(behind_kernel, heads, kvs), in_specs=[vm...  91.4 us
    pallas_call x1, Pallas kernels, hidden_part(): pl.pallas_call(hidden_kernel, grid=(4 * per,), in_specs=[banded(width)] *...  53.8 us

profile of v7, /device:TPU:0, one launch (start us, length us, event | category | flops | bytes accessed | tf_op | source)
XLA Modules:
  0.0 484.7 jit_solution(10880672707021534634)
XLA Ops:
  0.6 0.0 copy-start.8
  0.7 0.0 copy-start.10
  0.7 0.0 copy-start.9
  0.7 0.7 convert_element_type.6
  1.4 2.7 broadcast_multiply_fusion.g_in
  4.1 0.0 copy-done.8
  4.1 0.6 broadcast_in_dim.8.docs_in
  4.7 0.0 copy-done.10
  4.7 0.0 copy-done.9
  4.7 0.1 fusion.1
  4.8 0.6 broadcast_in_dim.7.gain_in
  5.4 200.1 %first.1 = (bf16[2,256,1536]{2,1,0:T(8,128)(2,1)}, bf16[2,512,1536]{2,1,0:T(8,128)(2,1)}, bf16[1024,1536]{1,0:T(8,128)(2,1)}, bf16[1024,768]{1,0:T(8,128)(2,1)},...) custom-call(bf16[2,256,1536]{2,1,0:T(8,128)(2,1)} %x_in.1, ...), custom_call_target="tpu_custom_call" | custom-call | tf_op jit(solution)/shard_map/first/pallas_call | solution.py:1766
  205.5 53.8 %hidden.1 = (bf16[2048,1024]{1,0:T(8,128)(2,1)}, bf16[2048,1024]{1,0:T(8,128)(2,1)}, bf16[2048,1024]{1,0:T(8,128)(2,1)}, f32[512,1536]{1,0:T(8,128)}, bf16[512,1...) custom-call(bf16[2048,1536]{1,0:T(8,128)(2,1)} %bitcast.18, bf16[2048,1536]{1,0:T(8,128)(2,1)} %bitcast.16, ...), custom_call_target="tpu_custom_call" | custom-call | flops 38654705664 | bytes 41943040 | tf_op jit(solution)/shard_map/hidden/pallas_call | solution.py:1895
  259.3 91.4 %behind.1 = (f32[1,1536]{1,0:T(1,128)}, bf16[1024,1536]{1,0:T(8,128)(2,1)}, f32[512,1536]{1,0:T(8,128)}, bf16[2,256,1536]{2,1,0:T(8,128)(2,1)}, bf16[768,1536]{1...) custom-call(f32[2,1536]{1,0:T(2,128)} %get-tuple-element.51.gain_rows, ...), custom_call_target="tpu_custom_call" | custom-call | flops 6039797760 | bytes 9437184 | tf_op jit(solution)/shard_map/behind/pallas_call | solution.py:1395
  350.7 123.1 %tail.1 = (f32[48,4096]{1,0:T(8,128)}, f32[48,4096]{1,0:T(8,128)}, f32[128,1536]{1,0:T(8,128)}, f32[48,1536]{1,0:T(8,128)}, f32[48,768]{1,0:T(8,128)}, /*index=5...) custom-call(f32[2,192,1024]{2,1,0:T(8,128)} %bitcast.23, ...), custom_call_target="tpu_custom_call" | custom-call | tf_op jit(solution)/shard_map/tail/pallas_call | solution.py:972
  473.8 0.0 copy-start
  473.8 0.9 constant_dynamic-slice_fusion
  474.7 0.5 slice_bitcast_fusion
  475.2 0.0 copy-start.5
  475.2 2.7 copy.35
  477.9 0.0 copy-done
  477.9 0.0 copy-start.7
  477.9 0.0 copy-start.6
  477.9 0.0 copy-start.4
  477.9 0.0 copy-start.3
  477.9 1.1 copy.36
  479.1 0.0 copy-done.5
  479.1 0.0 copy-start.2
  479.1 0.0 copy-start.1
  479.1 0.7 copy.37
  479.8 0.0 copy-done.7
  479.8 0.7 copy.38
  480.5 0.0 copy-done.6
  480.5 0.7 copy.39
  481.1 0.0 copy-done.4
  481.1 0.7 copy.40
  481.9 0.0 copy-done.3
  481.9 0.9 copy.41
  482.7 0.0 copy-done.2
  482.7 0.9 copy.42
  483.6 0.0 copy-done.1
  483.6 0.9 copy.43
Async XLA Ops:
  0.6 3.5 copy-start.8
  0.7 4.1 copy-start.10
  0.7 4.0 copy-start.9
  473.8 4.1 copy-start
  475.2 3.9 copy-start.5
  477.9 1.9 copy-start.7
  477.9 2.6 copy-start.6
  477.9 3.2 copy-start.4
  477.9 3.9 copy-start.3
  479.1 3.6 copy-start.2
  479.1 4.5 copy-start.1

commit v8 on v7

--- a/solution.py
+++ b/solution.py
@@ -1620,7 +1620,11 @@
 
     qkv_rest = plane_pass(move, qkv_hops, qkv_w, y, x, bands(width))
     out_x = move.copy(out_w.at[x], out_w.at[x], "x")
-    out_y = [move.copy(out_w.at[at], out_w.at[at], "y") for at in (x, 1 - x)]
+    near, left, right = (
+        out_w.at[x], out_w.at[1 - x, ..., bands(width)[0]], out_w.at[x, ..., bands(width)[1]]
+    )
+    out_y = [move.copy(near, near, "y"), move.copy(left, left, "y")]
+    out_far = move.copy(right, right, "x")
 
     @pl.when(mine)
     def _():
@@ -1675,6 +1679,11 @@
         out_x.wait_recv()
         out_y[1].start()
 
+    @pl.when(other)
+    def _():
+        out_y[0].wait_recv()
+        out_far.start()
+
     for step in range(1, SPAN // QB - 1):
         work(step, (step + 1) * QB)
     lax.fori_loop(SPAN // QB - 1, length // QB, block, 0)
@@ -1691,8 +1700,8 @@
 
     @pl.when(other)
     def _():
-        for made in out_y:
-            made.wait_recv()
+        out_y[1].wait_recv()
+        out_far.wait()
 
     stores.append(move.local(out_w, out_w_out))
 

time: 493 us -> 483 us (0.980)
  Pallas kernels: 468 us -> 458 us
    pallas_call x1, Pallas kernels: 200 us -> 190 us  [first_part(): pl.pallas_call(functools.partial(first_kernel, heads, kvs), in_specs=[hbm...]
where the time goes in v8:
time: 483 us; the launch traced here: 475 us
  Pallas kernels  458 us (95%)
  local copies, waits for them, and re-layouts  11.9 us (2%)
    pallas_call x1, Pallas kernels, first_part(): pl.pallas_call(functools.partial(first_kernel, heads, kvs), in_specs=[hbm...  190 us
    pallas_call x1, Pallas kernels, sum_tail(): pl.pallas_call(tail_kernel, in_specs=[hbm] * 8 + [vmem] * 2 + [hbm] * 2,...  124 us
    pallas_call x1, Pallas kernels, attend_behind(): pl.pallas_call(functools.partial(behind_kernel, heads, kvs), in_specs=[vm...  91.5 us
    pallas_call x1, Pallas kernels, hidden_part(): pl.pallas_call(hidden_kernel, grid=(4 * per,), in_specs=[banded(width)] *...  53.3 us

profile of v8, /device:TPU:0, one launch (start us, length us, event | category | flops | bytes accessed | tf_op | source)
XLA Modules:
  0.0 474.8 jit_solution(4047367605993033610)
XLA Ops:
  0.6 0.0 copy-start.8
  0.7 0.0 copy-start.10
  0.7 0.0 copy-start.9
  0.7 0.7 convert_element_type.6
  1.4 2.7 broadcast_multiply_fusion.g_in
  4.1 0.0 copy-done.8
  4.1 0.6 broadcast_in_dim.8.docs_in
  4.7 0.0 copy-done.10
  4.7 0.0 copy-done.9
  4.7 0.1 fusion.1
  4.8 0.6 broadcast_in_dim.7.gain_in
  5.4 189.9 %first.1 = (bf16[2,256,1536]{2,1,0:T(8,128)(2,1)}, bf16[2,512,1536]{2,1,0:T(8,128)(2,1)}, bf16[1024,1536]{1,0:T(8,128)(2,1)}, bf16[1024,768]{1,0:T(8,128)(2,1)},...) custom-call(bf16[2,256,1536]{2,1,0:T(8,128)(2,1)} %x_in.1, ...), custom_call_target="tpu_custom_call" | custom-call | tf_op jit(solution)/shard_map/first/pallas_call | solution.py:1775
  195.3 53.3 %hidden.1 = (bf16[2048,1024]{1,0:T(8,128)(2,1)}, bf16[2048,1024]{1,0:T(8,128)(2,1)}, bf16[2048,1024]{1,0:T(8,128)(2,1)}, f32[512,1536]{1,0:T(8,128)}, bf16[512,1...) custom-call(bf16[2048,1536]{1,0:T(8,128)(2,1)} %bitcast.18, bf16[2048,1536]{1,0:T(8,128)(2,1)} %bitcast.16, ...), custom_call_target="tpu_custom_call" | custom-call | flops 38654705664 | bytes 41943040 | tf_op jit(solution)/shard_map/hidden/pallas_call | solution.py:1904
  248.7 91.5 %behind.1 = (f32[1,1536]{1,0:T(1,128)}, bf16[1024,1536]{1,0:T(8,128)(2,1)}, f32[512,1536]{1,0:T(8,128)}, bf16[2,256,1536]{2,1,0:T(8,128)(2,1)}, bf16[768,1536]{1...) custom-call(f32[2,1536]{1,0:T(2,128)} %get-tuple-element.51.gain_rows, ...), custom_call_target="tpu_custom_call" | custom-call | flops 6039797760 | bytes 9437184 | tf_op jit(solution)/shard_map/behind/pallas_call | solution.py:1395
  340.2 123.7 %tail.1 = (f32[48,4096]{1,0:T(8,128)}, f32[48,4096]{1,0:T(8,128)}, f32[128,1536]{1,0:T(8,128)}, f32[48,1536]{1,0:T(8,128)}, f32[48,768]{1,0:T(8,128)}, /*index=5...) custom-call(f32[2,192,1024]{2,1,0:T(8,128)} %bitcast.23, ...), custom_call_target="tpu_custom_call" | custom-call | tf_op jit(solution)/shard_map/tail/pallas_call | solution.py:972
  463.9 0.0 copy-start
  463.9 0.9 constant_dynamic-slice_fusion
  464.8 0.5 slice_bitcast_fusion
  465.3 0.0 copy-start.5
  465.3 2.7 copy.35
  468.0 0.0 copy-done
  468.0 0.0 copy-start.7
  468.0 0.0 copy-start.6
  468.0 0.0 copy-start.4
  468.0 0.0 copy-start.3
  468.0 1.1 copy.36
  469.2 0.0 copy-done.5
  469.2 0.0 copy-start.2
  469.2 0.0 copy-start.1
  469.2 0.7 copy.37
  469.9 0.0 copy-done.7
  469.9 0.7 copy.38
  470.6 0.0 copy-done.6
  470.6 0.7 copy.39
  471.2 0.0 copy-done.4
  471.2 0.7 copy.40
  471.9 0.0 copy-done.3
  471.9 0.9 copy.41
  472.8 0.0 copy-done.2
  472.8 0.9 copy.42
  473.7 0.0 copy-done.1
  473.7 0.9 copy.43
Async XLA Ops:
  0.6 3.5 copy-start.8
  0.7 4.1 copy-start.10
  0.7 4.0 copy-start.9
  463.9 4.1 copy-start
  465.3 3.9 copy-start.5
  468.0 1.9 copy-start.7
  468.0 2.6 copy-start.6
  468.0 3.2 copy-start.4
  468.0 3.9 copy-start.3
  469.2 3.6 copy-start.2
  469.2 4.5 copy-start.1

commit v9 on v8

--- a/solution.py
+++ b/solution.py
@@ -784,7 +784,6 @@
     for made in loads[6:]:
         made.wait()
     pl.when(other)(out_y.start)
-    y_turn = turn_start(move, me, y_in, y_out)
     part_move.wait()
     project(ours)
     gain_out[...] = jnp.zeros_like(gain_out)
@@ -856,6 +855,8 @@
         out_x_move.start()
         half(x)
 
+    pl.when(other)(out_y.wait_send)
+    y_turn = turn_start(move, me, y_in, y_out)
     gain_round(2)
 
     spread = []
@@ -939,7 +940,6 @@
 
     @pl.when(other)
     def _():
-        out_y.wait_send()
         out_swap.wait_recv()
 
     gain_round(5)
@@ -1664,11 +1664,6 @@
                 made.start()
             start_some((1,))
 
-        @pl.when(step == SPAN // QB)
-        def _():
-            pairs[0].wait_recv()
-            start_some((3,))
-
         work(step, SPAN)
         return carry
 
@@ -1688,9 +1683,9 @@
         work(step, (step + 1) * QB)
     lax.fori_loop(SPAN // QB - 1, length // QB, block, 0)
     stores.append(move.local(mixed, mixed_out))
-    for made in pairs[1:]:
+    for made in pairs:
         made.wait_recv()
-    start_some((4, 5))
+    start_some((3, 4, 5))
 
     @pl.when(mine)
     def _():

time: 483 us -> 483 us (level)
  no operation moved by 1% of the time
where the time goes in v9:
time: 483 us; the launch traced here: 475 us
  Pallas kernels  458 us (95%)
  local copies, waits for them, and re-layouts  11.9 us (2%)
    pallas_call x1, Pallas kernels, first_part(): pl.pallas_call(functools.partial(first_kernel, heads, kvs), in_specs=[hbm...  190 us
    pallas_call x1, Pallas kernels, sum_tail(): pl.pallas_call(tail_kernel, in_specs=[hbm] * 8 + [vmem] * 2 + [hbm] * 2,...  124 us
    pallas_call x1, Pallas kernels, attend_behind(): pl.pallas_call(functools.partial(behind_kernel, heads, kvs), in_specs=[vm...  91.5 us
    pallas_call x1, Pallas kernels, hidden_part(): pl.pallas_call(hidden_kernel, grid=(4 * per,), in_specs=[banded(width)] *...  53.3 us

profile of v9, /device:TPU:0, one launch (start us, length us, event | category | flops | bytes accessed | tf_op | source)
XLA Modules:
  0.0 474.8 jit_solution(9330409922566839020)
XLA Ops:
  0.6 0.0 copy-start.8
  0.7 0.0 copy-start.10
  0.7 0.0 copy-start.9
  0.7 0.7 convert_element_type.6
  1.4 2.7 broadcast_multiply_fusion.g_in
  4.1 0.0 copy-done.8
  4.1 0.6 broadcast_in_dim.8.docs_in
  4.7 0.0 copy-done.10
  4.7 0.0 copy-done.9
  4.7 0.1 fusion.1
  4.8 0.6 broadcast_in_dim.7.gain_in
  5.4 189.9 %first.1 = (bf16[2,256,1536]{2,1,0:T(8,128)(2,1)}, bf16[2,512,1536]{2,1,0:T(8,128)(2,1)}, bf16[1024,1536]{1,0:T(8,128)(2,1)}, bf16[1024,768]{1,0:T(8,128)(2,1)},...) custom-call(bf16[2,256,1536]{2,1,0:T(8,128)(2,1)} %x_in.1, ...), custom_call_target="tpu_custom_call" | custom-call | tf_op jit(solution)/shard_map/first/pallas_call | solution.py:1770
  195.3 53.3 %hidden.1 = (bf16[2048,1024]{1,0:T(8,128)(2,1)}, bf16[2048,1024]{1,0:T(8,128)(2,1)}, bf16[2048,1024]{1,0:T(8,128)(2,1)}, f32[512,1536]{1,0:T(8,128)}, bf16[512,1...) custom-call(bf16[2048,1536]{1,0:T(8,128)(2,1)} %bitcast.18, bf16[2048,1536]{1,0:T(8,128)(2,1)} %bitcast.16, ...), custom_call_target="tpu_custom_call" | custom-call | flops 38654705664 | bytes 41943040 | tf_op jit(solution)/shard_map/hidden/pallas_call | solution.py:1899
  248.7 91.5 %behind.1 = (f32[1,1536]{1,0:T(1,128)}, bf16[1024,1536]{1,0:T(8,128)(2,1)}, f32[512,1536]{1,0:T(8,128)}, bf16[2,256,1536]{2,1,0:T(8,128)(2,1)}, bf16[768,1536]{1...) custom-call(f32[2,1536]{1,0:T(2,128)} %get-tuple-element.51.gain_rows, ...), custom_call_target="tpu_custom_call" | custom-call | flops 6039797760 | bytes 9437184 | tf_op jit(solution)/shard_map/behind/pallas_call | solution.py:1395
  340.2 123.7 %tail.1 = (f32[48,4096]{1,0:T(8,128)}, f32[48,4096]{1,0:T(8,128)}, f32[128,1536]{1,0:T(8,128)}, f32[48,1536]{1,0:T(8,128)}, f32[48,768]{1,0:T(8,128)}, /*index=5...) custom-call(f32[2,192,1024]{2,1,0:T(8,128)} %bitcast.23, ...), custom_call_target="tpu_custom_call" | custom-call | tf_op jit(solution)/shard_map/tail/pallas_call | solution.py:972
  463.9 0.0 copy-start
  463.9 0.9 constant_dynamic-slice_fusion
  464.8 0.5 slice_bitcast_fusion
  465.3 0.0 copy-start.5
  465.3 2.7 copy.35
  468.0 0.0 copy-done
  468.0 0.0 copy-start.7
  468.0 0.0 copy-start.6
  468.0 0.0 copy-start.4
  468.0 0.0 copy-start.3
  468.0 1.1 copy.36
  469.2 0.0 copy-done.5
  469.2 0.0 copy-start.2
  469.2 0.0 copy-start.1
  469.2 0.7 copy.37
  469.9 0.0 copy-done.7
  469.9 0.7 copy.38
  470.6 0.0 copy-done.6
  470.6 0.7 copy.39
  471.2 0.0 copy-done.4
  471.2 0.7 copy.40
  471.9 0.0 copy-done.3
  471.9 0.9 copy.41
  472.8 0.0 copy-done.2
  472.8 0.9 copy.42
  473.7 0.0 copy-done.1
  473.7 0.9 copy.43
Async XLA Ops:
  0.6 3.5 copy-start.8
  0.7 4.1 copy-start.10
  0.7 4.0 copy-start.9
  463.9 4.1 copy-start
  465.3 3.9 copy-start.5
  468.0 1.9 copy-start.7
  468.0 2.6 copy-start.6
  468.0 3.2 copy-start.4
  468.0 3.9 copy-start.3
  469.2 3.6 copy-start.2
  469.2 4.5 copy-start.1
